TPU v7x, 256 devices: a whole 4x4x8 slice. The times are simulated.
256 devices in a mesh: seq: 8 (over z), files: 32 (over x, y, core).
Axes of the slice: x: 4, y: 4, z: 8, core: 2. Of those that a mesh axis runs over, the one named last changes fastest.
Arguments:
- q_lin: bfloat16 [32, 2048, 320], P('files', 'seq'), may hold values from -6 to 6
- k_lin: bfloat16 [32, 2048, 320], P('files', 'seq'), may hold values from -6 to 6
- v_lin: bfloat16 [32, 2048, 2560], P('files', 'seq'), may hold values from -6 to 6
- q_soft: bfloat16 [32, 2048, 1280], P('files', 'seq'), may hold values from -48 to 48
- k_soft: bfloat16 [32, 2048, 1280], P('files', 'seq'), may hold values from -6 to 6
- v_soft: bfloat16 [32, 2048, 1280], P('files', 'seq'), may hold values from -6 to 6
- import_ids: int32 [32, 8, 8], P('files', 'seq'), may hold values from -1 to 63, as said below
- import_counts: int32 [32, 8], P('files', 'seq'), may hold values from 6 to 8, as said below
Outputs:
- lin_out: bfloat16 [32, 2048, 2560], P('files', 'seq')
- soft_out: bfloat16 [32, 2048, 1280], P('files', 'seq')
Inputs may be any that keep to these rules, and one draw needn't show every extreme that they name: `import_ids`: entries before the count name distinct file groups other than the reader's own, entry = group * 2 + block; entries from the count on are -1. For each sequence shard index, some file group is listed before the count by every other file group's list of that index. `import_counts`: some sequence shard lists 8 blocks.
All inputs are finite; a program needn't handle non-finite values.
Results may differ from a plain program's by a relative error of at most 0.005.
Values may be sent and summed in bfloat16 or wider, within the bound.
No kernel may reach another device: no remote copies, remote signals or barrier semaphores. Data moves between devices by JAX's collectives and lax.ppermute only.
A program may use at most 192 MiB of HBM per device.

v0:
```python
import math

import jax
import jax.numpy as jnp
import numpy as np
from jax import lax
from jax.sharding import PartitionSpec as P

D = 2560
HEADS = 20
FEAT = 16
FEATS = 153
SM_HEADS = 10
SM_HD = 128
SM_W = 1280
BLK = 128


inv_root_two = 0.7071067811865476
highest_precision = lax.Precision.HIGHEST


def entering(part, axis, combine, identity):
    place = lax.axis_index(axis)
    gathered = jax.tree.map(lambda a: lax.all_gather(a, axis), part)
    state = jax.tree.map(lambda a, e: jnp.zeros_like(a) + jnp.asarray(e, a.dtype), part, identity)

    def one(lap, state):
        return combine(
            state, jax.tree.map(lambda a: lax.dynamic_index_in_dim(a, lap, 0, False), gathered)
        )

    return lax.fori_loop(0, place, one, state)


def feature_map(inputs):
    count_in = inputs.shape[-1]
    rows, cols = np.triu_indices(count_in)
    factor = np.where(rows == cols, inv_root_two, 1.0).astype(np.float32)
    quadratic = inputs[..., rows] * inputs[..., cols] * factor
    ones = jnp.ones(inputs.shape[:-1] + (1,), inputs.dtype)
    return jnp.concatenate([ones, inputs, quadratic], axis=-1)


def exclusive(values):
    shifted = jnp.concatenate([jnp.zeros_like(values[:1]), values[:-1]], axis=0)
    return jnp.cumsum(shifted, axis=0)


def add_pairs(earlier, later):
    return (earlier[0] + later[0], earlier[1] + later[1])


def carried_prefix(running_state, norm_sum):
    empty = (jnp.zeros_like(running_state), jnp.zeros_like(norm_sum))
    return entering((running_state, norm_sum), "seq", add_pairs, empty)


def linear_layer(query_rows, key_rows, value_rows, tokens, blocks):
    head_dim = D // HEADS
    causal_masking = jnp.tril(jnp.ones((BLK, BLK), jnp.float32))
    feat_q = feature_map(query_rows.astype(jnp.float32).reshape(tokens, HEADS, FEAT) * 0.5).astype(
        jnp.bfloat16
    )
    feat_k = feature_map(key_rows.astype(jnp.float32).reshape(tokens, HEADS, FEAT) * 0.5).astype(
        jnp.bfloat16
    )
    feat_q = feat_q.reshape(blocks, BLK, HEADS, FEATS)
    feat_k = feat_k.reshape(blocks, BLK, HEADS, FEATS)
    values = value_rows.reshape(blocks, BLK, HEADS, head_dim)
    weight_matrix = (
        jnp.einsum("bqhf,bkhf->bhqk", feat_q, feat_k, preferred_element_type=jnp.float32)
        * causal_masking
    )
    local_num = jnp.einsum(
        "bhqk,bkhd->bqhd",
        weight_matrix.astype(jnp.bfloat16),
        values,
        preferred_element_type=jnp.float32,
    )
    block_states = jnp.einsum("bkhf,bkhd->bhfd", feat_k, values, preferred_element_type=jnp.float32)
    block_norms = jnp.sum(feat_k.astype(jnp.float32), axis=1)
    carried_state, carried_norm = carried_prefix(
        jnp.sum(block_states, axis=0), jnp.sum(block_norms, axis=0)
    )
    state_in = carried_state[None] + exclusive(block_states)
    norm_in = carried_norm[None] + exclusive(block_norms)
    feat_q32 = feat_q.astype(jnp.float32)
    carried_term = jnp.einsum("bqhf,bhfd->bqhd", feat_q32, state_in, precision=highest_precision)
    denominator = jnp.transpose(jnp.sum(weight_matrix, axis=-1), (0, 2, 1))
    denominator = denominator + jnp.einsum(
        "bqhf,bhf->bqh", feat_q32, norm_in, precision=highest_precision
    )
    output = (local_num + carried_term) / denominator[..., None]
    return output.astype(jnp.bfloat16).reshape(1, tokens, D)


def owner_selection(import_ids, import_counts, blocks):
    list_len = import_ids.shape[2]
    all_ids, all_counts = (
        lax.all_gather(import_ids, "files", axis=0, tiled=True),
        lax.all_gather(import_counts, "files", axis=0, tiled=True),
    )
    id_rows = all_ids[:, 0, :]
    listed = jnp.arange(list_len)[None, :] < all_counts
    myself = lax.axis_index("files")
    wanted = listed & (id_rows // blocks == myself)
    local_code = jnp.sum(jnp.where(wanted, id_rows % blocks + 1, 0), axis=1)
    return (jnp.arange(blocks)[None, :] + 1 == local_code[:, None]).astype(jnp.bfloat16)


def softmax_layer(q_soft, k_soft, v_soft, import_ids, import_counts, tokens, blocks):
    groups = lax.axis_size("files")
    list_len = import_ids.shape[2]
    scale = 1.0 / math.sqrt(SM_HD)
    selection = owner_selection(import_ids, import_counts, blocks)
    key_blocks = k_soft[0].reshape(blocks, BLK * SM_W)
    value_blocks = v_soft[0].reshape(blocks, BLK * SM_W)
    send_keys = jnp.einsum(
        "rj,jc->rc", selection, key_blocks, preferred_element_type=jnp.bfloat16
    ).reshape(groups, BLK, SM_W)
    send_values = jnp.einsum(
        "rj,jc->rc", selection, value_blocks, preferred_element_type=jnp.bfloat16
    ).reshape(groups, BLK, SM_W)
    recv_keys, recv_values = (
        lax.all_to_all(send_keys, "files", split_axis=0, concat_axis=0, tiled=True),
        lax.all_to_all(send_values, "files", split_axis=0, concat_axis=0, tiled=True),
    )
    id_row = import_ids[0, 0]
    listed = jnp.arange(list_len) < import_counts[0, 0]
    owners = jnp.maximum(id_row, 0) // blocks
    imp_keys = jnp.take(recv_keys, owners, axis=0).reshape(list_len * BLK, SM_HEADS, SM_HD)
    key_valid = jnp.repeat(listed, BLK)
    queries = q_soft[0].reshape(tokens, SM_HEADS, SM_HD)
    own_q = q_soft[0].reshape(blocks, BLK, SM_HEADS, SM_HD)
    own_k = k_soft[0].reshape(blocks, BLK, SM_HEADS, SM_HD)
    own_v = v_soft[0].reshape(blocks, BLK, SM_HEADS, SM_HD)
    own_scores = (
        jnp.einsum("bqhd,bkhd->hbqk", own_q, own_k, preferred_element_type=jnp.float32) * scale
    )
    own_scores = own_scores.reshape(SM_HEADS, tokens, BLK)
    imp_scores = (
        jnp.einsum("qhd,khd->hqk", queries, imp_keys, preferred_element_type=jnp.float32) * scale
    )
    imp_scores = jnp.where(key_valid[None, None, :], imp_scores, -jnp.inf)
    top = jnp.maximum(jnp.max(own_scores, axis=-1), jnp.max(imp_scores, axis=-1))
    own_prob = jnp.exp(own_scores - top[..., None])
    imp_prob = jnp.exp(imp_scores - top[..., None])
    total = jnp.sum(own_prob, axis=-1) + jnp.sum(imp_prob, axis=-1)
    own_prob4 = own_prob.astype(jnp.bfloat16).reshape(SM_HEADS, blocks, BLK, BLK)
    own_num = jnp.einsum("hbqk,bkhd->bqhd", own_prob4, own_v, preferred_element_type=jnp.float32)
    own_num = own_num.reshape(tokens, SM_HEADS, SM_HD)
    imp_prob_b = imp_prob.astype(jnp.bfloat16)
    imp_values = jnp.take(recv_values, owners, axis=0).reshape(list_len * BLK, SM_HEADS, SM_HD)
    imp_num = jnp.einsum("hqk,khd->qhd", imp_prob_b, imp_values, preferred_element_type=jnp.float32)
    output = (own_num + imp_num) / total.T[..., None]
    return output.astype(jnp.bfloat16).reshape(1, tokens, SM_W)


def body(q_lin, k_lin, v_lin, q_soft, k_soft, v_soft, import_ids, import_counts):
    tokens = q_lin.shape[1]
    blocks = tokens // BLK
    lin_out = linear_layer(q_lin[0], k_lin[0], v_lin[0], tokens, blocks)
    soft_out = softmax_layer(q_soft, k_soft, v_soft, import_ids, import_counts, tokens, blocks)
    return (lin_out, soft_out)


def solution(mesh):
    placed = (
        P("files", "seq", None),
        P("files", "seq", None),
        P("files", "seq", None),
        P("files", "seq", None),
        P("files", "seq", None),
        P("files", "seq", None),
        P("files", "seq", None),
        P("files", "seq"),
    )
    return jax.shard_map(
        body,
        mesh=mesh,
        in_specs=placed,
        out_specs=(P("files", "seq", None), P("files", "seq", None)),
        check_vma=False,
    )
```

profile of v0, /device:TPU:236, one launch (start us, length us, event | category | flops | bytes accessed | tf_op | source)
XLA Modules:
  0.0 479.6 jit_solution(2510680406660428192)
XLA Ops:
  7.8 1.3 dynamic-slice
  9.1 0.7 bitcast_dynamic-update-slice_fusion
  9.8 13.4 %all-reduce = s32[32]{0:T(128)S(1)} all-reduce(s32[32]{0:T(128)S(1)} %bitcast_dynamic-update-slice_fusion), channel_id=1, replica_groups=mesh['seq'=8,'files'=32] {'files'}, use_global_device_ids=true, to_apply=%add | all-reduce | flops 32 | bytes 256
  23.2 21.5 %all_gather.23 = s32[32,1,8]{2,1,0:T(1,128)S(1)} all-gather(s32[1,1,8]{2,1,0:T(1,128)} %param.28), channel_id=1, replica_groups=mesh['seq'=8,'files'=32] {'files'}, dimensions={0}, use_global_device_ids=true | all-gather | bytes 1056 | tf_op jit(solution)/shard_map/all_gather | solution.py:101
  44.7 1.2 reshape_squeeze.24
  46.1 5.8 %fusion.58 = bf16[32,128,1280]{2,0,1:T(8,128)(2,1)} fusion(bf16[128,1280,2]{1,2,0:T(2,128)(2,1)S(1)} %bitcast.113, s32[32]{0:T(128)S(1)} %fusion.52, s32[2]{0:T(128)S(1)} %iota_add_fusion), kind=kOutput, calls=%fused_computation.94 | convolution fusion | flops 20971584 | bytes 11141256 | tf_op jit(solution)/shard_map/rj,jc->rc/dot_general | solution.py:119
  51.9 13.7 %copy.117 = bf16[32,128,1280]{2,1,0:T(8,128)(2,1)} copy(bf16[32,128,1280]{2,0,1:T(8,128)(2,1)} %fusion.58) | data formatting | bytes 20971520 | tf_op jit(solution)/shard_map/rj,jc->rc/dot_general | solution.py:119
  65.5 7.0 %all-to-all-start = ((bf16[32,128,1280]{2,1,0:T(8,128)(2,1)}), bf16[32,128,1280]{2,1,0:T(8,128)(2,1)}, u32[]{:S(2)}, u32[]{:S(2)}) async-start(bf16[32,128,1280]{2,1,0:T(8,128)(2,1)} %copy.117), calls=%async_computation | async-start | bytes 20971520 | tf_op jit(solution)/shard_map/all_to_all | solution.py:126
  73.1 2.6 gather_fusion
  75.7 2.6 gather_fusion.1
  78.3 0.7 fusion.44
  79.2 2.5 gather_fusion.2
  81.8 2.6 gather_fusion.3
  84.3 5.2 %multiply_bitcast_fusion.1 = f32[256,20,136]{0,1,2:T(8,128)} fusion(f32[136,256,20]{1,2,0:T(8,128)} %gather_fusion, f32[136,256,20]{1,2,0:T(8,128)} %gather_fusion.1), kind=kLoop, calls=%fused_computation.22 | loop fusion | flops 696320 | bytes 8355840 | tf_op jit(solution)/shard_map/mul | solution.py:40
  89.5 5.3 %reshape.185 = f32[2,128,20,136]{1,0,2,3:T(2,128)} reshape(f32[256,20,136]{0,1,2:T(8,128)} %multiply_bitcast_fusion.1) | data formatting | bytes 5570560 | tf_op jit(solution)/shard_map/mul | solution.py:40
  94.8 4.1 multiply_bitcast_fusion
  98.9 5.2 %reshape.186 = f32[2,128,20,136]{1,0,2,3:T(2,128)} reshape(f32[256,20,136]{0,1,2:T(8,128)} %multiply_bitcast_fusion) | data formatting | bytes 5570560 | tf_op jit(solution)/shard_map/mul | solution.py:40
  104.1 0.8 reshape.187
  105.0 4.9 %fusion.11 = (bf16[2,128,20,136]{1,3,2,0:T(8,128)(2,1)S(1)}, bf16[2,128,20,136]{1,3,2,0:T(8,128)(2,1)}) fusion(f32[2,128,20,136]{1,0,2,3:T(2,128)} %reshape.186, f32[136]{0:T(256)S(1)} %copy-done.16, f32[2,128,20,136]{1,0,2,3:T(2,128)} %reshape.185), kind=kLoop, calls=%fused_computation.26 | loop fusion | flops 2785280 | bytes 8356384 | tf_op jit(solution)/shard_map/convert.2
  109.9 3.8 fusion.69
  113.7 2.1 reshape_squeeze.27
  115.8 7.1 %fusion.56 = bf16[32,128,1280]{2,0,1:T(8,128)(2,1)} fusion(bf16[128,1280,2]{1,2,0:T(2,128)(2,1)} %bitcast.114, s32[32]{0:T(128)S(1)} %fusion.52, s32[2]{0:T(128)S(1)} %iota_add_fusion), kind=kOutput, calls=%fused_computation.92 | convolution fusion | flops 20971584 | bytes 11141256 | tf_op jit(solution)/shard_map/rj,jc->rc/dot_general | solution.py:122
  123.0 14.2 %copy.126 = bf16[32,128,1280]{2,1,0:T(8,128)(2,1)} copy(bf16[32,128,1280]{2,0,1:T(8,128)(2,1)} %fusion.56) | data formatting | bytes 20971520 | tf_op jit(solution)/shard_map/rj,jc->rc/dot_general | solution.py:122
  137.2 97.9 %all-to-all-done = bf16[32,128,1280]{2,1,0:T(8,128)(2,1)} async-done(((bf16[32,128,1280]{2,1,0:T(8,128)(2,1)}), bf16[32,128,1280]{2,1,0:T(8,128)(2,1)}, u32[]{:S(2)}, u32[]{:S(2)}) %all-to-all-start) | async-done | bytes 10485792 | tf_op jit(solution)/shard_map/all_to_all | solution.py:126
  235.1 5.9 %all-to-all-start.1 = ((bf16[32,128,1280]{2,1,0:T(8,128)(2,1)}), bf16[32,128,1280]{2,1,0:T(8,128)(2,1)}, u32[]{:S(2)}, u32[]{:S(2)}) async-start(bf16[32,128,1280]{2,1,0:T(8,128)(2,1)} %copy.126), calls=%async_computation.1 | async-start | bytes 20971520 | tf_op jit(solution)/shard_map/all_to_all | solution.py:127
  241.0 2.2 copy.119
  243.1 2.2 reshape.189
  245.4 2.2 reshape.190
  247.6 2.2 reshape.192
  249.8 3.2 fusion.70
  253.2 2.3 convert_reduce_fusion
  255.5 24.9 %all-gather.2 = f32[8,20,153]{2,1,0:T(8,128)S(1)} all-gather(f32[1,20,153]{2,1,0:T(8,128)S(1)} %bitcast.119), channel_id=3, replica_groups=mesh['seq'=8,'files'=32] {'seq'}, dimensions={0}, use_global_device_ids=true | all-gather | bytes 110160 | tf_op jit(solution)/shard_map/all_gather | solution.py:25
  280.4 0.7 compare_and_fusion
  281.1 0.7 broadcast_bitcast_fusion
  281.7 3.9 multiply_reduce_fusion
  285.6 2.1 fusion.19
  287.7 2.1 fusion.28
  289.8 6.2 %gather_fusion.4 = bf16[8,128,1280]{2,1,0:T(8,128)(2,1)} fusion(bf16[32,128,1280]{2,1,0:T(8,128)(2,1)} %all-to-all-done, s32[1024]{0:T(1024)S(1)} %pad_clamp_fusion), kind=kCustom, calls=%fused_computation.clone | custom fusion | bytes 5242912 | tf_op jit(solution)/shard_map/jit(_take)/gather | solution.py:132
  296.0 107.5 %all-to-all-done.1 = bf16[32,128,1280]{2,1,0:T(8,128)(2,1)} async-done(((bf16[32,128,1280]{2,1,0:T(8,128)(2,1)}), bf16[32,128,1280]{2,1,0:T(8,128)(2,1)}, u32[]{:S(2)}, u32[]{:S(2)}) %all-to-all-start.1) | async-done | bytes 10485792 | tf_op jit(solution)/shard_map/all_to_all | solution.py:127
  403.5 6.2 %gather_fusion.5 = bf16[8,128,1280]{2,1,0:T(8,128)(2,1)} fusion(bf16[32,128,1280]{2,1,0:T(8,128)(2,1)} %all-to-all-done.1, s32[1024]{0:T(1024)S(1)} %pad_clamp_fusion), kind=kCustom, calls=%fused_computation.1.clone | custom fusion | bytes 5242912 | tf_op jit(solution)/shard_map/jit(_take)/gather | solution.py:154
  409.6 4.5 broadcast_select_fusion
  414.2 3.3 reshape.191
  417.4 8.0 %bitcast_reduce_fusion = (f32[10,256]{1,0:T(8,128)S(1)}, f32[10,1024,256]{2,1,0:T(8,128)}) fusion(pred[1024]{0:T(1024)(128)(4,1)} %broadcast_bitcast_fusion, bf16[256,10,128]{0,2,1:T(8,128)(2,1)S(1)} %bitcast.117, bf16[1024,10,128]{2,1,0:T(8,128)(2,1)} %reshape.191), kind=kOutput, calls=%fused_computation.9 | convolution fusion | flops 678950400 | bytes 13773824 | tf_op jit(solution)/shard_map/qhd,khd->hqk/dot_general | solution.py:143
  425.5 0.3 fusion.30
  425.8 0.4 convolution_bitcast_fusion
  426.3 1.5 copy.129
  427.8 4.0 copy.127
  431.8 3.2 reshape.115
  435.1 6.1 %fusion.1 = f32[10,256]{1,0:T(8,128)S(1)} fusion(f32[10,1024,256]{2,1,0:T(8,128)} %get-tuple-element.80, f32[10,256]{1,0:T(8,128)S(1)} %max.16, pred[1024]{0:T(1024)(128)(4,1)S(1)} %copy-done.19), kind=kLoop, calls=%fused_computation.12 | loop fusion | flops 10483200 | bytes 10507264 | tf_op jit(solution)/shard_map/reduce_sum | solution.py:149
  441.2 6.5 %divide_convert_fusion = bf16[256,10,128]{0,2,1:T(8,128)(2,1)S(1)} fusion(f32[256,10,128]{0,2,1:T(8,128)S(1)} %copy-done.8, bf16[1024,10,128]{0,2,1:T(8,128)(2,1)S(1)} %copy-done.5, f32[10,1024,256]{2,1,0:T(8,128)} %get-tuple-element.80, f32[10,256]{1,0:T(8,128)S(1)} %max.16, pred[1024]{0:T(1024)(128)(4,1)S(1)} %copy-done.19, f32[256,10]{0,1:T(8,128)S(1)} %add_bitcast_fusion), kind=kOutput, calls=%fused_computation.48 | convolution fusion | flops 682557440 | bytes 15094784 | tf_op jit(solution)/shard_map/hqk,khd->qhd/dot_general | solution.py:155
  447.8 1.1 copy.131
  449.0 13.6 %while.12 = (s32[]{:T(128)}, f32[20,153,128]{2,1,0:T(8,128)S(1)}, f32[20,153]{1,0:T(8,128)S(1)}, s32[]{:T(128)}, f32[8,20,153,128]{3,2,1,0:T(8,128)}, /*index=5*...) while((s32[]{:T(128)}, f32[20,153,128]{2,1,0:T(8,128)S(1)}, f32[20,153]{1,0:T(8,128)S(1)}, ...), condition=%wide.region_3.4_spmd, body=%wide.region_2.3_spmd.sunk | while | flops 394745 | bytes 4737015 | solution.py:33
  449.1 2.0 bitcast_add_fusion.6
  451.1 1.8 bitcast_add_fusion.6
  452.9 1.8 bitcast_add_fusion.6
  454.8 1.8 bitcast_add_fusion.6
  456.7 1.8 bitcast_add_fusion.6
  458.6 1.8 bitcast_add_fusion.6
  460.5 1.8 bitcast_add_fusion.6
  462.7 1.5 fusion.45
  464.3 0.3 copy-done.3
  464.6 5.4 %fusion.16 = bf16[2,128,20,128]{3,1,2,0:T(8,128)(2,1)S(1)} fusion(f32[2,20,128,128]{3,2,1,0:T(8,128)} %fusion.28, f32[2,20,153,128]{3,2,1,0:T(8,128)S(1)} %copy-done.3, f32[20,153,128]{2,1,0:T(8,128)S(1)} %get-tuple-element.37, f32[2,128,20]{1,2,0:T(8,128)S(1)} %fusion.48, bf16[2,128,20,136]{1,3,2,0:T(8,128)(2,1)S(1)} %copy-done.6, ...), kind=kOutput, calls=%fused_computation.33 | convolution fusion | flops 1210690560 | bytes 10209586 | tf_op jit(solution)/shard_map/bqhf,bhfd->bqhd/dot_general | solution.py:89
  470.0 0.9 copy.147
  470.9 1.6 reshape.188
  (78 shorter events, 1.6 us)
Async XLA Ops:
  65.5 7.3 %copy-start.11 = (bf16[1,256,320]{1,2,0:T(8,128)(2,1)S(1)}, bf16[1,256,320]{1,2,0:T(8,128)(2,1)}, u32[]{:S(2)}) copy-start(bf16[1,256,320]{1,2,0:T(8,128)(2,1)} %param.22) | copy-start | bytes 491524
  65.5 7.5 %copy-start.18 = (s32[136]{0:T(256)S(1)}, s32[136]{0:T(256)}, u32[]{:S(2)}) copy-start(s32[136]{0:T(256)} %constant.122) | copy-start | bytes 1636
  65.5 169.5 %all-to-all-start = ((bf16[32,128,1280]{2,1,0:T(8,128)(2,1)}), bf16[32,128,1280]{2,1,0:T(8,128)(2,1)}, u32[]{:S(2)}, u32[]{:S(2)}) async-start(bf16[32,128,1280]{2,1,0:T(8,128)(2,1)} %copy.117), calls=%async_computation | async-start | bytes 20971520 | tf_op jit(solution)/shard_map/all_to_all | solution.py:126
  72.6 376.3 %all-gather.5.cloned.1.call-start = ((), (), s32[]{:S(2)}) async-start(), calls=%async_computation.2 | async-start | bytes 14745600 | tf_op jit(solution)/shard_map/all_gather | solution.py:25
  73.1 2.6 copy-start.17
  75.7 2.6 copy-start.12
  89.5 5.3 %copy-start = (f32[136,256,20]{1,2,0:T(8,128)S(1)}, f32[136,256,20]{1,2,0:T(8,128)}, u32[]{:S(2)}) copy-start(f32[136,256,20]{1,2,0:T(8,128)} %gather_fusion.2) | copy-start | bytes 8355844
  98.9 5.2 %copy-start.9 = (bf16[1,256,320]{1,2,0:T(8,128)(2,1)S(1)}, bf16[1,256,320]{1,2,0:T(8,128)(2,1)}, u32[]{:S(2)}) copy-start(bf16[1,256,320]{1,2,0:T(8,128)(2,1)} %get-tuple-element.65) | copy-start | bytes 491524
  98.9 5.3 %copy-start.7 = (bf16[1,256,2560]{2,1,0:T(8,128)(2,1)S(1)}, bf16[1,256,2560]{2,1,0:T(8,128)(2,1)}, u32[]{:S(2)}) copy-start(bf16[1,256,2560]{2,1,0:T(8,128)(2,1)} %param.24) | copy-start | bytes 3932164
  104.0 1.0 copy-start.16
  235.1 168.4 %all-to-all-start.1 = ((bf16[32,128,1280]{2,1,0:T(8,128)(2,1)}), bf16[32,128,1280]{2,1,0:T(8,128)(2,1)}, u32[]{:S(2)}, u32[]{:S(2)}) async-start(bf16[32,128,1280]{2,1,0:T(8,128)(2,1)} %copy.126), calls=%async_computation.1 | async-start | bytes 20971520 | tf_op jit(solution)/shard_map/all_to_all | solution.py:127
  253.2 32.4 %copy-start.13 = (bf16[2,128,20,16]{1,3,2,0:T(8,128)(2,1)}, bf16[2,128,20,16]{1,3,2,0:T(8,128)(2,1)S(1)}, u32[]{:S(2)}) copy-start(bf16[2,128,20,16]{1,3,2,0:T(8,128)(2,1)S(1)} %copy.101) | copy-start | bytes 491524
  281.7 3.9 copy-start.1
  414.2 3.3 copy-start.10
  417.4 8.1 %copy-start.2 = (f32[10,2,128,128]{2,3,1,0:T(8,128)S(1)}, f32[10,2,128,128]{2,3,1,0:T(8,128)}, u32[]{:S(2)}) copy-start(f32[10,2,128,128]{2,3,1,0:T(8,128)} %get-tuple-element.78) | copy-start | bytes 3932164
  417.4 8.4 %copy-start.4 = (bf16[2,128,10,128]{3,2,1,0:T(8,128)(2,1)S(1)}, bf16[2,128,10,128]{3,2,1,0:T(8,128)(2,1)}, u32[]{:S(2)}) copy-start(bf16[2,128,10,128]{3,2,1,0:T(8,128)(2,1)} %reshape.192) | copy-start | bytes 1966084
  431.8 3.2 copy-start.19
  435.0 6.1 %copy-start.5 = (bf16[1024,10,128]{0,2,1:T(8,128)(2,1)S(1)}, bf16[1024,10,128]{0,2,1:T(8,128)(2,1)}, u32[]{:S(2)}) copy-start(bf16[1024,10,128]{0,2,1:T(8,128)(2,1)} %reshape.115) | copy-start | bytes 7864324
  435.1 6.2 %copy-start.8 = (f32[256,10,128]{0,2,1:T(8,128)S(1)}, f32[256,10,128]{0,2,1:T(8,128)}, u32[]{:S(2)}) copy-start(f32[256,10,128]{0,2,1:T(8,128)} %copy.129) | copy-start | bytes 3932164
  449.0 13.7 %copy-start.6 = (bf16[2,128,20,136]{1,3,2,0:T(8,128)(2,1)S(1)}, bf16[2,128,20,136]{1,3,2,0:T(8,128)(2,1)}, u32[]{:S(2)}) copy-start(bf16[2,128,20,136]{1,3,2,0:T(8,128)(2,1)} %get-tuple-element.70) | copy-start | bytes 4177924
  449.0 13.7 %copy-start.14 = (bf16[2,128,20,16]{1,3,2,0:T(8,128)(2,1)S(1)}, bf16[2,128,20,16]{1,3,2,0:T(8,128)(2,1)}, u32[]{:S(2)}) copy-start(bf16[2,128,20,16]{1,3,2,0:T(8,128)(2,1)} %copy-done.13) | copy-start | bytes 491524
  462.6 1.7 copy-start.15
  462.6 1.9 copy-start.3
Sparse Core Ops, SparseCore 0:
  113.9 136.5 all-gather.4
where the time goes:
time: 488 us; the launch traced here: 480 us
  waiting for transfers between devices  205 us (42%)
  local copies, waits for them, and re-layouts  93.3 us (19%)
  blocking collectives  59.7 us (12%)
  matrix products  47.8 us (10%)
  other arithmetic  44.3 us (9%)
  between operations  15.4 us (3%)
  starting transfers between devices  13.2 us (3%)
    all_to_all x1, waiting for transfers between devices, softmax_layer(): lax.all_to_all(send_values, 'files', split_axis=0, concat_axis=0, tiled=T...  107 us
    all_to_all x1, waiting for transfers between devices, softmax_layer(): lax.all_to_all(send_keys, 'files', split_axis=0, concat_axis=0, tiled=True)  97.9 us
    all_gather x1, blocking collectives, entering(): gathered = jax.tree.map(lambda a: lax.all_gather(a, axis), part)  24.9 us
    all_gather x1, blocking collectives, owner_selection(): lax.all_gather(import_ids, 'files', axis=0, tiled=True)  21.5 us
    dot_general x1, local copies, waits for them, and re-layouts, softmax_layer(): jnp.einsum('rj,jc->rc', selection, value_blocks, preferred_element_type=j...  14.2 us
    dot_general x1, local copies, waits for them, and re-layouts, softmax_layer(): jnp.einsum('rj,jc->rc', selection, key_blocks, preferred_element_type=jnp...  13.7 us
    unnamed x1, blocking collectives  13.4 us
    add x14, other arithmetic, add_pairs(): return (earlier[0] + later[0], earlier[1] + later[1])  13.1 us
  transfers between devices with their start and end apart: 3, of which 2 were waited for; matrix products, arithmetic and copies ran while one was open for 29% of the time, Pallas kernels for 0%

commit v1 on v0

v1 whole, which is shorter than its diff:
```python
import functools
import math

import jax
import jax.numpy as jnp
import numpy as np
from jax import lax
from jax.experimental import pallas as pl
from jax.experimental.pallas import tpu as pltpu
from jax.sharding import PartitionSpec as P

D = 2560
HEADS = 20
FEAT = 16
FEATS = 153
FROWS = 160
FPAD = 256
SM_HEADS = 10
SM_HD = 128
SM_W = 1280
BLK = 128
TOK = 256
LISTED = 8
HALF = 640
HALF_HEADS = 5
QROWS = 272
SIDE = 4
CORES = 2

inv_root_two = 0.7071067811865476
TO_LOG2 = math.log2(math.e) / math.sqrt(SM_HD)
NEG = -1e30
BF = jnp.bfloat16
F32 = jnp.float32
NT = (((1,), (1,)), ((), ()))
VMEM_LIMIT = 60 * 1024 * 1024


def along(what, step):
    pairs = []
    for x in range(SIDE):
        for y in range(SIDE):
            for c in range(CORES):
                on_x = (c == 0) == (what == "kv")
                x2 = (x + step) % SIDE if on_x else x
                y2 = y if on_x else (y + step) % SIDE
                pairs.append(((x * SIDE + y) * CORES + c, (x2 * SIDE + y2) * CORES + c))
    return pairs


def move(a, what, step):
    return lax.ppermute(a, "files", along(what, step))


def swap_cores(a):
    return lax.ppermute(a, "files", [(i, i ^ 1) for i in range(SIDE * SIDE * CORES)])


def feature_tables():
    rows, cols = np.triu_indices(FEAT)
    select = np.zeros((8, 2, FPAD, 128), np.float32)
    for j in range(8):
        for f in range(FEAT):
            select[j, 0, 1 + f, j * FEAT + f] = 0.5
        for n in range(len(rows)):
            select[j, 0, 1 + FEAT + n, j * FEAT + rows[n]] = 0.5
            select[j, 1, 1 + FEAT + n, j * FEAT + cols[n]] = 0.5
    first = np.zeros(FPAD, np.float32)
    first[0] = 1.0
    second = np.zeros(FPAD, np.float32)
    second[: 1 + FEAT] = 1.0
    factor = np.zeros(FPAD, np.float32)
    factor[:FEATS] = 1.0
    factor[1 + FEAT : FEATS] = np.where(rows == cols, inv_root_two, 1.0).astype(np.float32)
    vectors = np.stack([first, second, factor])
    tall = np.broadcast_to(vectors[:, :FROWS, None], (3, FROWS, 128))
    wide = np.zeros((8, FPAD), np.float32)
    wide[:3] = vectors
    return select.astype(jnp.bfloat16), np.ascontiguousarray(tall), wide


def pad_lanes(src_ref, dst_ref):
    dst_ref[:, 0:256] = src_ref[:, 0:256]
    dst_ref[:, 256:384] = jnp.zeros((TOK, 128), BF)
    dst_ref[:, 256:320] = src_ref[:, 256:320]


def head_group(ref, h):
    return ref[:, pl.ds(pl.multiple_of((h >> 3) * 128, 128), 128)]


def lanes_of(h):
    return pl.ds(pl.multiple_of(h * 128, 128), 128)


def features_tall(x, select, tall):
    a = lax.dot_general(select[0, :FROWS], x, NT, preferred_element_type=F32)
    b = lax.dot_general(select[1, :FROWS], x, NT, preferred_element_type=F32)
    first, second, factor = (jnp.concatenate([tall[i], tall[i]], axis=1) for i in range(3))
    return ((a + first) * (b + second) * factor).astype(BF)


def features_wide(x, select, wide):
    a = lax.dot_general(x, select[0], NT, preferred_element_type=F32)
    b = lax.dot_general(x, select[1], NT, preferred_element_type=F32)
    return ((a + wide[0:1]) * (b + wide[1:2]) * wide[2:3]).astype(BF)


def state_kernel(k_ref, v_ref, select_ref, tall_ref, out_ref, x_ref):
    pad_lanes(k_ref, x_ref)
    row = lax.broadcasted_iota(jnp.int32, (FROWS, 128), 0)
    ones = jnp.ones((8, TOK), BF)

    def head(h, carry):
        phi = features_tall(head_group(x_ref, h), select_ref[h & 7], tall_ref)
        state = jnp.dot(phi, v_ref[:, lanes_of(h)], preferred_element_type=F32)
        rest = jnp.concatenate([phi[128:FROWS], jnp.zeros((256 - FROWS, TOK), BF)], axis=0)
        n0 = lax.dot_general(ones, phi[:128], NT, preferred_element_type=F32)[0:1]
        n1 = lax.dot_general(ones, rest, NT, preferred_element_type=F32)[0:1]
        h0, h1 = n0.astype(BF).astype(F32), n1.astype(BF).astype(F32)
        for i, r in enumerate((h0, h1, n0 - h0, n1 - h1)):
            state = jnp.where(row == FEATS + i, r, state)
        out_ref[h] = state.astype(BF)
        return carry

    lax.fori_loop(0, HEADS, head, 0, unroll=4)


def prefix_kernel(place_ref, in_ref, out_ref):
    rows = in_ref.shape[1]
    row = lax.broadcasted_iota(jnp.int32, (rows, 128), 0) + (place_ref[0] & 1) * (FROWS // 2)
    row = jnp.where(row >= FROWS, row - FROWS, row)
    row = jnp.where(row >= FROWS, row - FROWS, row)
    high = (row == FEATS) | (row == FEATS + 1)
    low = (row == FEATS + 2) | (row == FEATS + 3)
    total = jnp.zeros((rows, 128), F32)
    for z in range(in_ref.shape[0]):
        both = total + pltpu.roll(total, rows - 2, 0)
        top = both.astype(BF).astype(F32)
        rest = pltpu.roll(both - top, 2, 0)
        out_ref[z] = jnp.where(high, top, jnp.where(low, rest, total)).astype(BF)
        total = total + in_ref[z].astype(F32)


def local_kernel(q_ref, k_ref, v_ref, select_ref, tall_ref, wide_ref, num_ref, den_ref, phi_ref, xq_ref, xk_ref):
    pad_lanes(q_ref, xq_ref)
    pad_lanes(k_ref, xk_ref)
    causal = lax.broadcasted_iota(jnp.int32, (TOK, TOK), 0) >= lax.broadcasted_iota(jnp.int32, (TOK, TOK), 1)
    lane = lax.broadcasted_iota(jnp.int32, (TOK, 128), 1)
    den_ref[...] = jnp.zeros((TOK, 128), F32)

    def head(h, carry):
        select = select_ref[h & 7]
        phi_q = features_wide(head_group(xq_ref, h), select, wide_ref)
        phi_k = features_tall(head_group(xk_ref, h), select, tall_ref)
        phi_k = jnp.concatenate([phi_k, jnp.zeros((FPAD - FROWS, TOK), BF)], axis=0)
        weight = jnp.dot(phi_q, phi_k, preferred_element_type=F32)
        weight = jnp.where(causal, weight, 0.0)
        num_ref[:, lanes_of(h)] = jnp.dot(weight.astype(BF), v_ref[:, lanes_of(h)], preferred_element_type=F32)
        den = jnp.sum(weight[:, :128] + weight[:, 128:], axis=1, keepdims=True)
        den_ref[...] = jnp.where(lane == h, den, den_ref[...])
        phi_ref[h] = phi_q
        return carry

    lax.fori_loop(0, HEADS, head, 0, unroll=2)


def finish_kernel(num_ref, den_ref, phi_ref, state_ref, out_ref):
    lane = lax.broadcasted_iota(jnp.int32, (TOK, 128), 1)

    def head(h, carry):
        phi = phi_ref[h]
        state = state_ref[h]
        padded = jnp.concatenate([state, jnp.zeros((FPAD - FROWS, 128), BF)], axis=0)
        carried = jnp.dot(phi, padded, preferred_element_type=F32)
        tail = state[FROWS - 16 : FROWS].astype(F32)
        at = FEATS - (FROWS - 16)
        n0 = tail[at : at + 1] + tail[at + 2 : at + 3]
        n1 = tail[at + 1 : at + 2] + tail[at + 3 : at + 4]
        phi32 = phi.astype(F32)
        den = jnp.where(lane == h, den_ref[...], 0.0) + phi32[:, :128] * n0 + phi32[:, 128:] * n1
        den = jnp.sum(den, axis=1, keepdims=True)
        out_ref[:, lanes_of(h)] = ((num_ref[:, lanes_of(h)] + carried) / den).astype(BF)
        return carry

    lax.fori_loop(0, HEADS, head, 0, unroll=4)


def pack_kernel(me_ref, ids_ref, count_ref, q_ref, k_ref, v_ref, kv_ref, kv_send_ref, q_out_ref, q_send_ref):
    core = me_ref[0] & 1
    lane = lax.broadcasted_iota(jnp.int32, (QROWS - TOK, HALF), 1)
    listed = jnp.full((QROWS - TOK, HALF), -1.0, F32)
    for i in range(LISTED):
        entry = jnp.where(i < count_ref[0], ids_ref[i], -1).astype(F32)
        listed = jnp.where(lane == i, entry, listed)
    for half, kv, q in ((core, kv_ref, q_out_ref), (1 - core, kv_send_ref, q_send_ref)):
        at = pl.ds(pl.multiple_of(half * HALF, 128), HALF)
        kv[0] = k_ref[:, at]
        kv[1] = v_ref[:, at]
        q[0:TOK] = q_ref[:, at]
        q[TOK:QROWS] = listed.astype(BF)


def attend_kernel(own, readers, me_ref, ids_ref, *refs):
    q_in, kv_in = refs[:readers], refs[readers : readers + 8]
    outs = refs[readers + 8 : readers + 8 + readers // 2]
    q_buf, kv_buf, o_buf, s_buf, m_buf, l_buf, a_buf, found, sems = refs[readers + 8 + readers // 2 :]
    copies = [pltpu.make_async_copy(q_in[i], q_buf.at[i], sems.at[i]) for i in range(readers)]
    copies += [pltpu.make_async_copy(kv_in[i], kv_buf.at[i], sems.at[readers + i]) for i in range(8)]
    for c in copies:
        c.start()
    me = me_ref[0]
    core, y, x = me & 1, (me >> 1) & (SIDE - 1), me >> 3
    lane = lax.broadcasted_iota(jnp.int32, (TOK, 128), 1)
    for c in copies:
        c.wait()

    def heads():
        return [(h, slice(h * 128, (h + 1) * 128)) for h in range(HALF_HEADS)]

    def reader(r, carry):
        count = jnp.int32(0)
        for i in range(LISTED):
            entry = ids_ref[r, i]
            xo, yo, co = entry >> 4, (entry >> 2) & (SIDE - 1), (entry >> 1) & 1
            mine = (entry >= 0) & jnp.where(core == 0, yo == y, xo == x)
            away = jnp.where(core == 0, xo - x, yo - y) & (SIDE - 1)
            found[count] = (away * 2 + (co ^ core)) * 2 + (entry & 1)
            count = count + mine.astype(jnp.int32)

        m_buf[...] = jnp.full(m_buf.shape, NEG, F32)
        l_buf[...] = jnp.zeros(l_buf.shape, F32)
        a_buf[...] = jnp.zeros(a_buf.shape, F32)

        def score(j, carry):
            slot, rows = found[j] >> 1, pl.ds(pl.multiple_of((found[j] & 1) * BLK, BLK), BLK)
            for h, at in heads():
                s = lax.dot_general(q_buf[r, 0:TOK, at], kv_buf[slot, 0, rows, at], NT, preferred_element_type=F32)
                s_buf[j, h] = s
                m_buf[h] = jnp.maximum(m_buf[h], s)
            return carry

        lax.fori_loop(0, count, score, 0)
        if own:
            for h, at in heads():
                parts = [
                    lax.dot_general(
                        q_buf[r, b * BLK : (b + 1) * BLK, at],
                        kv_buf[r, 0, b * BLK : (b + 1) * BLK, at],
                        NT,
                        preferred_element_type=F32,
                    )
                    for b in range(2)
                ]
                s = jnp.concatenate(parts, axis=0)
                s_buf[LISTED, h] = s
                m_buf[h] = jnp.maximum(m_buf[h], s)
        for h, at in heads():
            m_buf[h] = jnp.broadcast_to(jnp.max(m_buf[h], axis=1, keepdims=True) * TO_LOG2, (TOK, 128))

        def weigh(j, carry):
            slot, rows = found[j] >> 1, pl.ds(pl.multiple_of((found[j] & 1) * BLK, BLK), BLK)
            for h, at in heads():
                p = jnp.exp2(s_buf[j, h] * TO_LOG2 - m_buf[h])
                l_buf[h] = l_buf[h] + p
                a_buf[h] = a_buf[h] + jnp.dot(p.astype(BF), kv_buf[slot, 1, rows, at], preferred_element_type=F32)
            return carry

        lax.fori_loop(0, count, weigh, 0)
        if own:
            for h, at in heads():
                p = jnp.exp2(s_buf[LISTED, h] * TO_LOG2 - m_buf[h])
                l_buf[h] = l_buf[h] + p
                p = p.astype(BF)
                parts = [
                    jnp.dot(
                        p[b * BLK : (b + 1) * BLK],
                        kv_buf[r, 1, b * BLK : (b + 1) * BLK, at],
                        preferred_element_type=F32,
                    )
                    for b in range(2)
                ]
                a_buf[h] = a_buf[h] + jnp.concatenate(parts, axis=0)
        packed = jnp.zeros((TOK, 128), F32)
        for h, at in heads():
            total = jnp.sum(l_buf[h], axis=1, keepdims=True)
            empty = total == 0.0
            safe = jnp.where(empty, 1.0, total)
            o_buf[r, 0:TOK, at] = (a_buf[h] / safe).astype(BF)
            size = jnp.where(empty, NEG, m_buf[h][:, 0:1] + jnp.log2(safe))
            top = size.astype(BF).astype(F32)
            middle = (size - top).astype(BF).astype(F32)
            packed = jnp.where(lane == h, top, packed)
            packed = jnp.where(lane == HALF_HEADS + h, middle, packed)
            packed = jnp.where(lane == 2 * HALF_HEADS + h, size - top - middle, packed)
        o_buf[r, TOK:QROWS, :] = jnp.zeros((QROWS - TOK, HALF), BF)
        o_buf[r, TOK:QROWS, 0:TOK] = packed.T[0 : QROWS - TOK].astype(BF)
        return carry

    lax.fori_loop(0, readers, reader, 0)
    back = [
        pltpu.make_async_copy(o_buf.at[2 * i : 2 * i + 2], outs[i], sems.at[readers + 8 + i])
        for i in range(readers // 2)
    ]
    for c in back:
        c.start()
    for c in back:
        c.wait()


def join_kernel(*refs):
    parts, outs = refs[:4], refs[4:]
    for r in range(2):
        sizes = []
        for p in parts:
            packed = p[r, TOK:QROWS, 0:TOK].astype(F32)
            packed = jnp.concatenate([packed, jnp.zeros((128 - (QROWS - TOK), TOK), F32)], axis=0).T
            sizes.append(packed + pltpu.roll(packed, 128 - HALF_HEADS, 1) + pltpu.roll(packed, 128 - 2 * HALF_HEADS, 1))
        top = functools.reduce(jnp.maximum, sizes)
        shares = [jnp.exp2(s - top) for s in sizes]
        total = functools.reduce(jnp.add, shares)
        shares = [s / total for s in shares]
        for h in range(HALF_HEADS):
            at = slice(h * 128, (h + 1) * 128)
            o = sum(s[:, h : h + 1] * p[r, 0:TOK, at].astype(F32) for s, p in zip(shares, parts, strict=True))
            outs[r][:, at] = o.astype(BF)


def place_kernel(me_ref, mine_ref, other_ref, out_ref):
    core = me_ref[0] & 1
    out_ref[:, pl.ds(pl.multiple_of(core * HALF, 128), HALF)] = mine_ref[...]
    out_ref[:, pl.ds(pl.multiple_of((1 - core) * HALF, 128), HALF)] = other_ref[...]


def shape(*dims, dtype=BF):
    return jax.ShapeDtypeStruct(dims, dtype)


SMEM = pl.BlockSpec(memory_space=pltpu.SMEM)
VMEM = pl.BlockSpec(memory_space=pltpu.VMEM)
ANY = pl.BlockSpec(memory_space=pl.ANY)
PARAMS = pltpu.CompilerParams(vmem_limit_bytes=VMEM_LIMIT)


def cost(flops, moved):
    return pl.CostEstimate(flops=int(flops), bytes_accessed=int(moved), transcendentals=0)


def attend(own, me, ids, queries, blocks):
    readers = len(queries)
    return pl.pallas_call(
        functools.partial(attend_kernel, own, readers),
        name="attend_own" if own else "attend_far",
        out_shape=[shape(2, QROWS, HALF)] * (readers // 2),
        in_specs=[SMEM, SMEM] + [ANY] * (readers + 8),
        out_specs=[ANY] * (readers // 2),
        scratch_shapes=[
            pltpu.VMEM((readers, QROWS, HALF), BF),
            pltpu.VMEM((8, 2, TOK, HALF), BF),
            pltpu.VMEM((readers, QROWS, HALF), BF),
            pltpu.VMEM((LISTED + 1, HALF_HEADS, TOK, 128), F32),
            pltpu.VMEM((HALF_HEADS, TOK, 128), F32),
            pltpu.VMEM((HALF_HEADS, TOK, 128), F32),
            pltpu.VMEM((HALF_HEADS, TOK, 128), F32),
            pltpu.SMEM((LISTED + 1,), jnp.int32),
            pltpu.SemaphoreType.DMA((readers + 8 + readers // 2,)),
        ],
        compiler_params=PARAMS,
        cost_estimate=cost(readers * 4e8, 8e6),
    )(me, ids, *queries, *blocks)


def body(q_lin, k_lin, v_lin, q_soft, k_soft, v_soft, import_ids, import_counts):
    select, tall, wide = (jnp.asarray(t) for t in feature_tables())
    me = lax.axis_index("files").astype(jnp.int32).reshape(1)
    place = lax.axis_index("seq").astype(jnp.int32).reshape(1)
    shards = lax.axis_size("seq")

    kv_a, kv_send, q_a, q_send = pl.pallas_call(
        pack_kernel,
        name="pack",
        out_shape=[shape(2, TOK, HALF), shape(2, TOK, HALF), shape(QROWS, HALF), shape(QROWS, HALF)],
        in_specs=[SMEM] * 3 + [VMEM] * 3,
        out_specs=[VMEM] * 4,
        compiler_params=PARAMS,
        cost_estimate=cost(0, 4e6),
    )(me, import_ids[0, 0], import_counts[0], q_soft[0], k_soft[0], v_soft[0])

    kv_b, q_b = swap_cores(kv_send), swap_cores(q_send)
    kv_a_left, kv_a_right = move(kv_a, "kv", 1), move(kv_a, "kv", -1)
    kv_b_left, kv_b_right = move(kv_b, "kv", 1), move(kv_b, "kv", -1)
    q_a_left, q_a_right = move(q_a, "q", 1), move(q_a, "q", -1)
    q_b_left, q_b_right = move(q_b, "q", 1), move(q_b, "q", -1)
    kv_a_far, kv_b_far = move(kv_a_left, "kv", 1), move(kv_b_right, "kv", -1)
    q_a_far, q_b_far = move(q_a_left, "q", 1), move(q_b_right, "q", -1)

    state = pl.pallas_call(
        state_kernel,
        name="state",
        out_shape=shape(HEADS, FROWS, 128),
        in_specs=[VMEM] * 4,
        out_specs=VMEM,
        scratch_shapes=[pltpu.VMEM((TOK, 384), BF)],
        compiler_params=PARAMS,
        cost_estimate=cost(1e9, 4e6),
    )(k_lin[0], v_lin[0], select, tall)
    slices = lax.all_to_all(state.reshape(shards, HEADS * FROWS // shards, 128), "seq", 0, 0, tiled=True)

    num, den, phi = pl.pallas_call(
        local_kernel,
        name="local",
        out_shape=[shape(TOK, D, dtype=F32), shape(TOK, 128, dtype=F32), shape(HEADS, TOK, FPAD)],
        in_specs=[VMEM] * 6,
        out_specs=[VMEM] * 3,
        scratch_shapes=[pltpu.VMEM((TOK, 384), BF), pltpu.VMEM((TOK, 384), BF)],
        compiler_params=PARAMS,
        cost_estimate=cost(4e9, 8e6),
    )(q_lin[0], k_lin[0], v_lin[0], select, tall, wide)

    prefix = pl.pallas_call(
        prefix_kernel,
        name="prefix",
        out_shape=shape(*slices.shape),
        in_specs=[SMEM, VMEM],
        out_specs=VMEM,
        compiler_params=PARAMS,
        cost_estimate=cost(0, 2e6),
    )(place, slices)
    before = lax.all_to_all(prefix, "seq", 0, 0, tiled=True).reshape(HEADS, FROWS, 128)

    blocks = (kv_a, kv_b, kv_a_right, kv_b_right, kv_a_far, kv_b_far, kv_a_left, kv_b_left)

    def lists(queries):
        return jnp.stack([q[TOK, :LISTED] for q in queries]).astype(jnp.int32)

    far = (q_a_left, q_b_left, q_a_right, q_b_right, q_a_far, q_b_far)
    to_left, to_right, to_far = attend(False, me, lists(far), far, blocks)
    from_right, from_left, from_far = move(to_left, "q", -1), move(to_right, "q", 1), move(to_far, "q", 2)
    (here,) = attend(True, me, lists((q_a, q_b)), (q_a, q_b), blocks)
    mine, send = pl.pallas_call(
        join_kernel,
        name="join",
        out_shape=[shape(TOK, HALF)] * 2,
        in_specs=[VMEM] * 4,
        out_specs=[VMEM] * 2,
        compiler_params=PARAMS,
        cost_estimate=cost(0, 4e6),
    )(here, from_right, from_left, from_far)
    other = swap_cores(send)
    soft_out = pl.pallas_call(
        place_kernel,
        name="place",
        out_shape=shape(TOK, SM_W),
        in_specs=[SMEM, VMEM, VMEM],
        out_specs=VMEM,
        compiler_params=PARAMS,
        cost_estimate=cost(0, 1e6),
    )(me, mine, other)

    lin_out = pl.pallas_call(
        finish_kernel,
        name="finish",
        out_shape=shape(TOK, D),
        in_specs=[VMEM] * 4,
        out_specs=VMEM,
        compiler_params=PARAMS,
        cost_estimate=cost(4e8, 8e6),
    )(num, den, phi, before)
    return lin_out[None], soft_out[None]


def solution(mesh):
    wide = P("files", "seq", None)
    return jax.shard_map(
        body,
        mesh=mesh,
        in_specs=(wide,) * 7 + (P("files", "seq"),),
        out_specs=(wide, wide),
        check_vma=False,
    )
```

time: 488 us -> 140 us (0.29)
  the two profiles are of different devices: /device:TPU:236 before, /device:TPU:97 now
where the time goes in v1:
time: 140 us; the launch traced here: 138 us
  Pallas kernels  63.9 us (46%)
  starting transfers between devices  40.7 us (29%)
  waiting for transfers between devices  17.4 us (12%)
  local copies, waits for them, and re-layouts  13.8 us (10%)
    pallas_call x2, Pallas kernels, attend(): pl.pallas_call(functools.partial(attend_kernel, own, readers), name='atte...  24 us
    ppermute x15, starting transfers between devices, move(): return lax.ppermute(a, 'files', along(what, step))  21.8 us
    ppermute x15, waiting for transfers between devices, move(): return lax.ppermute(a, 'files', along(what, step))  17.3 us
    pallas_call x1, Pallas kernels, body(): pl.pallas_call(local_kernel, name='local', out_shape=[shape(TOK, D, dtype...  14.3 us
    unnamed x30, local copies, waits for them, and re-layouts  8.5 us
    pallas_call x1, Pallas kernels, body(): pl.pallas_call(state_kernel, name='state', out_shape=shape(HEADS, FROWS,...  7.39 us
    all_to_all x1, starting transfers between devices, body(): lax.all_to_all(state.reshape(shards, HEADS * FROWS // shards, 128), 'seq'...  7.1 us
    all_to_all x1, starting transfers between devices, body(): lax.all_to_all(prefix, 'seq', 0, 0, tiled=True).reshape(HEADS, FROWS, 128)  6.65 us
  transfers between devices with their start and end apart: 20, of which 5 were waited for; matrix products, arithmetic and copies ran while one was open for 7% of the time, Pallas kernels for 43%

profile of v1, /device:TPU:97, one launch (start us, length us, event | category | flops | bytes accessed | tf_op | source)
XLA Modules:
  0.0 138.3 jit_solution(2621267523252065028)
XLA Ops:
  1.3 2.9 %pack.1 = (bf16[2,256,640]{2,1,0:T(8,128)(2,1)}, bf16[2,256,640]{2,1,0:T(8,128)(2,1)}, bf16[272,640]{1,0:T(8,128)(2,1)}, bf16[272,640]{1,0:T(8,128)(2,1)}) custom-call(s32[1]{0:T(128)} %bitcast.7.me_ref, s32[8]{0:T(128)} %bitcast.25, s32[1]{0:T(128)} %bitcast.14.count_ref, bf16[256,1280]{1,0:T(8,128)(2,1)} %bitcast.18, bf16[256,1280]{1,0:T(8,128)(2,1)} %bitcast.19, ...), custom_call_target="tpu_custom_call" | custom-call | bytes 4000000 | tf_op jit(solution)/shard_map/pack/pallas_call | solution.py:379
  4.2 0.7 collective-permute-start.1
  4.9 1.7 %copy.14 = bf16[1,256,320]{2,1,0:T(8,128)(2,1)} copy(bf16[1,256,320]{1,2,0:T(8,128)(2,1)} %param.12) | data formatting | bytes 327680 | tf_op args[1]
  6.6 7.4 %state.1 = bf16[20,160,128]{2,1,0:T(8,128)(2,1)} custom-call(bf16[256,320]{1,0:T(8,128)(2,1)} %bitcast.22, bf16[256,2560]{1,0:T(8,128)(2,1)} %bitcast.26, bf16[8,2,256,128]{3,2,1,0:T(8,128)(2,1)} %constant.15.clone.select_ref, f32[3,160,128]{2,1,0:T(8,128)} %constant.16.clone.tall_ref), custom_call_target="tpu_custom_call" | custom-call | flops 1000000000 | bytes 4000000 | tf_op jit(solution)/shard_map/state/pallas_call | solution.py:397
  14.0 7.1 %all-to-all-start = ((bf16[8,400,128]{2,1,0:T(8,128)(2,1)}), bf16[8,400,128]{2,1,0:T(8,128)(2,1)S(1)}, u32[]{:S(2)}, u32[]{:S(2)}) async-start(bf16[8,400,128]{2,1,0:T(8,128)(2,1)} %bitcast.17), calls=%async_computation | async-start | bytes 1638400 | tf_op jit(solution)/shard_map/all_to_all | solution.py:407
  21.1 0.6 collective-permute-start
  21.7 1.2 collective-permute-start.8
  22.9 1.3 collective-permute-start.4
  24.2 0.0 collective-permute-done.1.refs_3_.refs_7_
  24.2 1.5 %collective-permute-start.3 = (bf16[2,256,640]{2,1,0:T(8,128)(2,1)S(1)}, bf16[2,256,640]{2,1,0:T(8,128)(2,1)S(1)}, u32[]{:S(2)}, u32[]{:S(2)}) collective-permute-start(bf16[2,256,640]{2,1,0:T(8,128)(2,1)S(1)} %collective-permute-done.1.refs_3_.refs_7_), channel_id=1, source_target_pairs={{0,24},{1,7},{2,26},{3,1},{4,28},{5,3},{6,30},{7,5},{8,0},{9,15},{... | collective-permute-start | bytes 1966088 | tf_op jit(solution)/shard_map/ppermute | solution.py:52
  25.7 1.5 %collective-permute-start.10 = (bf16[272,640]{1,0:T(8,128)(2,1)}, bf16[272,640]{1,0:T(8,128)(2,1)S(1)}, u32[]{:S(2)}, u32[]{:S(2)}) collective-permute-start(bf16[272,640]{1,0:T(8,128)(2,1)} %get-tuple-element.17.refs_0_), channel_id=1, source_target_pairs={{0,6},{1,25},{2,0},{3,27},{4,2},{5,29},{6,4},{7,31},{8,14},{9,1},{... | collective-permute-start | bytes 1044488 | tf_op jit(solution)/shard_map/ppermute | solution.py:52
  27.2 0.0 collective-permute-done.refs_1_
  27.2 1.3 collective-permute-start.11
  28.5 3.0 %collective-permute-done.8.refs_0_ = bf16[272,640]{1,0:T(8,128)(2,1)S(1)} collective-permute-done((bf16[272,640]{1,0:T(8,128)(2,1)}, bf16[272,640]{1,0:T(8,128)(2,1)S(1)}, u32[]{:S(2)}, u32[]{:S(2)}) %collective-permute-start.8) | collective-permute-done | bytes 348192 | tf_op jit(solution)/shard_map/ppermute | solution.py:52
  31.4 0.0 collective-permute-start.12
  31.4 4.6 %collective-permute-done.10.refs_2_ = bf16[272,640]{1,0:T(8,128)(2,1)S(1)} collective-permute-done((bf16[272,640]{1,0:T(8,128)(2,1)}, bf16[272,640]{1,0:T(8,128)(2,1)S(1)}, u32[]{:S(2)}, u32[]{:S(2)}) %collective-permute-start.10) | collective-permute-done | bytes 348192 | tf_op jit(solution)/shard_map/ppermute | solution.py:52
  36.1 1.2 collective-permute-start.9
  37.3 0.0 collective-permute-done.4.refs_8_.refs_12_
  37.3 1.5 %collective-permute-start.2 = (bf16[2,256,640]{2,1,0:T(8,128)(2,1)S(1)}, bf16[2,256,640]{2,1,0:T(8,128)(2,1)}, u32[]{:S(2)}, u32[]{:S(2)}) collective-permute-start(bf16[2,256,640]{2,1,0:T(8,128)(2,1)S(1)} %copy-done.5), channel_id=1, source_target_pairs={{0,24},{1,7},{2,26},{3,1},{4,28},{5,3},{6,30},{7,5},{8,0},{9,15},{... | collective-permute-start | bytes 1966088 | tf_op jit(solution)/shard_map/ppermute | solution.py:52
  38.8 3.7 %collective-permute-done.11.refs_3_ = bf16[272,640]{1,0:T(8,128)(2,1)} collective-permute-done((bf16[272,640]{1,0:T(8,128)(2,1)}, bf16[272,640]{1,0:T(8,128)(2,1)}, u32[]{:S(2)}, u32[]{:S(2)}) %collective-permute-start.11) | collective-permute-done | bytes 348192 | tf_op jit(solution)/shard_map/ppermute | solution.py:52
  42.5 0.4 collective-permute-start.7
  43.0 0.0 collective-permute-done.12.refs_4_
  43.0 1.5 %collective-permute-start.5 = (bf16[2,256,640]{2,1,0:T(8,128)(2,1)S(1)}, bf16[2,256,640]{2,1,0:T(8,128)(2,1)}, u32[]{:S(2)}, u32[]{:S(2)}) collective-permute-start(bf16[2,256,640]{2,1,0:T(8,128)(2,1)S(1)} %collective-permute-done.4.refs_8_.refs_12_), channel_id=1, source_target_pairs={{0,8},{1,3},{2,10},{3,5},{4,12},{5,7},{6,14},{7,1},{8,16},{9,11},{... | collective-permute-start | bytes 1966088 | tf_op jit(solution)/shard_map/ppermute | solution.py:52
  44.5 0.0 collective-permute-done.3.refs_5_.refs_9_
  44.5 1.2 collective-permute-start.6
  45.7 0.0 collective-permute-done.9.refs_1_
  45.7 0.7 copy-done.13
  46.5 2.6 %collective-permute-start.13 = (bf16[272,640]{1,0:T(8,128)(2,1)}, bf16[272,640]{1,0:T(8,128)(2,1)}, u32[]{:S(2)}, u32[]{:S(2)}) collective-permute-start(bf16[272,640]{1,0:T(8,128)(2,1)} %collective-permute-done.11.refs_3_), channel_id=1, source_target_pairs={{0,6},{1,25},{2,0},{3,27},{4,2},{5,29},{6,4},{7,31},{8,14},{9,1},{... | collective-permute-start | bytes 1044488 | tf_op jit(solution)/shard_map/ppermute | solution.py:52
  49.1 0.0 all-to-all-done.in_ref
  49.1 0.9 copy-done.1
  49.9 2.8 %prefix.1 = bf16[8,400,128]{2,1,0:T(8,128)(2,1)} custom-call(s32[1]{0:T(128)} %bitcast.3.place_ref, bf16[8,400,128]{2,1,0:T(8,128)(2,1)} %copy-done.1), custom_call_target="tpu_custom_call" | custom-call | bytes 2000000 | tf_op jit(solution)/shard_map/prefix/pallas_call | solution.py:420
  52.8 6.6 %all-to-all-start.1 = ((bf16[8,400,128]{2,1,0:T(8,128)(2,1)}), bf16[8,400,128]{2,1,0:T(8,128)(2,1)S(1)}, u32[]{:S(2)}, u32[]{:S(2)}) async-start(bf16[8,400,128]{2,1,0:T(8,128)(2,1)} %prefix.1), calls=%async_computation.1 | async-start | bytes 1638400 | tf_op jit(solution)/shard_map/all_to_all | solution.py:429
  59.4 0.7 slice.33
  60.1 0.7 slice.35
  60.8 0.6 slice.36
  61.4 0.7 slice.37
  62.1 0.7 slice.34
  62.7 0.0 collective-permute-done.13.refs_5_
  62.7 0.6 slice.38
  63.4 0.6 convert_element_type.7.ids_ref
  64.0 0.0 collective-permute-done.2.refs_4_.refs_8_
  64.0 0.0 collective-permute-done.5.refs_6_.refs_10_
  64.0 0.0 collective-permute-done.7.refs_9_.refs_13_
  64.0 0.0 collective-permute-done.6.refs_7_.refs_11_
  64.0 15.9 %attend_far.1 = (bf16[2,272,640]{2,1,0:T(8,128)(2,1)}, bf16[2,272,640]{2,1,0:T(8,128)(2,1)}, bf16[2,272,640]{2,1,0:T(8,128)(2,1)}) custom-call(s32[1]{0:T(128)} %bitcast.7.me_ref, s32[6,8]{1,0:T(8,128)} %convert_element_type.7.ids_ref, bf16[272,640]{1,0:T(8,128)(2,1)} %copy-done.10, bf16[272,640]{1,0:T(8,128)(2,1)} %copy-done.13, ...), custom_call_target="tpu_custom_call" | custom-call | flops 2400000000 | bytes 8000000 | tf_op jit(solution)/shard_map/attend_far/pallas_call | solution.py:351
  79.9 5.3 %collective-permute-start.14 = (bf16[2,272,640]{2,1,0:T(8,128)(2,1)}, bf16[2,272,640]{2,1,0:T(8,128)(2,1)S(1)}, u32[]{:S(2)}, u32[]{:S(2)}) collective-permute-start(bf16[2,272,640]{2,1,0:T(8,128)(2,1)} %get-tuple-element.21), channel_id=1, source_target_pairs={{0,6},{1,25},{2,0},{3,27},{4,2},{5,29},{6,4},{7,31},{8,14},{9,1},{... | collective-permute-start | bytes 2088968 | tf_op jit(solution)/shard_map/ppermute | solution.py:52
  85.2 0.0 collective-permute-start.15
  85.2 1.3 collective-permute-start.16
  86.5 0.7 slice.24
  87.1 1.7 %copy.13 = bf16[1,256,320]{2,1,0:T(8,128)(2,1)} copy(bf16[1,256,320]{1,2,0:T(8,128)(2,1)} %param.11) | data formatting | bytes 327680 | tf_op args[0]
  88.9 0.6 slice.32
  89.5 0.6 maximum_convert_fusion.ids_ref
  90.1 8.1 %attend_own.1.refs_0_ = bf16[2,272,640]{2,1,0:T(8,128)(2,1)} custom-call(s32[1]{0:T(128)} %bitcast.7.me_ref, s32[2,8]{1,0:T(2,128)} %maximum_convert_fusion.ids_ref, bf16[272,640]{1,0:T(8,128)(2,1)} %get-tuple-element.17.refs_0_, bf16[272,640]{1,0:T(8,128)(2,1)} %collective-permute-done.refs_1_, bf16[2,256,640]{2,1,0:T(8,128)(2,1)} %get-tuple-element.19.refs_2_.refs_6_, ...), custom_call_target="tpu_custom_call" | custom-call | flops 800000000 | bytes 8000000 | tf_op jit(solution)/shard_map/attend_own/pallas_call | solution.py:351
  98.2 2.7 %collective-permute-done.14.refs_1_ = bf16[2,272,640]{2,1,0:T(8,128)(2,1)S(1)} collective-permute-done((bf16[2,272,640]{2,1,0:T(8,128)(2,1)}, bf16[2,272,640]{2,1,0:T(8,128)(2,1)S(1)}, u32[]{:S(2)}, u32[]{:S(2)}) %collective-permute-start.14) | collective-permute-done | bytes 696352 | tf_op jit(solution)/shard_map/ppermute | solution.py:52
  100.9 3.3 %collective-permute-done.15.refs_2_ = bf16[2,272,640]{2,1,0:T(8,128)(2,1)S(1)} collective-permute-done((bf16[2,272,640]{2,1,0:T(8,128)(2,1)}, bf16[2,272,640]{2,1,0:T(8,128)(2,1)S(1)}, u32[]{:S(2)}, u32[]{:S(2)}) %collective-permute-start.15) | collective-permute-done | bytes 696352 | tf_op jit(solution)/shard_map/ppermute | solution.py:52
  104.3 0.9 copy-done.3
  105.1 0.9 copy-done.4
  106.0 5.1 %join.1 = (bf16[256,640]{1,0:T(8,128)(2,1)}, bf16[256,640]{1,0:T(8,128)(2,1)}) custom-call(bf16[2,272,640]{2,1,0:T(8,128)(2,1)} %attend_own.1.refs_0_, bf16[2,272,640]{2,1,0:T(8,128)(2,1)} %copy-done.2, bf16[2,272,640]{2,1,0:T(8,128)(2,1)} %copy-done.3, bf16[2,272,640]{2,1,0:T(8,128)(2,1)} %copy-done.4), custom_call_target="tpu_custom_call" | custom-call | bytes 4000000 | tf_op jit(solution)/shard_map/join/pallas_call | solution.py:440
  111.1 3.9 %collective-permute-start.17 = (bf16[256,640]{1,0:T(8,128)(2,1)}, bf16[256,640]{1,0:T(8,128)(2,1)S(1)}, u32[]{:S(2)}, u32[]{:S(2)}) collective-permute-start(bf16[256,640]{1,0:T(8,128)(2,1)} %get-tuple-element.25), channel_id=1, source_target_pairs={{0,1},{1,0},{2,3},{3,2},{4,5},{5,4},{6,7},{7,6},{8,9},{9,8},{10,11... | collective-permute-start | bytes 983048 | tf_op jit(solution)/shard_map/ppermute | solution.py:56
  115.0 14.3 %local.1 = (f32[256,2560]{1,0:T(8,128)}, f32[256,128]{1,0:T(8,128)}, bf16[20,256,256]{2,1,0:T(8,128)(2,1)}) custom-call(bf16[256,320]{1,0:T(8,128)(2,1)} %bitcast.24, bf16[256,320]{1,0:T(8,128)(2,1)} %bitcast.23, bf16[256,2560]{1,0:T(8,128)(2,1)} %bitcast.27, bf16[8,2,256,128]{3,2,1,0:T(8,128)(2,1)} %constant.15.clone.select_ref, ...), custom_call_target="tpu_custom_call" | custom-call | flops 4000000000 | bytes 8000000 | tf_op jit(solution)/shard_map/local/pallas_call | solution.py:409
  129.3 0.9 copy-done
  130.2 5.4 %finish.1 = bf16[256,2560]{1,0:T(8,128)(2,1)} custom-call(f32[256,2560]{1,0:T(8,128)} %get-tuple-element.14.num_ref, f32[256,128]{1,0:T(8,128)} %get-tuple-element.15.den_ref, bf16[20,256,256]{2,1,0:T(8,128)(2,1)} %get-tuple-element.16.phi_ref, bf16[20,160,128]{2,1,0:T(8,128)(2,1)} %bitcast.15), custom_call_target="tpu_custom_call" | custom-call | flops 400000000 | bytes 8000000 | tf_op jit(solution)/shard_map/finish/pallas_call | solution.py:460
  135.6 0.7 copy-done.9
  136.3 2.0 %place.1 = bf16[256,1280]{1,0:T(8,128)(2,1)} custom-call(s32[1]{0:T(128)} %bitcast.7.me_ref, bf16[256,640]{1,0:T(8,128)(2,1)} %get-tuple-element.24.mine_ref, bf16[256,640]{1,0:T(8,128)(2,1)} %copy-done.9), custom_call_target="tpu_custom_call" | custom-call | bytes 1000000 | tf_op jit(solution)/shard_map/place/pallas_call | solution.py:450
  (26 shorter events, 0.1 us)
Async XLA Ops:
  4.2 20.0 %collective-permute-start.1 = (bf16[2,256,640]{2,1,0:T(8,128)(2,1)}, bf16[2,256,640]{2,1,0:T(8,128)(2,1)S(1)}, u32[]{:S(2)}, u32[]{:S(2)}) collective-permute-start(bf16[2,256,640]{2,1,0:T(8,128)(2,1)} %get-tuple-element.20), channel_id=1, source_target_pairs={{0,1},{1,0},{2,3},{3,2},{4,5},{5,4},{6,7},{7,6},{8,9},{9,8},{10,11... | collective-permute-start | bytes 1966088 | tf_op jit(solution)/shard_map/ppermute | solution.py:56
  6.6 16.3 %copy-start.5 = (bf16[2,256,640]{2,1,0:T(8,128)(2,1)S(1)}, bf16[2,256,640]{2,1,0:T(8,128)(2,1)}, u32[]{:S(2)}) copy-start(bf16[2,256,640]{2,1,0:T(8,128)(2,1)} %get-tuple-element.19.refs_2_.refs_6_) | copy-start | bytes 1966084
  14.0 35.0 %all-to-all-start = ((bf16[8,400,128]{2,1,0:T(8,128)(2,1)}), bf16[8,400,128]{2,1,0:T(8,128)(2,1)S(1)}, u32[]{:S(2)}, u32[]{:S(2)}) async-start(bf16[8,400,128]{2,1,0:T(8,128)(2,1)} %bitcast.17), calls=%async_computation | async-start | bytes 1638400 | tf_op jit(solution)/shard_map/all_to_all | solution.py:407
  21.1 6.1 %collective-permute-start = (bf16[272,640]{1,0:T(8,128)(2,1)}, bf16[272,640]{1,0:T(8,128)(2,1)}, u32[]{:S(2)}, u32[]{:S(2)}) collective-permute-start(bf16[272,640]{1,0:T(8,128)(2,1)} %get-tuple-element.18), channel_id=1, source_target_pairs={{0,1},{1,0},{2,3},{3,2},{4,5},{5,4},{6,7},{7,6},{8,9},{9,8},{10,11... | collective-permute-start | bytes 1044488 | tf_op jit(solution)/shard_map/ppermute | solution.py:56
  21.7 9.8 %collective-permute-start.8 = (bf16[272,640]{1,0:T(8,128)(2,1)}, bf16[272,640]{1,0:T(8,128)(2,1)S(1)}, u32[]{:S(2)}, u32[]{:S(2)}) collective-permute-start(bf16[272,640]{1,0:T(8,128)(2,1)} %get-tuple-element.17.refs_0_), channel_id=1, source_target_pairs={{0,2},{1,9},{2,4},{3,11},{4,6},{5,13},{6,0},{7,15},{8,10},{9,17},{... | collective-permute-start | bytes 1044488 | tf_op jit(solution)/shard_map/ppermute | solution.py:52
  22.9 14.4 %collective-permute-start.4 = (bf16[2,256,640]{2,1,0:T(8,128)(2,1)S(1)}, bf16[2,256,640]{2,1,0:T(8,128)(2,1)S(1)}, u32[]{:S(2)}, u32[]{:S(2)}) collective-permute-start(bf16[2,256,640]{2,1,0:T(8,128)(2,1)S(1)} %copy-done.5), channel_id=1, source_target_pairs={{0,8},{1,3},{2,10},{3,5},{4,12},{5,7},{6,14},{7,1},{8,16},{9,11},{... | collective-permute-start | bytes 1966088 | tf_op jit(solution)/shard_map/ppermute | solution.py:52
  24.2 39.8 %copy-start.6 = (bf16[2,256,640]{2,1,0:T(8,128)(2,1)}, bf16[2,256,640]{2,1,0:T(8,128)(2,1)S(1)}, u32[]{:S(2)}) copy-start(bf16[2,256,640]{2,1,0:T(8,128)(2,1)S(1)} %collective-permute-done.1.refs_3_.refs_7_) | copy-start | bytes 1966084
  24.2 20.3 %collective-permute-start.3 = (bf16[2,256,640]{2,1,0:T(8,128)(2,1)S(1)}, bf16[2,256,640]{2,1,0:T(8,128)(2,1)S(1)}, u32[]{:S(2)}, u32[]{:S(2)}) collective-permute-start(bf16[2,256,640]{2,1,0:T(8,128)(2,1)S(1)} %collective-permute-done.1.refs_3_.refs_7_), channel_id=1, source_target_pairs={{0,24},{1,7},{2,26},{3,1},{4,28},{5,3},{6,30},{7,5},{8,0},{9,15},{... | collective-permute-start | bytes 1966088 | tf_op jit(solution)/shard_map/ppermute | solution.py:52
  25.7 10.4 %collective-permute-start.10 = (bf16[272,640]{1,0:T(8,128)(2,1)}, bf16[272,640]{1,0:T(8,128)(2,1)S(1)}, u32[]{:S(2)}, u32[]{:S(2)}) collective-permute-start(bf16[272,640]{1,0:T(8,128)(2,1)} %get-tuple-element.17.refs_0_), channel_id=1, source_target_pairs={{0,6},{1,25},{2,0},{3,27},{4,2},{5,29},{6,4},{7,31},{8,14},{9,1},{... | collective-permute-start | bytes 1044488 | tf_op jit(solution)/shard_map/ppermute | solution.py:52
  27.2 15.3 %collective-permute-start.11 = (bf16[272,640]{1,0:T(8,128)(2,1)}, bf16[272,640]{1,0:T(8,128)(2,1)}, u32[]{:S(2)}, u32[]{:S(2)}) collective-permute-start(bf16[272,640]{1,0:T(8,128)(2,1)} %collective-permute-done.refs_1_), channel_id=1, source_target_pairs={{0,6},{1,25},{2,0},{3,27},{4,2},{5,29},{6,4},{7,31},{8,14},{9,1},{... | collective-permute-start | bytes 1044488 | tf_op jit(solution)/shard_map/ppermute | solution.py:52
  31.4 13.0 %copy-start.10 = (bf16[272,640]{1,0:T(8,128)(2,1)}, bf16[272,640]{1,0:T(8,128)(2,1)S(1)}, u32[]{:S(2)}) copy-start(bf16[272,640]{1,0:T(8,128)(2,1)S(1)} %collective-permute-done.8.refs_0_) | copy-start | bytes 1044484
  31.4 11.5 %collective-permute-start.12 = (bf16[272,640]{1,0:T(8,128)(2,1)S(1)}, bf16[272,640]{1,0:T(8,128)(2,1)S(1)}, u32[]{:S(2)}, u32[]{:S(2)}) collective-permute-start(bf16[272,640]{1,0:T(8,128)(2,1)S(1)} %collective-permute-done.8.refs_0_), channel_id=1, source_target_pairs={{0,2},{1,9},{2,4},{3,11},{4,6},{5,13},{6,0},{7,15},{8,10},{9,17},{... | collective-permute-start | bytes 1044488 | tf_op jit(solution)/shard_map/ppermute | solution.py:52
  36.1 9.6 %copy-start.11 = (bf16[272,640]{1,0:T(8,128)(2,1)}, bf16[272,640]{1,0:T(8,128)(2,1)S(1)}, u32[]{:S(2)}) copy-start(bf16[272,640]{1,0:T(8,128)(2,1)S(1)} %collective-permute-done.10.refs_2_) | copy-start | bytes 1044484
  36.1 9.6 %collective-permute-start.9 = (bf16[272,640]{1,0:T(8,128)(2,1)}, bf16[272,640]{1,0:T(8,128)(2,1)S(1)}, u32[]{:S(2)}, u32[]{:S(2)}) collective-permute-start(bf16[272,640]{1,0:T(8,128)(2,1)} %collective-permute-done.refs_1_), channel_id=1, source_target_pairs={{0,2},{1,9},{2,4},{3,11},{4,6},{5,13},{6,0},{7,15},{8,10},{9,17},{... | collective-permute-start | bytes 1044488 | tf_op jit(solution)/shard_map/ppermute | solution.py:52
  37.3 26.7 %copy-start.7 = (bf16[2,256,640]{2,1,0:T(8,128)(2,1)}, bf16[2,256,640]{2,1,0:T(8,128)(2,1)S(1)}, u32[]{:S(2)}) copy-start(bf16[2,256,640]{2,1,0:T(8,128)(2,1)S(1)} %collective-permute-done.4.refs_8_.refs_12_) | copy-start | bytes 1966084
  37.3 26.7 %collective-permute-start.2 = (bf16[2,256,640]{2,1,0:T(8,128)(2,1)S(1)}, bf16[2,256,640]{2,1,0:T(8,128)(2,1)}, u32[]{:S(2)}, u32[]{:S(2)}) collective-permute-start(bf16[2,256,640]{2,1,0:T(8,128)(2,1)S(1)} %copy-done.5), channel_id=1, source_target_pairs={{0,24},{1,7},{2,26},{3,1},{4,28},{5,3},{6,30},{7,5},{8,0},{9,15},{... | collective-permute-start | bytes 1966088 | tf_op jit(solution)/shard_map/ppermute | solution.py:52
  42.5 21.5 %collective-permute-start.7 = (bf16[2,256,640]{2,1,0:T(8,128)(2,1)S(1)}, bf16[2,256,640]{2,1,0:T(8,128)(2,1)}, u32[]{:S(2)}, u32[]{:S(2)}) collective-permute-start(bf16[2,256,640]{2,1,0:T(8,128)(2,1)S(1)} %collective-permute-done.1.refs_3_.refs_7_), channel_id=1, source_target_pairs={{0,8},{1,3},{2,10},{3,5},{4,12},{5,7},{6,14},{7,1},{8,16},{9,11},{... | collective-permute-start | bytes 1966088 | tf_op jit(solution)/shard_map/ppermute | solution.py:52
  43.0 2.8 %copy-start.12 = (bf16[272,640]{1,0:T(8,128)(2,1)}, bf16[272,640]{1,0:T(8,128)(2,1)S(1)}, u32[]{:S(2)}) copy-start(bf16[272,640]{1,0:T(8,128)(2,1)S(1)} %collective-permute-done.12.refs_4_) | copy-start | bytes 1044484
  43.0 21.0 %collective-permute-start.5 = (bf16[2,256,640]{2,1,0:T(8,128)(2,1)S(1)}, bf16[2,256,640]{2,1,0:T(8,128)(2,1)}, u32[]{:S(2)}, u32[]{:S(2)}) collective-permute-start(bf16[2,256,640]{2,1,0:T(8,128)(2,1)S(1)} %collective-permute-done.4.refs_8_.refs_12_), channel_id=1, source_target_pairs={{0,8},{1,3},{2,10},{3,5},{4,12},{5,7},{6,14},{7,1},{8,16},{9,11},{... | collective-permute-start | bytes 1966088 | tf_op jit(solution)/shard_map/ppermute | solution.py:52
  44.5 19.6 %copy-start.8 = (bf16[2,256,640]{2,1,0:T(8,128)(2,1)}, bf16[2,256,640]{2,1,0:T(8,128)(2,1)S(1)}, u32[]{:S(2)}) copy-start(bf16[2,256,640]{2,1,0:T(8,128)(2,1)S(1)} %collective-permute-done.3.refs_5_.refs_9_) | copy-start | bytes 1966084
  44.5 19.5 %collective-permute-start.6 = (bf16[2,256,640]{2,1,0:T(8,128)(2,1)S(1)}, bf16[2,256,640]{2,1,0:T(8,128)(2,1)}, u32[]{:S(2)}, u32[]{:S(2)}) collective-permute-start(bf16[2,256,640]{2,1,0:T(8,128)(2,1)S(1)} %collective-permute-done.3.refs_5_.refs_9_), channel_id=1, source_target_pairs={{0,24},{1,7},{2,26},{3,1},{4,28},{5,3},{6,30},{7,5},{8,0},{9,15},{... | collective-permute-start | bytes 1966088 | tf_op jit(solution)/shard_map/ppermute | solution.py:52
  45.7 0.8 copy-start.13
  46.5 16.3 %collective-permute-start.13 = (bf16[272,640]{1,0:T(8,128)(2,1)}, bf16[272,640]{1,0:T(8,128)(2,1)}, u32[]{:S(2)}, u32[]{:S(2)}) collective-permute-start(bf16[272,640]{1,0:T(8,128)(2,1)} %collective-permute-done.11.refs_3_), channel_id=1, source_target_pairs={{0,6},{1,25},{2,0},{3,27},{4,2},{5,29},{6,4},{7,31},{8,14},{9,1},{... | collective-permute-start | bytes 1044488 | tf_op jit(solution)/shard_map/ppermute | solution.py:52
  49.1 0.9 copy-start.1
  52.8 76.6 %all-to-all-start.1 = ((bf16[8,400,128]{2,1,0:T(8,128)(2,1)}), bf16[8,400,128]{2,1,0:T(8,128)(2,1)S(1)}, u32[]{:S(2)}, u32[]{:S(2)}) async-start(bf16[8,400,128]{2,1,0:T(8,128)(2,1)} %prefix.1), calls=%async_computation.1 | async-start | bytes 1638400 | tf_op jit(solution)/shard_map/all_to_all | solution.py:429
  79.9 21.0 %collective-permute-start.14 = (bf16[2,272,640]{2,1,0:T(8,128)(2,1)}, bf16[2,272,640]{2,1,0:T(8,128)(2,1)S(1)}, u32[]{:S(2)}, u32[]{:S(2)}) collective-permute-start(bf16[2,272,640]{2,1,0:T(8,128)(2,1)} %get-tuple-element.21), channel_id=1, source_target_pairs={{0,6},{1,25},{2,0},{3,27},{4,2},{5,29},{6,4},{7,31},{8,14},{9,1},{... | collective-permute-start | bytes 2088968 | tf_op jit(solution)/shard_map/ppermute | solution.py:52
  85.2 19.1 %collective-permute-start.15 = (bf16[2,272,640]{2,1,0:T(8,128)(2,1)}, bf16[2,272,640]{2,1,0:T(8,128)(2,1)S(1)}, u32[]{:S(2)}, u32[]{:S(2)}) collective-permute-start(bf16[2,272,640]{2,1,0:T(8,128)(2,1)} %get-tuple-element.22), channel_id=1, source_target_pairs={{0,2},{1,9},{2,4},{3,11},{4,6},{5,13},{6,0},{7,15},{8,10},{9,17},{... | collective-permute-start | bytes 2088968 | tf_op jit(solution)/shard_map/ppermute | solution.py:52
  85.2 19.1 %collective-permute-start.16 = (bf16[2,272,640]{2,1,0:T(8,128)(2,1)}, bf16[2,272,640]{2,1,0:T(8,128)(2,1)S(1)}, u32[]{:S(2)}, u32[]{:S(2)}) collective-permute-start(bf16[2,272,640]{2,1,0:T(8,128)(2,1)} %get-tuple-element.23), channel_id=1, source_target_pairs={{0,4},{1,17},{2,6},{3,19},{4,0},{5,21},{6,2},{7,23},{8,12},{9,25},... | collective-permute-start | bytes 2088968 | tf_op jit(solution)/shard_map/ppermute | solution.py:52
  100.9 3.3 %copy-start.2 = (bf16[2,272,640]{2,1,0:T(8,128)(2,1)}, bf16[2,272,640]{2,1,0:T(8,128)(2,1)S(1)}, u32[]{:S(2)}) copy-start(bf16[2,272,640]{2,1,0:T(8,128)(2,1)S(1)} %collective-permute-done.14.refs_1_) | copy-start | bytes 2088964
  104.2 0.9 copy-start.3
  105.1 0.9 copy-start.4
  111.1 24.5 %collective-permute-start.17 = (bf16[256,640]{1,0:T(8,128)(2,1)}, bf16[256,640]{1,0:T(8,128)(2,1)S(1)}, u32[]{:S(2)}, u32[]{:S(2)}) collective-permute-start(bf16[256,640]{1,0:T(8,128)(2,1)} %get-tuple-element.25), channel_id=1, source_target_pairs={{0,1},{1,0},{2,3},{3,2},{4,5},{5,4},{6,7},{7,6},{8,9},{9,8},{10,11... | collective-permute-start | bytes 983048 | tf_op jit(solution)/shard_map/ppermute | solution.py:56
  129.3 0.9 copy-start
  135.6 0.7 copy-start.9

commit v2 on v1

v2 whole, which is shorter than its diff:
```python
import functools
import math

import jax
import jax.numpy as jnp
import numpy as np
from jax import lax
from jax.experimental import pallas as pl
from jax.experimental.pallas import tpu as pltpu
from jax.sharding import PartitionSpec as P

D = 2560
HEADS = 20
FEAT = 16
FEATS = 153
FROWS = 160
FPAD = 256
SM_HD = 128
SM_W = 1280
BLK = 128
TOK = 256
LISTED = 8
GROUP = 4
HALF = 640
HALF_HEADS = 5
QROWS = 272
SIDE = 4
CORES = 2

inv_root_two = 0.7071067811865476
TO_LOG2 = math.log2(math.e) / math.sqrt(SM_HD)
NEG = -1e30
BF = jnp.bfloat16
F32 = jnp.float32
NT = (((1,), (1,)), ((), ()))


def along(what, step):
    pairs = []
    for x in range(SIDE):
        for y in range(SIDE):
            for c in range(CORES):
                on_x = (c == 0) == (what == "kv")
                x2 = (x + step) % SIDE if on_x else x
                y2 = y if on_x else (y + step) % SIDE
                pairs.append(((x * SIDE + y) * CORES + c, (x2 * SIDE + y2) * CORES + c))
    return pairs


def move(a, what, step):
    return lax.ppermute(a, "files", along(what, step))


def swap_cores(a):
    return lax.ppermute(a, "files", [(i, i ^ 1) for i in range(SIDE * SIDE * CORES)])


def feature_tables():
    rows, cols = np.triu_indices(FEAT)
    one = np.zeros((GROUP, 2, FPAD, GROUP * FEAT), np.float32)
    for j in range(GROUP):
        for f in range(FEAT):
            one[j, 0, 1 + f, j * FEAT + f] = 0.5
        for n in range(len(rows)):
            one[j, 0, 1 + FEAT + n, j * FEAT + rows[n]] = 0.5
            one[j, 1, 1 + FEAT + n, j * FEAT + cols[n]] = 0.5
    first = np.zeros(FPAD, np.float32)
    first[0] = 1.0
    second = np.zeros(FPAD, np.float32)
    second[: 1 + FEAT] = 1.0
    factor = np.zeros(FPAD, np.float32)
    factor[:FEATS] = 1.0
    factor[1 + FEAT : FEATS] = np.where(rows == cols, inv_root_two, 1.0).astype(np.float32)
    vectors = np.stack([first, second, factor])
    tall = np.ascontiguousarray(np.broadcast_to(vectors[:, :FROWS, None], (3, FROWS, 128)))
    wide = np.zeros((8, FPAD), np.float32)
    wide[:3] = vectors
    by_row = np.ascontiguousarray(one[:, :, :FROWS]).reshape(GROUP, 2 * FROWS, GROUP * FEAT)
    by_lane = np.ascontiguousarray(one.transpose(0, 3, 1, 2)).reshape(GROUP, GROUP * FEAT, 2 * FPAD)
    return by_row.astype(jnp.bfloat16), by_lane.astype(jnp.bfloat16), tall, wide


def column(j):
    return slice(j * 128, (j + 1) * 128)


def with_ones(values):
    return jnp.concatenate([values, jnp.ones(values.shape, BF)], axis=1)


def state_kernel(k_ref, v_ref, select_ref, tall_ref, out_ref, phi_ref):
    row = lax.broadcasted_iota(jnp.int32, (FROWS, 128), 0)
    lane = lax.broadcasted_iota(jnp.int32, (FROWS, 128), 1)
    first, second, factor = (jnp.concatenate([tall_ref[i], tall_ref[i]], axis=1) for i in range(3))
    norms = jnp.zeros((FROWS, 128), F32)
    for j in range(GROUP):
        ab = jnp.dot(select_ref[j], k_ref[...], preferred_element_type=F32)
        phi = ((ab[:FROWS] + first) * (ab[FROWS:] + second) * factor).astype(BF)
        phi_ref[j] = phi
        both = jnp.dot(phi, with_ones(v_ref[:, column(j)]), preferred_element_type=F32)
        norms = jnp.where(lane == j, both[:, 128:], norms)
        out_ref[j] = both[:, :128].astype(BF)
    flat = jnp.concatenate([norms, jnp.zeros((256 - FROWS, 128), F32)], axis=0).T
    high = flat.astype(BF).astype(F32)
    low = flat - high
    at = row[FROWS - 16 :] - FEATS
    for j in range(GROUP):
        tail = jnp.zeros((16, 128), F32)
        pieces = (high[j : j + 1, :128], high[j : j + 1, 128:], low[j : j + 1, :128], low[j : j + 1, 128:])
        old = out_ref[j, FROWS - 16 :].astype(F32)
        for i, piece in enumerate(pieces):
            tail = jnp.where(at == i, piece, tail)
        out_ref[j, FROWS - 16 :] = jnp.where(at < 0, old, tail).astype(BF)


def prefix_kernel(place_ref, in_ref, out_ref):
    rows = in_ref.shape[1]
    row = lax.broadcasted_iota(jnp.int32, (rows, 128), 0) + (place_ref[0] & 1) * (FROWS // 2)
    row = jnp.where(row >= FROWS, row - FROWS, row)
    row = jnp.where(row >= FROWS, row - FROWS, row)
    high = (row == FEATS) | (row == FEATS + 1)
    low = (row == FEATS + 2) | (row == FEATS + 3)
    total = jnp.zeros((rows, 128), F32)
    for z in range(in_ref.shape[0]):
        both = total + pltpu.roll(total, rows - 2, 0)
        top = both.astype(BF).astype(F32)
        rest = pltpu.roll(both - top, 2, 0)
        out_ref[z] = jnp.where(high, top, jnp.where(low, rest, total)).astype(BF)
        total = total + in_ref[z].astype(F32)


def local_kernel(q_ref, phi_k_ref, v_ref, select_ref, wide_ref, num_ref, den_ref, phi_ref):
    causal = lax.broadcasted_iota(jnp.int32, (TOK, TOK), 0) >= lax.broadcasted_iota(jnp.int32, (TOK, TOK), 1)
    lane = lax.broadcasted_iota(jnp.int32, (TOK, 128), 1)
    x = q_ref[...].T
    den = jnp.zeros((TOK, 128), F32)
    for j in range(GROUP):
        a = jnp.dot(x, select_ref[j, :, :FPAD], preferred_element_type=F32)
        b = jnp.dot(x, select_ref[j, :, FPAD:], preferred_element_type=F32)
        phi_q = ((a + wide_ref[0:1]) * (b + wide_ref[1:2]) * wide_ref[2:3]).astype(BF)
        phi_ref[j] = phi_q
        phi_k = jnp.concatenate([phi_k_ref[j], jnp.zeros((FPAD - FROWS, TOK), BF)], axis=0)
        weight = jnp.where(causal, jnp.dot(phi_q, phi_k, preferred_element_type=F32), 0.0)
        both = jnp.dot(weight.astype(BF), with_ones(v_ref[:, column(j)]), preferred_element_type=F32)
        num_ref[:, column(j)] = both[:, :128]
        den = jnp.where(lane == j, both[:, 128:], den)
    den_ref[...] = den


def finish_kernel(num_ref, den_ref, phi_ref, state_ref, out_ref):
    lane = lax.broadcasted_iota(jnp.int32, (TOK, 128), 1)
    for j in range(GROUP):
        phi = phi_ref[j]
        state = state_ref[j]
        padded = jnp.concatenate([state, jnp.zeros((FPAD - FROWS, 128), BF)], axis=0)
        carried = jnp.dot(phi, padded, preferred_element_type=F32)
        tail = state[FROWS - 16 : FROWS].astype(F32)
        at = FEATS - (FROWS - 16)
        n0 = tail[at : at + 1] + tail[at + 2 : at + 3]
        n1 = tail[at + 1 : at + 2] + tail[at + 3 : at + 4]
        phi32 = phi.astype(F32)
        den = jnp.where(lane == j, den_ref[...], 0.0) + phi32[:, :128] * n0 + phi32[:, 128:] * n1
        den = jnp.sum(den, axis=1, keepdims=True)
        out_ref[:, column(j)] = ((num_ref[:, column(j)] + carried) / den).astype(BF)


def halves(core, refs):
    at = pl.ds(pl.multiple_of(core * HALF, 128), HALF)
    return [r.at[:, at] for r in refs]


def listed_rows(ids_ref, count_ref):
    lane = lax.broadcasted_iota(jnp.int32, (QROWS - TOK, HALF), 1)
    listed = jnp.full((QROWS - TOK, HALF), -1.0, F32)
    for i in range(LISTED):
        entry = jnp.where(i < count_ref[0], ids_ref[i], -1).astype(F32)
        listed = jnp.where(lane == i, entry, listed)
    return listed.astype(BF)


def pack_kernel(me_ref, ids_ref, count_ref, k_ref, v_ref, q_ref, out_ref, sems):
    copies = [
        pltpu.make_async_copy(half, out_ref.at[pl.ds(i * TOK, TOK)], sems.at[i])
        for i, half in enumerate(halves(1 - (me_ref[0] & 1), (k_ref, v_ref, q_ref)))
    ]
    for c in copies:
        c.start()
    out_ref[3 * TOK :] = listed_rows(ids_ref, count_ref)
    for c in copies:
        c.wait()


def pair_kernel(me_ref, ids_ref, count_ref, k_ref, v_ref, q_ref, mate_ref, kv_ref, both_ref, sems):
    targets = (kv_ref.at[0, 0], kv_ref.at[0, 1], both_ref.at[0, pl.ds(0, TOK)])
    copies = [
        pltpu.make_async_copy(half, to, sems.at[i])
        for i, (half, to) in enumerate(zip(halves(me_ref[0] & 1, (k_ref, v_ref, q_ref)), targets, strict=True))
    ]
    for c in copies:
        c.start()
    both_ref[0, TOK:QROWS] = listed_rows(ids_ref, count_ref)
    kv_ref[1, 0] = mate_ref[0:TOK]
    kv_ref[1, 1] = mate_ref[TOK : 2 * TOK]
    both_ref[1] = mate_ref[2 * TOK :]
    for c in copies:
        c.wait()


def attend_kernel(own, readers, me_ref, *refs):
    groups = readers // 2
    q_in, kv_in, outs = refs[:groups], refs[groups : groups + SIDE], refs[groups + SIDE : readers + SIDE]
    q_buf, g_buf, s_buf, m_buf, a_buf, wanted, ids, found, counts, q_sems, id_sem, g_sems = refs[readers + SIDE :]
    copies = [pltpu.make_async_copy(q_in[i], q_buf.at[pl.ds(2 * i, 2)], q_sems.at[i]) for i in range(groups)]
    for c in copies:
        c.start()
    me = me_ref[0]
    core, y, x = me & 1, (me >> 1) & (SIDE - 1), me >> 3
    lane = lax.broadcasted_iota(jnp.int32, (TOK, 128), 1)
    wanted[...] = jnp.full(wanted.shape, -1, jnp.int32)
    for c in copies:
        c.wait()
    for r in range(readers):
        wanted[r : r + 1] = q_buf[r, TOK:QROWS, 0:128].astype(F32).astype(jnp.int32)[0:1]
    pltpu.async_copy(wanted, ids, id_sem).wait()

    def search(r, carry):
        count = jnp.int32(0)
        for i in range(LISTED):
            entry = ids[r, i]
            xo, yo, co = entry >> 4, (entry >> 2) & (SIDE - 1), (entry >> 1) & 1
            mine = (entry >= 0) & jnp.where(core == 0, yo == y, xo == x)
            away = jnp.where(core == 0, xo - x, yo - y) & (SIDE - 1)
            found[r, count] = (away * 2 + (co ^ core)) * 2 + (entry & 1)
            count = count + mine.astype(jnp.int32)
        counts[r] = count
        return carry

    lax.fori_loop(0, readers, search, 0)
    heads = [(h, slice(h * 128, (h + 1) * 128)) for h in range(HALF_HEADS)]

    def fetch(r, slot):
        def one(i, carry):
            code = found[r, i]
            rows = pl.ds(pl.multiple_of((code & 1) * BLK, BLK), BLK)
            for away in range(SIDE):

                @pl.when((code >> 2) == away)
                def _():
                    source = kv_in[away].at[(code >> 1) & 1, :, rows, :]
                    pltpu.make_async_copy(source, g_buf.at[slot, i], g_sems.at[slot, i]).start()

            return carry

        lax.fori_loop(0, counts[r], one, 0)

    def arrived(r, slot):
        def one(i, carry):
            source = kv_in[0].at[0, :, pl.ds(0, BLK), :]
            pltpu.make_async_copy(source, g_buf.at[slot, i], g_sems.at[slot, i]).wait()
            return carry

        lax.fori_loop(0, counts[r], one, 0)

    def blank(slot, i):
        g_buf[slot, i, 1] = jnp.zeros((BLK, HALF), BF)

    def reader(r, slot, out_ref):
        count = counts[r]
        pairs = (count + 1) >> 1

        @pl.when((count & 1) == 1)
        def _():
            blank(slot, count)

        if not own:

            @pl.when(count == 0)
            def _():
                blank(slot, 0)
                blank(slot, 1)

        def blocks(j, kind, at):
            return jnp.concatenate([g_buf[slot, 2 * j, kind, :, at], g_buf[slot, 2 * j + 1, kind, :, at]], axis=0)

        def score(j, fresh):
            for h, at in heads:
                s = lax.dot_general(q_buf[r, 0:TOK, at], blocks(j, 0, at), NT, preferred_element_type=F32)
                s0, s1 = s[:, :128], jnp.where(2 * j + 1 < count, s[:, 128:], NEG)
                if fresh:
                    s0 = jnp.where(count > 0, s0, NEG)
                s_buf[j, h, :, 0:128] = s0
                s_buf[j, h, :, 128:256] = s1
                m = jnp.maximum(s0, s1)
                m_buf[h] = m if fresh else jnp.maximum(m_buf[h], m)

        def weigh(j, fresh):
            for h, at in heads:
                m = m_buf[h]
                p = jnp.exp2(s_buf[j, h] * TO_LOG2 - jnp.concatenate([m, m], axis=1)).astype(BF)
                a = jnp.dot(p, with_ones(blocks(j, 1, at)), preferred_element_type=F32)
                a_buf[h] = a if fresh else a_buf[h] + a

        if own:
            for h, at in heads:
                parts = []
                for b in range(2):
                    rows = slice(b * BLK, (b + 1) * BLK)
                    k = own_kv[r, 0, rows, at]
                    parts.append(lax.dot_general(q_buf[r, rows, at], k, NT, preferred_element_type=F32))
                s = jnp.concatenate(parts, axis=0)
                s_buf[LISTED // 2, h, :, 0:128] = s
                m_buf[h] = s
        else:
            score(0, True)
        start = 0 if own else 1

        def more_scores(j, carry):
            score(j, False)
            return carry

        lax.fori_loop(start, pairs, more_scores, 0)
        tops = jnp.zeros((TOK, 128), F32)
        for h, at in heads:
            m = jnp.broadcast_to(jnp.max(m_buf[h], axis=1, keepdims=True) * TO_LOG2, (TOK, 128))
            m_buf[h] = m
            tops = jnp.where(lane == h, m, tops)
        if own:
            for h, at in heads:
                p = jnp.exp2(s_buf[LISTED // 2, h, :, 0:128] * TO_LOG2 - m_buf[h]).astype(BF)
                parts = []
                for b in range(2):
                    rows = slice(b * BLK, (b + 1) * BLK)
                    v = with_ones(own_kv[r, 1, rows, at])
                    parts.append(jnp.dot(p[rows], v, preferred_element_type=F32))
                a_buf[h] = jnp.concatenate(parts, axis=0)
        else:
            weigh(0, True)

        def more_weights(j, carry):
            weigh(j, False)
            return carry

        lax.fori_loop(start, pairs, more_weights, 0)
        totals = jnp.ones((TOK, 128), F32)
        for h, at in heads:
            total = a_buf[h, :, 128:]
            out_ref[slot, 0:TOK, at] = (a_buf[h, :, :128] / total).astype(BF)
            totals = jnp.where(lane == h, total, totals)
        sizes = tops + jnp.log2(totals)
        if not own:
            sizes = jnp.where(jnp.logical_and(count == 0, lane < HALF_HEADS), NEG, sizes)
        high = sizes.astype(BF).astype(F32)
        middle = (sizes - high).astype(BF).astype(F32)
        low = sizes - high - middle
        packed = high + pltpu.roll(middle, HALF_HEADS, 1) + pltpu.roll(low, 2 * HALF_HEADS, 1)
        out_ref[slot, TOK:QROWS, :] = jnp.zeros((QROWS - TOK, HALF), BF)
        out_ref[slot, TOK:QROWS, 0:TOK] = packed.T[0 : QROWS - TOK].astype(BF)

    own_kv = kv_in[0]
    fetch(0, 0)
    for g, out_ref in enumerate(outs):

        def one(i, carry, g=g, out_ref=out_ref):
            r = 2 * g + i

            @pl.when(r + 1 < readers)
            def _():
                fetch(r + 1, 1 - i)

            arrived(r, i)
            reader(r, i, out_ref)
            return carry

        lax.fori_loop(0, 2, one, 0)


def join_kernel(*refs):
    parts, outs = refs[:4], refs[4:]
    for r in range(2):
        sizes = []
        for p in parts:
            packed = p[r, TOK:QROWS, 0:TOK].astype(F32)
            packed = jnp.concatenate([packed, jnp.zeros((128 - (QROWS - TOK), TOK), F32)], axis=0).T
            sizes.append(packed + pltpu.roll(packed, 128 - HALF_HEADS, 1) + pltpu.roll(packed, 128 - 2 * HALF_HEADS, 1))
        top = functools.reduce(jnp.maximum, sizes)
        shares = [jnp.exp2(s - top) for s in sizes]
        total = functools.reduce(jnp.add, shares)
        shares = [s / total for s in shares]
        for h in range(HALF_HEADS):
            at = slice(h * 128, (h + 1) * 128)
            o = sum(s[:, h : h + 1] * p[r, 0:TOK, at].astype(F32) for s, p in zip(shares, parts, strict=True))
            outs[r][:, at] = o.astype(BF)


def place_kernel(me_ref, kept_ref, other_ref, out_ref, sems):
    core = me_ref[0] & 1
    copies = [
        pltpu.make_async_copy(half, to, sems.at[i])
        for i, (half, to) in enumerate(zip((kept_ref, other_ref), halves(core, (out_ref,)) + halves(1 - core, (out_ref,)), strict=True))
    ]
    for c in copies:
        c.start()
    for c in copies:
        c.wait()


def shape(*dims, dtype=BF):
    return jax.ShapeDtypeStruct(dims, dtype)


SMEM = pl.BlockSpec(memory_space=pltpu.SMEM)
VMEM = pl.BlockSpec(memory_space=pltpu.VMEM)
ANY = pl.BlockSpec(memory_space=pl.ANY)
HBM = pl.BlockSpec(memory_space=pltpu.HBM)


def room(mib):
    return pltpu.CompilerParams(vmem_limit_bytes=mib * 1024 * 1024)


def cost(flops, moved):
    return pl.CostEstimate(flops=int(flops), bytes_accessed=int(moved), transcendentals=0)


def in_hbm(*arrays):
    return tuple(pltpu.with_memory_space_constraint(a, pltpu.HBM) for a in arrays)


def hbm_shape(*dims, dtype=BF):
    return pltpu.HBM(dims, dtype)


def whole(*dims):
    return pl.BlockSpec(dims, lambda g: (0,) * len(dims))


def attend(name, me, queries, blocks):
    own = name == "attend_own"
    groups = len(queries)
    readers = 2 * groups
    first = VMEM if own else ANY
    return pl.pallas_call(
        functools.partial(attend_kernel, own, readers),
        out_shape=[shape(2, QROWS, HALF)] * groups,
        in_specs=[SMEM] + [ANY] * groups + [first] + [ANY] * (SIDE - 1),
        out_specs=[VMEM] * groups,
        scratch_shapes=[
            pltpu.VMEM((readers, QROWS, HALF), BF),
            pltpu.VMEM((2, LISTED, 2, BLK, HALF), BF),
            pltpu.VMEM((LISTED // 2 + 1, HALF_HEADS, TOK, 256), F32),
            pltpu.VMEM((HALF_HEADS, TOK, 128), F32),
            pltpu.VMEM((HALF_HEADS, TOK, 256), F32),
            pltpu.VMEM((8, 128), jnp.int32),
            pltpu.SMEM((8, 128), jnp.int32),
            pltpu.SMEM((readers, LISTED), jnp.int32),
            pltpu.SMEM((readers,), jnp.int32),
            pltpu.SemaphoreType.DMA((groups,)),
            pltpu.SemaphoreType.DMA,
            pltpu.SemaphoreType.DMA((2, LISTED)),
        ],
        compiler_params=room(24),
        cost_estimate=cost(readers * 4e8, 8e6),
    )(me, *queries, *blocks)


def layers(q_lin, k_lin, v_lin, q_soft, k_soft, v_soft, import_ids, import_counts):
    by_row, by_lane, tall, wide = (jnp.asarray(t) for t in feature_tables())
    me = lax.axis_index("files").astype(jnp.int32).reshape(1)
    place = lax.axis_index("seq").astype(jnp.int32).reshape(1)
    shards = lax.axis_size("seq")
    mine = (me, import_ids[0, 0], import_counts[0]) + in_hbm(k_soft[0], v_soft[0], q_soft[0])
    steps = (HEADS // GROUP,)
    lanes = GROUP * 128

    sent = pl.pallas_call(
        pack_kernel,
        name="pack",
        out_shape=shape(2 * TOK + QROWS, HALF),
        in_specs=[SMEM] * 3 + [HBM] * 3,
        out_specs=VMEM,
        scratch_shapes=[pltpu.SemaphoreType.DMA((3,))],
        compiler_params=room(4),
        cost_estimate=cost(0, 2e6),
    )(*mine)
    mate = swap_cores(sent)

    state, phi_k = pl.pallas_call(
        state_kernel,
        name="state",
        grid=steps,
        out_shape=[hbm_shape(HEADS, FROWS, 128), hbm_shape(HEADS, FROWS, TOK)],
        in_specs=[
            pl.BlockSpec((GROUP * FEAT, TOK), lambda g: (g, 0)),
            pl.BlockSpec((TOK, lanes), lambda g: (0, g)),
            whole(*by_row.shape),
            whole(*tall.shape),
        ],
        out_specs=[
            pl.BlockSpec((GROUP, FROWS, 128), lambda g: (g, 0, 0)),
            pl.BlockSpec((GROUP, FROWS, TOK), lambda g: (g, 0, 0)),
        ],
        compiler_params=room(12),
        cost_estimate=cost(1e9, 4e6),
    )(*in_hbm(k_lin[0].T, v_lin[0], by_row, tall))
    mate, state, phi_k = lax.optimization_barrier((mate, state, phi_k))

    kv, q = pl.pallas_call(
        pair_kernel,
        name="pair",
        out_shape=[shape(2, 2, TOK, HALF), shape(2, QROWS, HALF)],
        in_specs=[SMEM] * 3 + [HBM] * 3 + [VMEM],
        out_specs=[VMEM] * 2,
        scratch_shapes=[pltpu.SemaphoreType.DMA((3,))],
        compiler_params=room(8),
        cost_estimate=cost(0, 4e6),
    )(*mine, mate)
    kv_right = move(kv, "kv", -1)
    kv_left = move(kv, "kv", 1)
    q_left = move(q, "q", 1)
    q_right = move(q, "q", -1)
    kv_far = move(kv_right, "kv", -1)
    q_far = move(q_left, "q", 1)

    slices = lax.all_to_all(state.reshape(shards, HEADS * FROWS // shards, 128), "seq", 0, 0, tiled=True)

    num, den, phi = pl.pallas_call(
        local_kernel,
        name="local",
        grid=steps,
        out_shape=[hbm_shape(TOK, D, dtype=F32), hbm_shape(TOK, HEADS // GROUP * 128, dtype=F32), hbm_shape(HEADS, TOK, FPAD)],
        in_specs=[
            pl.BlockSpec((GROUP * FEAT, TOK), lambda g: (g, 0)),
            pl.BlockSpec((GROUP, FROWS, TOK), lambda g: (g, 0, 0)),
            pl.BlockSpec((TOK, lanes), lambda g: (0, g)),
            whole(*by_lane.shape),
            whole(*wide.shape),
        ],
        out_specs=[
            pl.BlockSpec((TOK, lanes), lambda g: (0, g)),
            pl.BlockSpec((TOK, 128), lambda g: (0, g)),
            pl.BlockSpec((GROUP, TOK, FPAD), lambda g: (g, 0, 0)),
        ],
        compiler_params=room(16),
        cost_estimate=cost(4e9, 8e6),
    )(*in_hbm(q_lin[0].T, phi_k, v_lin[0], by_lane, wide))
    slices, num, den, phi = lax.optimization_barrier((slices, num, den, phi))

    prefix = pl.pallas_call(
        prefix_kernel,
        name="prefix",
        out_shape=shape(*slices.shape),
        in_specs=[SMEM, VMEM],
        out_specs=VMEM,
        compiler_params=room(8),
        cost_estimate=cost(0, 2e6),
    )(place, slices)
    before = lax.all_to_all(prefix, "seq", 0, 0, tiled=True).reshape(HEADS, FROWS, 128)

    blocks = (kv, kv_right, kv_far, kv_left)
    (to_far,) = attend("attend_far", me, (q_far,), blocks)
    to_far, q_left, q_right = lax.optimization_barrier((to_far, q_left, q_right))
    from_far = move(to_far, "q", 2)
    to_left, to_right = attend("attend_sides", me, (q_left, q_right), blocks)
    from_right = move(to_left, "q", -1)
    from_left = move(to_right, "q", 1)
    (here,) = attend("attend_own", me, (q,), blocks)
    kept, send = pl.pallas_call(
        join_kernel,
        name="join",
        out_shape=[shape(TOK, HALF)] * 2,
        in_specs=[VMEM] * 4,
        out_specs=[VMEM] * 2,
        compiler_params=room(8),
        cost_estimate=cost(0, 4e6),
    )(here, from_right, from_left, from_far)
    other = swap_cores(send)
    soft_out = pl.pallas_call(
        place_kernel,
        name="place",
        out_shape=shape(TOK, SM_W),
        in_specs=[SMEM, VMEM, VMEM],
        out_specs=HBM,
        scratch_shapes=[pltpu.SemaphoreType.DMA((2,))],
        compiler_params=room(4),
        cost_estimate=cost(0, 1e6),
    )(me, kept, other)

    lin_out = pl.pallas_call(
        finish_kernel,
        name="finish",
        grid=steps,
        out_shape=shape(TOK, D),
        in_specs=[
            pl.BlockSpec((TOK, lanes), lambda g: (0, g)),
            pl.BlockSpec((TOK, 128), lambda g: (0, g)),
            pl.BlockSpec((GROUP, TOK, FPAD), lambda g: (g, 0, 0)),
            pl.BlockSpec((GROUP, FROWS, 128), lambda g: (g, 0, 0)),
        ],
        out_specs=pl.BlockSpec((TOK, lanes), lambda g: (0, g)),
        compiler_params=room(16),
        cost_estimate=cost(4e8, 8e6),
    )(*in_hbm(num, den, phi), before)
    return lin_out[None], soft_out[None]


def solution(mesh):
    wide = P("files", "seq", None)
    return jax.shard_map(
        layers,
        mesh=mesh,
        in_specs=(wide,) * 7 + (P("files", "seq"),),
        out_specs=(wide, wide),
        check_vma=False,
    )
```

time: 140 us -> 114 us (0.81)
  the two profiles are of different devices: /device:TPU:97 before, /device:TPU:1 now
where the time goes in v2:
time: 114 us; the launch traced here: 113 us
  Pallas kernels  49.6 us (44%)
  starting transfers between devices  35.4 us (31%)
  waiting for transfers between devices  25.4 us (22%)
  between operations  1.56 us (1%)
  local copies, waits for them, and re-layouts  1.49 us (1%)
    ppermute x9, waiting for transfers between devices, move(): return lax.ppermute(a, 'files', along(what, step))  25.4 us
    pallas_call x3, Pallas kernels, attend(): pl.pallas_call(functools.partial(attend_kernel, own, readers), out_shape=...  18.6 us
    ppermute x9, starting transfers between devices, move(): return lax.ppermute(a, 'files', along(what, step))  13 us
    pallas_call x1, Pallas kernels, layers(): pl.pallas_call(local_kernel, name='local', grid=steps, out_shape=[hbm_sha...  9.51 us
    all_to_all x1, starting transfers between devices, layers(): lax.all_to_all(state.reshape(shards, HEADS * FROWS // shards, 128), 'seq'...  8.19 us
    ppermute x2, starting transfers between devices, swap_cores(): lax.ppermute(a, 'files', [(i, i ^ 1) for i in range(SIDE * SIDE * CORES)])  7.81 us
    pallas_call x1, Pallas kernels, layers(): pl.pallas_call(state_kernel, name='state', grid=steps, out_shape=[hbm_sha...  7.05 us
    all_to_all x1, starting transfers between devices, layers(): lax.all_to_all(prefix, 'seq', 0, 0, tiled=True).reshape(HEADS, FROWS, 128)  6.36 us
  transfers between devices with their start and end apart: 13, of which 4 were waited for; matrix products, arithmetic and copies ran while one was open for 0% of the time, Pallas kernels for 40%

profile of v2, /device:TPU:1, one launch (start us, length us, event | category | flops | bytes accessed | tf_op | source)
XLA Modules:
  0.0 113.5 jit_solution(12624048222263206219)
XLA Ops:
  1.3 0.0 copy-start.2
  1.3 0.6 copy-done.2
  1.9 1.7 %pack.1 = bf16[784,640]{1,0:T(8,128)(2,1)S(1)} custom-call(s32[1]{0:T(128)} %bitcast.me_ref, s32[8]{0:T(128)S(1)} %bitcast.21, s32[1]{0:T(128)} %bitcast.18.count_ref, bf16[256,1280]{1,0:T(8,128)(2,1)} %bitcast.23, bf16[256,1280]{1,0:T(8,128)(2,1)} %bitcast.25, bf16[256,1280]{1,0:T(8,128)(2,1)} %bitcast.27), custom_call_target="tpu_custom_call" | custom-call | bytes 2000000 | tf_op jit(solution)/shard_map/pack/pallas_call | solution.py:475
  3.7 3.3 %collective-permute-start = (bf16[784,640]{1,0:T(8,128)(2,1)S(1)}, bf16[784,640]{1,0:T(8,128)(2,1)S(1)}, u32[]{:S(2)}, u32[]{:S(2)}) collective-permute-start(bf16[784,640]{1,0:T(8,128)(2,1)S(1)} %pack.1), channel_id=1, source_target_pairs={{0,1},{1,0},{2,3},{3,2},{4,5},{5,4},{6,7},{7,6},{8,9},{9,8},{10,11... | collective-permute-start | bytes 3010568 | tf_op jit(solution)/shard_map/ppermute | solution.py:55
  7.0 0.0 copy-start.3
  7.0 7.0 %state.1 = (bf16[20,160,128]{2,1,0:T(8,128)(2,1)}, bf16[20,160,256]{2,1,0:T(8,128)(2,1)}) custom-call(bf16[320,256]{1,0:T(8,128)(2,1)} %bitcast.34, bf16[256,2560]{1,0:T(8,128)(2,1)} %bitcast.32, bf16[4,320,64]{2,1,0:T(8,128)(2,1)} %constant.17.clone.select_ref, f32[3,160,128]{2,1,0:T(8,128)} %constant.19.clone.tall_ref), custom_call_target="tpu_custom_call" | custom-call | flops 1000000000 | bytes 4000000 | tf_op jit(solution)/shard_map/state/pallas_call | solution.py:487
  14.0 0.0 collective-permute-done.mate_ref
  14.0 0.0 copy-done.3
  14.0 1.7 %pair.1 = (bf16[2,2,256,640]{3,2,1,0:T(8,128)(2,1)S(1)}, bf16[2,272,640]{2,1,0:T(8,128)(2,1)S(1)}) custom-call(s32[1]{0:T(128)} %bitcast.me_ref, s32[8]{0:T(128)S(1)} %bitcast.22, s32[1]{0:T(128)} %bitcast.19.count_ref, bf16[256,1280]{1,0:T(8,128)(2,1)} %bitcast.24, bf16[256,1280]{1,0:T(8,128)(2,1)} %bitcast.26, bf16[256,1280]{1,0:T(8,128)(2,1)} %bitcast.28, ...), custom_call_target="tpu_custom_call" | custom-call | bytes 4000000 | tf_op jit(solution)/shard_map/pair/pallas_call | solution.py:507
  15.8 0.0 copy-start
  15.8 0.8 copy-done
  16.6 1.0 collective-permute-start.1
  17.7 8.2 %all-to-all-start = ((bf16[8,400,128]{2,1,0:T(8,128)(2,1)}), bf16[8,400,128]{2,1,0:T(8,128)(2,1)S(1)}, u32[]{:S(2)}, u32[]{:S(2)}) async-start(bf16[8,400,128]{2,1,0:T(8,128)(2,1)} %bitcast.30), calls=%async_computation | async-start | bytes 1638400 | tf_op jit(solution)/shard_map/all_to_all | solution.py:524
  25.8 1.2 %collective-permute-start.4 = (bf16[2,272,640]{2,1,0:T(8,128)(2,1)}, bf16[2,272,640]{2,1,0:T(8,128)(2,1)}, u32[]{:S(2)}, u32[]{:S(2)}) collective-permute-start(bf16[2,272,640]{2,1,0:T(8,128)(2,1)} %copy-done), channel_id=1, source_target_pairs={{0,2},{1,9},{2,4},{3,11},{4,6},{5,13},{6,0},{7,15},{8,10},{9,17},{... | collective-permute-start | bytes 2088968 | tf_op jit(solution)/shard_map/ppermute | solution.py:51
  27.1 0.0 collective-permute-start.3
  27.1 6.4 %collective-permute-done.1.refs_2_.refs_3_ = bf16[2,2,256,640]{3,2,1,0:T(8,128)(2,1)S(1)} collective-permute-done((bf16[2,2,256,640]{3,2,1,0:T(8,128)(2,1)S(1)}, bf16[2,2,256,640]{3,2,1,0:T(8,128)(2,1)S(1)}, u32[]{:S(2)}, u32[]{:S(2)}) %collective-permute-start.1) | collective-permute-done | bytes 1310752 | tf_op jit(solution)/shard_map/ppermute | solution.py:51
  33.5 2.2 %collective-permute-start.2 = (bf16[2,2,256,640]{3,2,1,0:T(8,128)(2,1)S(1)}, bf16[2,2,256,640]{3,2,1,0:T(8,128)(2,1)}, u32[]{:S(2)}, u32[]{:S(2)}) collective-permute-start(bf16[2,2,256,640]{3,2,1,0:T(8,128)(2,1)S(1)} %collective-permute-done.1.refs_2_.refs_3_), channel_id=1, source_target_pairs={{0,24},{1,7},{2,26},{3,1},{4,28},{5,3},{6,30},{7,5},{8,0},{9,15},{... | collective-permute-start | bytes 3932168 | tf_op jit(solution)/shard_map/ppermute | solution.py:51
  35.7 7.1 %collective-permute-done.4.refs_0_ = bf16[2,272,640]{2,1,0:T(8,128)(2,1)} collective-permute-done((bf16[2,272,640]{2,1,0:T(8,128)(2,1)}, bf16[2,272,640]{2,1,0:T(8,128)(2,1)}, u32[]{:S(2)}, u32[]{:S(2)}) %collective-permute-start.4) | collective-permute-done | bytes 696352 | tf_op jit(solution)/shard_map/ppermute | solution.py:51
  42.8 1.5 %collective-permute-start.5 = (bf16[2,272,640]{2,1,0:T(8,128)(2,1)}, bf16[2,272,640]{2,1,0:T(8,128)(2,1)}, u32[]{:S(2)}, u32[]{:S(2)}) collective-permute-start(bf16[2,272,640]{2,1,0:T(8,128)(2,1)} %collective-permute-done.4.refs_0_), channel_id=1, source_target_pairs={{0,2},{1,9},{2,4},{3,11},{4,6},{5,13},{6,0},{7,15},{8,10},{9,17},{... | collective-permute-start | bytes 2088968 | tf_op jit(solution)/shard_map/ppermute | solution.py:51
  44.3 1.7 %collective-permute-start.6 = (bf16[2,272,640]{2,1,0:T(8,128)(2,1)}, bf16[2,272,640]{2,1,0:T(8,128)(2,1)}, u32[]{:S(2)}, u32[]{:S(2)}) collective-permute-start(bf16[2,272,640]{2,1,0:T(8,128)(2,1)} %copy-done), channel_id=1, source_target_pairs={{0,6},{1,25},{2,0},{3,27},{4,2},{5,29},{6,4},{7,31},{8,14},{9,1},{... | collective-permute-start | bytes 2088968 | tf_op jit(solution)/shard_map/ppermute | solution.py:51
  46.0 9.5 %local.1 = (f32[256,2560]{1,0:T(8,128)}, f32[256,640]{1,0:T(8,128)}, bf16[20,256,256]{2,1,0:T(8,128)(2,1)}) custom-call(bf16[320,256]{1,0:T(8,128)(2,1)} %bitcast.35, bf16[20,160,256]{2,1,0:T(8,128)(2,1)} %get-tuple-element.26.phi_k_ref, bf16[256,2560]{1,0:T(8,128)(2,1)} %bitcast.33, bf16[4,64,512]{2,1,0:T(8,128)(2,1)} %constant.18.clone.select_ref, ...), custom_call_target="tpu_custom_call" | custom-call | flops 4000000000 | bytes 8000000 | tf_op jit(solution)/shard_map/local/pallas_call | solution.py:526
  55.5 0.0 all-to-all-done.in_ref
  55.5 1.7 %prefix.1 = bf16[8,400,128]{2,1,0:T(8,128)(2,1)} custom-call(s32[1]{0:T(128)} %bitcast.12.place_ref, bf16[8,400,128]{2,1,0:T(8,128)(2,1)S(1)} %all-to-all-done.in_ref), custom_call_target="tpu_custom_call" | custom-call | bytes 2000000 | tf_op jit(solution)/shard_map/prefix/pallas_call | solution.py:548
  57.2 6.4 %all-to-all-start.1 = ((bf16[8,400,128]{2,1,0:T(8,128)(2,1)}), bf16[8,400,128]{2,1,0:T(8,128)(2,1)S(1)}, u32[]{:S(2)}, u32[]{:S(2)}) async-start(bf16[8,400,128]{2,1,0:T(8,128)(2,1)} %prefix.1), calls=%async_computation.1 | async-start | bytes 1638400 | tf_op jit(solution)/shard_map/all_to_all | solution.py:557
  63.6 0.0 collective-permute-done.3.refs_4_.refs_5_
  63.6 0.0 collective-permute-done.5.refs_0_
  63.6 0.0 collective-permute-done.2.refs_3_.refs_4_
  63.6 5.1 %shard_map.132 = bf16[2,272,640]{2,1,0:T(8,128)(2,1)S(1)} custom-call(s32[1]{0:T(128)} %bitcast.me_ref, bf16[2,272,640]{2,1,0:T(8,128)(2,1)} %collective-permute-done.5.refs_0_, bf16[2,2,256,640]{3,2,1,0:T(8,128)(2,1)S(1)} %get-tuple-element.36.refs_1_.refs_2_, bf16[2,2,256,640]{3,2,1,0:T(8,128)(2,1)S(1)} %collective-permute-done.1.refs_2_.refs_3_, ...), custom_call_target="tpu_custom_call" | custom-call | flops 800000000 | bytes 8000000 | tf_op jit(solution)/shard_map/pallas_call | solution.py:442
  68.8 0.0 copy-start.1
  68.8 0.0 collective-permute-done.6.refs_1_
  68.8 7.8 %shard_map.133 = (bf16[2,272,640]{2,1,0:T(8,128)(2,1)S(1)}, bf16[2,272,640]{2,1,0:T(8,128)(2,1)S(1)}) custom-call(s32[1]{0:T(128)} %bitcast.me_ref, bf16[2,272,640]{2,1,0:T(8,128)(2,1)} %collective-permute-done.4.refs_0_, bf16[2,272,640]{2,1,0:T(8,128)(2,1)} %collective-permute-done.6.refs_1_, ...), custom_call_target="tpu_custom_call" | custom-call | flops 1600000000 | bytes 8000000 | tf_op jit(solution)/shard_map/pallas_call | solution.py:442
  76.6 4.1 %collective-permute-start.7 = (bf16[2,272,640]{2,1,0:T(8,128)(2,1)S(1)}, bf16[2,272,640]{2,1,0:T(8,128)(2,1)S(1)}, u32[]{:S(2)}, u32[]{:S(2)}) collective-permute-start(bf16[2,272,640]{2,1,0:T(8,128)(2,1)S(1)} %get-tuple-element.39), channel_id=1, source_target_pairs={{0,6},{1,25},{2,0},{3,27},{4,2},{5,29},{6,4},{7,31},{8,14},{9,1},{... | collective-permute-start | bytes 2088968 | tf_op jit(solution)/shard_map/ppermute | solution.py:51
  80.6 0.0 collective-permute-start.8
  80.6 1.3 %collective-permute-start.9 = (bf16[2,272,640]{2,1,0:T(8,128)(2,1)S(1)}, bf16[2,272,640]{2,1,0:T(8,128)(2,1)S(1)}, u32[]{:S(2)}, u32[]{:S(2)}) collective-permute-start(bf16[2,272,640]{2,1,0:T(8,128)(2,1)S(1)} %shard_map.132), channel_id=1, source_target_pairs={{0,4},{1,17},{2,6},{3,19},{4,0},{5,21},{6,2},{7,23},{8,12},{9,25},... | collective-permute-start | bytes 2088968 | tf_op jit(solution)/shard_map/ppermute | solution.py:51
  81.9 0.0 copy-done.1
  81.9 5.7 %shard_map.131.refs_0_ = bf16[2,272,640]{2,1,0:T(8,128)(2,1)S(1)} custom-call(s32[1]{0:T(128)} %bitcast.me_ref, bf16[2,272,640]{2,1,0:T(8,128)(2,1)S(1)} %copy-done.1, bf16[2,2,256,640]{3,2,1,0:T(8,128)(2,1)S(1)} %get-tuple-element.36.refs_1_.refs_2_, bf16[2,2,256,640]{3,2,1,0:T(8,128)(2,1)S(1)} %collective-permute-done.1.refs_2_.refs_3_, ...), custom_call_target="tpu_custom_call" | custom-call | flops 800000000 | bytes 8000000 | tf_op jit(solution)/shard_map/pallas_call | solution.py:442
  87.6 8.5 %collective-permute-done.7.refs_1_ = bf16[2,272,640]{2,1,0:T(8,128)(2,1)S(1)} collective-permute-done((bf16[2,272,640]{2,1,0:T(8,128)(2,1)S(1)}, bf16[2,272,640]{2,1,0:T(8,128)(2,1)S(1)}, u32[]{:S(2)}, u32[]{:S(2)}) %collective-permute-start.7) | collective-permute-done | bytes 696352 | tf_op jit(solution)/shard_map/ppermute | solution.py:51
  96.1 3.4 %collective-permute-done.8.refs_2_ = bf16[2,272,640]{2,1,0:T(8,128)(2,1)S(1)} collective-permute-done((bf16[2,272,640]{2,1,0:T(8,128)(2,1)S(1)}, bf16[2,272,640]{2,1,0:T(8,128)(2,1)S(1)}, u32[]{:S(2)}, u32[]{:S(2)}) %collective-permute-start.8) | collective-permute-done | bytes 696352 | tf_op jit(solution)/shard_map/ppermute | solution.py:51
  99.5 0.0 collective-permute-done.9.refs_3_
  99.5 2.7 %join.1 = (bf16[256,640]{1,0:T(8,128)(2,1)S(1)}, bf16[256,640]{1,0:T(8,128)(2,1)S(1)}) custom-call(bf16[2,272,640]{2,1,0:T(8,128)(2,1)S(1)} %shard_map.131.refs_0_, bf16[2,272,640]{2,1,0:T(8,128)(2,1)S(1)} %collective-permute-done.7.refs_1_, bf16[2,272,640]{2,1,0:T(8,128)(2,1)S(1)} %collective-permute-done.8.refs_2_, ...), custom_call_target="tpu_custom_call" | custom-call | bytes 4000000 | tf_op jit(solution)/shard_map/join/pallas_call | solution.py:567
  102.2 4.5 %collective-permute-start.10 = (bf16[256,640]{1,0:T(8,128)(2,1)S(1)}, bf16[256,640]{1,0:T(8,128)(2,1)S(1)}, u32[]{:S(2)}, u32[]{:S(2)}) collective-permute-start(bf16[256,640]{1,0:T(8,128)(2,1)S(1)} %get-tuple-element.43), channel_id=1, source_target_pairs={{0,1},{1,0},{2,3},{3,2},{4,5},{5,4},{6,7},{7,6},{8,9},{9,8},{10,11... | collective-permute-start | bytes 983048 | tf_op jit(solution)/shard_map/ppermute | solution.py:55
  106.7 0.0 all-to-all-done.1
  106.7 5.8 %finish.1 = bf16[256,2560]{1,0:T(8,128)(2,1)} custom-call(f32[256,2560]{1,0:T(8,128)} %get-tuple-element.30.num_ref, f32[256,640]{1,0:T(8,128)} %get-tuple-element.31.den_ref, bf16[20,256,256]{2,1,0:T(8,128)(2,1)} %get-tuple-element.32.phi_ref, bf16[20,160,128]{2,1,0:T(8,128)(2,1)S(1)} %bitcast.20), custom_call_target="tpu_custom_call" | custom-call | flops 400000000 | bytes 8000000 | tf_op jit(solution)/shard_map/finish/pallas_call | solution.py:588
  112.4 0.0 collective-permute-done.10.other_ref
  112.5 0.8 place.1
Async XLA Ops:
  1.3 0.7 copy-start.2
  3.7 10.3 %collective-permute-start = (bf16[784,640]{1,0:T(8,128)(2,1)S(1)}, bf16[784,640]{1,0:T(8,128)(2,1)S(1)}, u32[]{:S(2)}, u32[]{:S(2)}) collective-permute-start(bf16[784,640]{1,0:T(8,128)(2,1)S(1)} %pack.1), channel_id=1, source_target_pairs={{0,1},{1,0},{2,3},{3,2},{4,5},{5,4},{6,7},{7,6},{8,9},{9,8},{10,11... | collective-permute-start | bytes 3010568 | tf_op jit(solution)/shard_map/ppermute | solution.py:55
  7.0 7.1 %copy-start.3 = (s32[1,1,8]{2,1,0:T(1,128)S(1)}, s32[1,1,8]{2,1,0:T(1,128)}, u32[]{:S(2)}) copy-start(s32[1,1,8]{2,1,0:T(1,128)} %param.18) | copy-start | bytes 100
  15.8 0.8 copy-start
  16.6 16.9 %collective-permute-start.1 = (bf16[2,2,256,640]{3,2,1,0:T(8,128)(2,1)S(1)}, bf16[2,2,256,640]{3,2,1,0:T(8,128)(2,1)S(1)}, u32[]{:S(2)}, u32[]{:S(2)}) collective-permute-start(bf16[2,2,256,640]{3,2,1,0:T(8,128)(2,1)S(1)} %get-tuple-element.36.refs_1_.refs_2_), channel_id=1, source_target_pairs={{0,24},{1,7},{2,26},{3,1},{4,28},{5,3},{6,30},{7,5},{8,0},{9,15},{... | collective-permute-start | bytes 3932168 | tf_op jit(solution)/shard_map/ppermute | solution.py:51
  17.7 37.9 %all-to-all-start = ((bf16[8,400,128]{2,1,0:T(8,128)(2,1)}), bf16[8,400,128]{2,1,0:T(8,128)(2,1)S(1)}, u32[]{:S(2)}, u32[]{:S(2)}) async-start(bf16[8,400,128]{2,1,0:T(8,128)(2,1)} %bitcast.30), calls=%async_computation | async-start | bytes 1638400 | tf_op jit(solution)/shard_map/all_to_all | solution.py:524
  25.8 17.0 %collective-permute-start.4 = (bf16[2,272,640]{2,1,0:T(8,128)(2,1)}, bf16[2,272,640]{2,1,0:T(8,128)(2,1)}, u32[]{:S(2)}, u32[]{:S(2)}) collective-permute-start(bf16[2,272,640]{2,1,0:T(8,128)(2,1)} %copy-done), channel_id=1, source_target_pairs={{0,2},{1,9},{2,4},{3,11},{4,6},{5,13},{6,0},{7,15},{8,10},{9,17},{... | collective-permute-start | bytes 2088968 | tf_op jit(solution)/shard_map/ppermute | solution.py:51
  27.1 36.5 %collective-permute-start.3 = (bf16[2,2,256,640]{3,2,1,0:T(8,128)(2,1)S(1)}, bf16[2,2,256,640]{3,2,1,0:T(8,128)(2,1)}, u32[]{:S(2)}, u32[]{:S(2)}) collective-permute-start(bf16[2,2,256,640]{3,2,1,0:T(8,128)(2,1)S(1)} %get-tuple-element.36.refs_1_.refs_2_), channel_id=1, source_target_pairs={{0,8},{1,3},{2,10},{3,5},{4,12},{5,7},{6,14},{7,1},{8,16},{9,11},{... | collective-permute-start | bytes 3932168 | tf_op jit(solution)/shard_map/ppermute | solution.py:51
  33.5 30.1 %collective-permute-start.2 = (bf16[2,2,256,640]{3,2,1,0:T(8,128)(2,1)S(1)}, bf16[2,2,256,640]{3,2,1,0:T(8,128)(2,1)}, u32[]{:S(2)}, u32[]{:S(2)}) collective-permute-start(bf16[2,2,256,640]{3,2,1,0:T(8,128)(2,1)S(1)} %collective-permute-done.1.refs_2_.refs_3_), channel_id=1, source_target_pairs={{0,24},{1,7},{2,26},{3,1},{4,28},{5,3},{6,30},{7,5},{8,0},{9,15},{... | collective-permute-start | bytes 3932168 | tf_op jit(solution)/shard_map/ppermute | solution.py:51
  42.8 20.8 %collective-permute-start.5 = (bf16[2,272,640]{2,1,0:T(8,128)(2,1)}, bf16[2,272,640]{2,1,0:T(8,128)(2,1)}, u32[]{:S(2)}, u32[]{:S(2)}) collective-permute-start(bf16[2,272,640]{2,1,0:T(8,128)(2,1)} %collective-permute-done.4.refs_0_), channel_id=1, source_target_pairs={{0,2},{1,9},{2,4},{3,11},{4,6},{5,13},{6,0},{7,15},{8,10},{9,17},{... | collective-permute-start | bytes 2088968 | tf_op jit(solution)/shard_map/ppermute | solution.py:51
  44.3 24.5 %collective-permute-start.6 = (bf16[2,272,640]{2,1,0:T(8,128)(2,1)}, bf16[2,272,640]{2,1,0:T(8,128)(2,1)}, u32[]{:S(2)}, u32[]{:S(2)}) collective-permute-start(bf16[2,272,640]{2,1,0:T(8,128)(2,1)} %copy-done), channel_id=1, source_target_pairs={{0,6},{1,25},{2,0},{3,27},{4,2},{5,29},{6,4},{7,31},{8,14},{9,1},{... | collective-permute-start | bytes 2088968 | tf_op jit(solution)/shard_map/ppermute | solution.py:51
  57.2 49.5 %all-to-all-start.1 = ((bf16[8,400,128]{2,1,0:T(8,128)(2,1)}), bf16[8,400,128]{2,1,0:T(8,128)(2,1)S(1)}, u32[]{:S(2)}, u32[]{:S(2)}) async-start(bf16[8,400,128]{2,1,0:T(8,128)(2,1)} %prefix.1), calls=%async_computation.1 | async-start | bytes 1638400 | tf_op jit(solution)/shard_map/all_to_all | solution.py:557
  68.8 13.1 %copy-start.1 = (bf16[2,272,640]{2,1,0:T(8,128)(2,1)S(1)}, bf16[2,272,640]{2,1,0:T(8,128)(2,1)}, u32[]{:S(2)}) copy-start(bf16[2,272,640]{2,1,0:T(8,128)(2,1)} %copy-done) | copy-start | bytes 2088964
  76.6 19.5 %collective-permute-start.7 = (bf16[2,272,640]{2,1,0:T(8,128)(2,1)S(1)}, bf16[2,272,640]{2,1,0:T(8,128)(2,1)S(1)}, u32[]{:S(2)}, u32[]{:S(2)}) collective-permute-start(bf16[2,272,640]{2,1,0:T(8,128)(2,1)S(1)} %get-tuple-element.39), channel_id=1, source_target_pairs={{0,6},{1,25},{2,0},{3,27},{4,2},{5,29},{6,4},{7,31},{8,14},{9,1},{... | collective-permute-start | bytes 2088968 | tf_op jit(solution)/shard_map/ppermute | solution.py:51
  80.6 18.8 %collective-permute-start.8 = (bf16[2,272,640]{2,1,0:T(8,128)(2,1)S(1)}, bf16[2,272,640]{2,1,0:T(8,128)(2,1)S(1)}, u32[]{:S(2)}, u32[]{:S(2)}) collective-permute-start(bf16[2,272,640]{2,1,0:T(8,128)(2,1)S(1)} %get-tuple-element.40), channel_id=1, source_target_pairs={{0,2},{1,9},{2,4},{3,11},{4,6},{5,13},{6,0},{7,15},{8,10},{9,17},{... | collective-permute-start | bytes 2088968 | tf_op jit(solution)/shard_map/ppermute | solution.py:51
  80.6 18.8 %collective-permute-start.9 = (bf16[2,272,640]{2,1,0:T(8,128)(2,1)S(1)}, bf16[2,272,640]{2,1,0:T(8,128)(2,1)S(1)}, u32[]{:S(2)}, u32[]{:S(2)}) collective-permute-start(bf16[2,272,640]{2,1,0:T(8,128)(2,1)S(1)} %shard_map.132), channel_id=1, source_target_pairs={{0,4},{1,17},{2,6},{3,19},{4,0},{5,21},{6,2},{7,23},{8,12},{9,25},... | collective-permute-start | bytes 2088968 | tf_op jit(solution)/shard_map/ppermute | solution.py:51
  102.2 10.3 %collective-permute-start.10 = (bf16[256,640]{1,0:T(8,128)(2,1)S(1)}, bf16[256,640]{1,0:T(8,128)(2,1)S(1)}, u32[]{:S(2)}, u32[]{:S(2)}) collective-permute-start(bf16[256,640]{1,0:T(8,128)(2,1)S(1)} %get-tuple-element.43), channel_id=1, source_target_pairs={{0,1},{1,0},{2,3},{3,2},{4,5},{5,4},{6,7},{7,6},{8,9},{9,8},{10,11... | collective-permute-start | bytes 983048 | tf_op jit(solution)/shard_map/ppermute | solution.py:55

commit v3 on v2

--- a/solution.py
+++ b/solution.py
@@ -57,60 +57,59 @@
 
 def feature_tables():
     rows, cols = np.triu_indices(FEAT)
-    one = np.zeros((GROUP, 2, FPAD, GROUP * FEAT), np.float32)
+    select = np.zeros((GROUP, 2, FROWS, GROUP * FEAT), np.float32)
     for j in range(GROUP):
         for f in range(FEAT):
-            one[j, 0, 1 + f, j * FEAT + f] = 0.5
+            select[j, 0, 1 + f, j * FEAT + f] = 0.5
         for n in range(len(rows)):
-            one[j, 0, 1 + FEAT + n, j * FEAT + rows[n]] = 0.5
-            one[j, 1, 1 + FEAT + n, j * FEAT + cols[n]] = 0.5
-    first = np.zeros(FPAD, np.float32)
-    first[0] = 1.0
-    second = np.zeros(FPAD, np.float32)
-    second[: 1 + FEAT] = 1.0
-    factor = np.zeros(FPAD, np.float32)
-    factor[:FEATS] = 1.0
-    factor[1 + FEAT : FEATS] = np.where(rows == cols, inv_root_two, 1.0).astype(np.float32)
-    vectors = np.stack([first, second, factor])
-    tall = np.ascontiguousarray(np.broadcast_to(vectors[:, :FROWS, None], (3, FROWS, 128)))
-    wide = np.zeros((8, FPAD), np.float32)
-    wide[:3] = vectors
-    by_row = np.ascontiguousarray(one[:, :, :FROWS]).reshape(GROUP, 2 * FROWS, GROUP * FEAT)
-    by_lane = np.ascontiguousarray(one.transpose(0, 3, 1, 2)).reshape(GROUP, GROUP * FEAT, 2 * FPAD)
-    return by_row.astype(jnp.bfloat16), by_lane.astype(jnp.bfloat16), tall, wide
+            select[j, 0, 1 + FEAT + n, j * FEAT + rows[n]] = 0.5
+            select[j, 1, 1 + FEAT + n, j * FEAT + cols[n]] = 0.5
+    vectors = np.zeros((3, FROWS), np.float32)
+    vectors[0, 0] = 1.0
+    vectors[1, : 1 + FEAT] = 1.0
+    vectors[2, :FEATS] = 1.0
+    vectors[2, 1 + FEAT : FEATS] = np.where(rows == cols, inv_root_two, 1.0).astype(np.float32)
+    vectors = np.ascontiguousarray(np.broadcast_to(vectors[:, :, None], (3, FROWS, 128)))
+    return select.reshape(GROUP, 2 * FROWS, GROUP * FEAT).astype(jnp.bfloat16), vectors
 
 
 def column(j):
     return slice(j * 128, (j + 1) * 128)
 
 
+def features(select, x, vectors):
+    first, second, factor = (jnp.concatenate([vectors[i], vectors[i]], axis=1) for i in range(3))
+    ab = jnp.dot(select, x, preferred_element_type=F32)
+    return ((ab[:FROWS] + first) * (ab[FROWS:] + second) * factor).astype(BF)
+
+
+def taller(phi):
+    return jnp.concatenate([phi, jnp.zeros((FPAD - FROWS, phi.shape[1]), BF)], axis=0)
+
+
 def with_ones(values):
     return jnp.concatenate([values, jnp.ones(values.shape, BF)], axis=1)
 
 
-def state_kernel(k_ref, v_ref, select_ref, tall_ref, out_ref, phi_ref):
-    row = lax.broadcasted_iota(jnp.int32, (FROWS, 128), 0)
+def state_kernel(k_ref, v_ref, select_ref, vector_ref, out_ref):
+    row = lax.broadcasted_iota(jnp.int32, (16, 128), 0)
     lane = lax.broadcasted_iota(jnp.int32, (FROWS, 128), 1)
-    first, second, factor = (jnp.concatenate([tall_ref[i], tall_ref[i]], axis=1) for i in range(3))
     norms = jnp.zeros((FROWS, 128), F32)
     for j in range(GROUP):
-        ab = jnp.dot(select_ref[j], k_ref[...], preferred_element_type=F32)
-        phi = ((ab[:FROWS] + first) * (ab[FROWS:] + second) * factor).astype(BF)
-        phi_ref[j] = phi
+        phi = features(select_ref[j], k_ref[...], vector_ref)
         both = jnp.dot(phi, with_ones(v_ref[:, column(j)]), preferred_element_type=F32)
         norms = jnp.where(lane == j, both[:, 128:], norms)
         out_ref[j] = both[:, :128].astype(BF)
-    flat = jnp.concatenate([norms, jnp.zeros((256 - FROWS, 128), F32)], axis=0).T
+    flat = jnp.concatenate([norms, jnp.zeros((FPAD - FROWS, 128), F32)], axis=0).T
     high = flat.astype(BF).astype(F32)
     low = flat - high
-    at = row[FROWS - 16 :] - FEATS
+    at = row + (FROWS - 16 - FEATS)
     for j in range(GROUP):
-        tail = jnp.zeros((16, 128), F32)
+        tail = out_ref[j, FROWS - 16 :].astype(F32)
         pieces = (high[j : j + 1, :128], high[j : j + 1, 128:], low[j : j + 1, :128], low[j : j + 1, 128:])
-        old = out_ref[j, FROWS - 16 :].astype(F32)
         for i, piece in enumerate(pieces):
             tail = jnp.where(at == i, piece, tail)
-        out_ref[j, FROWS - 16 :] = jnp.where(at < 0, old, tail).astype(BF)
+        out_ref[j, FROWS - 16 :] = tail.astype(BF)
 
 
 def prefix_kernel(place_ref, in_ref, out_ref):
@@ -129,39 +128,43 @@
         total = total + in_ref[z].astype(F32)
 
 
-def local_kernel(q_ref, phi_k_ref, v_ref, select_ref, wide_ref, num_ref, den_ref, phi_ref):
+def local_kernel(q_ref, k_ref, v_ref, select_ref, vector_ref, num_ref, den_ref, phi_ref):
     causal = lax.broadcasted_iota(jnp.int32, (TOK, TOK), 0) >= lax.broadcasted_iota(jnp.int32, (TOK, TOK), 1)
     lane = lax.broadcasted_iota(jnp.int32, (TOK, 128), 1)
-    x = q_ref[...].T
-    den = jnp.zeros((TOK, 128), F32)
+    group = pl.program_id(0)
+
+    @pl.when(group == 0)
+    def _():
+        den_ref[...] = jnp.zeros((TOK, 128), F32)
+
+    den = den_ref[...]
     for j in range(GROUP):
-        a = jnp.dot(x, select_ref[j, :, :FPAD], preferred_element_type=F32)
-        b = jnp.dot(x, select_ref[j, :, FPAD:], preferred_element_type=F32)
-        phi_q = ((a + wide_ref[0:1]) * (b + wide_ref[1:2]) * wide_ref[2:3]).astype(BF)
+        phi_q = features(select_ref[j], q_ref[...], vector_ref)
         phi_ref[j] = phi_q
-        phi_k = jnp.concatenate([phi_k_ref[j], jnp.zeros((FPAD - FROWS, TOK), BF)], axis=0)
-        weight = jnp.where(causal, jnp.dot(phi_q, phi_k, preferred_element_type=F32), 0.0)
-        both = jnp.dot(weight.astype(BF), with_ones(v_ref[:, column(j)]), preferred_element_type=F32)
-        num_ref[:, column(j)] = both[:, :128]
-        den = jnp.where(lane == j, both[:, 128:], den)
+        phi_k = features(select_ref[j], k_ref[...], vector_ref)
+        weight = jnp.dot(taller(phi_q).T, taller(phi_k), preferred_element_type=F32)
+        weight = jnp.where(causal, weight, 0.0).astype(BF)
+        both = jnp.dot(weight, with_ones(v_ref[:, column(j)]), preferred_element_type=F32)
+        num_ref[:, column(j)] = both[:, :128].astype(BF)
+        den = jnp.where(lane == group * GROUP + j, both[:, 128:], den)
     den_ref[...] = den
 
 
 def finish_kernel(num_ref, den_ref, phi_ref, state_ref, out_ref):
     lane = lax.broadcasted_iota(jnp.int32, (TOK, 128), 1)
+    group = pl.program_id(0)
+    at = FEATS - (FROWS - 16)
     for j in range(GROUP):
-        phi = phi_ref[j]
+        phi = taller(phi_ref[j]).T
         state = state_ref[j]
-        padded = jnp.concatenate([state, jnp.zeros((FPAD - FROWS, 128), BF)], axis=0)
-        carried = jnp.dot(phi, padded, preferred_element_type=F32)
+        carried = jnp.dot(phi, taller(state), preferred_element_type=F32)
         tail = state[FROWS - 16 : FROWS].astype(F32)
-        at = FEATS - (FROWS - 16)
         n0 = tail[at : at + 1] + tail[at + 2 : at + 3]
         n1 = tail[at + 1 : at + 2] + tail[at + 3 : at + 4]
         phi32 = phi.astype(F32)
-        den = jnp.where(lane == j, den_ref[...], 0.0) + phi32[:, :128] * n0 + phi32[:, 128:] * n1
+        den = jnp.where(lane == group * GROUP + j, den_ref[...], 0.0) + phi32[:, :128] * n0 + phi32[:, 128:] * n1
         den = jnp.sum(den, axis=1, keepdims=True)
-        out_ref[:, column(j)] = ((num_ref[:, column(j)] + carried) / den).astype(BF)
+        out_ref[:, column(j)] = ((num_ref[:, column(j)].astype(F32) + carried) / den).astype(BF)
 
 
 def halves(core, refs):
@@ -206,41 +209,50 @@
         c.wait()
 
 
-def attend_kernel(own, readers, me_ref, *refs):
-    groups = readers // 2
-    q_in, kv_in, outs = refs[:groups], refs[groups : groups + SIDE], refs[groups + SIDE : readers + SIDE]
-    q_buf, g_buf, s_buf, m_buf, a_buf, wanted, ids, found, counts, q_sems, id_sem, g_sems = refs[readers + SIDE :]
-    copies = [pltpu.make_async_copy(q_in[i], q_buf.at[pl.ds(2 * i, 2)], q_sems.at[i]) for i in range(groups)]
-    for c in copies:
-        c.start()
+def search_kernel(me_ref, *refs):
+    q_in, (found_ref, count_ref, wanted, ids, sems) = refs[:SIDE], refs[SIDE:]
     me = me_ref[0]
     core, y, x = me & 1, (me >> 1) & (SIDE - 1), me >> 3
-    lane = lax.broadcasted_iota(jnp.int32, (TOK, 128), 1)
-    wanted[...] = jnp.full(wanted.shape, -1, jnp.int32)
+    rows = pl.ds(TOK, QROWS - TOK)
+    copies = [
+        pltpu.make_async_copy(q_in[i].at[:, rows, pl.ds(0, 128)], ids.at[pl.ds(2 * i, 2)], sems.at[i]) for i in range(SIDE)
+    ]
+    for c in copies:
+        c.start()
     for c in copies:
         c.wait()
-    for r in range(readers):
-        wanted[r : r + 1] = q_buf[r, TOK:QROWS, 0:128].astype(F32).astype(jnp.int32)[0:1]
-    pltpu.async_copy(wanted, ids, id_sem).wait()
+    for r in range(2 * SIDE):
+        wanted[r : r + 1] = ids[r].astype(F32).astype(jnp.int32)[0:1]
+    pltpu.async_copy(wanted, found_ref, sems.at[SIDE]).wait()
 
     def search(r, carry):
         count = jnp.int32(0)
         for i in range(LISTED):
-            entry = ids[r, i]
+            entry = found_ref[r, i]
             xo, yo, co = entry >> 4, (entry >> 2) & (SIDE - 1), (entry >> 1) & 1
             mine = (entry >= 0) & jnp.where(core == 0, yo == y, xo == x)
             away = jnp.where(core == 0, xo - x, yo - y) & (SIDE - 1)
-            found[r, count] = (away * 2 + (co ^ core)) * 2 + (entry & 1)
+            found_ref[r, count] = (away * 2 + (co ^ core)) * 2 + (entry & 1)
             count = count + mine.astype(jnp.int32)
-        counts[r] = count
+        count_ref[r] = count
         return carry
 
-    lax.fori_loop(0, readers, search, 0)
+    lax.fori_loop(0, 2 * SIDE, search, 0)
+
+
+def attend_kernel(own, base, readers, found, counts, *refs):
+    groups = readers // 2
+    q_in, kv_in, outs = refs[:groups], refs[groups : groups + SIDE], refs[groups + SIDE : readers + SIDE]
+    q_buf, g_buf, s_buf, m_buf, a_buf, q_sems, g_sems = refs[readers + SIDE :]
+    copies = [pltpu.make_async_copy(q_in[i], q_buf.at[pl.ds(2 * i, 2)], q_sems.at[i]) for i in range(groups)]
+    for c in copies:
+        c.start()
+    lane = lax.broadcasted_iota(jnp.int32, (TOK, 128), 1)
     heads = [(h, slice(h * 128, (h + 1) * 128)) for h in range(HALF_HEADS)]
 
     def fetch(r, slot):
         def one(i, carry):
-            code = found[r, i]
+            code = found[base + r, i]
             rows = pl.ds(pl.multiple_of((code & 1) * BLK, BLK), BLK)
             for away in range(SIDE):
 
@@ -251,7 +263,7 @@
 
             return carry
 
-        lax.fori_loop(0, counts[r], one, 0)
+        lax.fori_loop(0, counts[base + r], one, 0)
 
     def arrived(r, slot):
         def one(i, carry):
@@ -259,13 +271,13 @@
             pltpu.make_async_copy(source, g_buf.at[slot, i], g_sems.at[slot, i]).wait()
             return carry
 
-        lax.fori_loop(0, counts[r], one, 0)
+        lax.fori_loop(0, counts[base + r], one, 0)
 
     def blank(slot, i):
         g_buf[slot, i, 1] = jnp.zeros((BLK, HALF), BF)
 
     def reader(r, slot, out_ref):
-        count = counts[r]
+        count = counts[base + r]
         pairs = (count + 1) >> 1
 
         @pl.when((count & 1) == 1)
@@ -358,6 +370,8 @@
 
     own_kv = kv_in[0]
     fetch(0, 0)
+    for c in copies:
+        c.wait()
     for g, out_ref in enumerate(outs):
 
         def one(i, carry, g=g, out_ref=out_ref):
@@ -434,15 +448,15 @@
     return pl.BlockSpec(dims, lambda g: (0,) * len(dims))
 
 
-def attend(name, me, queries, blocks):
+def attend(name, base, lists, queries, blocks):
     own = name == "attend_own"
     groups = len(queries)
     readers = 2 * groups
     first = VMEM if own else ANY
     return pl.pallas_call(
-        functools.partial(attend_kernel, own, readers),
+        functools.partial(attend_kernel, own, base, readers),
         out_shape=[shape(2, QROWS, HALF)] * groups,
-        in_specs=[SMEM] + [ANY] * groups + [first] + [ANY] * (SIDE - 1),
+        in_specs=[SMEM, SMEM] + [ANY] * groups + [first] + [ANY] * (SIDE - 1),
         out_specs=[VMEM] * groups,
         scratch_shapes=[
             pltpu.VMEM((readers, QROWS, HALF), BF),
@@ -450,27 +464,23 @@
             pltpu.VMEM((LISTED // 2 + 1, HALF_HEADS, TOK, 256), F32),
             pltpu.VMEM((HALF_HEADS, TOK, 128), F32),
             pltpu.VMEM((HALF_HEADS, TOK, 256), F32),
-            pltpu.VMEM((8, 128), jnp.int32),
-            pltpu.SMEM((8, 128), jnp.int32),
-            pltpu.SMEM((readers, LISTED), jnp.int32),
-            pltpu.SMEM((readers,), jnp.int32),
             pltpu.SemaphoreType.DMA((groups,)),
-            pltpu.SemaphoreType.DMA,
             pltpu.SemaphoreType.DMA((2, LISTED)),
         ],
-        compiler_params=room(24),
+        compiler_params=room(20),
         cost_estimate=cost(readers * 4e8, 8e6),
-    )(me, *queries, *blocks)
+    )(*lists, *queries, *blocks)
 
 
 def layers(q_lin, k_lin, v_lin, q_soft, k_soft, v_soft, import_ids, import_counts):
-    by_row, by_lane, tall, wide = (jnp.asarray(t) for t in feature_tables())
+    select, vectors = (jnp.asarray(t) for t in feature_tables())
     me = lax.axis_index("files").astype(jnp.int32).reshape(1)
     place = lax.axis_index("seq").astype(jnp.int32).reshape(1)
     shards = lax.axis_size("seq")
+    steps = (HEADS // GROUP,)
+    heads16 = pl.BlockSpec((GROUP * FEAT, TOK), lambda g: (g, 0))
+    heads128 = pl.BlockSpec((TOK, GROUP * 128), lambda g: (0, g))
     mine = (me, import_ids[0, 0], import_counts[0]) + in_hbm(k_soft[0], v_soft[0], q_soft[0])
-    steps = (HEADS // GROUP,)
-    lanes = GROUP * 128
 
     sent = pl.pallas_call(
         pack_kernel,
@@ -484,25 +494,17 @@
     )(*mine)
     mate = swap_cores(sent)
 
-    state, phi_k = pl.pallas_call(
+    state = pl.pallas_call(
         state_kernel,
         name="state",
         grid=steps,
-        out_shape=[hbm_shape(HEADS, FROWS, 128), hbm_shape(HEADS, FROWS, TOK)],
-        in_specs=[
-            pl.BlockSpec((GROUP * FEAT, TOK), lambda g: (g, 0)),
-            pl.BlockSpec((TOK, lanes), lambda g: (0, g)),
-            whole(*by_row.shape),
-            whole(*tall.shape),
-        ],
-        out_specs=[
-            pl.BlockSpec((GROUP, FROWS, 128), lambda g: (g, 0, 0)),
-            pl.BlockSpec((GROUP, FROWS, TOK), lambda g: (g, 0, 0)),
-        ],
+        out_shape=hbm_shape(HEADS, FROWS, 128),
+        in_specs=[heads16, heads128, whole(*select.shape), whole(*vectors.shape)],
+        out_specs=pl.BlockSpec((GROUP, FROWS, 128), lambda g: (g, 0, 0)),
         compiler_params=room(12),
         cost_estimate=cost(1e9, 4e6),
-    )(*in_hbm(k_lin[0].T, v_lin[0], by_row, tall))
-    mate, state, phi_k = lax.optimization_barrier((mate, state, phi_k))
+    )(*in_hbm(k_lin[0].T, v_lin[0], select, vectors))
+    mate, state = lax.optimization_barrier((mate, state))
 
     kv, q = pl.pallas_call(
         pair_kernel,
@@ -527,28 +529,18 @@
         local_kernel,
         name="local",
         grid=steps,
-        out_shape=[hbm_shape(TOK, D, dtype=F32), hbm_shape(TOK, HEADS // GROUP * 128, dtype=F32), hbm_shape(HEADS, TOK, FPAD)],
-        in_specs=[
-            pl.BlockSpec((GROUP * FEAT, TOK), lambda g: (g, 0)),
-            pl.BlockSpec((GROUP, FROWS, TOK), lambda g: (g, 0, 0)),
-            pl.BlockSpec((TOK, lanes), lambda g: (0, g)),
-            whole(*by_lane.shape),
-            whole(*wide.shape),
-        ],
-        out_specs=[
-            pl.BlockSpec((TOK, lanes), lambda g: (0, g)),
-            pl.BlockSpec((TOK, 128), lambda g: (0, g)),
-            pl.BlockSpec((GROUP, TOK, FPAD), lambda g: (g, 0, 0)),
-        ],
+        out_shape=[hbm_shape(TOK, D), hbm_shape(TOK, 128, dtype=F32), hbm_shape(HEADS, FROWS, TOK)],
+        in_specs=[heads16, heads16, heads128, whole(*select.shape), whole(*vectors.shape)],
+        out_specs=[heads128, whole(TOK, 128), pl.BlockSpec((GROUP, FROWS, TOK), lambda g: (g, 0, 0))],
         compiler_params=room(16),
         cost_estimate=cost(4e9, 8e6),
-    )(*in_hbm(q_lin[0].T, phi_k, v_lin[0], by_lane, wide))
+    )(*in_hbm(q_lin[0].T, k_lin[0].T, v_lin[0], select, vectors))
     slices, num, den, phi = lax.optimization_barrier((slices, num, den, phi))
 
     prefix = pl.pallas_call(
         prefix_kernel,
         name="prefix",
-        out_shape=shape(*slices.shape),
+        out_shape=hbm_shape(*slices.shape),
         in_specs=[SMEM, VMEM],
         out_specs=VMEM,
         compiler_params=room(8),
@@ -557,13 +549,27 @@
     before = lax.all_to_all(prefix, "seq", 0, 0, tiled=True).reshape(HEADS, FROWS, 128)
 
     blocks = (kv, kv_right, kv_far, kv_left)
-    (to_far,) = attend("attend_far", me, (q_far,), blocks)
+    lists = pl.pallas_call(
+        search_kernel,
+        name="search",
+        out_shape=[shape(2 * SIDE, 128, dtype=jnp.int32), shape(2 * SIDE, dtype=jnp.int32)],
+        in_specs=[SMEM] + [ANY] * SIDE,
+        out_specs=[SMEM] * 2,
+        scratch_shapes=[
+            pltpu.VMEM((2 * SIDE, 128), jnp.int32),
+            pltpu.VMEM((2 * SIDE, QROWS - TOK, 128), BF),
+            pltpu.SemaphoreType.DMA((SIDE + 1,)),
+        ],
+        compiler_params=room(2),
+        cost_estimate=cost(0, 1e5),
+    )(me, q_far, q_left, q_right, q)
+    (to_far,) = attend("attend_far", 0, lists, (q_far,), blocks)
     to_far, q_left, q_right = lax.optimization_barrier((to_far, q_left, q_right))
     from_far = move(to_far, "q", 2)
-    to_left, to_right = attend("attend_sides", me, (q_left, q_right), blocks)
+    to_left, to_right = attend("attend_sides", 2, lists, (q_left, q_right), blocks)
     from_right = move(to_left, "q", -1)
     from_left = move(to_right, "q", 1)
-    (here,) = attend("attend_own", me, (q,), blocks)
+    (here,) = attend("attend_own", 6, lists, (q,), blocks)
     kept, send = pl.pallas_call(
         join_kernel,
         name="join",
@@ -591,12 +597,12 @@
         grid=steps,
         out_shape=shape(TOK, D),
         in_specs=[
-            pl.BlockSpec((TOK, lanes), lambda g: (0, g)),
-            pl.BlockSpec((TOK, 128), lambda g: (0, g)),
-            pl.BlockSpec((GROUP, TOK, FPAD), lambda g: (g, 0, 0)),
+            heads128,
+            whole(TOK, 128),
+            pl.BlockSpec((GROUP, FROWS, TOK), lambda g: (g, 0, 0)),
             pl.BlockSpec((GROUP, FROWS, 128), lambda g: (g, 0, 0)),
         ],
-        out_specs=pl.BlockSpec((TOK, lanes), lambda g: (0, g)),
+        out_specs=heads128,
         compiler_params=room(16),
         cost_estimate=cost(4e8, 8e6),
     )(*in_hbm(num, den, phi), before)

time: 114 us -> 114 us (level)
  waiting for transfers between devices: 25.4 us -> 23.3 us
  Pallas kernels: 49.6 us -> 50.8 us
    ppermute x9, waiting for transfers between devices: 25.4 us -> 23.3 us  [move(): return lax.ppermute(a, 'files', along(what, step))]
    ppermute x2, starting transfers between devices: 7.81 us -> 5.66 us  [swap_cores(): lax.ppermute(a, 'files', [(i, i ^ 1) for i in range(SIDE * SIDE * CORES)])]
    ppermute x9, starting transfers between devices: 13 us -> 14.7 us  [move(): return lax.ppermute(a, 'files', along(what, step))]
    pallas_call x1, Pallas kernels: 9.51 us -> 10.9 us  [layers(): pl.pallas_call(local_kernel, name='local', grid=steps, out_shape=[hbm_sha...]
    unnamed x8 -> x10, local copies, waits for them, and re-layouts: 1.49 us -> 2.6 us
    pallas_call x5 -> x6, Pallas kernels: 27.3 us -> 27.5 us  [the longest x3 16 us: attend(): pl.pallas_call(functools.partial(attend_kernel, own, base, readers), out_...]
  transfers between devices with their start and end apart: 13 -> 13, of which waited for: 4 -> 4; matrix products, arithmetic and copies ran while one was open for 0% -> 0% of each run, Pallas kernels for 40% -> 41%
where the time goes in v3:
time: 114 us; the launch traced here: 113 us
  Pallas kernels  50.8 us (45%)
  starting transfers between devices  34.9 us (31%)
  waiting for transfers between devices  23.3 us (20%)
  local copies, waits for them, and re-layouts  2.6 us (2%)
  between operations  1.58 us (1%)
    ppermute x9, waiting for transfers between devices, move(): return lax.ppermute(a, 'files', along(what, step))  23.3 us
    pallas_call x3, Pallas kernels, attend(): pl.pallas_call(functools.partial(attend_kernel, own, base, readers), out_...  16 us
    ppermute x9, starting transfers between devices, move(): return lax.ppermute(a, 'files', along(what, step))  14.7 us
    pallas_call x1, Pallas kernels, layers(): pl.pallas_call(local_kernel, name='local', grid=steps, out_shape=[hbm_sha...  10.9 us
    all_to_all x1, starting transfers between devices, layers(): lax.all_to_all(state.reshape(shards, HEADS * FROWS // shards, 128), 'seq'...  8.19 us
    pallas_call x1, Pallas kernels, layers(): pl.pallas_call(state_kernel, name='state', grid=steps, out_shape=hbm_shap...  7 us
    all_to_all x1, starting transfers between devices, layers(): lax.all_to_all(prefix, 'seq', 0, 0, tiled=True).reshape(HEADS, FROWS, 128)  6.36 us
    ppermute x2, starting transfers between devices, swap_cores(): lax.ppermute(a, 'files', [(i, i ^ 1) for i in range(SIDE * SIDE * CORES)])  5.66 us
  transfers between devices with their start and end apart: 13, of which 4 were waited for; matrix products, arithmetic and copies ran while one was open for 0% of the time, Pallas kernels for 41%

profile of v3, /device:TPU:1, one launch (start us, length us, event | category | flops | bytes accessed | tf_op | source)
XLA Modules:
  0.0 113.1 jit_solution(15860736820264617041)
XLA Ops:
  1.3 0.0 copy-start.3
  1.3 0.6 copy-done.3
  1.9 1.7 %pack.1 = bf16[784,640]{1,0:T(8,128)(2,1)S(1)} custom-call(s32[1]{0:T(128)} %bitcast.me_ref, s32[8]{0:T(128)S(1)} %bitcast.21, s32[1]{0:T(128)} %bitcast.18.count_ref, bf16[256,1280]{1,0:T(8,128)(2,1)} %bitcast.23, bf16[256,1280]{1,0:T(8,128)(2,1)} %bitcast.25, bf16[256,1280]{1,0:T(8,128)(2,1)} %bitcast.27), custom_call_target="tpu_custom_call" | custom-call | bytes 2000000 | tf_op jit(solution)/shard_map/pack/pallas_call | solution.py:485
  3.7 3.3 %collective-permute-start = (bf16[784,640]{1,0:T(8,128)(2,1)S(1)}, bf16[784,640]{1,0:T(8,128)(2,1)S(1)}, u32[]{:S(2)}, u32[]{:S(2)}) collective-permute-start(bf16[784,640]{1,0:T(8,128)(2,1)S(1)} %pack.1), channel_id=1, source_target_pairs={{0,1},{1,0},{2,3},{3,2},{4,5},{5,4},{6,7},{7,6},{8,9},{9,8},{10,11... | collective-permute-start | bytes 3010568 | tf_op jit(solution)/shard_map/ppermute | solution.py:55
  7.0 0.0 copy-start.4
  7.0 7.0 %state.1 = bf16[20,160,128]{2,1,0:T(8,128)(2,1)} custom-call(bf16[320,256]{1,0:T(8,128)(2,1)} %bitcast.35, bf16[256,2560]{1,0:T(8,128)(2,1)} %bitcast.32, bf16[4,320,64]{2,1,0:T(8,128)(2,1)} %constant.13.clone.select_ref, f32[3,160,128]{2,1,0:T(8,128)} %constant.14.clone.vector_ref), custom_call_target="tpu_custom_call" | custom-call | flops 1000000000 | bytes 4000000 | tf_op jit(solution)/shard_map/state/pallas_call | solution.py:497
  14.0 0.0 collective-permute-done.mate_ref
  14.0 0.0 copy-done.4
  14.0 1.7 %pair.1 = (bf16[2,2,256,640]{3,2,1,0:T(8,128)(2,1)S(1)}, bf16[2,272,640]{2,1,0:T(8,128)(2,1)S(1)}) custom-call(s32[1]{0:T(128)} %bitcast.me_ref, s32[8]{0:T(128)S(1)} %bitcast.22, s32[1]{0:T(128)} %bitcast.19.count_ref, bf16[256,1280]{1,0:T(8,128)(2,1)} %bitcast.24, bf16[256,1280]{1,0:T(8,128)(2,1)} %bitcast.26, bf16[256,1280]{1,0:T(8,128)(2,1)} %bitcast.28, ...), custom_call_target="tpu_custom_call" | custom-call | bytes 4000000 | tf_op jit(solution)/shard_map/pair/pallas_call | solution.py:509
  15.7 0.0 copy-start
  15.7 0.8 copy-done
  16.6 1.0 collective-permute-start.4
  17.6 8.2 %all-to-all-start = ((bf16[8,400,128]{2,1,0:T(8,128)(2,1)}), bf16[8,400,128]{2,1,0:T(8,128)(2,1)S(1)}, u32[]{:S(2)}, u32[]{:S(2)}) async-start(bf16[8,400,128]{2,1,0:T(8,128)(2,1)} %bitcast.30), calls=%async_computation | async-start | bytes 1638400 | tf_op jit(solution)/shard_map/all_to_all | solution.py:526
  25.8 1.2 %collective-permute-start.1 = (bf16[2,272,640]{2,1,0:T(8,128)(2,1)}, bf16[2,272,640]{2,1,0:T(8,128)(2,1)}, u32[]{:S(2)}, u32[]{:S(2)}) collective-permute-start(bf16[2,272,640]{2,1,0:T(8,128)(2,1)} %copy-done), channel_id=1, source_target_pairs={{0,2},{1,9},{2,4},{3,11},{4,6},{5,13},{6,0},{7,15},{8,10},{9,17},{... | collective-permute-start | bytes 2088968 | tf_op jit(solution)/shard_map/ppermute | solution.py:51
  27.0 0.0 collective-permute-start.6
  27.0 6.4 %collective-permute-done.4.refs_2_.refs_3_ = bf16[2,2,256,640]{3,2,1,0:T(8,128)(2,1)S(1)} collective-permute-done((bf16[2,2,256,640]{3,2,1,0:T(8,128)(2,1)S(1)}, bf16[2,2,256,640]{3,2,1,0:T(8,128)(2,1)S(1)}, u32[]{:S(2)}, u32[]{:S(2)}) %collective-permute-start.4) | collective-permute-done | bytes 1310752 | tf_op jit(solution)/shard_map/ppermute | solution.py:51
  33.4 2.2 %collective-permute-start.5 = (bf16[2,2,256,640]{3,2,1,0:T(8,128)(2,1)S(1)}, bf16[2,2,256,640]{3,2,1,0:T(8,128)(2,1)}, u32[]{:S(2)}, u32[]{:S(2)}) collective-permute-start(bf16[2,2,256,640]{3,2,1,0:T(8,128)(2,1)S(1)} %collective-permute-done.4.refs_2_.refs_3_), channel_id=1, source_target_pairs={{0,24},{1,7},{2,26},{3,1},{4,28},{5,3},{6,30},{7,5},{8,0},{9,15},{... | collective-permute-start | bytes 3932168 | tf_op jit(solution)/shard_map/ppermute | solution.py:51
  35.7 2.4 %collective-permute-start.3 = (bf16[2,272,640]{2,1,0:T(8,128)(2,1)}, bf16[2,272,640]{2,1,0:T(8,128)(2,1)}, u32[]{:S(2)}, u32[]{:S(2)}) collective-permute-start(bf16[2,272,640]{2,1,0:T(8,128)(2,1)} %copy-done), channel_id=1, source_target_pairs={{0,6},{1,25},{2,0},{3,27},{4,2},{5,29},{6,4},{7,31},{8,14},{9,1},{... | collective-permute-start | bytes 2088968 | tf_op jit(solution)/shard_map/ppermute | solution.py:51
  38.1 4.7 %collective-permute-done.1.refs_1_.refs_0_ = bf16[2,272,640]{2,1,0:T(8,128)(2,1)} collective-permute-done((bf16[2,272,640]{2,1,0:T(8,128)(2,1)}, bf16[2,272,640]{2,1,0:T(8,128)(2,1)}, u32[]{:S(2)}, u32[]{:S(2)}) %collective-permute-start.1) | collective-permute-done | bytes 696352 | tf_op jit(solution)/shard_map/ppermute | solution.py:51
  42.8 1.5 %collective-permute-start.2 = (bf16[2,272,640]{2,1,0:T(8,128)(2,1)}, bf16[2,272,640]{2,1,0:T(8,128)(2,1)}, u32[]{:S(2)}, u32[]{:S(2)}) collective-permute-start(bf16[2,272,640]{2,1,0:T(8,128)(2,1)} %collective-permute-done.1.refs_1_.refs_0_), channel_id=1, source_target_pairs={{0,2},{1,9},{2,4},{3,11},{4,6},{5,13},{6,0},{7,15},{8,10},{9,17},{... | collective-permute-start | bytes 2088968 | tf_op jit(solution)/shard_map/ppermute | solution.py:51
  44.3 10.9 %local.1 = (bf16[256,2560]{1,0:T(8,128)(2,1)}, f32[256,128]{1,0:T(8,128)}, bf16[20,160,256]{2,1,0:T(8,128)(2,1)}) custom-call(bf16[320,256]{1,0:T(8,128)(2,1)} %bitcast.34, bf16[320,256]{1,0:T(8,128)(2,1)} %bitcast.36, bf16[256,2560]{1,0:T(8,128)(2,1)} %bitcast.33, bf16[4,320,64]{2,1,0:T(8,128)(2,1)} %constant.13.clone.select_ref, ...), custom_call_target="tpu_custom_call" | custom-call | flops 4000000000 | bytes 8000000 | tf_op jit(solution)/shard_map/local/pallas_call | solution.py:528
  55.2 0.0 all-to-all-done.in_ref
  55.2 1.7 %prefix.1 = bf16[8,400,128]{2,1,0:T(8,128)(2,1)} custom-call(s32[1]{0:T(128)} %bitcast.13.place_ref, bf16[8,400,128]{2,1,0:T(8,128)(2,1)S(1)} %all-to-all-done.in_ref), custom_call_target="tpu_custom_call" | custom-call | bytes 2000000 | tf_op jit(solution)/shard_map/prefix/pallas_call | solution.py:540
  56.9 6.4 %all-to-all-start.1 = ((bf16[8,400,128]{2,1,0:T(8,128)(2,1)}), bf16[8,400,128]{2,1,0:T(8,128)(2,1)S(1)}, u32[]{:S(2)}, u32[]{:S(2)}) async-start(bf16[8,400,128]{2,1,0:T(8,128)(2,1)} %prefix.1), calls=%async_computation.1 | async-start | bytes 1638400 | tf_op jit(solution)/shard_map/all_to_all | solution.py:549
  63.3 0.0 collective-permute-done.3.refs_2_.refs_1_
  63.3 0.0 collective-permute-done.2.refs_0_
  63.3 0.0 copy-start.1
  63.3 1.1 copy-done.1
  64.4 2.8 %search.1 = (s32[8,128]{1,0:T(8,128)S(1)}, s32[8]{0:T(128)S(1)}) custom-call(s32[1]{0:T(128)} %bitcast.me_ref, bf16[2,272,640]{2,1,0:T(8,128)(2,1)} %collective-permute-done.2.refs_0_, bf16[2,272,640]{2,1,0:T(8,128)(2,1)} %collective-permute-done.1.refs_1_.refs_0_, bf16[2,272,640]{2,1,0:T(8,128)(2,1)} %collective-permute-done.3.refs_2_.refs_1_, ...), custom_call_target="tpu_custom_call" | custom-call | bytes 100000 | tf_op jit(solution)/shard_map/search/pallas_call | solution.py:552
  67.2 0.0 collective-permute-done.6.refs_4_.refs_5_
  67.2 0.0 collective-permute-done.5.refs_3_.refs_4_
  67.2 4.1 %shard_map.114 = bf16[2,272,640]{2,1,0:T(8,128)(2,1)S(1)} custom-call(s32[8,128]{1,0:T(8,128)S(1)} %get-tuple-element.32.found, s32[8]{0:T(128)S(1)} %get-tuple-element.33.counts, bf16[2,272,640]{2,1,0:T(8,128)(2,1)} %collective-permute-done.2.refs_0_, bf16[2,2,256,640]{3,2,1,0:T(8,128)(2,1)S(1)} %get-tuple-element.34.refs_1_.refs_2_, ...), custom_call_target="tpu_custom_call" | custom-call | flops 800000000 | bytes 8000000 | tf_op jit(solution)/shard_map/pallas_call | solution.py:456
  71.3 0.0 copy-start.2
  71.3 6.4 %shard_map.115 = (bf16[2,272,640]{2,1,0:T(8,128)(2,1)S(1)}, bf16[2,272,640]{2,1,0:T(8,128)(2,1)S(1)}) custom-call(s32[8,128]{1,0:T(8,128)S(1)} %get-tuple-element.32.found, s32[8]{0:T(128)S(1)} %get-tuple-element.33.counts, bf16[2,272,640]{2,1,0:T(8,128)(2,1)} %collective-permute-done.1.refs_1_.refs_0_, ...), custom_call_target="tpu_custom_call" | custom-call | flops 1600000000 | bytes 8000000 | tf_op jit(solution)/shard_map/pallas_call | solution.py:456
  77.8 5.1 %collective-permute-start.7 = (bf16[2,272,640]{2,1,0:T(8,128)(2,1)S(1)}, bf16[2,272,640]{2,1,0:T(8,128)(2,1)S(1)}, u32[]{:S(2)}, u32[]{:S(2)}) collective-permute-start(bf16[2,272,640]{2,1,0:T(8,128)(2,1)S(1)} %get-tuple-element.37), channel_id=1, source_target_pairs={{0,6},{1,25},{2,0},{3,27},{4,2},{5,29},{6,4},{7,31},{8,14},{9,1},{... | collective-permute-start | bytes 2088968 | tf_op jit(solution)/shard_map/ppermute | solution.py:51
  82.8 0.0 collective-permute-start.8
  82.8 1.3 %collective-permute-start.9 = (bf16[2,272,640]{2,1,0:T(8,128)(2,1)S(1)}, bf16[2,272,640]{2,1,0:T(8,128)(2,1)S(1)}, u32[]{:S(2)}, u32[]{:S(2)}) collective-permute-start(bf16[2,272,640]{2,1,0:T(8,128)(2,1)S(1)} %shard_map.114), channel_id=1, source_target_pairs={{0,4},{1,17},{2,6},{3,19},{4,0},{5,21},{6,2},{7,23},{8,12},{9,25},... | collective-permute-start | bytes 2088968 | tf_op jit(solution)/shard_map/ppermute | solution.py:51
  84.1 0.0 copy-done.2
  84.1 5.5 %shard_map.113.refs_0_ = bf16[2,272,640]{2,1,0:T(8,128)(2,1)S(1)} custom-call(s32[8,128]{1,0:T(8,128)S(1)} %get-tuple-element.32.found, s32[8]{0:T(128)S(1)} %get-tuple-element.33.counts, bf16[2,272,640]{2,1,0:T(8,128)(2,1)S(1)} %copy-done.2, bf16[2,2,256,640]{3,2,1,0:T(8,128)(2,1)S(1)} %get-tuple-element.34.refs_1_.refs_2_, ...), custom_call_target="tpu_custom_call" | custom-call | flops 800000000 | bytes 8000000 | tf_op jit(solution)/shard_map/pallas_call | solution.py:456
  89.6 8.7 %collective-permute-done.7.refs_1_ = bf16[2,272,640]{2,1,0:T(8,128)(2,1)S(1)} collective-permute-done((bf16[2,272,640]{2,1,0:T(8,128)(2,1)S(1)}, bf16[2,272,640]{2,1,0:T(8,128)(2,1)S(1)}, u32[]{:S(2)}, u32[]{:S(2)}) %collective-permute-start.7) | collective-permute-done | bytes 696352 | tf_op jit(solution)/shard_map/ppermute | solution.py:51
  98.2 3.4 %collective-permute-done.8.refs_2_ = bf16[2,272,640]{2,1,0:T(8,128)(2,1)S(1)} collective-permute-done((bf16[2,272,640]{2,1,0:T(8,128)(2,1)S(1)}, bf16[2,272,640]{2,1,0:T(8,128)(2,1)S(1)}, u32[]{:S(2)}, u32[]{:S(2)}) %collective-permute-start.8) | collective-permute-done | bytes 696352 | tf_op jit(solution)/shard_map/ppermute | solution.py:51
  101.7 0.0 collective-permute-done.9.refs_3_
  101.7 2.7 %join.1 = (bf16[256,640]{1,0:T(8,128)(2,1)S(1)}, bf16[256,640]{1,0:T(8,128)(2,1)S(1)}) custom-call(bf16[2,272,640]{2,1,0:T(8,128)(2,1)S(1)} %shard_map.113.refs_0_, bf16[2,272,640]{2,1,0:T(8,128)(2,1)S(1)} %collective-permute-done.7.refs_1_, bf16[2,272,640]{2,1,0:T(8,128)(2,1)S(1)} %collective-permute-done.8.refs_2_, ...), custom_call_target="tpu_custom_call" | custom-call | bytes 4000000 | tf_op jit(solution)/shard_map/join/pallas_call | solution.py:573
  104.4 2.4 %collective-permute-start.10 = (bf16[256,640]{1,0:T(8,128)(2,1)S(1)}, bf16[256,640]{1,0:T(8,128)(2,1)S(1)}, u32[]{:S(2)}, u32[]{:S(2)}) collective-permute-start(bf16[256,640]{1,0:T(8,128)(2,1)S(1)} %get-tuple-element.41), channel_id=1, source_target_pairs={{0,1},{1,0},{2,3},{3,2},{4,5},{5,4},{6,7},{7,6},{8,9},{9,8},{10,11... | collective-permute-start | bytes 983048 | tf_op jit(solution)/shard_map/ppermute | solution.py:55
  106.7 0.0 all-to-all-done.1
  106.7 5.4 %finish.1 = bf16[256,2560]{1,0:T(8,128)(2,1)} custom-call(bf16[256,2560]{1,0:T(8,128)(2,1)} %get-tuple-element.26.num_ref, f32[256,128]{1,0:T(8,128)} %get-tuple-element.27.den_ref, bf16[20,160,256]{2,1,0:T(8,128)(2,1)} %get-tuple-element.28.phi_ref, bf16[20,160,128]{2,1,0:T(8,128)(2,1)S(1)} %bitcast.20), custom_call_target="tpu_custom_call" | custom-call | flops 400000000 | bytes 8000000 | tf_op jit(solution)/shard_map/finish/pallas_call | solution.py:594
  112.1 0.0 collective-permute-done.10.other_ref
  112.1 0.8 place.1
Async XLA Ops:
  1.3 0.7 copy-start.3
  3.7 10.3 %collective-permute-start = (bf16[784,640]{1,0:T(8,128)(2,1)S(1)}, bf16[784,640]{1,0:T(8,128)(2,1)S(1)}, u32[]{:S(2)}, u32[]{:S(2)}) collective-permute-start(bf16[784,640]{1,0:T(8,128)(2,1)S(1)} %pack.1), channel_id=1, source_target_pairs={{0,1},{1,0},{2,3},{3,2},{4,5},{5,4},{6,7},{7,6},{8,9},{9,8},{10,11... | collective-permute-start | bytes 3010568 | tf_op jit(solution)/shard_map/ppermute | solution.py:55
  7.0 7.0 %copy-start.4 = (s32[1,1,8]{2,1,0:T(1,128)S(1)}, s32[1,1,8]{2,1,0:T(1,128)}, u32[]{:S(2)}) copy-start(s32[1,1,8]{2,1,0:T(1,128)} %param.16) | copy-start | bytes 100
  15.7 0.9 copy-start
  16.6 16.9 %collective-permute-start.4 = (bf16[2,2,256,640]{3,2,1,0:T(8,128)(2,1)S(1)}, bf16[2,2,256,640]{3,2,1,0:T(8,128)(2,1)S(1)}, u32[]{:S(2)}, u32[]{:S(2)}) collective-permute-start(bf16[2,2,256,640]{3,2,1,0:T(8,128)(2,1)S(1)} %get-tuple-element.34.refs_1_.refs_2_), channel_id=1, source_target_pairs={{0,24},{1,7},{2,26},{3,1},{4,28},{5,3},{6,30},{7,5},{8,0},{9,15},{... | collective-permute-start | bytes 3932168 | tf_op jit(solution)/shard_map/ppermute | solution.py:51
  17.6 37.6 %all-to-all-start = ((bf16[8,400,128]{2,1,0:T(8,128)(2,1)}), bf16[8,400,128]{2,1,0:T(8,128)(2,1)S(1)}, u32[]{:S(2)}, u32[]{:S(2)}) async-start(bf16[8,400,128]{2,1,0:T(8,128)(2,1)} %bitcast.30), calls=%async_computation | async-start | bytes 1638400 | tf_op jit(solution)/shard_map/all_to_all | solution.py:526
  25.8 17.0 %collective-permute-start.1 = (bf16[2,272,640]{2,1,0:T(8,128)(2,1)}, bf16[2,272,640]{2,1,0:T(8,128)(2,1)}, u32[]{:S(2)}, u32[]{:S(2)}) collective-permute-start(bf16[2,272,640]{2,1,0:T(8,128)(2,1)} %copy-done), channel_id=1, source_target_pairs={{0,2},{1,9},{2,4},{3,11},{4,6},{5,13},{6,0},{7,15},{8,10},{9,17},{... | collective-permute-start | bytes 2088968 | tf_op jit(solution)/shard_map/ppermute | solution.py:51
  27.0 40.2 %collective-permute-start.6 = (bf16[2,2,256,640]{3,2,1,0:T(8,128)(2,1)S(1)}, bf16[2,2,256,640]{3,2,1,0:T(8,128)(2,1)}, u32[]{:S(2)}, u32[]{:S(2)}) collective-permute-start(bf16[2,2,256,640]{3,2,1,0:T(8,128)(2,1)S(1)} %get-tuple-element.34.refs_1_.refs_2_), channel_id=1, source_target_pairs={{0,8},{1,3},{2,10},{3,5},{4,12},{5,7},{6,14},{7,1},{8,16},{9,11},{... | collective-permute-start | bytes 3932168 | tf_op jit(solution)/shard_map/ppermute | solution.py:51
  33.4 33.8 %collective-permute-start.5 = (bf16[2,2,256,640]{3,2,1,0:T(8,128)(2,1)S(1)}, bf16[2,2,256,640]{3,2,1,0:T(8,128)(2,1)}, u32[]{:S(2)}, u32[]{:S(2)}) collective-permute-start(bf16[2,2,256,640]{3,2,1,0:T(8,128)(2,1)S(1)} %collective-permute-done.4.refs_2_.refs_3_), channel_id=1, source_target_pairs={{0,24},{1,7},{2,26},{3,1},{4,28},{5,3},{6,30},{7,5},{8,0},{9,15},{... | collective-permute-start | bytes 3932168 | tf_op jit(solution)/shard_map/ppermute | solution.py:51
  35.7 27.6 %collective-permute-start.3 = (bf16[2,272,640]{2,1,0:T(8,128)(2,1)}, bf16[2,272,640]{2,1,0:T(8,128)(2,1)}, u32[]{:S(2)}, u32[]{:S(2)}) collective-permute-start(bf16[2,272,640]{2,1,0:T(8,128)(2,1)} %copy-done), channel_id=1, source_target_pairs={{0,6},{1,25},{2,0},{3,27},{4,2},{5,29},{6,4},{7,31},{8,14},{9,1},{... | collective-permute-start | bytes 2088968 | tf_op jit(solution)/shard_map/ppermute | solution.py:51
  42.8 20.5 %collective-permute-start.2 = (bf16[2,272,640]{2,1,0:T(8,128)(2,1)}, bf16[2,272,640]{2,1,0:T(8,128)(2,1)}, u32[]{:S(2)}, u32[]{:S(2)}) collective-permute-start(bf16[2,272,640]{2,1,0:T(8,128)(2,1)} %collective-permute-done.1.refs_1_.refs_0_), channel_id=1, source_target_pairs={{0,2},{1,9},{2,4},{3,11},{4,6},{5,13},{6,0},{7,15},{8,10},{9,17},{... | collective-permute-start | bytes 2088968 | tf_op jit(solution)/shard_map/ppermute | solution.py:51
  56.9 49.8 %all-to-all-start.1 = ((bf16[8,400,128]{2,1,0:T(8,128)(2,1)}), bf16[8,400,128]{2,1,0:T(8,128)(2,1)S(1)}, u32[]{:S(2)}, u32[]{:S(2)}) async-start(bf16[8,400,128]{2,1,0:T(8,128)(2,1)} %prefix.1), calls=%async_computation.1 | async-start | bytes 1638400 | tf_op jit(solution)/shard_map/all_to_all | solution.py:549
  63.3 1.1 copy-start.1
  71.3 12.8 %copy-start.2 = (bf16[2,272,640]{2,1,0:T(8,128)(2,1)S(1)}, bf16[2,272,640]{2,1,0:T(8,128)(2,1)}, u32[]{:S(2)}) copy-start(bf16[2,272,640]{2,1,0:T(8,128)(2,1)} %copy-done) | copy-start | bytes 2088964
  77.8 20.5 %collective-permute-start.7 = (bf16[2,272,640]{2,1,0:T(8,128)(2,1)S(1)}, bf16[2,272,640]{2,1,0:T(8,128)(2,1)S(1)}, u32[]{:S(2)}, u32[]{:S(2)}) collective-permute-start(bf16[2,272,640]{2,1,0:T(8,128)(2,1)S(1)} %get-tuple-element.37), channel_id=1, source_target_pairs={{0,6},{1,25},{2,0},{3,27},{4,2},{5,29},{6,4},{7,31},{8,14},{9,1},{... | collective-permute-start | bytes 2088968 | tf_op jit(solution)/shard_map/ppermute | solution.py:51
  82.8 18.8 %collective-permute-start.8 = (bf16[2,272,640]{2,1,0:T(8,128)(2,1)S(1)}, bf16[2,272,640]{2,1,0:T(8,128)(2,1)S(1)}, u32[]{:S(2)}, u32[]{:S(2)}) collective-permute-start(bf16[2,272,640]{2,1,0:T(8,128)(2,1)S(1)} %get-tuple-element.38), channel_id=1, source_target_pairs={{0,2},{1,9},{2,4},{3,11},{4,6},{5,13},{6,0},{7,15},{8,10},{9,17},{... | collective-permute-start | bytes 2088968 | tf_op jit(solution)/shard_map/ppermute | solution.py:51
  82.8 18.8 %collective-permute-start.9 = (bf16[2,272,640]{2,1,0:T(8,128)(2,1)S(1)}, bf16[2,272,640]{2,1,0:T(8,128)(2,1)S(1)}, u32[]{:S(2)}, u32[]{:S(2)}) collective-permute-start(bf16[2,272,640]{2,1,0:T(8,128)(2,1)S(1)} %shard_map.114), channel_id=1, source_target_pairs={{0,4},{1,17},{2,6},{3,19},{4,0},{5,21},{6,2},{7,23},{8,12},{9,25},... | collective-permute-start | bytes 2088968 | tf_op jit(solution)/shard_map/ppermute | solution.py:51
  104.4 7.8 %collective-permute-start.10 = (bf16[256,640]{1,0:T(8,128)(2,1)S(1)}, bf16[256,640]{1,0:T(8,128)(2,1)S(1)}, u32[]{:S(2)}, u32[]{:S(2)}) collective-permute-start(bf16[256,640]{1,0:T(8,128)(2,1)S(1)} %get-tuple-element.41), channel_id=1, source_target_pairs={{0,1},{1,0},{2,3},{3,2},{4,5},{5,4},{6,7},{7,6},{8,9},{9,8},{10,11... | collective-permute-start | bytes 983048 | tf_op jit(solution)/shard_map/ppermute | solution.py:55

commit v4 on v3

--- a/solution.py
+++ b/solution.py
@@ -193,7 +193,7 @@
         c.wait()
 
 
-def pair_kernel(me_ref, ids_ref, count_ref, k_ref, v_ref, q_ref, mate_ref, kv_ref, both_ref, sems):
+def own_kernel(me_ref, ids_ref, count_ref, k_ref, v_ref, q_ref, kv_ref, both_ref, sems):
     targets = (kv_ref.at[0, 0], kv_ref.at[0, 1], both_ref.at[0, pl.ds(0, TOK)])
     copies = [
         pltpu.make_async_copy(half, to, sems.at[i])
@@ -202,9 +202,16 @@
     for c in copies:
         c.start()
     both_ref[0, TOK:QROWS] = listed_rows(ids_ref, count_ref)
-    kv_ref[1, 0] = mate_ref[0:TOK]
-    kv_ref[1, 1] = mate_ref[TOK : 2 * TOK]
-    both_ref[1] = mate_ref[2 * TOK :]
+    for c in copies:
+        c.wait()
+
+
+def merge_kernel(mate_ref, kv_in, both_in, kv_ref, both_ref, sems):
+    del kv_in, both_in
+    pieces = ((pl.ds(0, TOK), kv_ref.at[1, 0]), (pl.ds(TOK, TOK), kv_ref.at[1, 1]), (pl.ds(2 * TOK, QROWS), both_ref.at[1]))
+    copies = [pltpu.make_async_copy(mate_ref.at[at], to, sems.at[i]) for i, (at, to) in enumerate(pieces)]
+    for c in copies:
+        c.start()
     for c in copies:
         c.wait()
 
@@ -493,6 +500,35 @@
         cost_estimate=cost(0, 2e6),
     )(*mine)
     mate = swap_cores(sent)
+    pair = [shape(2, 2, TOK, HALF), shape(2, QROWS, HALF)]
+    kv, q = pl.pallas_call(
+        own_kernel,
+        name="own",
+        out_shape=pair,
+        in_specs=[SMEM] * 3 + [HBM] * 3,
+        out_specs=[VMEM] * 2,
+        scratch_shapes=[pltpu.SemaphoreType.DMA((3,))],
+        compiler_params=room(6),
+        cost_estimate=cost(0, 2e6),
+    )(*mine)
+
+    kv, q = pl.pallas_call(
+        merge_kernel,
+        name="merge",
+        out_shape=pair,
+        in_specs=[VMEM, ANY, ANY],
+        out_specs=[ANY] * 2,
+        scratch_shapes=[pltpu.SemaphoreType.DMA((3,))],
+        input_output_aliases={1: 0, 2: 1},
+        compiler_params=room(4),
+        cost_estimate=cost(0, 2e6),
+    )(mate, kv, q)
+    kv_right = move(kv, "kv", -1)
+    kv_left = move(kv, "kv", 1)
+    q_left = move(q, "q", 1)
+    q_right = move(q, "q", -1)
+    kv_far = move(kv_right, "kv", -1)
+    q_far = move(q_left, "q", 1)
 
     state = pl.pallas_call(
         state_kernel,
@@ -504,25 +540,6 @@
         compiler_params=room(12),
         cost_estimate=cost(1e9, 4e6),
     )(*in_hbm(k_lin[0].T, v_lin[0], select, vectors))
-    mate, state = lax.optimization_barrier((mate, state))
-
-    kv, q = pl.pallas_call(
-        pair_kernel,
-        name="pair",
-        out_shape=[shape(2, 2, TOK, HALF), shape(2, QROWS, HALF)],
-        in_specs=[SMEM] * 3 + [HBM] * 3 + [VMEM],
-        out_specs=[VMEM] * 2,
-        scratch_shapes=[pltpu.SemaphoreType.DMA((3,))],
-        compiler_params=room(8),
-        cost_estimate=cost(0, 4e6),
-    )(*mine, mate)
-    kv_right = move(kv, "kv", -1)
-    kv_left = move(kv, "kv", 1)
-    q_left = move(q, "q", 1)
-    q_right = move(q, "q", -1)
-    kv_far = move(kv_right, "kv", -1)
-    q_far = move(q_left, "q", 1)
-
     slices = lax.all_to_all(state.reshape(shards, HEADS * FROWS // shards, 128), "seq", 0, 0, tiled=True)
 
     num, den, phi = pl.pallas_call(
@@ -535,18 +552,6 @@
         compiler_params=room(16),
         cost_estimate=cost(4e9, 8e6),
     )(*in_hbm(q_lin[0].T, k_lin[0].T, v_lin[0], select, vectors))
-    slices, num, den, phi = lax.optimization_barrier((slices, num, den, phi))
-
-    prefix = pl.pallas_call(
-        prefix_kernel,
-        name="prefix",
-        out_shape=hbm_shape(*slices.shape),
-        in_specs=[SMEM, VMEM],
-        out_specs=VMEM,
-        compiler_params=room(8),
-        cost_estimate=cost(0, 2e6),
-    )(place, slices)
-    before = lax.all_to_all(prefix, "seq", 0, 0, tiled=True).reshape(HEADS, FROWS, 128)
 
     blocks = (kv, kv_right, kv_far, kv_left)
     lists = pl.pallas_call(
@@ -565,6 +570,17 @@
     )(me, q_far, q_left, q_right, q)
     (to_far,) = attend("attend_far", 0, lists, (q_far,), blocks)
     to_far, q_left, q_right = lax.optimization_barrier((to_far, q_left, q_right))
+    _, slices, num, den, phi = lax.optimization_barrier((to_far, slices, num, den, phi))
+    prefix = pl.pallas_call(
+        prefix_kernel,
+        name="prefix",
+        out_shape=hbm_shape(*slices.shape),
+        in_specs=[SMEM, VMEM],
+        out_specs=VMEM,
+        compiler_params=room(8),
+        cost_estimate=cost(0, 2e6),
+    )(place, slices)
+    before = lax.all_to_all(prefix, "seq", 0, 0, tiled=True).reshape(HEADS, FROWS, 128)
     from_far = move(to_far, "q", 2)
     to_left, to_right = attend("attend_sides", 2, lists, (q_left, q_right), blocks)
     from_right = move(to_left, "q", -1)

time: 114 us -> 111 us (0.974)
  Pallas kernels: 50.8 us -> 52.5 us
  starting transfers between devices: 34.9 us -> 33.3 us
  waiting for transfers between devices: 23.3 us -> 21.9 us
    ppermute x9, starting transfers between devices: 14.7 us -> 10.4 us  [move(): return lax.ppermute(a, 'files', along(what, step))]
    ppermute x9, waiting for transfers between devices: 23.3 us -> 20.2 us  [move(): return lax.ppermute(a, 'files', along(what, step))]
    ppermute x2, waiting for transfers between devices: 0.01 us -> 1.73 us  [swap_cores(): lax.ppermute(a, 'files', [(i, i ^ 1) for i in range(SIDE * SIDE * CORES)])]
    all_to_all x1, starting transfers between devices: 6.36 us -> 8.07 us  [layers(): lax.all_to_all(prefix, 'seq', 0, 0, tiled=True).reshape(HEADS, FROWS, 128)]
    unnamed x10 -> x8, local copies, waits for them, and re-layouts: 2.6 us -> 1.57 us
  transfers between devices with their start and end apart: 13 -> 13, of which waited for: 4 -> 6; matrix products, arithmetic and copies ran while one was open for 0% -> 0% of each run, Pallas kernels for 41% -> 38%
where the time goes in v4:
time: 111 us
  Pallas kernels  52.5 us (47%)
  starting transfers between devices  33.3 us (30%)
  waiting for transfers between devices  21.9 us (20%)
  local copies, waits for them, and re-layouts  1.57 us (1%)
  between operations  1.42 us (1%)
    ppermute x9, waiting for transfers between devices, move(): return lax.ppermute(a, 'files', along(what, step))  20.2 us
    pallas_call x3, Pallas kernels, attend(): pl.pallas_call(functools.partial(attend_kernel, own, base, readers), out_...  16 us
    pallas_call x1, Pallas kernels, layers(): pl.pallas_call(local_kernel, name='local', grid=steps, out_shape=[hbm_sha...  11 us
    ppermute x9, starting transfers between devices, move(): return lax.ppermute(a, 'files', along(what, step))  10.4 us
    all_to_all x1, starting transfers between devices, layers(): lax.all_to_all(state.reshape(shards, HEADS * FROWS // shards, 128), 'seq'...  8.18 us
    all_to_all x1, starting transfers between devices, layers(): lax.all_to_all(prefix, 'seq', 0, 0, tiled=True).reshape(HEADS, FROWS, 128)  8.07 us
    pallas_call x1, Pallas kernels, layers(): pl.pallas_call(state_kernel, name='state', grid=steps, out_shape=hbm_shap...  6.99 us
    ppermute x2, starting transfers between devices, swap_cores(): lax.ppermute(a, 'files', [(i, i ^ 1) for i in range(SIDE * SIDE * CORES)])  6.65 us
  transfers between devices with their start and end apart: 13, of which 6 were waited for; matrix products, arithmetic and copies ran while one was open for 0% of the time, Pallas kernels for 38%

profile of v4, /device:TPU:1, one launch (start us, length us, event | category | flops | bytes accessed | tf_op | source)
XLA Modules:
  0.0 110.7 jit_solution(14088962163627644791)
XLA Ops:
  1.3 0.0 copy-start.2
  1.3 0.6 copy-done.2
  1.9 0.0 copy-start.3
  1.9 1.7 %pack.1 = bf16[784,640]{1,0:T(8,128)(2,1)S(1)} custom-call(s32[1]{0:T(128)} %bitcast.me_ref, s32[8]{0:T(128)S(1)} %bitcast.20, s32[1]{0:T(128)} %bitcast.18.count_ref, bf16[256,1280]{1,0:T(8,128)(2,1)} %bitcast.22, bf16[256,1280]{1,0:T(8,128)(2,1)} %bitcast.24, bf16[256,1280]{1,0:T(8,128)(2,1)} %bitcast.26), custom_call_target="tpu_custom_call" | custom-call | bytes 2000000 | tf_op jit(solution)/shard_map/pack/pallas_call | solution.py:492
  3.7 3.3 %collective-permute-start = (bf16[784,640]{1,0:T(8,128)(2,1)S(1)}, bf16[784,640]{1,0:T(8,128)(2,1)S(1)}, u32[]{:S(2)}, u32[]{:S(2)}) collective-permute-start(bf16[784,640]{1,0:T(8,128)(2,1)S(1)} %pack.1), channel_id=1, source_target_pairs={{0,1},{1,0},{2,3},{3,2},{4,5},{5,4},{6,7},{7,6},{8,9},{9,8},{10,11... | collective-permute-start | bytes 3010568 | tf_op jit(solution)/shard_map/ppermute | solution.py:55
  7.0 0.0 copy-done.3
  7.0 1.7 %own.1 = (bf16[2,2,256,640]{3,2,1,0:T(8,128)(2,1)S(1)}, bf16[2,272,640]{2,1,0:T(8,128)(2,1)S(1)}) custom-call(s32[1]{0:T(128)} %bitcast.me_ref, s32[8]{0:T(128)S(1)} %bitcast.21, s32[1]{0:T(128)} %bitcast.19.count_ref, bf16[256,1280]{1,0:T(8,128)(2,1)} %bitcast.23, bf16[256,1280]{1,0:T(8,128)(2,1)} %bitcast.25, bf16[256,1280]{1,0:T(8,128)(2,1)} %bitcast.27), custom_call_target="tpu_custom_call" | custom-call | bytes 2000000 | tf_op jit(solution)/shard_map/own/pallas_call | solution.py:504
  8.7 0.5 collective-permute-done.mate_ref
  9.2 0.4 merge.1
  9.6 1.1 collective-permute-start.4
  10.7 1.2 %collective-permute-start.1 = (bf16[2,272,640]{2,1,0:T(8,128)(2,1)S(1)}, bf16[2,272,640]{2,1,0:T(8,128)(2,1)}, u32[]{:S(2)}, u32[]{:S(2)}) collective-permute-start(bf16[2,272,640]{2,1,0:T(8,128)(2,1)S(1)} %get-tuple-element.24.refs_3_.refs_0_), channel_id=1, source_target_pairs={{0,2},{1,9},{2,4},{3,11},{4,6},{5,13},{6,0},{7,15},{8,10},{9,17},{... | collective-permute-start | bytes 2088968 | tf_op jit(solution)/shard_map/ppermute | solution.py:51
  11.9 7.0 %state.1 = bf16[20,160,128]{2,1,0:T(8,128)(2,1)} custom-call(bf16[320,256]{1,0:T(8,128)(2,1)} %bitcast.34, bf16[256,2560]{1,0:T(8,128)(2,1)} %bitcast.31, bf16[4,320,64]{2,1,0:T(8,128)(2,1)} %constant.13.clone.select_ref, f32[3,160,128]{2,1,0:T(8,128)} %constant.14.clone.vector_ref), custom_call_target="tpu_custom_call" | custom-call | flops 1000000000 | bytes 4000000 | tf_op jit(solution)/shard_map/state/pallas_call | solution.py:533
  18.9 8.2 %all-to-all-start = ((bf16[8,400,128]{2,1,0:T(8,128)(2,1)}), bf16[8,400,128]{2,1,0:T(8,128)(2,1)}, u32[]{:S(2)}, u32[]{:S(2)}) async-start(bf16[8,400,128]{2,1,0:T(8,128)(2,1)} %bitcast.29), calls=%async_computation | async-start | bytes 1638400 | tf_op jit(solution)/shard_map/all_to_all | solution.py:543
  27.1 0.0 collective-permute-start.6
  27.1 0.0 collective-permute-done.4.refs_2_.refs_3_
  27.1 2.7 %collective-permute-start.5 = (bf16[2,2,256,640]{3,2,1,0:T(8,128)(2,1)S(1)}, bf16[2,2,256,640]{3,2,1,0:T(8,128)(2,1)}, u32[]{:S(2)}, u32[]{:S(2)}) collective-permute-start(bf16[2,2,256,640]{3,2,1,0:T(8,128)(2,1)S(1)} %collective-permute-done.4.refs_2_.refs_3_), channel_id=1, source_target_pairs={{0,24},{1,7},{2,26},{3,1},{4,28},{5,3},{6,30},{7,5},{8,0},{9,15},{... | collective-permute-start | bytes 3932168 | tf_op jit(solution)/shard_map/ppermute | solution.py:51
  29.7 1.5 %collective-permute-start.3 = (bf16[2,272,640]{2,1,0:T(8,128)(2,1)S(1)}, bf16[2,272,640]{2,1,0:T(8,128)(2,1)}, u32[]{:S(2)}, u32[]{:S(2)}) collective-permute-start(bf16[2,272,640]{2,1,0:T(8,128)(2,1)S(1)} %get-tuple-element.24.refs_3_.refs_0_), channel_id=1, source_target_pairs={{0,6},{1,25},{2,0},{3,27},{4,2},{5,29},{6,4},{7,31},{8,14},{9,1},{... | collective-permute-start | bytes 2088968 | tf_op jit(solution)/shard_map/ppermute | solution.py:51
  31.2 0.0 collective-permute-done.1.refs_1_.refs_0_
  31.2 0.0 collective-permute-start.2
  31.2 11.0 %local.1 = (bf16[256,2560]{1,0:T(8,128)(2,1)}, f32[256,128]{1,0:T(8,128)}, bf16[20,160,256]{2,1,0:T(8,128)(2,1)}) custom-call(bf16[320,256]{1,0:T(8,128)(2,1)} %bitcast.33, bf16[320,256]{1,0:T(8,128)(2,1)} %bitcast.35, bf16[256,2560]{1,0:T(8,128)(2,1)} %bitcast.32, bf16[4,320,64]{2,1,0:T(8,128)(2,1)} %constant.13.clone.select_ref, ...), custom_call_target="tpu_custom_call" | custom-call | flops 4000000000 | bytes 8000000 | tf_op jit(solution)/shard_map/local/pallas_call | solution.py:545
  42.2 5.3 %collective-permute-done.3.refs_2_.refs_1_ = bf16[2,272,640]{2,1,0:T(8,128)(2,1)} collective-permute-done((bf16[2,272,640]{2,1,0:T(8,128)(2,1)S(1)}, bf16[2,272,640]{2,1,0:T(8,128)(2,1)}, u32[]{:S(2)}, u32[]{:S(2)}) %collective-permute-start.3) | collective-permute-done | bytes 696352 | tf_op jit(solution)/shard_map/ppermute | solution.py:51
  47.5 2.9 %collective-permute-done.2.refs_0_ = bf16[2,272,640]{2,1,0:T(8,128)(2,1)} collective-permute-done((bf16[2,272,640]{2,1,0:T(8,128)(2,1)}, bf16[2,272,640]{2,1,0:T(8,128)(2,1)}, u32[]{:S(2)}, u32[]{:S(2)}) %collective-permute-start.2) | collective-permute-done | bytes 696352 | tf_op jit(solution)/shard_map/ppermute | solution.py:51
  50.4 2.8 %search.1 = (s32[8,128]{1,0:T(8,128)S(1)}, s32[8]{0:T(128)S(1)}) custom-call(s32[1]{0:T(128)} %bitcast.me_ref, bf16[2,272,640]{2,1,0:T(8,128)(2,1)} %collective-permute-done.2.refs_0_, bf16[2,272,640]{2,1,0:T(8,128)(2,1)} %collective-permute-done.1.refs_1_.refs_0_, bf16[2,272,640]{2,1,0:T(8,128)(2,1)} %collective-permute-done.3.refs_2_.refs_1_, ...), custom_call_target="tpu_custom_call" | custom-call | bytes 100000 | tf_op jit(solution)/shard_map/search/pallas_call | solution.py:557
  53.1 0.0 collective-permute-done.6.refs_4_.refs_5_
  53.2 0.0 collective-permute-done.5.refs_3_.refs_4_
  53.2 4.1 %shard_map.113 = bf16[2,272,640]{2,1,0:T(8,128)(2,1)S(1)} custom-call(s32[8,128]{1,0:T(8,128)S(1)} %get-tuple-element.25.found, s32[8]{0:T(128)S(1)} %get-tuple-element.26.counts, bf16[2,272,640]{2,1,0:T(8,128)(2,1)} %collective-permute-done.2.refs_0_, bf16[2,2,256,640]{3,2,1,0:T(8,128)(2,1)S(1)} %get-tuple-element.27.refs_1_.refs_2_, ...), custom_call_target="tpu_custom_call" | custom-call | flops 800000000 | bytes 8000000 | tf_op jit(solution)/shard_map/pallas_call | solution.py:463
  57.3 0.0 copy-start
  57.3 0.9 copy-done
  58.2 0.0 all-to-all-done.in_ref
  58.2 2.8 %prefix.1 = bf16[8,400,128]{2,1,0:T(8,128)(2,1)} custom-call(s32[1]{0:T(128)} %bitcast.13.place_ref, bf16[8,400,128]{2,1,0:T(8,128)(2,1)} %all-to-all-done.in_ref), custom_call_target="tpu_custom_call" | custom-call | bytes 2000000 | tf_op jit(solution)/shard_map/prefix/pallas_call | solution.py:574
  61.0 8.1 %all-to-all-start.1 = ((bf16[8,400,128]{2,1,0:T(8,128)(2,1)}), bf16[8,400,128]{2,1,0:T(8,128)(2,1)}, u32[]{:S(2)}, u32[]{:S(2)}) async-start(bf16[8,400,128]{2,1,0:T(8,128)(2,1)} %prefix.1), calls=%async_computation.1 | async-start | bytes 1638400 | tf_op jit(solution)/shard_map/all_to_all | solution.py:583
  69.1 0.0 copy-start.1
  69.1 6.5 %shard_map.115 = (bf16[2,272,640]{2,1,0:T(8,128)(2,1)S(1)}, bf16[2,272,640]{2,1,0:T(8,128)(2,1)S(1)}) custom-call(s32[8,128]{1,0:T(8,128)S(1)} %get-tuple-element.25.found, s32[8]{0:T(128)S(1)} %get-tuple-element.26.counts, bf16[2,272,640]{2,1,0:T(8,128)(2,1)} %collective-permute-done.1.refs_1_.refs_0_, ...), custom_call_target="tpu_custom_call" | custom-call | flops 1600000000 | bytes 8000000 | tf_op jit(solution)/shard_map/pallas_call | solution.py:463
  75.6 2.6 %collective-permute-start.7 = (bf16[2,272,640]{2,1,0:T(8,128)(2,1)S(1)}, bf16[2,272,640]{2,1,0:T(8,128)(2,1)S(1)}, u32[]{:S(2)}, u32[]{:S(2)}) collective-permute-start(bf16[2,272,640]{2,1,0:T(8,128)(2,1)S(1)} %get-tuple-element.38), channel_id=1, source_target_pairs={{0,6},{1,25},{2,0},{3,27},{4,2},{5,29},{6,4},{7,31},{8,14},{9,1},{... | collective-permute-start | bytes 2088968 | tf_op jit(solution)/shard_map/ppermute | solution.py:51
  78.1 0.0 collective-permute-start.8
  78.1 0.0 copy-done.1
  78.1 1.4 %collective-permute-start.9 = (bf16[2,272,640]{2,1,0:T(8,128)(2,1)S(1)}, bf16[2,272,640]{2,1,0:T(8,128)(2,1)S(1)}, u32[]{:S(2)}, u32[]{:S(2)}) collective-permute-start(bf16[2,272,640]{2,1,0:T(8,128)(2,1)S(1)} %copy-done.1), channel_id=1, source_target_pairs={{0,4},{1,17},{2,6},{3,19},{4,0},{5,21},{6,2},{7,23},{8,12},{9,25},... | collective-permute-start | bytes 2088968 | tf_op jit(solution)/shard_map/ppermute | solution.py:51
  79.5 5.5 %shard_map.114.refs_0_ = bf16[2,272,640]{2,1,0:T(8,128)(2,1)S(1)} custom-call(s32[8,128]{1,0:T(8,128)S(1)} %get-tuple-element.25.found, s32[8]{0:T(128)S(1)} %get-tuple-element.26.counts, bf16[2,272,640]{2,1,0:T(8,128)(2,1)S(1)} %get-tuple-element.24.refs_3_.refs_0_, bf16[2,2,256,640]{3,2,1,0:T(8,128)(2,1)S(1)} %get-tuple-element.27.refs_1_.refs_2_, ...), custom_call_target="tpu_custom_call" | custom-call | flops 800000000 | bytes 8000000 | tf_op jit(solution)/shard_map/pallas_call | solution.py:463
  85.0 8.6 %collective-permute-done.7.refs_1_ = bf16[2,272,640]{2,1,0:T(8,128)(2,1)S(1)} collective-permute-done((bf16[2,272,640]{2,1,0:T(8,128)(2,1)S(1)}, bf16[2,272,640]{2,1,0:T(8,128)(2,1)S(1)}, u32[]{:S(2)}, u32[]{:S(2)}) %collective-permute-start.7) | collective-permute-done | bytes 696352 | tf_op jit(solution)/shard_map/ppermute | solution.py:51
  93.6 3.4 %collective-permute-done.8.refs_2_ = bf16[2,272,640]{2,1,0:T(8,128)(2,1)S(1)} collective-permute-done((bf16[2,272,640]{2,1,0:T(8,128)(2,1)S(1)}, bf16[2,272,640]{2,1,0:T(8,128)(2,1)S(1)}, u32[]{:S(2)}, u32[]{:S(2)}) %collective-permute-start.8) | collective-permute-done | bytes 696352 | tf_op jit(solution)/shard_map/ppermute | solution.py:51
  97.0 0.0 collective-permute-done.9.refs_3_
  97.0 2.7 %join.1 = (bf16[256,640]{1,0:T(8,128)(2,1)S(1)}, bf16[256,640]{1,0:T(8,128)(2,1)S(1)}) custom-call(bf16[2,272,640]{2,1,0:T(8,128)(2,1)S(1)} %shard_map.114.refs_0_, bf16[2,272,640]{2,1,0:T(8,128)(2,1)S(1)} %collective-permute-done.7.refs_1_, bf16[2,272,640]{2,1,0:T(8,128)(2,1)S(1)} %collective-permute-done.8.refs_2_, ...), custom_call_target="tpu_custom_call" | custom-call | bytes 4000000 | tf_op jit(solution)/shard_map/join/pallas_call | solution.py:589
  99.7 3.4 %collective-permute-start.10 = (bf16[256,640]{1,0:T(8,128)(2,1)S(1)}, bf16[256,640]{1,0:T(8,128)(2,1)S(1)}, u32[]{:S(2)}, u32[]{:S(2)}) collective-permute-start(bf16[256,640]{1,0:T(8,128)(2,1)S(1)} %get-tuple-element.41), channel_id=1, source_target_pairs={{0,1},{1,0},{2,3},{3,2},{4,5},{5,4},{6,7},{7,6},{8,9},{9,8},{10,11... | collective-permute-start | bytes 983048 | tf_op jit(solution)/shard_map/ppermute | solution.py:55
  103.0 1.3 %collective-permute-done.10.other_ref = bf16[256,640]{1,0:T(8,128)(2,1)S(1)} collective-permute-done((bf16[256,640]{1,0:T(8,128)(2,1)S(1)}, bf16[256,640]{1,0:T(8,128)(2,1)S(1)}, u32[]{:S(2)}, u32[]{:S(2)}) %collective-permute-start.10) | collective-permute-done | bytes 327712 | tf_op jit(solution)/shard_map/ppermute | solution.py:55
  104.3 0.8 place.1
  105.1 0.0 all-to-all-done.1
  105.2 5.5 %finish.1 = bf16[256,2560]{1,0:T(8,128)(2,1)} custom-call(bf16[256,2560]{1,0:T(8,128)(2,1)} %get-tuple-element.32.num_ref, f32[256,128]{1,0:T(8,128)} %get-tuple-element.33.den_ref, bf16[20,160,256]{2,1,0:T(8,128)(2,1)} %get-tuple-element.34.phi_ref, bf16[20,160,128]{2,1,0:T(8,128)(2,1)} %bitcast.14.state_ref), custom_call_target="tpu_custom_call" | custom-call | flops 400000000 | bytes 8000000 | tf_op jit(solution)/shard_map/finish/pallas_call | solution.py:610
Async XLA Ops:
  1.3 0.7 copy-start.2
  1.9 5.0 %copy-start.3 = (s32[1,1,8]{2,1,0:T(1,128)S(1)}, s32[1,1,8]{2,1,0:T(1,128)}, u32[]{:S(2)}) copy-start(s32[1,1,8]{2,1,0:T(1,128)} %param.16) | copy-start | bytes 100
  3.7 5.5 %collective-permute-start = (bf16[784,640]{1,0:T(8,128)(2,1)S(1)}, bf16[784,640]{1,0:T(8,128)(2,1)S(1)}, u32[]{:S(2)}, u32[]{:S(2)}) collective-permute-start(bf16[784,640]{1,0:T(8,128)(2,1)S(1)} %pack.1), channel_id=1, source_target_pairs={{0,1},{1,0},{2,3},{3,2},{4,5},{5,4},{6,7},{7,6},{8,9},{9,8},{10,11... | collective-permute-start | bytes 3010568 | tf_op jit(solution)/shard_map/ppermute | solution.py:55
  9.6 17.5 %collective-permute-start.4 = (bf16[2,2,256,640]{3,2,1,0:T(8,128)(2,1)S(1)}, bf16[2,2,256,640]{3,2,1,0:T(8,128)(2,1)S(1)}, u32[]{:S(2)}, u32[]{:S(2)}) collective-permute-start(bf16[2,2,256,640]{3,2,1,0:T(8,128)(2,1)S(1)} %get-tuple-element.27.refs_1_.refs_2_), channel_id=1, source_target_pairs={{0,24},{1,7},{2,26},{3,1},{4,28},{5,3},{6,30},{7,5},{8,0},{9,15},{... | collective-permute-start | bytes 3932168 | tf_op jit(solution)/shard_map/ppermute | solution.py:51
  10.7 20.5 %collective-permute-start.1 = (bf16[2,272,640]{2,1,0:T(8,128)(2,1)S(1)}, bf16[2,272,640]{2,1,0:T(8,128)(2,1)}, u32[]{:S(2)}, u32[]{:S(2)}) collective-permute-start(bf16[2,272,640]{2,1,0:T(8,128)(2,1)S(1)} %get-tuple-element.24.refs_3_.refs_0_), channel_id=1, source_target_pairs={{0,2},{1,9},{2,4},{3,11},{4,6},{5,13},{6,0},{7,15},{8,10},{9,17},{... | collective-permute-start | bytes 2088968 | tf_op jit(solution)/shard_map/ppermute | solution.py:51
  18.9 39.3 %all-to-all-start = ((bf16[8,400,128]{2,1,0:T(8,128)(2,1)}), bf16[8,400,128]{2,1,0:T(8,128)(2,1)}, u32[]{:S(2)}, u32[]{:S(2)}) async-start(bf16[8,400,128]{2,1,0:T(8,128)(2,1)} %bitcast.29), calls=%async_computation | async-start | bytes 1638400 | tf_op jit(solution)/shard_map/all_to_all | solution.py:543
  27.1 26.1 %collective-permute-start.6 = (bf16[2,2,256,640]{3,2,1,0:T(8,128)(2,1)S(1)}, bf16[2,2,256,640]{3,2,1,0:T(8,128)(2,1)}, u32[]{:S(2)}, u32[]{:S(2)}) collective-permute-start(bf16[2,2,256,640]{3,2,1,0:T(8,128)(2,1)S(1)} %get-tuple-element.27.refs_1_.refs_2_), channel_id=1, source_target_pairs={{0,8},{1,3},{2,10},{3,5},{4,12},{5,7},{6,14},{7,1},{8,16},{9,11},{... | collective-permute-start | bytes 3932168 | tf_op jit(solution)/shard_map/ppermute | solution.py:51
  27.1 26.1 %collective-permute-start.5 = (bf16[2,2,256,640]{3,2,1,0:T(8,128)(2,1)S(1)}, bf16[2,2,256,640]{3,2,1,0:T(8,128)(2,1)}, u32[]{:S(2)}, u32[]{:S(2)}) collective-permute-start(bf16[2,2,256,640]{3,2,1,0:T(8,128)(2,1)S(1)} %collective-permute-done.4.refs_2_.refs_3_), channel_id=1, source_target_pairs={{0,24},{1,7},{2,26},{3,1},{4,28},{5,3},{6,30},{7,5},{8,0},{9,15},{... | collective-permute-start | bytes 3932168 | tf_op jit(solution)/shard_map/ppermute | solution.py:51
  29.7 17.7 %collective-permute-start.3 = (bf16[2,272,640]{2,1,0:T(8,128)(2,1)S(1)}, bf16[2,272,640]{2,1,0:T(8,128)(2,1)}, u32[]{:S(2)}, u32[]{:S(2)}) collective-permute-start(bf16[2,272,640]{2,1,0:T(8,128)(2,1)S(1)} %get-tuple-element.24.refs_3_.refs_0_), channel_id=1, source_target_pairs={{0,6},{1,25},{2,0},{3,27},{4,2},{5,29},{6,4},{7,31},{8,14},{9,1},{... | collective-permute-start | bytes 2088968 | tf_op jit(solution)/shard_map/ppermute | solution.py:51
  31.2 19.2 %collective-permute-start.2 = (bf16[2,272,640]{2,1,0:T(8,128)(2,1)}, bf16[2,272,640]{2,1,0:T(8,128)(2,1)}, u32[]{:S(2)}, u32[]{:S(2)}) collective-permute-start(bf16[2,272,640]{2,1,0:T(8,128)(2,1)} %collective-permute-done.1.refs_1_.refs_0_), channel_id=1, source_target_pairs={{0,2},{1,9},{2,4},{3,11},{4,6},{5,13},{6,0},{7,15},{8,10},{9,17},{... | collective-permute-start | bytes 2088968 | tf_op jit(solution)/shard_map/ppermute | solution.py:51
  57.3 0.9 copy-start
  61.0 44.1 %all-to-all-start.1 = ((bf16[8,400,128]{2,1,0:T(8,128)(2,1)}), bf16[8,400,128]{2,1,0:T(8,128)(2,1)}, u32[]{:S(2)}, u32[]{:S(2)}) async-start(bf16[8,400,128]{2,1,0:T(8,128)(2,1)} %prefix.1), calls=%async_computation.1 | async-start | bytes 1638400 | tf_op jit(solution)/shard_map/all_to_all | solution.py:583
  69.1 9.0 %copy-start.1 = (bf16[2,272,640]{2,1,0:T(8,128)(2,1)S(1)}, bf16[2,272,640]{2,1,0:T(8,128)(2,1)}, u32[]{:S(2)}) copy-start(bf16[2,272,640]{2,1,0:T(8,128)(2,1)} %copy-done) | copy-start | bytes 2088964
  75.6 18.0 %collective-permute-start.7 = (bf16[2,272,640]{2,1,0:T(8,128)(2,1)S(1)}, bf16[2,272,640]{2,1,0:T(8,128)(2,1)S(1)}, u32[]{:S(2)}, u32[]{:S(2)}) collective-permute-start(bf16[2,272,640]{2,1,0:T(8,128)(2,1)S(1)} %get-tuple-element.38), channel_id=1, source_target_pairs={{0,6},{1,25},{2,0},{3,27},{4,2},{5,29},{6,4},{7,31},{8,14},{9,1},{... | collective-permute-start | bytes 2088968 | tf_op jit(solution)/shard_map/ppermute | solution.py:51
  78.1 18.8 %collective-permute-start.8 = (bf16[2,272,640]{2,1,0:T(8,128)(2,1)S(1)}, bf16[2,272,640]{2,1,0:T(8,128)(2,1)S(1)}, u32[]{:S(2)}, u32[]{:S(2)}) collective-permute-start(bf16[2,272,640]{2,1,0:T(8,128)(2,1)S(1)} %get-tuple-element.39), channel_id=1, source_target_pairs={{0,2},{1,9},{2,4},{3,11},{4,6},{5,13},{6,0},{7,15},{8,10},{9,17},{... | collective-permute-start | bytes 2088968 | tf_op jit(solution)/shard_map/ppermute | solution.py:51
  78.1 18.8 %collective-permute-start.9 = (bf16[2,272,640]{2,1,0:T(8,128)(2,1)S(1)}, bf16[2,272,640]{2,1,0:T(8,128)(2,1)S(1)}, u32[]{:S(2)}, u32[]{:S(2)}) collective-permute-start(bf16[2,272,640]{2,1,0:T(8,128)(2,1)S(1)} %copy-done.1), channel_id=1, source_target_pairs={{0,4},{1,17},{2,6},{3,19},{4,0},{5,21},{6,2},{7,23},{8,12},{9,25},... | collective-permute-start | bytes 2088968 | tf_op jit(solution)/shard_map/ppermute | solution.py:51
  99.7 4.6 %collective-permute-start.10 = (bf16[256,640]{1,0:T(8,128)(2,1)S(1)}, bf16[256,640]{1,0:T(8,128)(2,1)S(1)}, u32[]{:S(2)}, u32[]{:S(2)}) collective-permute-start(bf16[256,640]{1,0:T(8,128)(2,1)S(1)} %get-tuple-element.41), channel_id=1, source_target_pairs={{0,1},{1,0},{2,3},{3,2},{4,5},{5,4},{6,7},{7,6},{8,9},{9,8},{10,11... | collective-permute-start | bytes 983048 | tf_op jit(solution)/shard_map/ppermute | solution.py:55

commit v5 on v4

--- a/solution.py
+++ b/solution.py
@@ -95,11 +95,11 @@
     row = lax.broadcasted_iota(jnp.int32, (16, 128), 0)
     lane = lax.broadcasted_iota(jnp.int32, (FROWS, 128), 1)
     norms = jnp.zeros((FROWS, 128), F32)
+    phis = [features(select_ref[j], k_ref[...], vector_ref) for j in range(GROUP)]
+    boths = [jnp.dot(phis[j], with_ones(v_ref[:, column(j)]), preferred_element_type=F32) for j in range(GROUP)]
     for j in range(GROUP):
-        phi = features(select_ref[j], k_ref[...], vector_ref)
-        both = jnp.dot(phi, with_ones(v_ref[:, column(j)]), preferred_element_type=F32)
-        norms = jnp.where(lane == j, both[:, 128:], norms)
-        out_ref[j] = both[:, :128].astype(BF)
+        norms = jnp.where(lane == j, boths[j][:, 128:], norms)
+        out_ref[j] = boths[j][:, :128].astype(BF)
     flat = jnp.concatenate([norms, jnp.zeros((FPAD - FROWS, 128), F32)], axis=0).T
     high = flat.astype(BF).astype(F32)
     low = flat - high
@@ -138,15 +138,17 @@
         den_ref[...] = jnp.zeros((TOK, 128), F32)
 
     den = den_ref[...]
+    phis_q = [features(select_ref[j], q_ref[...], vector_ref) for j in range(GROUP)]
+    phis_k = [features(select_ref[j], k_ref[...], vector_ref) for j in range(GROUP)]
     for j in range(GROUP):
-        phi_q = features(select_ref[j], q_ref[...], vector_ref)
-        phi_ref[j] = phi_q
-        phi_k = features(select_ref[j], k_ref[...], vector_ref)
-        weight = jnp.dot(taller(phi_q).T, taller(phi_k), preferred_element_type=F32)
-        weight = jnp.where(causal, weight, 0.0).astype(BF)
-        both = jnp.dot(weight, with_ones(v_ref[:, column(j)]), preferred_element_type=F32)
-        num_ref[:, column(j)] = both[:, :128].astype(BF)
-        den = jnp.where(lane == group * GROUP + j, both[:, 128:], den)
+        phi_ref[j] = phis_q[j]
+    turned = [taller(p).T for p in phis_q]
+    weights = [jnp.dot(turned[j], taller(phis_k[j]), preferred_element_type=F32) for j in range(GROUP)]
+    weights = [jnp.where(causal, w, 0.0).astype(BF) for w in weights]
+    boths = [jnp.dot(weights[j], with_ones(v_ref[:, column(j)]), preferred_element_type=F32) for j in range(GROUP)]
+    for j in range(GROUP):
+        num_ref[:, column(j)] = boths[j][:, :128].astype(BF)
+        den = jnp.where(lane == group * GROUP + j, boths[j][:, 128:], den)
     den_ref[...] = den
 
 
@@ -154,17 +156,18 @@
     lane = lax.broadcasted_iota(jnp.int32, (TOK, 128), 1)
     group = pl.program_id(0)
     at = FEATS - (FROWS - 16)
+    phis = [taller(phi_ref[j]).T for j in range(GROUP)]
+    carried = [jnp.dot(phis[j], taller(state_ref[j]), preferred_element_type=F32) for j in range(GROUP)]
+    dens = []
     for j in range(GROUP):
-        phi = taller(phi_ref[j]).T
-        state = state_ref[j]
-        carried = jnp.dot(phi, taller(state), preferred_element_type=F32)
-        tail = state[FROWS - 16 : FROWS].astype(F32)
+        tail = state_ref[j, FROWS - 16 :].astype(F32)
         n0 = tail[at : at + 1] + tail[at + 2 : at + 3]
         n1 = tail[at + 1 : at + 2] + tail[at + 3 : at + 4]
-        phi32 = phi.astype(F32)
+        phi32 = phis[j].astype(F32)
         den = jnp.where(lane == group * GROUP + j, den_ref[...], 0.0) + phi32[:, :128] * n0 + phi32[:, 128:] * n1
-        den = jnp.sum(den, axis=1, keepdims=True)
-        out_ref[:, column(j)] = ((num_ref[:, column(j)].astype(F32) + carried) / den).astype(BF)
+        dens.append(jnp.sum(den, axis=1, keepdims=True))
+    for j in range(GROUP):
+        out_ref[:, column(j)] = ((num_ref[:, column(j)].astype(F32) + carried[j]) / dens[j]).astype(BF)
 
 
 def halves(core, refs):
@@ -474,7 +477,7 @@
             pltpu.SemaphoreType.DMA((groups,)),
             pltpu.SemaphoreType.DMA((2, LISTED)),
         ],
-        compiler_params=room(20),
+        compiler_params=room(18),
         cost_estimate=cost(readers * 4e8, 8e6),
     )(*lists, *queries, *blocks)
 
@@ -537,7 +540,7 @@
         out_shape=hbm_shape(HEADS, FROWS, 128),
         in_specs=[heads16, heads128, whole(*select.shape), whole(*vectors.shape)],
         out_specs=pl.BlockSpec((GROUP, FROWS, 128), lambda g: (g, 0, 0)),
-        compiler_params=room(12),
+        compiler_params=room(8),
         cost_estimate=cost(1e9, 4e6),
     )(*in_hbm(k_lin[0].T, v_lin[0], select, vectors))
     slices = lax.all_to_all(state.reshape(shards, HEADS * FROWS // shards, 128), "seq", 0, 0, tiled=True)
@@ -549,7 +552,7 @@
         out_shape=[hbm_shape(TOK, D), hbm_shape(TOK, 128, dtype=F32), hbm_shape(HEADS, FROWS, TOK)],
         in_specs=[heads16, heads16, heads128, whole(*select.shape), whole(*vectors.shape)],
         out_specs=[heads128, whole(TOK, 128), pl.BlockSpec((GROUP, FROWS, TOK), lambda g: (g, 0, 0))],
-        compiler_params=room(16),
+        compiler_params=room(10),
         cost_estimate=cost(4e9, 8e6),
     )(*in_hbm(q_lin[0].T, k_lin[0].T, v_lin[0], select, vectors))
 
@@ -568,19 +571,19 @@
         compiler_params=room(2),
         cost_estimate=cost(0, 1e5),
     )(me, q_far, q_left, q_right, q)
-    (to_far,) = attend("attend_far", 0, lists, (q_far,), blocks)
-    to_far, q_left, q_right = lax.optimization_barrier((to_far, q_left, q_right))
-    _, slices, num, den, phi = lax.optimization_barrier((to_far, slices, num, den, phi))
+    slices, num, den, phi, *lists = lax.optimization_barrier((slices, num, den, phi, *lists))
     prefix = pl.pallas_call(
         prefix_kernel,
         name="prefix",
         out_shape=hbm_shape(*slices.shape),
         in_specs=[SMEM, VMEM],
         out_specs=VMEM,
-        compiler_params=room(8),
+        compiler_params=room(6),
         cost_estimate=cost(0, 2e6),
     )(place, slices)
     before = lax.all_to_all(prefix, "seq", 0, 0, tiled=True).reshape(HEADS, FROWS, 128)
+    (to_far,) = attend("attend_far", 0, lists, (q_far,), blocks)
+    to_far, q_left, q_right = lax.optimization_barrier((to_far, q_left, q_right))
     from_far = move(to_far, "q", 2)
     to_left, to_right = attend("attend_sides", 2, lists, (q_left, q_right), blocks)
     from_right = move(to_left, "q", -1)
@@ -619,7 +622,7 @@
             pl.BlockSpec((GROUP, FROWS, 128), lambda g: (g, 0, 0)),
         ],
         out_specs=heads128,
-        compiler_params=room(16),
+        compiler_params=room(8),
         cost_estimate=cost(4e8, 8e6),
     )(*in_hbm(num, den, phi), before)
     return lin_out[None], soft_out[None]

time: 111 us -> 115 us (1.036)
  waiting for transfers between devices: 21.9 us -> 31.3 us
  Pallas kernels: 52.5 us -> 46.9 us
    ppermute x9, waiting for transfers between devices: 20.2 us -> 30.9 us  [move(): return lax.ppermute(a, 'files', along(what, step))]
    pallas_call x1, Pallas kernels: 11 us -> 6.81 us  [layers(): pl.pallas_call(local_kernel, name='local', grid=steps, out_shape=[hbm_sha...]
    ppermute x9, starting transfers between devices: 10.4 us -> 14.4 us  [move(): return lax.ppermute(a, 'files', along(what, step))]
    ppermute x2, starting transfers between devices: 6.65 us -> 4.95 us  [swap_cores(): lax.ppermute(a, 'files', [(i, i ^ 1) for i in range(SIDE * SIDE * CORES)])]
    pallas_call x1, Pallas kernels: 6.99 us -> 5.45 us  [layers(): pl.pallas_call(state_kernel, name='state', grid=steps, out_shape=hbm_shap...]
    all_to_all x1, starting transfers between devices: 8.07 us -> 6.65 us  [layers(): lax.all_to_all(prefix, 'seq', 0, 0, tiled=True).reshape(HEADS, FROWS, 128)]
    ppermute x2, waiting for transfers between devices: 1.73 us -> 0.48 us  [swap_cores(): lax.ppermute(a, 'files', [(i, i ^ 1) for i in range(SIDE * SIDE * CORES)])]
where the time goes in v5:
time: 115 us
  Pallas kernels  46.9 us (41%)
  starting transfers between devices  34.2 us (30%)
  waiting for transfers between devices  31.3 us (27%)
  between operations  1.55 us (1%)
    ppermute x9, waiting for transfers between devices, move(): return lax.ppermute(a, 'files', along(what, step))  30.9 us
    pallas_call x3, Pallas kernels, attend(): pl.pallas_call(functools.partial(attend_kernel, own, base, readers), out_...  16 us
    ppermute x9, starting transfers between devices, move(): return lax.ppermute(a, 'files', along(what, step))  14.4 us
    all_to_all x1, starting transfers between devices, layers(): lax.all_to_all(state.reshape(shards, HEADS * FROWS // shards, 128), 'seq'...  8.17 us
    pallas_call x1, Pallas kernels, layers(): pl.pallas_call(local_kernel, name='local', grid=steps, out_shape=[hbm_sha...  6.81 us
    all_to_all x1, starting transfers between devices, layers(): lax.all_to_all(prefix, 'seq', 0, 0, tiled=True).reshape(HEADS, FROWS, 128)  6.65 us
    pallas_call x1, Pallas kernels, layers(): pl.pallas_call(finish_kernel, name='finish', grid=steps, out_shape=shape(...  5.62 us
    pallas_call x1, Pallas kernels, layers(): pl.pallas_call(state_kernel, name='state', grid=steps, out_shape=hbm_shap...  5.45 us
  transfers between devices with their start and end apart: 13, of which 6 were waited for; matrix products, arithmetic and copies ran while one was open for 0% of the time, Pallas kernels for 38%

profile of v5, /device:TPU:1, one launch (start us, length us, event | category | flops | bytes accessed | tf_op | source)
XLA Modules:
  0.0 114.6 jit_solution(10851696122789466130)
XLA Ops:
  1.3 0.0 copy-start
  1.3 0.6 copy-done
  1.9 0.0 copy-start.1
  1.9 1.7 %pack.1 = bf16[784,640]{1,0:T(8,128)(2,1)S(1)} custom-call(s32[1]{0:T(128)} %bitcast.7.me_ref, s32[8]{0:T(128)S(1)} %bitcast.20, s32[1]{0:T(128)} %bitcast.18.count_ref, bf16[256,1280]{1,0:T(8,128)(2,1)} %bitcast.22, bf16[256,1280]{1,0:T(8,128)(2,1)} %bitcast.24, bf16[256,1280]{1,0:T(8,128)(2,1)} %bitcast.26), custom_call_target="tpu_custom_call" | custom-call | bytes 2000000 | tf_op jit(solution)/shard_map/pack/pallas_call | solution.py:495
  3.7 3.3 %collective-permute-start = (bf16[784,640]{1,0:T(8,128)(2,1)S(1)}, bf16[784,640]{1,0:T(8,128)(2,1)S(1)}, u32[]{:S(2)}, u32[]{:S(2)}) collective-permute-start(bf16[784,640]{1,0:T(8,128)(2,1)S(1)} %pack.1), channel_id=1, source_target_pairs={{0,1},{1,0},{2,3},{3,2},{4,5},{5,4},{6,7},{7,6},{8,9},{9,8},{10,11... | collective-permute-start | bytes 3010568 | tf_op jit(solution)/shard_map/ppermute | solution.py:55
  7.0 0.0 copy-done.1
  7.0 1.7 %own.1 = (bf16[2,2,256,640]{3,2,1,0:T(8,128)(2,1)S(1)}, bf16[2,272,640]{2,1,0:T(8,128)(2,1)S(1)}) custom-call(s32[1]{0:T(128)} %bitcast.7.me_ref, s32[8]{0:T(128)S(1)} %bitcast.21, s32[1]{0:T(128)} %bitcast.19.count_ref, bf16[256,1280]{1,0:T(8,128)(2,1)} %bitcast.23, bf16[256,1280]{1,0:T(8,128)(2,1)} %bitcast.25, bf16[256,1280]{1,0:T(8,128)(2,1)} %bitcast.27), custom_call_target="tpu_custom_call" | custom-call | bytes 2000000 | tf_op jit(solution)/shard_map/own/pallas_call | solution.py:507
  8.7 0.5 collective-permute-done.mate_ref
  9.2 0.4 merge.1
  9.6 1.1 collective-permute-start.4
  10.7 5.5 %state.1 = bf16[20,160,128]{2,1,0:T(8,128)(2,1)} custom-call(bf16[320,256]{1,0:T(8,128)(2,1)} %bitcast.34, bf16[256,2560]{1,0:T(8,128)(2,1)} %bitcast.31, bf16[4,320,64]{2,1,0:T(8,128)(2,1)} %constant.13.clone.select_ref, f32[3,160,128]{2,1,0:T(8,128)} %constant.14.clone.vector_ref), custom_call_target="tpu_custom_call" | custom-call | flops 1000000000 | bytes 4000000 | tf_op jit(solution)/shard_map/state/pallas_call | solution.py:536
  16.1 8.2 %all-to-all-start = ((bf16[8,400,128]{2,1,0:T(8,128)(2,1)}), bf16[8,400,128]{2,1,0:T(8,128)(2,1)}, u32[]{:S(2)}, u32[]{:S(2)}) async-start(bf16[8,400,128]{2,1,0:T(8,128)(2,1)} %bitcast.29), calls=%async_computation | async-start | bytes 1638400 | tf_op jit(solution)/shard_map/all_to_all | solution.py:546
  24.3 1.2 %collective-permute-start.1 = (bf16[2,272,640]{2,1,0:T(8,128)(2,1)S(1)}, bf16[2,272,640]{2,1,0:T(8,128)(2,1)}, u32[]{:S(2)}, u32[]{:S(2)}) collective-permute-start(bf16[2,272,640]{2,1,0:T(8,128)(2,1)S(1)} %get-tuple-element.29.refs_3_.refs_0_), channel_id=1, source_target_pairs={{0,2},{1,9},{2,4},{3,11},{4,6},{5,13},{6,0},{7,15},{8,10},{9,17},{... | collective-permute-start | bytes 2088968 | tf_op jit(solution)/shard_map/ppermute | solution.py:51
  25.5 0.0 collective-permute-start.6
  25.5 0.9 collective-permute-done.4.refs_2_.refs_3_
  26.4 1.9 %collective-permute-start.5 = (bf16[2,2,256,640]{3,2,1,0:T(8,128)(2,1)S(1)}, bf16[2,2,256,640]{3,2,1,0:T(8,128)(2,1)}, u32[]{:S(2)}, u32[]{:S(2)}) collective-permute-start(bf16[2,2,256,640]{3,2,1,0:T(8,128)(2,1)S(1)} %collective-permute-done.4.refs_2_.refs_3_), channel_id=1, source_target_pairs={{0,24},{1,7},{2,26},{3,1},{4,28},{5,3},{6,30},{7,5},{8,0},{9,15},{... | collective-permute-start | bytes 3932168 | tf_op jit(solution)/shard_map/ppermute | solution.py:51
  28.3 2.8 %collective-permute-start.3 = (bf16[2,272,640]{2,1,0:T(8,128)(2,1)S(1)}, bf16[2,272,640]{2,1,0:T(8,128)(2,1)}, u32[]{:S(2)}, u32[]{:S(2)}) collective-permute-start(bf16[2,272,640]{2,1,0:T(8,128)(2,1)S(1)} %get-tuple-element.29.refs_3_.refs_0_), channel_id=1, source_target_pairs={{0,6},{1,25},{2,0},{3,27},{4,2},{5,29},{6,4},{7,31},{8,14},{9,1},{... | collective-permute-start | bytes 2088968 | tf_op jit(solution)/shard_map/ppermute | solution.py:51
  31.1 9.4 %collective-permute-done.1.refs_1_.refs_0_ = bf16[2,272,640]{2,1,0:T(8,128)(2,1)} collective-permute-done((bf16[2,272,640]{2,1,0:T(8,128)(2,1)S(1)}, bf16[2,272,640]{2,1,0:T(8,128)(2,1)}, u32[]{:S(2)}, u32[]{:S(2)}) %collective-permute-start.1) | collective-permute-done | bytes 696352 | tf_op jit(solution)/shard_map/ppermute | solution.py:51
  40.5 1.5 %collective-permute-start.2 = (bf16[2,272,640]{2,1,0:T(8,128)(2,1)}, bf16[2,272,640]{2,1,0:T(8,128)(2,1)}, u32[]{:S(2)}, u32[]{:S(2)}) collective-permute-start(bf16[2,272,640]{2,1,0:T(8,128)(2,1)} %collective-permute-done.1.refs_1_.refs_0_), channel_id=1, source_target_pairs={{0,2},{1,9},{2,4},{3,11},{4,6},{5,13},{6,0},{7,15},{8,10},{9,17},{... | collective-permute-start | bytes 2088968 | tf_op jit(solution)/shard_map/ppermute | solution.py:51
  42.0 6.8 %local.1 = (bf16[256,2560]{1,0:T(8,128)(2,1)}, f32[256,128]{1,0:T(8,128)}, bf16[20,160,256]{2,1,0:T(8,128)(2,1)}) custom-call(bf16[320,256]{1,0:T(8,128)(2,1)} %bitcast.33, bf16[320,256]{1,0:T(8,128)(2,1)} %bitcast.35, bf16[256,2560]{1,0:T(8,128)(2,1)} %bitcast.32, bf16[4,320,64]{2,1,0:T(8,128)(2,1)} %constant.13.clone.select_ref, ...), custom_call_target="tpu_custom_call" | custom-call | flops 4000000000 | bytes 8000000 | tf_op jit(solution)/shard_map/local/pallas_call | solution.py:548
  48.8 0.0 collective-permute-done.3.refs_2_.refs_1_
  48.8 8.5 %collective-permute-done.2.refs_0_ = bf16[2,272,640]{2,1,0:T(8,128)(2,1)} collective-permute-done((bf16[2,272,640]{2,1,0:T(8,128)(2,1)}, bf16[2,272,640]{2,1,0:T(8,128)(2,1)}, u32[]{:S(2)}, u32[]{:S(2)}) %collective-permute-start.2) | collective-permute-done | bytes 696352 | tf_op jit(solution)/shard_map/ppermute | solution.py:51
  57.3 2.8 %search.1 = (s32[8,128]{1,0:T(8,128)S(1)}, s32[8]{0:T(128)S(1)}) custom-call(s32[1]{0:T(128)} %bitcast.7.me_ref, bf16[2,272,640]{2,1,0:T(8,128)(2,1)} %collective-permute-done.2.refs_0_, bf16[2,272,640]{2,1,0:T(8,128)(2,1)} %collective-permute-done.1.refs_1_.refs_0_, bf16[2,272,640]{2,1,0:T(8,128)(2,1)} %collective-permute-done.3.refs_2_.refs_1_, ...), custom_call_target="tpu_custom_call" | custom-call | bytes 100000 | tf_op jit(solution)/shard_map/search/pallas_call | solution.py:560
  60.1 0.0 all-to-all-done.in_ref
  60.1 2.8 %prefix.1 = bf16[8,400,128]{2,1,0:T(8,128)(2,1)} custom-call(s32[1]{0:T(128)} %bitcast.13.place_ref, bf16[8,400,128]{2,1,0:T(8,128)(2,1)} %all-to-all-done.in_ref), custom_call_target="tpu_custom_call" | custom-call | bytes 2000000 | tf_op jit(solution)/shard_map/prefix/pallas_call | solution.py:575
  62.9 6.6 %all-to-all-start.1 = ((bf16[8,400,128]{2,1,0:T(8,128)(2,1)}), bf16[8,400,128]{2,1,0:T(8,128)(2,1)}, u32[]{:S(2)}, u32[]{:S(2)}) async-start(bf16[8,400,128]{2,1,0:T(8,128)(2,1)} %prefix.1), calls=%async_computation.1 | async-start | bytes 1638400 | tf_op jit(solution)/shard_map/all_to_all | solution.py:584
  69.6 0.0 collective-permute-done.6.refs_4_.refs_5_
  69.6 0.0 collective-permute-done.5.refs_3_.refs_4_
  69.6 4.1 %shard_map.114 = bf16[2,272,640]{2,1,0:T(8,128)(2,1)S(1)} custom-call(s32[8,128]{1,0:T(8,128)S(1)} %get-tuple-element.36.found, s32[8]{0:T(128)S(1)} %get-tuple-element.37.counts, bf16[2,272,640]{2,1,0:T(8,128)(2,1)} %collective-permute-done.2.refs_0_, bf16[2,2,256,640]{3,2,1,0:T(8,128)(2,1)S(1)} %get-tuple-element.38.refs_1_.refs_2_, ...), custom_call_target="tpu_custom_call" | custom-call | flops 800000000 | bytes 8000000 | tf_op jit(solution)/shard_map/pallas_call | solution.py:466
  73.7 6.5 %shard_map.115 = (bf16[2,272,640]{2,1,0:T(8,128)(2,1)S(1)}, bf16[2,272,640]{2,1,0:T(8,128)(2,1)S(1)}) custom-call(s32[8,128]{1,0:T(8,128)S(1)} %get-tuple-element.36.found, s32[8]{0:T(128)S(1)} %get-tuple-element.37.counts, bf16[2,272,640]{2,1,0:T(8,128)(2,1)} %collective-permute-done.1.refs_1_.refs_0_, ...), custom_call_target="tpu_custom_call" | custom-call | flops 1600000000 | bytes 8000000 | tf_op jit(solution)/shard_map/pallas_call | solution.py:466
  80.1 4.6 %collective-permute-start.7 = (bf16[2,272,640]{2,1,0:T(8,128)(2,1)S(1)}, bf16[2,272,640]{2,1,0:T(8,128)(2,1)S(1)}, u32[]{:S(2)}, u32[]{:S(2)}) collective-permute-start(bf16[2,272,640]{2,1,0:T(8,128)(2,1)S(1)} %get-tuple-element.41), channel_id=1, source_target_pairs={{0,6},{1,25},{2,0},{3,27},{4,2},{5,29},{6,4},{7,31},{8,14},{9,1},{... | collective-permute-start | bytes 2088968 | tf_op jit(solution)/shard_map/ppermute | solution.py:51
  84.7 0.0 collective-permute-start.8
  84.7 1.3 %collective-permute-start.9 = (bf16[2,272,640]{2,1,0:T(8,128)(2,1)S(1)}, bf16[2,272,640]{2,1,0:T(8,128)(2,1)S(1)}, u32[]{:S(2)}, u32[]{:S(2)}) collective-permute-start(bf16[2,272,640]{2,1,0:T(8,128)(2,1)S(1)} %shard_map.114), channel_id=1, source_target_pairs={{0,4},{1,17},{2,6},{3,19},{4,0},{5,21},{6,2},{7,23},{8,12},{9,25},... | collective-permute-start | bytes 2088968 | tf_op jit(solution)/shard_map/ppermute | solution.py:51
  86.0 5.5 %shard_map.113.refs_0_ = bf16[2,272,640]{2,1,0:T(8,128)(2,1)S(1)} custom-call(s32[8,128]{1,0:T(8,128)S(1)} %get-tuple-element.36.found, s32[8]{0:T(128)S(1)} %get-tuple-element.37.counts, bf16[2,272,640]{2,1,0:T(8,128)(2,1)S(1)} %get-tuple-element.29.refs_3_.refs_0_, bf16[2,2,256,640]{3,2,1,0:T(8,128)(2,1)S(1)} %get-tuple-element.38.refs_1_.refs_2_, ...), custom_call_target="tpu_custom_call" | custom-call | flops 800000000 | bytes 8000000 | tf_op jit(solution)/shard_map/pallas_call | solution.py:466
  91.5 8.7 %collective-permute-done.7.refs_1_ = bf16[2,272,640]{2,1,0:T(8,128)(2,1)S(1)} collective-permute-done((bf16[2,272,640]{2,1,0:T(8,128)(2,1)S(1)}, bf16[2,272,640]{2,1,0:T(8,128)(2,1)S(1)}, u32[]{:S(2)}, u32[]{:S(2)}) %collective-permute-start.7) | collective-permute-done | bytes 696352 | tf_op jit(solution)/shard_map/ppermute | solution.py:51
  100.2 3.4 %collective-permute-done.8.refs_2_ = bf16[2,272,640]{2,1,0:T(8,128)(2,1)S(1)} collective-permute-done((bf16[2,272,640]{2,1,0:T(8,128)(2,1)S(1)}, bf16[2,272,640]{2,1,0:T(8,128)(2,1)S(1)}, u32[]{:S(2)}, u32[]{:S(2)}) %collective-permute-start.8) | collective-permute-done | bytes 696352 | tf_op jit(solution)/shard_map/ppermute | solution.py:51
  103.6 0.0 collective-permute-done.9.refs_3_
  103.6 2.7 %join.1 = (bf16[256,640]{1,0:T(8,128)(2,1)S(1)}, bf16[256,640]{1,0:T(8,128)(2,1)S(1)}) custom-call(bf16[2,272,640]{2,1,0:T(8,128)(2,1)S(1)} %shard_map.113.refs_0_, bf16[2,272,640]{2,1,0:T(8,128)(2,1)S(1)} %collective-permute-done.7.refs_1_, bf16[2,272,640]{2,1,0:T(8,128)(2,1)S(1)} %collective-permute-done.8.refs_2_, ...), custom_call_target="tpu_custom_call" | custom-call | bytes 4000000 | tf_op jit(solution)/shard_map/join/pallas_call | solution.py:592
  106.3 1.7 %collective-permute-start.10 = (bf16[256,640]{1,0:T(8,128)(2,1)S(1)}, bf16[256,640]{1,0:T(8,128)(2,1)S(1)}, u32[]{:S(2)}, u32[]{:S(2)}) collective-permute-start(bf16[256,640]{1,0:T(8,128)(2,1)S(1)} %get-tuple-element.45), channel_id=1, source_target_pairs={{0,1},{1,0},{2,3},{3,2},{4,5},{5,4},{6,7},{7,6},{8,9},{9,8},{10,11... | collective-permute-start | bytes 983048 | tf_op jit(solution)/shard_map/ppermute | solution.py:55
  107.9 0.0 all-to-all-done.1
  107.9 5.6 %finish.1 = bf16[256,2560]{1,0:T(8,128)(2,1)} custom-call(bf16[256,2560]{1,0:T(8,128)(2,1)} %get-tuple-element.32.num_ref, f32[256,128]{1,0:T(8,128)} %get-tuple-element.33.den_ref, bf16[20,160,256]{2,1,0:T(8,128)(2,1)} %get-tuple-element.34.phi_ref, bf16[20,160,128]{2,1,0:T(8,128)(2,1)} %bitcast.14.state_ref), custom_call_target="tpu_custom_call" | custom-call | flops 400000000 | bytes 8000000 | tf_op jit(solution)/shard_map/finish/pallas_call | solution.py:613
  113.6 0.0 collective-permute-done.10.other_ref
  113.6 0.8 place.1
Async XLA Ops:
  1.3 0.7 copy-start
  1.9 5.0 %copy-start.1 = (s32[1,1,8]{2,1,0:T(1,128)S(1)}, s32[1,1,8]{2,1,0:T(1,128)}, u32[]{:S(2)}) copy-start(s32[1,1,8]{2,1,0:T(1,128)} %param.16) | copy-start | bytes 100
  3.7 5.5 %collective-permute-start = (bf16[784,640]{1,0:T(8,128)(2,1)S(1)}, bf16[784,640]{1,0:T(8,128)(2,1)S(1)}, u32[]{:S(2)}, u32[]{:S(2)}) collective-permute-start(bf16[784,640]{1,0:T(8,128)(2,1)S(1)} %pack.1), channel_id=1, source_target_pairs={{0,1},{1,0},{2,3},{3,2},{4,5},{5,4},{6,7},{7,6},{8,9},{9,8},{10,11... | collective-permute-start | bytes 3010568 | tf_op jit(solution)/shard_map/ppermute | solution.py:55
  9.6 16.8 %collective-permute-start.4 = (bf16[2,2,256,640]{3,2,1,0:T(8,128)(2,1)S(1)}, bf16[2,2,256,640]{3,2,1,0:T(8,128)(2,1)S(1)}, u32[]{:S(2)}, u32[]{:S(2)}) collective-permute-start(bf16[2,2,256,640]{3,2,1,0:T(8,128)(2,1)S(1)} %get-tuple-element.38.refs_1_.refs_2_), channel_id=1, source_target_pairs={{0,24},{1,7},{2,26},{3,1},{4,28},{5,3},{6,30},{7,5},{8,0},{9,15},{... | collective-permute-start | bytes 3932168 | tf_op jit(solution)/shard_map/ppermute | solution.py:51
  16.1 44.0 %all-to-all-start = ((bf16[8,400,128]{2,1,0:T(8,128)(2,1)}), bf16[8,400,128]{2,1,0:T(8,128)(2,1)}, u32[]{:S(2)}, u32[]{:S(2)}) async-start(bf16[8,400,128]{2,1,0:T(8,128)(2,1)} %bitcast.29), calls=%async_computation | async-start | bytes 1638400 | tf_op jit(solution)/shard_map/all_to_all | solution.py:546
  24.3 16.2 %collective-permute-start.1 = (bf16[2,272,640]{2,1,0:T(8,128)(2,1)S(1)}, bf16[2,272,640]{2,1,0:T(8,128)(2,1)}, u32[]{:S(2)}, u32[]{:S(2)}) collective-permute-start(bf16[2,272,640]{2,1,0:T(8,128)(2,1)S(1)} %get-tuple-element.29.refs_3_.refs_0_), channel_id=1, source_target_pairs={{0,2},{1,9},{2,4},{3,11},{4,6},{5,13},{6,0},{7,15},{8,10},{9,17},{... | collective-permute-start | bytes 2088968 | tf_op jit(solution)/shard_map/ppermute | solution.py:51
  25.5 44.0 %collective-permute-start.6 = (bf16[2,2,256,640]{3,2,1,0:T(8,128)(2,1)S(1)}, bf16[2,2,256,640]{3,2,1,0:T(8,128)(2,1)}, u32[]{:S(2)}, u32[]{:S(2)}) collective-permute-start(bf16[2,2,256,640]{3,2,1,0:T(8,128)(2,1)S(1)} %get-tuple-element.38.refs_1_.refs_2_), channel_id=1, source_target_pairs={{0,8},{1,3},{2,10},{3,5},{4,12},{5,7},{6,14},{7,1},{8,16},{9,11},{... | collective-permute-start | bytes 3932168 | tf_op jit(solution)/shard_map/ppermute | solution.py:51
  26.4 43.2 %collective-permute-start.5 = (bf16[2,2,256,640]{3,2,1,0:T(8,128)(2,1)S(1)}, bf16[2,2,256,640]{3,2,1,0:T(8,128)(2,1)}, u32[]{:S(2)}, u32[]{:S(2)}) collective-permute-start(bf16[2,2,256,640]{3,2,1,0:T(8,128)(2,1)S(1)} %collective-permute-done.4.refs_2_.refs_3_), channel_id=1, source_target_pairs={{0,24},{1,7},{2,26},{3,1},{4,28},{5,3},{6,30},{7,5},{8,0},{9,15},{... | collective-permute-start | bytes 3932168 | tf_op jit(solution)/shard_map/ppermute | solution.py:51
  28.3 20.5 %collective-permute-start.3 = (bf16[2,272,640]{2,1,0:T(8,128)(2,1)S(1)}, bf16[2,272,640]{2,1,0:T(8,128)(2,1)}, u32[]{:S(2)}, u32[]{:S(2)}) collective-permute-start(bf16[2,272,640]{2,1,0:T(8,128)(2,1)S(1)} %get-tuple-element.29.refs_3_.refs_0_), channel_id=1, source_target_pairs={{0,6},{1,25},{2,0},{3,27},{4,2},{5,29},{6,4},{7,31},{8,14},{9,1},{... | collective-permute-start | bytes 2088968 | tf_op jit(solution)/shard_map/ppermute | solution.py:51
  40.5 16.8 %collective-permute-start.2 = (bf16[2,272,640]{2,1,0:T(8,128)(2,1)}, bf16[2,272,640]{2,1,0:T(8,128)(2,1)}, u32[]{:S(2)}, u32[]{:S(2)}) collective-permute-start(bf16[2,272,640]{2,1,0:T(8,128)(2,1)} %collective-permute-done.1.refs_1_.refs_0_), channel_id=1, source_target_pairs={{0,2},{1,9},{2,4},{3,11},{4,6},{5,13},{6,0},{7,15},{8,10},{9,17},{... | collective-permute-start | bytes 2088968 | tf_op jit(solution)/shard_map/ppermute | solution.py:51
  62.9 45.0 %all-to-all-start.1 = ((bf16[8,400,128]{2,1,0:T(8,128)(2,1)}), bf16[8,400,128]{2,1,0:T(8,128)(2,1)}, u32[]{:S(2)}, u32[]{:S(2)}) async-start(bf16[8,400,128]{2,1,0:T(8,128)(2,1)} %prefix.1), calls=%async_computation.1 | async-start | bytes 1638400 | tf_op jit(solution)/shard_map/all_to_all | solution.py:584
  80.1 20.0 %collective-permute-start.7 = (bf16[2,272,640]{2,1,0:T(8,128)(2,1)S(1)}, bf16[2,272,640]{2,1,0:T(8,128)(2,1)S(1)}, u32[]{:S(2)}, u32[]{:S(2)}) collective-permute-start(bf16[2,272,640]{2,1,0:T(8,128)(2,1)S(1)} %get-tuple-element.41), channel_id=1, source_target_pairs={{0,6},{1,25},{2,0},{3,27},{4,2},{5,29},{6,4},{7,31},{8,14},{9,1},{... | collective-permute-start | bytes 2088968 | tf_op jit(solution)/shard_map/ppermute | solution.py:51
  84.7 18.8 %collective-permute-start.8 = (bf16[2,272,640]{2,1,0:T(8,128)(2,1)S(1)}, bf16[2,272,640]{2,1,0:T(8,128)(2,1)S(1)}, u32[]{:S(2)}, u32[]{:S(2)}) collective-permute-start(bf16[2,272,640]{2,1,0:T(8,128)(2,1)S(1)} %get-tuple-element.42), channel_id=1, source_target_pairs={{0,2},{1,9},{2,4},{3,11},{4,6},{5,13},{6,0},{7,15},{8,10},{9,17},{... | collective-permute-start | bytes 2088968 | tf_op jit(solution)/shard_map/ppermute | solution.py:51
  84.7 18.8 %collective-permute-start.9 = (bf16[2,272,640]{2,1,0:T(8,128)(2,1)S(1)}, bf16[2,272,640]{2,1,0:T(8,128)(2,1)S(1)}, u32[]{:S(2)}, u32[]{:S(2)}) collective-permute-start(bf16[2,272,640]{2,1,0:T(8,128)(2,1)S(1)} %shard_map.114), channel_id=1, source_target_pairs={{0,4},{1,17},{2,6},{3,19},{4,0},{5,21},{6,2},{7,23},{8,12},{9,25},... | collective-permute-start | bytes 2088968 | tf_op jit(solution)/shard_map/ppermute | solution.py:51
  106.3 7.3 %collective-permute-start.10 = (bf16[256,640]{1,0:T(8,128)(2,1)S(1)}, bf16[256,640]{1,0:T(8,128)(2,1)S(1)}, u32[]{:S(2)}, u32[]{:S(2)}) collective-permute-start(bf16[256,640]{1,0:T(8,128)(2,1)S(1)} %get-tuple-element.45), channel_id=1, source_target_pairs={{0,1},{1,0},{2,3},{3,2},{4,5},{5,4},{6,7},{7,6},{8,9},{9,8},{10,11... | collective-permute-start | bytes 983048 | tf_op jit(solution)/shard_map/ppermute | solution.py:55

commit v6 on v5

--- a/solution.py
+++ b/solution.py
@@ -26,6 +26,7 @@
 QROWS = 272
 SIDE = 4
 CORES = 2
+JOIN_ROWS = 64
 
 inv_root_two = 0.7071067811865476
 TO_LOG2 = math.log2(math.e) / math.sqrt(SM_HD)
@@ -128,7 +129,7 @@
         total = total + in_ref[z].astype(F32)
 
 
-def local_kernel(q_ref, k_ref, v_ref, select_ref, vector_ref, num_ref, den_ref, phi_ref):
+def local_kernel(q_ref, k_ref, v_ref, select_ref, vector_ref, num_ref, den_ref):
     causal = lax.broadcasted_iota(jnp.int32, (TOK, TOK), 0) >= lax.broadcasted_iota(jnp.int32, (TOK, TOK), 1)
     lane = lax.broadcasted_iota(jnp.int32, (TOK, 128), 1)
     group = pl.program_id(0)
@@ -140,8 +141,6 @@
     den = den_ref[...]
     phis_q = [features(select_ref[j], q_ref[...], vector_ref) for j in range(GROUP)]
     phis_k = [features(select_ref[j], k_ref[...], vector_ref) for j in range(GROUP)]
-    for j in range(GROUP):
-        phi_ref[j] = phis_q[j]
     turned = [taller(p).T for p in phis_q]
     weights = [jnp.dot(turned[j], taller(phis_k[j]), preferred_element_type=F32) for j in range(GROUP)]
     weights = [jnp.where(causal, w, 0.0).astype(BF) for w in weights]
@@ -152,11 +151,12 @@
     den_ref[...] = den
 
 
-def finish_kernel(num_ref, den_ref, phi_ref, state_ref, out_ref):
+def finish_kernel(num_ref, den_ref, q_ref, select_ref, vector_ref, state_ref, out_ref):
     lane = lax.broadcasted_iota(jnp.int32, (TOK, 128), 1)
     group = pl.program_id(0)
     at = FEATS - (FROWS - 16)
-    phis = [taller(phi_ref[j]).T for j in range(GROUP)]
+    phis = [features(select_ref[j], q_ref[...], vector_ref) for j in range(GROUP)]
+    phis = [taller(p).T for p in phis]
     carried = [jnp.dot(phis[j], taller(state_ref[j]), preferred_element_type=F32) for j in range(GROUP)]
     dens = []
     for j in range(GROUP):
@@ -399,21 +399,24 @@
 
 
 def join_kernel(*refs):
-    parts, outs = refs[:4], refs[4:]
+    parts, outs, size_ref = refs[:4], refs[4:6], refs[6]
     for r in range(2):
-        sizes = []
-        for p in parts:
+        for i, p in enumerate(parts):
             packed = p[r, TOK:QROWS, 0:TOK].astype(F32)
             packed = jnp.concatenate([packed, jnp.zeros((128 - (QROWS - TOK), TOK), F32)], axis=0).T
-            sizes.append(packed + pltpu.roll(packed, 128 - HALF_HEADS, 1) + pltpu.roll(packed, 128 - 2 * HALF_HEADS, 1))
-        top = functools.reduce(jnp.maximum, sizes)
-        shares = [jnp.exp2(s - top) for s in sizes]
-        total = functools.reduce(jnp.add, shares)
-        shares = [s / total for s in shares]
-        for h in range(HALF_HEADS):
-            at = slice(h * 128, (h + 1) * 128)
-            o = sum(s[:, h : h + 1] * p[r, 0:TOK, at].astype(F32) for s, p in zip(shares, parts, strict=True))
-            outs[r][:, at] = o.astype(BF)
+            size_ref[r, i] = packed + pltpu.roll(packed, 128 - HALF_HEADS, 1) + pltpu.roll(packed, 128 - 2 * HALF_HEADS, 1)
+    for r in range(2):
+        for t in range(TOK // JOIN_ROWS):
+            rows = slice(t * JOIN_ROWS, (t + 1) * JOIN_ROWS)
+            sizes = [size_ref[r, i, rows] for i in range(4)]
+            top = functools.reduce(jnp.maximum, sizes)
+            shares = [jnp.exp2(s - top) for s in sizes]
+            total = functools.reduce(jnp.add, shares)
+            shares = [s / total for s in shares]
+            for h in range(HALF_HEADS):
+                at = slice(h * 128, (h + 1) * 128)
+                o = sum(s[:, h : h + 1] * p[r, rows, at].astype(F32) for s, p in zip(shares, parts, strict=True))
+                outs[r][rows, at] = o.astype(BF)
 
 
 def place_kernel(me_ref, kept_ref, other_ref, out_ref, sems):
@@ -545,13 +548,13 @@
     )(*in_hbm(k_lin[0].T, v_lin[0], select, vectors))
     slices = lax.all_to_all(state.reshape(shards, HEADS * FROWS // shards, 128), "seq", 0, 0, tiled=True)
 
-    num, den, phi = pl.pallas_call(
+    num, den = pl.pallas_call(
         local_kernel,
         name="local",
         grid=steps,
-        out_shape=[hbm_shape(TOK, D), hbm_shape(TOK, 128, dtype=F32), hbm_shape(HEADS, FROWS, TOK)],
+        out_shape=[hbm_shape(TOK, D), hbm_shape(TOK, 128, dtype=F32)],
         in_specs=[heads16, heads16, heads128, whole(*select.shape), whole(*vectors.shape)],
-        out_specs=[heads128, whole(TOK, 128), pl.BlockSpec((GROUP, FROWS, TOK), lambda g: (g, 0, 0))],
+        out_specs=[heads128, whole(TOK, 128)],
         compiler_params=room(10),
         cost_estimate=cost(4e9, 8e6),
     )(*in_hbm(q_lin[0].T, k_lin[0].T, v_lin[0], select, vectors))
@@ -571,7 +574,7 @@
         compiler_params=room(2),
         cost_estimate=cost(0, 1e5),
     )(me, q_far, q_left, q_right, q)
-    slices, num, den, phi, *lists = lax.optimization_barrier((slices, num, den, phi, *lists))
+    slices, num, den, *lists = lax.optimization_barrier((slices, num, den, *lists))
     prefix = pl.pallas_call(
         prefix_kernel,
         name="prefix",
@@ -595,6 +598,7 @@
         out_shape=[shape(TOK, HALF)] * 2,
         in_specs=[VMEM] * 4,
         out_specs=[VMEM] * 2,
+        scratch_shapes=[pltpu.VMEM((2, 4, TOK, 128), F32)],
         compiler_params=room(8),
         cost_estimate=cost(0, 4e6),
     )(here, from_right, from_left, from_far)
@@ -618,13 +622,15 @@
         in_specs=[
             heads128,
             whole(TOK, 128),
-            pl.BlockSpec((GROUP, FROWS, TOK), lambda g: (g, 0, 0)),
+            heads16,
+            whole(*select.shape),
+            whole(*vectors.shape),
             pl.BlockSpec((GROUP, FROWS, 128), lambda g: (g, 0, 0)),
         ],
         out_specs=heads128,
         compiler_params=room(8),
         cost_estimate=cost(4e8, 8e6),
-    )(*in_hbm(num, den, phi), before)
+    )(*in_hbm(num, den, q_lin[0].T, select, vectors), before)
     return lin_out[None], soft_out[None]
 
 

time: 115 us -> 115 us (level)
  no operation moved by 1% of the time
where the time goes in v6:
time: 115 us
  Pallas kernels  46.8 us (41%)
  starting transfers between devices  34.2 us (30%)
  waiting for transfers between devices  31.4 us (27%)
  between operations  1.54 us (1%)
    ppermute x9, waiting for transfers between devices, move(): return lax.ppermute(a, 'files', along(what, step))  30.9 us
    pallas_call x3, Pallas kernels, attend(): pl.pallas_call(functools.partial(attend_kernel, own, base, readers), out_...  16 us
    ppermute x9, starting transfers between devices, move(): return lax.ppermute(a, 'files', along(what, step))  14.4 us
    all_to_all x1, starting transfers between devices, layers(): lax.all_to_all(state.reshape(shards, HEADS * FROWS // shards, 128), 'seq'...  8.17 us
    pallas_call x1, Pallas kernels, layers(): pl.pallas_call(local_kernel, name='local', grid=steps, out_shape=[hbm_sha...  6.78 us
    all_to_all x1, starting transfers between devices, layers(): lax.all_to_all(prefix, 'seq', 0, 0, tiled=True).reshape(HEADS, FROWS, 128)  6.65 us
    pallas_call x1, Pallas kernels, layers(): pl.pallas_call(finish_kernel, name='finish', grid=steps, out_shape=shape(...  6.23 us
    pallas_call x1, Pallas kernels, layers(): pl.pallas_call(state_kernel, name='state', grid=steps, out_shape=hbm_shap...  5.45 us
  transfers between devices with their start and end apart: 13, of which 6 were waited for; matrix products, arithmetic and copies ran while one was open for 0% of the time, Pallas kernels for 38%

profile of v6, /device:TPU:1, one launch (start us, length us, event | category | flops | bytes accessed | tf_op | source)
XLA Modules:
  0.0 114.5 jit_solution(5932471488175709337)
XLA Ops:
  1.3 0.0 copy-start
  1.3 0.6 copy-done
  1.9 0.0 copy-start.1
  1.9 1.7 %pack.1 = bf16[784,640]{1,0:T(8,128)(2,1)S(1)} custom-call(s32[1]{0:T(128)} %bitcast.7.me_ref, s32[8]{0:T(128)S(1)} %bitcast.20, s32[1]{0:T(128)} %bitcast.18.count_ref, bf16[256,1280]{1,0:T(8,128)(2,1)} %bitcast.22, bf16[256,1280]{1,0:T(8,128)(2,1)} %bitcast.24, bf16[256,1280]{1,0:T(8,128)(2,1)} %bitcast.26), custom_call_target="tpu_custom_call" | custom-call | bytes 2000000 | tf_op jit(solution)/shard_map/pack/pallas_call | solution.py:498
  3.7 3.3 %collective-permute-start = (bf16[784,640]{1,0:T(8,128)(2,1)S(1)}, bf16[784,640]{1,0:T(8,128)(2,1)S(1)}, u32[]{:S(2)}, u32[]{:S(2)}) collective-permute-start(bf16[784,640]{1,0:T(8,128)(2,1)S(1)} %pack.1), channel_id=1, source_target_pairs={{0,1},{1,0},{2,3},{3,2},{4,5},{5,4},{6,7},{7,6},{8,9},{9,8},{10,11... | collective-permute-start | bytes 3010568 | tf_op jit(solution)/shard_map/ppermute | solution.py:56
  7.0 0.0 copy-done.1
  7.0 1.7 %own.1 = (bf16[2,2,256,640]{3,2,1,0:T(8,128)(2,1)S(1)}, bf16[2,272,640]{2,1,0:T(8,128)(2,1)S(1)}) custom-call(s32[1]{0:T(128)} %bitcast.7.me_ref, s32[8]{0:T(128)S(1)} %bitcast.21, s32[1]{0:T(128)} %bitcast.19.count_ref, bf16[256,1280]{1,0:T(8,128)(2,1)} %bitcast.23, bf16[256,1280]{1,0:T(8,128)(2,1)} %bitcast.25, bf16[256,1280]{1,0:T(8,128)(2,1)} %bitcast.27), custom_call_target="tpu_custom_call" | custom-call | bytes 2000000 | tf_op jit(solution)/shard_map/own/pallas_call | solution.py:510
  8.7 0.5 collective-permute-done.mate_ref
  9.2 0.4 merge.1
  9.6 1.1 collective-permute-start.4
  10.7 5.5 %state.1 = bf16[20,160,128]{2,1,0:T(8,128)(2,1)} custom-call(bf16[320,256]{1,0:T(8,128)(2,1)} %bitcast.35, bf16[256,2560]{1,0:T(8,128)(2,1)} %bitcast.33, bf16[4,320,64]{2,1,0:T(8,128)(2,1)} %constant.13.clone.select_ref, f32[3,160,128]{2,1,0:T(8,128)} %constant.14.clone.vector_ref), custom_call_target="tpu_custom_call" | custom-call | flops 1000000000 | bytes 4000000 | tf_op jit(solution)/shard_map/state/pallas_call | solution.py:539
  16.1 8.2 %all-to-all-start = ((bf16[8,400,128]{2,1,0:T(8,128)(2,1)}), bf16[8,400,128]{2,1,0:T(8,128)(2,1)}, u32[]{:S(2)}, u32[]{:S(2)}) async-start(bf16[8,400,128]{2,1,0:T(8,128)(2,1)} %bitcast.29), calls=%async_computation | async-start | bytes 1638400 | tf_op jit(solution)/shard_map/all_to_all | solution.py:549
  24.3 1.2 %collective-permute-start.1 = (bf16[2,272,640]{2,1,0:T(8,128)(2,1)S(1)}, bf16[2,272,640]{2,1,0:T(8,128)(2,1)}, u32[]{:S(2)}, u32[]{:S(2)}) collective-permute-start(bf16[2,272,640]{2,1,0:T(8,128)(2,1)S(1)} %get-tuple-element.26.refs_3_.refs_0_), channel_id=1, source_target_pairs={{0,2},{1,9},{2,4},{3,11},{4,6},{5,13},{6,0},{7,15},{8,10},{9,17},{... | collective-permute-start | bytes 2088968 | tf_op jit(solution)/shard_map/ppermute | solution.py:52
  25.5 0.0 collective-permute-start.6
  25.5 0.9 collective-permute-done.4.refs_2_.refs_3_
  26.4 1.9 %collective-permute-start.5 = (bf16[2,2,256,640]{3,2,1,0:T(8,128)(2,1)S(1)}, bf16[2,2,256,640]{3,2,1,0:T(8,128)(2,1)}, u32[]{:S(2)}, u32[]{:S(2)}) collective-permute-start(bf16[2,2,256,640]{3,2,1,0:T(8,128)(2,1)S(1)} %collective-permute-done.4.refs_2_.refs_3_), channel_id=1, source_target_pairs={{0,24},{1,7},{2,26},{3,1},{4,28},{5,3},{6,30},{7,5},{8,0},{9,15},{... | collective-permute-start | bytes 3932168 | tf_op jit(solution)/shard_map/ppermute | solution.py:52
  28.3 2.8 %collective-permute-start.3 = (bf16[2,272,640]{2,1,0:T(8,128)(2,1)S(1)}, bf16[2,272,640]{2,1,0:T(8,128)(2,1)}, u32[]{:S(2)}, u32[]{:S(2)}) collective-permute-start(bf16[2,272,640]{2,1,0:T(8,128)(2,1)S(1)} %get-tuple-element.26.refs_3_.refs_0_), channel_id=1, source_target_pairs={{0,6},{1,25},{2,0},{3,27},{4,2},{5,29},{6,4},{7,31},{8,14},{9,1},{... | collective-permute-start | bytes 2088968 | tf_op jit(solution)/shard_map/ppermute | solution.py:52
  31.1 9.4 %collective-permute-done.1.refs_1_.refs_0_ = bf16[2,272,640]{2,1,0:T(8,128)(2,1)} collective-permute-done((bf16[2,272,640]{2,1,0:T(8,128)(2,1)S(1)}, bf16[2,272,640]{2,1,0:T(8,128)(2,1)}, u32[]{:S(2)}, u32[]{:S(2)}) %collective-permute-start.1) | collective-permute-done | bytes 696352 | tf_op jit(solution)/shard_map/ppermute | solution.py:52
  40.5 1.5 %collective-permute-start.2 = (bf16[2,272,640]{2,1,0:T(8,128)(2,1)}, bf16[2,272,640]{2,1,0:T(8,128)(2,1)}, u32[]{:S(2)}, u32[]{:S(2)}) collective-permute-start(bf16[2,272,640]{2,1,0:T(8,128)(2,1)} %collective-permute-done.1.refs_1_.refs_0_), channel_id=1, source_target_pairs={{0,2},{1,9},{2,4},{3,11},{4,6},{5,13},{6,0},{7,15},{8,10},{9,17},{... | collective-permute-start | bytes 2088968 | tf_op jit(solution)/shard_map/ppermute | solution.py:52
  42.0 6.8 %local.1 = (bf16[256,2560]{1,0:T(8,128)(2,1)}, f32[256,128]{1,0:T(8,128)}) custom-call(bf16[320,256]{1,0:T(8,128)(2,1)} %bitcast.31, bf16[320,256]{1,0:T(8,128)(2,1)} %bitcast.36, bf16[256,2560]{1,0:T(8,128)(2,1)} %bitcast.34, bf16[4,320,64]{2,1,0:T(8,128)(2,1)} %constant.13.clone.select_ref, f32[3,160,128]{2,1,0:T(8,128)} %constant.14.clone.vector_ref), custom_call_target="tpu_custom_call" | custom-call | flops 4000000000 | bytes 8000000 | tf_op jit(solution)/shard_map/local/pallas_call | solution.py:551
  48.8 0.0 collective-permute-done.3.refs_2_.refs_1_
  48.8 8.5 %collective-permute-done.2.refs_0_ = bf16[2,272,640]{2,1,0:T(8,128)(2,1)} collective-permute-done((bf16[2,272,640]{2,1,0:T(8,128)(2,1)}, bf16[2,272,640]{2,1,0:T(8,128)(2,1)}, u32[]{:S(2)}, u32[]{:S(2)}) %collective-permute-start.2) | collective-permute-done | bytes 696352 | tf_op jit(solution)/shard_map/ppermute | solution.py:52
  57.3 2.8 %search.1 = (s32[8,128]{1,0:T(8,128)S(1)}, s32[8]{0:T(128)S(1)}) custom-call(s32[1]{0:T(128)} %bitcast.7.me_ref, bf16[2,272,640]{2,1,0:T(8,128)(2,1)} %collective-permute-done.2.refs_0_, bf16[2,272,640]{2,1,0:T(8,128)(2,1)} %collective-permute-done.1.refs_1_.refs_0_, bf16[2,272,640]{2,1,0:T(8,128)(2,1)} %collective-permute-done.3.refs_2_.refs_1_, ...), custom_call_target="tpu_custom_call" | custom-call | bytes 100000 | tf_op jit(solution)/shard_map/search/pallas_call | solution.py:563
  60.1 0.0 all-to-all-done.in_ref
  60.1 2.8 %prefix.1 = bf16[8,400,128]{2,1,0:T(8,128)(2,1)} custom-call(s32[1]{0:T(128)} %bitcast.13.place_ref, bf16[8,400,128]{2,1,0:T(8,128)(2,1)} %all-to-all-done.in_ref), custom_call_target="tpu_custom_call" | custom-call | bytes 2000000 | tf_op jit(solution)/shard_map/prefix/pallas_call | solution.py:578
  62.9 6.6 %all-to-all-start.1 = ((bf16[8,400,128]{2,1,0:T(8,128)(2,1)}), bf16[8,400,128]{2,1,0:T(8,128)(2,1)}, u32[]{:S(2)}, u32[]{:S(2)}) async-start(bf16[8,400,128]{2,1,0:T(8,128)(2,1)} %prefix.1), calls=%async_computation.1 | async-start | bytes 1638400 | tf_op jit(solution)/shard_map/all_to_all | solution.py:587
  69.6 0.0 collective-permute-done.6.refs_4_.refs_5_
  69.6 0.0 collective-permute-done.5.refs_3_.refs_4_
  69.6 4.1 %shard_map.114 = bf16[2,272,640]{2,1,0:T(8,128)(2,1)S(1)} custom-call(s32[8,128]{1,0:T(8,128)S(1)} %get-tuple-element.32.found, s32[8]{0:T(128)S(1)} %get-tuple-element.33.counts, bf16[2,272,640]{2,1,0:T(8,128)(2,1)} %collective-permute-done.2.refs_0_, bf16[2,2,256,640]{3,2,1,0:T(8,128)(2,1)S(1)} %get-tuple-element.34.refs_1_.refs_2_, ...), custom_call_target="tpu_custom_call" | custom-call | flops 800000000 | bytes 8000000 | tf_op jit(solution)/shard_map/pallas_call | solution.py:469
  73.7 6.5 %shard_map.115 = (bf16[2,272,640]{2,1,0:T(8,128)(2,1)S(1)}, bf16[2,272,640]{2,1,0:T(8,128)(2,1)S(1)}) custom-call(s32[8,128]{1,0:T(8,128)S(1)} %get-tuple-element.32.found, s32[8]{0:T(128)S(1)} %get-tuple-element.33.counts, bf16[2,272,640]{2,1,0:T(8,128)(2,1)} %collective-permute-done.1.refs_1_.refs_0_, ...), custom_call_target="tpu_custom_call" | custom-call | flops 1600000000 | bytes 8000000 | tf_op jit(solution)/shard_map/pallas_call | solution.py:469
  80.1 4.6 %collective-permute-start.7 = (bf16[2,272,640]{2,1,0:T(8,128)(2,1)S(1)}, bf16[2,272,640]{2,1,0:T(8,128)(2,1)S(1)}, u32[]{:S(2)}, u32[]{:S(2)}) collective-permute-start(bf16[2,272,640]{2,1,0:T(8,128)(2,1)S(1)} %get-tuple-element.37), channel_id=1, source_target_pairs={{0,6},{1,25},{2,0},{3,27},{4,2},{5,29},{6,4},{7,31},{8,14},{9,1},{... | collective-permute-start | bytes 2088968 | tf_op jit(solution)/shard_map/ppermute | solution.py:52
  84.7 0.0 collective-permute-start.8
  84.7 1.3 %collective-permute-start.9 = (bf16[2,272,640]{2,1,0:T(8,128)(2,1)S(1)}, bf16[2,272,640]{2,1,0:T(8,128)(2,1)S(1)}, u32[]{:S(2)}, u32[]{:S(2)}) collective-permute-start(bf16[2,272,640]{2,1,0:T(8,128)(2,1)S(1)} %shard_map.114), channel_id=1, source_target_pairs={{0,4},{1,17},{2,6},{3,19},{4,0},{5,21},{6,2},{7,23},{8,12},{9,25},... | collective-permute-start | bytes 2088968 | tf_op jit(solution)/shard_map/ppermute | solution.py:52
  86.0 5.5 %shard_map.113.refs_0_ = bf16[2,272,640]{2,1,0:T(8,128)(2,1)S(1)} custom-call(s32[8,128]{1,0:T(8,128)S(1)} %get-tuple-element.32.found, s32[8]{0:T(128)S(1)} %get-tuple-element.33.counts, bf16[2,272,640]{2,1,0:T(8,128)(2,1)S(1)} %get-tuple-element.26.refs_3_.refs_0_, bf16[2,2,256,640]{3,2,1,0:T(8,128)(2,1)S(1)} %get-tuple-element.34.refs_1_.refs_2_, ...), custom_call_target="tpu_custom_call" | custom-call | flops 800000000 | bytes 8000000 | tf_op jit(solution)/shard_map/pallas_call | solution.py:469
  91.5 8.7 %collective-permute-done.7.refs_1_ = bf16[2,272,640]{2,1,0:T(8,128)(2,1)S(1)} collective-permute-done((bf16[2,272,640]{2,1,0:T(8,128)(2,1)S(1)}, bf16[2,272,640]{2,1,0:T(8,128)(2,1)S(1)}, u32[]{:S(2)}, u32[]{:S(2)}) %collective-permute-start.7) | collective-permute-done | bytes 696352 | tf_op jit(solution)/shard_map/ppermute | solution.py:52
  100.2 3.4 %collective-permute-done.8.refs_2_ = bf16[2,272,640]{2,1,0:T(8,128)(2,1)S(1)} collective-permute-done((bf16[2,272,640]{2,1,0:T(8,128)(2,1)S(1)}, bf16[2,272,640]{2,1,0:T(8,128)(2,1)S(1)}, u32[]{:S(2)}, u32[]{:S(2)}) %collective-permute-start.8) | collective-permute-done | bytes 696352 | tf_op jit(solution)/shard_map/ppermute | solution.py:52
  103.6 0.0 collective-permute-done.9.refs_3_
  103.6 2.0 %join.1 = (bf16[256,640]{1,0:T(8,128)(2,1)S(1)}, bf16[256,640]{1,0:T(8,128)(2,1)S(1)}) custom-call(bf16[2,272,640]{2,1,0:T(8,128)(2,1)S(1)} %shard_map.113.refs_0_, bf16[2,272,640]{2,1,0:T(8,128)(2,1)S(1)} %collective-permute-done.7.refs_1_, bf16[2,272,640]{2,1,0:T(8,128)(2,1)S(1)} %collective-permute-done.8.refs_2_, ...), custom_call_target="tpu_custom_call" | custom-call | bytes 4000000 | tf_op jit(solution)/shard_map/join/pallas_call | solution.py:595
  105.6 1.7 %collective-permute-start.10 = (bf16[256,640]{1,0:T(8,128)(2,1)S(1)}, bf16[256,640]{1,0:T(8,128)(2,1)S(1)}, u32[]{:S(2)}, u32[]{:S(2)}) collective-permute-start(bf16[256,640]{1,0:T(8,128)(2,1)S(1)} %get-tuple-element.41), channel_id=1, source_target_pairs={{0,1},{1,0},{2,3},{3,2},{4,5},{5,4},{6,7},{7,6},{8,9},{9,8},{10,11... | collective-permute-start | bytes 983048 | tf_op jit(solution)/shard_map/ppermute | solution.py:56
  107.3 0.0 all-to-all-done.1
  107.3 6.2 %finish.1 = bf16[256,2560]{1,0:T(8,128)(2,1)} custom-call(bf16[256,2560]{1,0:T(8,128)(2,1)} %get-tuple-element.29.num_ref, f32[256,128]{1,0:T(8,128)} %get-tuple-element.30.den_ref, bf16[320,256]{1,0:T(8,128)(2,1)} %bitcast.32, bf16[4,320,64]{2,1,0:T(8,128)(2,1)} %constant.13.clone.select_ref, f32[3,160,128]{2,1,0:T(8,128)} %constant.14.clone.vector_ref, ...), custom_call_target="tpu_custom_call" | custom-call | flops 400000000 | bytes 8000000 | tf_op jit(solution)/shard_map/finish/pallas_call | solution.py:617
  113.5 0.0 collective-permute-done.10.other_ref
  113.5 0.8 place.1
Async XLA Ops:
  1.3 0.7 copy-start
  1.9 5.0 %copy-start.1 = (s32[1,1,8]{2,1,0:T(1,128)S(1)}, s32[1,1,8]{2,1,0:T(1,128)}, u32[]{:S(2)}) copy-start(s32[1,1,8]{2,1,0:T(1,128)} %param.16) | copy-start | bytes 100
  3.7 5.5 %collective-permute-start = (bf16[784,640]{1,0:T(8,128)(2,1)S(1)}, bf16[784,640]{1,0:T(8,128)(2,1)S(1)}, u32[]{:S(2)}, u32[]{:S(2)}) collective-permute-start(bf16[784,640]{1,0:T(8,128)(2,1)S(1)} %pack.1), channel_id=1, source_target_pairs={{0,1},{1,0},{2,3},{3,2},{4,5},{5,4},{6,7},{7,6},{8,9},{9,8},{10,11... | collective-permute-start | bytes 3010568 | tf_op jit(solution)/shard_map/ppermute | solution.py:56
  9.6 16.8 %collective-permute-start.4 = (bf16[2,2,256,640]{3,2,1,0:T(8,128)(2,1)S(1)}, bf16[2,2,256,640]{3,2,1,0:T(8,128)(2,1)S(1)}, u32[]{:S(2)}, u32[]{:S(2)}) collective-permute-start(bf16[2,2,256,640]{3,2,1,0:T(8,128)(2,1)S(1)} %get-tuple-element.34.refs_1_.refs_2_), channel_id=1, source_target_pairs={{0,24},{1,7},{2,26},{3,1},{4,28},{5,3},{6,30},{7,5},{8,0},{9,15},{... | collective-permute-start | bytes 3932168 | tf_op jit(solution)/shard_map/ppermute | solution.py:52
  16.1 44.0 %all-to-all-start = ((bf16[8,400,128]{2,1,0:T(8,128)(2,1)}), bf16[8,400,128]{2,1,0:T(8,128)(2,1)}, u32[]{:S(2)}, u32[]{:S(2)}) async-start(bf16[8,400,128]{2,1,0:T(8,128)(2,1)} %bitcast.29), calls=%async_computation | async-start | bytes 1638400 | tf_op jit(solution)/shard_map/all_to_all | solution.py:549
  24.3 16.2 %collective-permute-start.1 = (bf16[2,272,640]{2,1,0:T(8,128)(2,1)S(1)}, bf16[2,272,640]{2,1,0:T(8,128)(2,1)}, u32[]{:S(2)}, u32[]{:S(2)}) collective-permute-start(bf16[2,272,640]{2,1,0:T(8,128)(2,1)S(1)} %get-tuple-element.26.refs_3_.refs_0_), channel_id=1, source_target_pairs={{0,2},{1,9},{2,4},{3,11},{4,6},{5,13},{6,0},{7,15},{8,10},{9,17},{... | collective-permute-start | bytes 2088968 | tf_op jit(solution)/shard_map/ppermute | solution.py:52
  25.5 44.0 %collective-permute-start.6 = (bf16[2,2,256,640]{3,2,1,0:T(8,128)(2,1)S(1)}, bf16[2,2,256,640]{3,2,1,0:T(8,128)(2,1)}, u32[]{:S(2)}, u32[]{:S(2)}) collective-permute-start(bf16[2,2,256,640]{3,2,1,0:T(8,128)(2,1)S(1)} %get-tuple-element.34.refs_1_.refs_2_), channel_id=1, source_target_pairs={{0,8},{1,3},{2,10},{3,5},{4,12},{5,7},{6,14},{7,1},{8,16},{9,11},{... | collective-permute-start | bytes 3932168 | tf_op jit(solution)/shard_map/ppermute | solution.py:52
  26.4 43.2 %collective-permute-start.5 = (bf16[2,2,256,640]{3,2,1,0:T(8,128)(2,1)S(1)}, bf16[2,2,256,640]{3,2,1,0:T(8,128)(2,1)}, u32[]{:S(2)}, u32[]{:S(2)}) collective-permute-start(bf16[2,2,256,640]{3,2,1,0:T(8,128)(2,1)S(1)} %collective-permute-done.4.refs_2_.refs_3_), channel_id=1, source_target_pairs={{0,24},{1,7},{2,26},{3,1},{4,28},{5,3},{6,30},{7,5},{8,0},{9,15},{... | collective-permute-start | bytes 3932168 | tf_op jit(solution)/shard_map/ppermute | solution.py:52
  28.3 20.5 %collective-permute-start.3 = (bf16[2,272,640]{2,1,0:T(8,128)(2,1)S(1)}, bf16[2,272,640]{2,1,0:T(8,128)(2,1)}, u32[]{:S(2)}, u32[]{:S(2)}) collective-permute-start(bf16[2,272,640]{2,1,0:T(8,128)(2,1)S(1)} %get-tuple-element.26.refs_3_.refs_0_), channel_id=1, source_target_pairs={{0,6},{1,25},{2,0},{3,27},{4,2},{5,29},{6,4},{7,31},{8,14},{9,1},{... | collective-permute-start | bytes 2088968 | tf_op jit(solution)/shard_map/ppermute | solution.py:52
  40.5 16.8 %collective-permute-start.2 = (bf16[2,272,640]{2,1,0:T(8,128)(2,1)}, bf16[2,272,640]{2,1,0:T(8,128)(2,1)}, u32[]{:S(2)}, u32[]{:S(2)}) collective-permute-start(bf16[2,272,640]{2,1,0:T(8,128)(2,1)} %collective-permute-done.1.refs_1_.refs_0_), channel_id=1, source_target_pairs={{0,2},{1,9},{2,4},{3,11},{4,6},{5,13},{6,0},{7,15},{8,10},{9,17},{... | collective-permute-start | bytes 2088968 | tf_op jit(solution)/shard_map/ppermute | solution.py:52
  62.9 44.4 %all-to-all-start.1 = ((bf16[8,400,128]{2,1,0:T(8,128)(2,1)}), bf16[8,400,128]{2,1,0:T(8,128)(2,1)}, u32[]{:S(2)}, u32[]{:S(2)}) async-start(bf16[8,400,128]{2,1,0:T(8,128)(2,1)} %prefix.1), calls=%async_computation.1 | async-start | bytes 1638400 | tf_op jit(solution)/shard_map/all_to_all | solution.py:587
  80.1 20.0 %collective-permute-start.7 = (bf16[2,272,640]{2,1,0:T(8,128)(2,1)S(1)}, bf16[2,272,640]{2,1,0:T(8,128)(2,1)S(1)}, u32[]{:S(2)}, u32[]{:S(2)}) collective-permute-start(bf16[2,272,640]{2,1,0:T(8,128)(2,1)S(1)} %get-tuple-element.37), channel_id=1, source_target_pairs={{0,6},{1,25},{2,0},{3,27},{4,2},{5,29},{6,4},{7,31},{8,14},{9,1},{... | collective-permute-start | bytes 2088968 | tf_op jit(solution)/shard_map/ppermute | solution.py:52
  84.7 18.8 %collective-permute-start.8 = (bf16[2,272,640]{2,1,0:T(8,128)(2,1)S(1)}, bf16[2,272,640]{2,1,0:T(8,128)(2,1)S(1)}, u32[]{:S(2)}, u32[]{:S(2)}) collective-permute-start(bf16[2,272,640]{2,1,0:T(8,128)(2,1)S(1)} %get-tuple-element.38), channel_id=1, source_target_pairs={{0,2},{1,9},{2,4},{3,11},{4,6},{5,13},{6,0},{7,15},{8,10},{9,17},{... | collective-permute-start | bytes 2088968 | tf_op jit(solution)/shard_map/ppermute | solution.py:52
  84.7 18.8 %collective-permute-start.9 = (bf16[2,272,640]{2,1,0:T(8,128)(2,1)S(1)}, bf16[2,272,640]{2,1,0:T(8,128)(2,1)S(1)}, u32[]{:S(2)}, u32[]{:S(2)}) collective-permute-start(bf16[2,272,640]{2,1,0:T(8,128)(2,1)S(1)} %shard_map.114), channel_id=1, source_target_pairs={{0,4},{1,17},{2,6},{3,19},{4,0},{5,21},{6,2},{7,23},{8,12},{9,25},... | collective-permute-start | bytes 2088968 | tf_op jit(solution)/shard_map/ppermute | solution.py:52
  105.6 7.9 %collective-permute-start.10 = (bf16[256,640]{1,0:T(8,128)(2,1)S(1)}, bf16[256,640]{1,0:T(8,128)(2,1)S(1)}, u32[]{:S(2)}, u32[]{:S(2)}) collective-permute-start(bf16[256,640]{1,0:T(8,128)(2,1)S(1)} %get-tuple-element.41), channel_id=1, source_target_pairs={{0,1},{1,0},{2,3},{3,2},{4,5},{5,4},{6,7},{7,6},{8,9},{9,8},{10,11... | collective-permute-start | bytes 983048 | tf_op jit(solution)/shard_map/ppermute | solution.py:56

commit v7 on v6

--- a/solution.py
+++ b/solution.py
@@ -115,9 +115,7 @@
 
 def prefix_kernel(place_ref, in_ref, out_ref):
     rows = in_ref.shape[1]
-    row = lax.broadcasted_iota(jnp.int32, (rows, 128), 0) + (place_ref[0] & 1) * (FROWS // 2)
-    row = jnp.where(row >= FROWS, row - FROWS, row)
-    row = jnp.where(row >= FROWS, row - FROWS, row)
+    row = lax.broadcasted_iota(jnp.int32, (rows, 128), 0) + ((place_ref[0] + pl.program_id(0)) & 1) * rows
     high = (row == FEATS) | (row == FEATS + 1)
     low = (row == FEATS + 2) | (row == FEATS + 3)
     total = jnp.zeros((rows, 128), F32)
@@ -129,7 +127,7 @@
         total = total + in_ref[z].astype(F32)
 
 
-def local_kernel(q_ref, k_ref, v_ref, select_ref, vector_ref, num_ref, den_ref):
+def local_kernel(q_ref, k_ref, v_ref, select_ref, vector_ref, num_ref, den_ref, phi_ref):
     causal = lax.broadcasted_iota(jnp.int32, (TOK, TOK), 0) >= lax.broadcasted_iota(jnp.int32, (TOK, TOK), 1)
     lane = lax.broadcasted_iota(jnp.int32, (TOK, 128), 1)
     group = pl.program_id(0)
@@ -141,6 +139,8 @@
     den = den_ref[...]
     phis_q = [features(select_ref[j], q_ref[...], vector_ref) for j in range(GROUP)]
     phis_k = [features(select_ref[j], k_ref[...], vector_ref) for j in range(GROUP)]
+    for j in range(GROUP):
+        phi_ref[j] = phis_q[j]
     turned = [taller(p).T for p in phis_q]
     weights = [jnp.dot(turned[j], taller(phis_k[j]), preferred_element_type=F32) for j in range(GROUP)]
     weights = [jnp.where(causal, w, 0.0).astype(BF) for w in weights]
@@ -151,12 +151,11 @@
     den_ref[...] = den
 
 
-def finish_kernel(num_ref, den_ref, q_ref, select_ref, vector_ref, state_ref, out_ref):
+def finish_kernel(num_ref, den_ref, phi_ref, state_ref, out_ref):
     lane = lax.broadcasted_iota(jnp.int32, (TOK, 128), 1)
     group = pl.program_id(0)
     at = FEATS - (FROWS - 16)
-    phis = [features(select_ref[j], q_ref[...], vector_ref) for j in range(GROUP)]
-    phis = [taller(p).T for p in phis]
+    phis = [taller(phi_ref[j]).T for j in range(GROUP)]
     carried = [jnp.dot(phis[j], taller(state_ref[j]), preferred_element_type=F32) for j in range(GROUP)]
     dens = []
     for j in range(GROUP):
@@ -548,18 +547,31 @@
     )(*in_hbm(k_lin[0].T, v_lin[0], select, vectors))
     slices = lax.all_to_all(state.reshape(shards, HEADS * FROWS // shards, 128), "seq", 0, 0, tiled=True)
 
-    num, den = pl.pallas_call(
+    num, den, phi = pl.pallas_call(
         local_kernel,
         name="local",
         grid=steps,
-        out_shape=[hbm_shape(TOK, D), hbm_shape(TOK, 128, dtype=F32)],
+        out_shape=[hbm_shape(TOK, D), hbm_shape(TOK, 128, dtype=F32), hbm_shape(HEADS, FROWS, TOK)],
         in_specs=[heads16, heads16, heads128, whole(*select.shape), whole(*vectors.shape)],
-        out_specs=[heads128, whole(TOK, 128)],
+        out_specs=[heads128, whole(TOK, 128), pl.BlockSpec((GROUP, FROWS, TOK), lambda g: (g, 0, 0))],
         compiler_params=room(10),
         cost_estimate=cost(4e9, 8e6),
     )(*in_hbm(q_lin[0].T, k_lin[0].T, v_lin[0], select, vectors))
 
     blocks = (kv, kv_right, kv_far, kv_left)
+    slices, num, den, phi = lax.optimization_barrier((slices, num, den, phi))
+    part = pl.BlockSpec((shards, FROWS // 2, 128), lambda g: (0, g, 0))
+    prefix = pl.pallas_call(
+        prefix_kernel,
+        name="prefix",
+        grid=(slices.shape[1] // (FROWS // 2),),
+        out_shape=hbm_shape(*slices.shape),
+        in_specs=[SMEM, part],
+        out_specs=part,
+        compiler_params=room(6),
+        cost_estimate=cost(0, 2e6),
+    )(place, slices)
+    before = lax.all_to_all(prefix, "seq", 0, 0, tiled=True).reshape(HEADS, FROWS, 128)
     lists = pl.pallas_call(
         search_kernel,
         name="search",
@@ -574,22 +586,14 @@
         compiler_params=room(2),
         cost_estimate=cost(0, 1e5),
     )(me, q_far, q_left, q_right, q)
-    slices, num, den, *lists = lax.optimization_barrier((slices, num, den, *lists))
-    prefix = pl.pallas_call(
-        prefix_kernel,
-        name="prefix",
-        out_shape=hbm_shape(*slices.shape),
-        in_specs=[SMEM, VMEM],
-        out_specs=VMEM,
-        compiler_params=room(6),
-        cost_estimate=cost(0, 2e6),
-    )(place, slices)
-    before = lax.all_to_all(prefix, "seq", 0, 0, tiled=True).reshape(HEADS, FROWS, 128)
     (to_far,) = attend("attend_far", 0, lists, (q_far,), blocks)
-    to_far, q_left, q_right = lax.optimization_barrier((to_far, q_left, q_right))
+    to_far, q_left = lax.optimization_barrier((to_far, q_left))
     from_far = move(to_far, "q", 2)
-    to_left, to_right = attend("attend_sides", 2, lists, (q_left, q_right), blocks)
+    (to_left,) = attend("attend_left", 2, lists, (q_left,), blocks)
+    to_left, q_right = lax.optimization_barrier((to_left, q_right))
     from_right = move(to_left, "q", -1)
+    (to_right,) = attend("attend_right", 4, lists, (q_right,), blocks)
+    to_right, q = lax.optimization_barrier((to_right, q))
     from_left = move(to_right, "q", 1)
     (here,) = attend("attend_own", 6, lists, (q,), blocks)
     kept, send = pl.pallas_call(
@@ -622,15 +626,13 @@
         in_specs=[
             heads128,
             whole(TOK, 128),
-            heads16,
-            whole(*select.shape),
-            whole(*vectors.shape),
+            pl.BlockSpec((GROUP, FROWS, TOK), lambda g: (g, 0, 0)),
             pl.BlockSpec((GROUP, FROWS, 128), lambda g: (g, 0, 0)),
         ],
         out_specs=heads128,
         compiler_params=room(8),
         cost_estimate=cost(4e8, 8e6),
-    )(*in_hbm(num, den, q_lin[0].T, select, vectors), before)
+    )(*in_hbm(num, den, phi), before)
     return lin_out[None], soft_out[None]
 
 

time: 115 us -> 111 us (0.965)
  waiting for transfers between devices: 31.4 us -> 21.5 us
  starting transfers between devices: 34.2 us -> 37.1 us
  Pallas kernels: 46.8 us -> 49.1 us
    ppermute x9, waiting for transfers between devices: 30.9 us -> 21 us  [move(): return lax.ppermute(a, 'files', along(what, step))]
    ppermute x2, starting transfers between devices: 4.95 us -> 7.82 us  [swap_cores(): lax.ppermute(a, 'files', [(i, i ^ 1) for i in range(SIDE * SIDE * CORES)])]
    pallas_call x3 -> x4, Pallas kernels: 16 us -> 17.6 us  [attend(): pl.pallas_call(functools.partial(attend_kernel, own, base, readers), out_...]
    pallas_call x1, Pallas kernels: 2.82 us -> 4.04 us  [layers(): pl.pallas_call(prefix_kernel, name='prefix', grid=(slices.shape[1] // (FR...]
  transfers between devices with their start and end apart: 13 -> 13, of which waited for: 6 -> 6; matrix products, arithmetic and copies ran while one was open for 0% -> 0% of each run, Pallas kernels for 38% -> 42%
where the time goes in v7:
time: 111 us; the launch traced here: 110 us
  Pallas kernels  49.1 us (44%)
  starting transfers between devices  37.1 us (33%)
  waiting for transfers between devices  21.5 us (19%)
  between operations  1.57 us (1%)
    ppermute x9, waiting for transfers between devices, move(): return lax.ppermute(a, 'files', along(what, step))  21 us
    pallas_call x4, Pallas kernels, attend(): pl.pallas_call(functools.partial(attend_kernel, own, base, readers), out_...  17.6 us
    ppermute x9, starting transfers between devices, move(): return lax.ppermute(a, 'files', along(what, step))  14.7 us
    all_to_all x1, starting transfers between devices, layers(): lax.all_to_all(state.reshape(shards, HEADS * FROWS // shards, 128), 'seq'...  8.17 us
    ppermute x2, starting transfers between devices, swap_cores(): lax.ppermute(a, 'files', [(i, i ^ 1) for i in range(SIDE * SIDE * CORES)])  7.82 us
    pallas_call x1, Pallas kernels, layers(): pl.pallas_call(local_kernel, name='local', grid=steps, out_shape=[hbm_sha...  6.81 us
    all_to_all x1, starting transfers between devices, layers(): lax.all_to_all(prefix, 'seq', 0, 0, tiled=True).reshape(HEADS, FROWS, 128)  6.32 us
    pallas_call x1, Pallas kernels, layers(): pl.pallas_call(finish_kernel, name='finish', grid=steps, out_shape=shape(...  5.62 us
  transfers between devices with their start and end apart: 13, of which 6 were waited for; matrix products, arithmetic and copies ran while one was open for 0% of the time, Pallas kernels for 42%

profile of v7, /device:TPU:1, one launch (start us, length us, event | category | flops | bytes accessed | tf_op | source)
XLA Modules:
  0.0 109.8 jit_solution(8969187457741899039)
XLA Ops:
  1.3 0.0 copy-start
  1.3 0.6 copy-done
  1.9 0.0 copy-start.1
  1.9 1.7 %pack.1 = bf16[784,640]{1,0:T(8,128)(2,1)S(1)} custom-call(s32[1]{0:T(128)} %bitcast.10.me_ref, s32[8]{0:T(128)S(1)} %bitcast.20, s32[1]{0:T(128)} %bitcast.18.count_ref, bf16[256,1280]{1,0:T(8,128)(2,1)} %bitcast.22, bf16[256,1280]{1,0:T(8,128)(2,1)} %bitcast.24, bf16[256,1280]{1,0:T(8,128)(2,1)} %bitcast.26), custom_call_target="tpu_custom_call" | custom-call | bytes 2000000 | tf_op jit(solution)/shard_map/pack/pallas_call | solution.py:497
  3.7 3.3 %collective-permute-start = (bf16[784,640]{1,0:T(8,128)(2,1)S(1)}, bf16[784,640]{1,0:T(8,128)(2,1)S(1)}, u32[]{:S(2)}, u32[]{:S(2)}) collective-permute-start(bf16[784,640]{1,0:T(8,128)(2,1)S(1)} %pack.1), channel_id=1, source_target_pairs={{0,1},{1,0},{2,3},{3,2},{4,5},{5,4},{6,7},{7,6},{8,9},{9,8},{10,11... | collective-permute-start | bytes 3010568 | tf_op jit(solution)/shard_map/ppermute | solution.py:56
  7.0 0.0 copy-done.1
  7.0 1.7 %own.1 = (bf16[2,2,256,640]{3,2,1,0:T(8,128)(2,1)S(1)}, bf16[2,272,640]{2,1,0:T(8,128)(2,1)S(1)}) custom-call(s32[1]{0:T(128)} %bitcast.10.me_ref, s32[8]{0:T(128)S(1)} %bitcast.21, s32[1]{0:T(128)} %bitcast.19.count_ref, bf16[256,1280]{1,0:T(8,128)(2,1)} %bitcast.23, bf16[256,1280]{1,0:T(8,128)(2,1)} %bitcast.25, bf16[256,1280]{1,0:T(8,128)(2,1)} %bitcast.27), custom_call_target="tpu_custom_call" | custom-call | bytes 2000000 | tf_op jit(solution)/shard_map/own/pallas_call | solution.py:509
  8.7 0.5 collective-permute-done.mate_ref
  9.2 0.4 merge.1
  9.6 1.1 %collective-permute-start.4 = (bf16[2,2,256,640]{3,2,1,0:T(8,128)(2,1)S(1)}, bf16[2,2,256,640]{3,2,1,0:T(8,128)(2,1)S(1)}, u32[]{:S(2)}, u32[]{:S(2)}) collective-permute-start(bf16[2,2,256,640]{3,2,1,0:T(8,128)(2,1)S(1)} %get-tuple-element.35.refs_1_), channel_id=1, source_target_pairs={{0,24},{1,7},{2,26},{3,1},{4,28},{5,3},{6,30},{7,5},{8,0},{9,15},{... | collective-permute-start | bytes 3932168 | tf_op jit(solution)/shard_map/ppermute | solution.py:52
  10.7 5.5 %state.1 = bf16[20,160,128]{2,1,0:T(8,128)(2,1)} custom-call(bf16[320,256]{1,0:T(8,128)(2,1)} %bitcast.34, bf16[256,2560]{1,0:T(8,128)(2,1)} %bitcast.31, bf16[4,320,64]{2,1,0:T(8,128)(2,1)} %constant.13.clone.select_ref, f32[3,160,128]{2,1,0:T(8,128)} %constant.14.clone.vector_ref), custom_call_target="tpu_custom_call" | custom-call | flops 1000000000 | bytes 4000000 | tf_op jit(solution)/shard_map/state/pallas_call | solution.py:538
  16.1 8.2 %all-to-all-start = ((bf16[8,400,128]{2,1,0:T(8,128)(2,1)}), bf16[8,400,128]{2,1,0:T(8,128)(2,1)}, u32[]{:S(2)}, u32[]{:S(2)}) async-start(bf16[8,400,128]{2,1,0:T(8,128)(2,1)} %bitcast.29), calls=%async_computation | async-start | bytes 1638400 | tf_op jit(solution)/shard_map/all_to_all | solution.py:548
  24.3 1.2 %collective-permute-start.1 = (bf16[2,272,640]{2,1,0:T(8,128)(2,1)S(1)}, bf16[2,272,640]{2,1,0:T(8,128)(2,1)}, u32[]{:S(2)}, u32[]{:S(2)}) collective-permute-start(bf16[2,272,640]{2,1,0:T(8,128)(2,1)S(1)} %get-tuple-element.38.refs_3_.refs_0_), channel_id=1, source_target_pairs={{0,2},{1,9},{2,4},{3,11},{4,6},{5,13},{6,0},{7,15},{8,10},{9,17},{... | collective-permute-start | bytes 2088968 | tf_op jit(solution)/shard_map/ppermute | solution.py:52
  25.5 0.0 collective-permute-start.6
  25.5 0.9 collective-permute-done.4.refs_2_
  26.4 1.9 %collective-permute-start.5 = (bf16[2,2,256,640]{3,2,1,0:T(8,128)(2,1)S(1)}, bf16[2,2,256,640]{3,2,1,0:T(8,128)(2,1)}, u32[]{:S(2)}, u32[]{:S(2)}) collective-permute-start(bf16[2,2,256,640]{3,2,1,0:T(8,128)(2,1)S(1)} %collective-permute-done.4.refs_2_), channel_id=1, source_target_pairs={{0,24},{1,7},{2,26},{3,1},{4,28},{5,3},{6,30},{7,5},{8,0},{9,15},{... | collective-permute-start | bytes 3932168 | tf_op jit(solution)/shard_map/ppermute | solution.py:52
  28.3 2.8 %collective-permute-start.3 = (bf16[2,272,640]{2,1,0:T(8,128)(2,1)S(1)}, bf16[2,272,640]{2,1,0:T(8,128)(2,1)}, u32[]{:S(2)}, u32[]{:S(2)}) collective-permute-start(bf16[2,272,640]{2,1,0:T(8,128)(2,1)S(1)} %get-tuple-element.38.refs_3_.refs_0_), channel_id=1, source_target_pairs={{0,6},{1,25},{2,0},{3,27},{4,2},{5,29},{6,4},{7,31},{8,14},{9,1},{... | collective-permute-start | bytes 2088968 | tf_op jit(solution)/shard_map/ppermute | solution.py:52
  31.1 9.4 %collective-permute-done.1.refs_1_.refs_0_ = bf16[2,272,640]{2,1,0:T(8,128)(2,1)} collective-permute-done((bf16[2,272,640]{2,1,0:T(8,128)(2,1)S(1)}, bf16[2,272,640]{2,1,0:T(8,128)(2,1)}, u32[]{:S(2)}, u32[]{:S(2)}) %collective-permute-start.1) | collective-permute-done | bytes 696352 | tf_op jit(solution)/shard_map/ppermute | solution.py:52
  40.5 1.5 %collective-permute-start.2 = (bf16[2,272,640]{2,1,0:T(8,128)(2,1)}, bf16[2,272,640]{2,1,0:T(8,128)(2,1)}, u32[]{:S(2)}, u32[]{:S(2)}) collective-permute-start(bf16[2,272,640]{2,1,0:T(8,128)(2,1)} %collective-permute-done.1.refs_1_.refs_0_), channel_id=1, source_target_pairs={{0,2},{1,9},{2,4},{3,11},{4,6},{5,13},{6,0},{7,15},{8,10},{9,17},{... | collective-permute-start | bytes 2088968 | tf_op jit(solution)/shard_map/ppermute | solution.py:52
  42.0 6.8 %local.1 = (bf16[256,2560]{1,0:T(8,128)(2,1)}, f32[256,128]{1,0:T(8,128)}, bf16[20,160,256]{2,1,0:T(8,128)(2,1)}) custom-call(bf16[320,256]{1,0:T(8,128)(2,1)} %bitcast.33, bf16[320,256]{1,0:T(8,128)(2,1)} %bitcast.35, bf16[256,2560]{1,0:T(8,128)(2,1)} %bitcast.32, bf16[4,320,64]{2,1,0:T(8,128)(2,1)} %constant.13.clone.select_ref, ...), custom_call_target="tpu_custom_call" | custom-call | flops 4000000000 | bytes 8000000 | tf_op jit(solution)/shard_map/local/pallas_call | solution.py:550
  48.8 0.0 all-to-all-done.in_ref
  48.8 4.0 %prefix.1 = bf16[8,400,128]{2,1,0:T(8,128)(2,1)} custom-call(s32[1]{0:T(128)} %bitcast.7.place_ref, bf16[8,400,128]{2,1,0:T(8,128)(2,1)} %all-to-all-done.in_ref), custom_call_target="tpu_custom_call" | custom-call | bytes 2000000 | tf_op jit(solution)/shard_map/prefix/pallas_call | solution.py:564
  52.9 6.3 %all-to-all-start.1 = ((bf16[8,400,128]{2,1,0:T(8,128)(2,1)}), bf16[8,400,128]{2,1,0:T(8,128)(2,1)}, u32[]{:S(2)}, u32[]{:S(2)}) async-start(bf16[8,400,128]{2,1,0:T(8,128)(2,1)} %prefix.1), calls=%async_computation.1 | async-start | bytes 1638400 | tf_op jit(solution)/shard_map/all_to_all | solution.py:574
  59.2 0.0 collective-permute-done.3.refs_2_.refs_0_
  59.2 0.0 collective-permute-done.2.refs_0_
  59.2 2.8 %search.1 = (s32[8,128]{1,0:T(8,128)S(1)}, s32[8]{0:T(128)S(1)}) custom-call(s32[1]{0:T(128)} %bitcast.10.me_ref, bf16[2,272,640]{2,1,0:T(8,128)(2,1)} %collective-permute-done.2.refs_0_, bf16[2,272,640]{2,1,0:T(8,128)(2,1)} %collective-permute-done.1.refs_1_.refs_0_, bf16[2,272,640]{2,1,0:T(8,128)(2,1)} %collective-permute-done.3.refs_2_.refs_0_, ...), custom_call_target="tpu_custom_call" | custom-call | bytes 100000 | tf_op jit(solution)/shard_map/search/pallas_call | solution.py:575
  62.0 0.0 collective-permute-done.6.refs_4_
  62.0 0.0 collective-permute-done.5.refs_3_
  62.0 4.1 %shard_map.113 = bf16[2,272,640]{2,1,0:T(8,128)(2,1)S(1)} custom-call(s32[8,128]{1,0:T(8,128)S(1)} %get-tuple-element.33.found, s32[8]{0:T(128)S(1)} %get-tuple-element.34.counts, bf16[2,272,640]{2,1,0:T(8,128)(2,1)} %collective-permute-done.2.refs_0_, bf16[2,2,256,640]{3,2,1,0:T(8,128)(2,1)S(1)} %get-tuple-element.35.refs_1_, ...), custom_call_target="tpu_custom_call" | custom-call | flops 800000000 | bytes 8000000 | tf_op jit(solution)/shard_map/pallas_call | solution.py:468
  66.1 4.1 %shard_map.114 = bf16[2,272,640]{2,1,0:T(8,128)(2,1)S(1)} custom-call(s32[8,128]{1,0:T(8,128)S(1)} %get-tuple-element.33.found, s32[8]{0:T(128)S(1)} %get-tuple-element.34.counts, bf16[2,272,640]{2,1,0:T(8,128)(2,1)} %collective-permute-done.1.refs_1_.refs_0_, bf16[2,2,256,640]{3,2,1,0:T(8,128)(2,1)S(1)} %get-tuple-element.35.refs_1_, ...), custom_call_target="tpu_custom_call" | custom-call | flops 800000000 | bytes 8000000 | tf_op jit(solution)/shard_map/pallas_call | solution.py:468
  70.2 4.0 %shard_map.115 = bf16[2,272,640]{2,1,0:T(8,128)(2,1)S(1)} custom-call(s32[8,128]{1,0:T(8,128)S(1)} %get-tuple-element.33.found, s32[8]{0:T(128)S(1)} %get-tuple-element.34.counts, bf16[2,272,640]{2,1,0:T(8,128)(2,1)} %collective-permute-done.3.refs_2_.refs_0_, bf16[2,2,256,640]{3,2,1,0:T(8,128)(2,1)S(1)} %get-tuple-element.35.refs_1_, ...), custom_call_target="tpu_custom_call" | custom-call | flops 800000000 | bytes 8000000 | tf_op jit(solution)/shard_map/pallas_call | solution.py:468
  74.2 2.8 %collective-permute-start.8 = (bf16[2,272,640]{2,1,0:T(8,128)(2,1)S(1)}, bf16[2,272,640]{2,1,0:T(8,128)(2,1)S(1)}, u32[]{:S(2)}, u32[]{:S(2)}) collective-permute-start(bf16[2,272,640]{2,1,0:T(8,128)(2,1)S(1)} %shard_map.115), channel_id=1, source_target_pairs={{0,2},{1,9},{2,4},{3,11},{4,6},{5,13},{6,0},{7,15},{8,10},{9,17},{... | collective-permute-start | bytes 2088968 | tf_op jit(solution)/shard_map/ppermute | solution.py:52
  77.0 2.3 %collective-permute-start.7 = (bf16[2,272,640]{2,1,0:T(8,128)(2,1)S(1)}, bf16[2,272,640]{2,1,0:T(8,128)(2,1)S(1)}, u32[]{:S(2)}, u32[]{:S(2)}) collective-permute-start(bf16[2,272,640]{2,1,0:T(8,128)(2,1)S(1)} %shard_map.114), channel_id=1, source_target_pairs={{0,6},{1,25},{2,0},{3,27},{4,2},{5,29},{6,4},{7,31},{8,14},{9,1},{... | collective-permute-start | bytes 2088968 | tf_op jit(solution)/shard_map/ppermute | solution.py:52
  79.3 1.1 collective-permute-start.9
  80.4 5.5 %shard_map.116.refs_0_ = bf16[2,272,640]{2,1,0:T(8,128)(2,1)S(1)} custom-call(s32[8,128]{1,0:T(8,128)S(1)} %get-tuple-element.33.found, s32[8]{0:T(128)S(1)} %get-tuple-element.34.counts, bf16[2,272,640]{2,1,0:T(8,128)(2,1)S(1)} %get-tuple-element.38.refs_3_.refs_0_, bf16[2,2,256,640]{3,2,1,0:T(8,128)(2,1)S(1)} %get-tuple-element.35.refs_1_, ...), custom_call_target="tpu_custom_call" | custom-call | flops 800000000 | bytes 8000000 | tf_op jit(solution)/shard_map/pallas_call | solution.py:468
  85.9 2.0 %collective-permute-done.8.refs_2_ = bf16[2,272,640]{2,1,0:T(8,128)(2,1)S(1)} collective-permute-done((bf16[2,272,640]{2,1,0:T(8,128)(2,1)S(1)}, bf16[2,272,640]{2,1,0:T(8,128)(2,1)S(1)}, u32[]{:S(2)}, u32[]{:S(2)}) %collective-permute-start.8) | collective-permute-done | bytes 696352 | tf_op jit(solution)/shard_map/ppermute | solution.py:52
  88.0 6.8 %collective-permute-done.7.refs_1_ = bf16[2,272,640]{2,1,0:T(8,128)(2,1)S(1)} collective-permute-done((bf16[2,272,640]{2,1,0:T(8,128)(2,1)S(1)}, bf16[2,272,640]{2,1,0:T(8,128)(2,1)S(1)}, u32[]{:S(2)}, u32[]{:S(2)}) %collective-permute-start.7) | collective-permute-done | bytes 696352 | tf_op jit(solution)/shard_map/ppermute | solution.py:52
  94.8 1.8 %collective-permute-done.9.refs_3_ = bf16[2,272,640]{2,1,0:T(8,128)(2,1)S(1)} collective-permute-done((bf16[2,272,640]{2,1,0:T(8,128)(2,1)S(1)}, bf16[2,272,640]{2,1,0:T(8,128)(2,1)S(1)}, u32[]{:S(2)}, u32[]{:S(2)}) %collective-permute-start.9) | collective-permute-done | bytes 696352 | tf_op jit(solution)/shard_map/ppermute | solution.py:52
  96.6 2.0 %join.1 = (bf16[256,640]{1,0:T(8,128)(2,1)S(1)}, bf16[256,640]{1,0:T(8,128)(2,1)S(1)}) custom-call(bf16[2,272,640]{2,1,0:T(8,128)(2,1)S(1)} %shard_map.116.refs_0_, bf16[2,272,640]{2,1,0:T(8,128)(2,1)S(1)} %collective-permute-done.7.refs_1_, bf16[2,272,640]{2,1,0:T(8,128)(2,1)S(1)} %collective-permute-done.8.refs_2_, ...), custom_call_target="tpu_custom_call" | custom-call | bytes 4000000 | tf_op jit(solution)/shard_map/join/pallas_call | solution.py:599
  98.6 4.5 %collective-permute-start.10 = (bf16[256,640]{1,0:T(8,128)(2,1)S(1)}, bf16[256,640]{1,0:T(8,128)(2,1)S(1)}, u32[]{:S(2)}, u32[]{:S(2)}) collective-permute-start(bf16[256,640]{1,0:T(8,128)(2,1)S(1)} %get-tuple-element.43), channel_id=1, source_target_pairs={{0,1},{1,0},{2,3},{3,2},{4,5},{5,4},{6,7},{7,6},{8,9},{9,8},{10,11... | collective-permute-start | bytes 983048 | tf_op jit(solution)/shard_map/ppermute | solution.py:56
  103.2 0.0 all-to-all-done.1
  103.2 5.6 %finish.1 = bf16[256,2560]{1,0:T(8,128)(2,1)} custom-call(bf16[256,2560]{1,0:T(8,128)(2,1)} %get-tuple-element.26.num_ref, f32[256,128]{1,0:T(8,128)} %get-tuple-element.27.den_ref, bf16[20,160,256]{2,1,0:T(8,128)(2,1)} %get-tuple-element.28.phi_ref, bf16[20,160,128]{2,1,0:T(8,128)(2,1)} %bitcast.8.state_ref), custom_call_target="tpu_custom_call" | custom-call | flops 400000000 | bytes 8000000 | tf_op jit(solution)/shard_map/finish/pallas_call | solution.py:621
  108.8 0.0 collective-permute-done.10.other_ref
  108.8 0.8 place.1
Async XLA Ops:
  1.3 0.7 copy-start
  1.9 5.0 %copy-start.1 = (s32[1,1,8]{2,1,0:T(1,128)S(1)}, s32[1,1,8]{2,1,0:T(1,128)}, u32[]{:S(2)}) copy-start(s32[1,1,8]{2,1,0:T(1,128)} %param.16) | copy-start | bytes 100
  3.7 5.5 %collective-permute-start = (bf16[784,640]{1,0:T(8,128)(2,1)S(1)}, bf16[784,640]{1,0:T(8,128)(2,1)S(1)}, u32[]{:S(2)}, u32[]{:S(2)}) collective-permute-start(bf16[784,640]{1,0:T(8,128)(2,1)S(1)} %pack.1), channel_id=1, source_target_pairs={{0,1},{1,0},{2,3},{3,2},{4,5},{5,4},{6,7},{7,6},{8,9},{9,8},{10,11... | collective-permute-start | bytes 3010568 | tf_op jit(solution)/shard_map/ppermute | solution.py:56
  9.6 16.8 %collective-permute-start.4 = (bf16[2,2,256,640]{3,2,1,0:T(8,128)(2,1)S(1)}, bf16[2,2,256,640]{3,2,1,0:T(8,128)(2,1)S(1)}, u32[]{:S(2)}, u32[]{:S(2)}) collective-permute-start(bf16[2,2,256,640]{3,2,1,0:T(8,128)(2,1)S(1)} %get-tuple-element.35.refs_1_), channel_id=1, source_target_pairs={{0,24},{1,7},{2,26},{3,1},{4,28},{5,3},{6,30},{7,5},{8,0},{9,15},{... | collective-permute-start | bytes 3932168 | tf_op jit(solution)/shard_map/ppermute | solution.py:52
  16.1 32.7 %all-to-all-start = ((bf16[8,400,128]{2,1,0:T(8,128)(2,1)}), bf16[8,400,128]{2,1,0:T(8,128)(2,1)}, u32[]{:S(2)}, u32[]{:S(2)}) async-start(bf16[8,400,128]{2,1,0:T(8,128)(2,1)} %bitcast.29), calls=%async_computation | async-start | bytes 1638400 | tf_op jit(solution)/shard_map/all_to_all | solution.py:548
  24.3 16.2 %collective-permute-start.1 = (bf16[2,272,640]{2,1,0:T(8,128)(2,1)S(1)}, bf16[2,272,640]{2,1,0:T(8,128)(2,1)}, u32[]{:S(2)}, u32[]{:S(2)}) collective-permute-start(bf16[2,272,640]{2,1,0:T(8,128)(2,1)S(1)} %get-tuple-element.38.refs_3_.refs_0_), channel_id=1, source_target_pairs={{0,2},{1,9},{2,4},{3,11},{4,6},{5,13},{6,0},{7,15},{8,10},{9,17},{... | collective-permute-start | bytes 2088968 | tf_op jit(solution)/shard_map/ppermute | solution.py:52
  25.5 36.5 %collective-permute-start.6 = (bf16[2,2,256,640]{3,2,1,0:T(8,128)(2,1)S(1)}, bf16[2,2,256,640]{3,2,1,0:T(8,128)(2,1)}, u32[]{:S(2)}, u32[]{:S(2)}) collective-permute-start(bf16[2,2,256,640]{3,2,1,0:T(8,128)(2,1)S(1)} %get-tuple-element.35.refs_1_), channel_id=1, source_target_pairs={{0,8},{1,3},{2,10},{3,5},{4,12},{5,7},{6,14},{7,1},{8,16},{9,11},{... | collective-permute-start | bytes 3932168 | tf_op jit(solution)/shard_map/ppermute | solution.py:52
  26.4 35.6 %collective-permute-start.5 = (bf16[2,2,256,640]{3,2,1,0:T(8,128)(2,1)S(1)}, bf16[2,2,256,640]{3,2,1,0:T(8,128)(2,1)}, u32[]{:S(2)}, u32[]{:S(2)}) collective-permute-start(bf16[2,2,256,640]{3,2,1,0:T(8,128)(2,1)S(1)} %collective-permute-done.4.refs_2_), channel_id=1, source_target_pairs={{0,24},{1,7},{2,26},{3,1},{4,28},{5,3},{6,30},{7,5},{8,0},{9,15},{... | collective-permute-start | bytes 3932168 | tf_op jit(solution)/shard_map/ppermute | solution.py:52
  28.3 30.9 %collective-permute-start.3 = (bf16[2,272,640]{2,1,0:T(8,128)(2,1)S(1)}, bf16[2,272,640]{2,1,0:T(8,128)(2,1)}, u32[]{:S(2)}, u32[]{:S(2)}) collective-permute-start(bf16[2,272,640]{2,1,0:T(8,128)(2,1)S(1)} %get-tuple-element.38.refs_3_.refs_0_), channel_id=1, source_target_pairs={{0,6},{1,25},{2,0},{3,27},{4,2},{5,29},{6,4},{7,31},{8,14},{9,1},{... | collective-permute-start | bytes 2088968 | tf_op jit(solution)/shard_map/ppermute | solution.py:52
  40.5 18.7 %collective-permute-start.2 = (bf16[2,272,640]{2,1,0:T(8,128)(2,1)}, bf16[2,272,640]{2,1,0:T(8,128)(2,1)}, u32[]{:S(2)}, u32[]{:S(2)}) collective-permute-start(bf16[2,272,640]{2,1,0:T(8,128)(2,1)} %collective-permute-done.1.refs_1_.refs_0_), channel_id=1, source_target_pairs={{0,2},{1,9},{2,4},{3,11},{4,6},{5,13},{6,0},{7,15},{8,10},{9,17},{... | collective-permute-start | bytes 2088968 | tf_op jit(solution)/shard_map/ppermute | solution.py:52
  52.9 50.3 %all-to-all-start.1 = ((bf16[8,400,128]{2,1,0:T(8,128)(2,1)}), bf16[8,400,128]{2,1,0:T(8,128)(2,1)}, u32[]{:S(2)}, u32[]{:S(2)}) async-start(bf16[8,400,128]{2,1,0:T(8,128)(2,1)} %prefix.1), calls=%async_computation.1 | async-start | bytes 1638400 | tf_op jit(solution)/shard_map/all_to_all | solution.py:574
  74.2 13.7 %collective-permute-start.8 = (bf16[2,272,640]{2,1,0:T(8,128)(2,1)S(1)}, bf16[2,272,640]{2,1,0:T(8,128)(2,1)S(1)}, u32[]{:S(2)}, u32[]{:S(2)}) collective-permute-start(bf16[2,272,640]{2,1,0:T(8,128)(2,1)S(1)} %shard_map.115), channel_id=1, source_target_pairs={{0,2},{1,9},{2,4},{3,11},{4,6},{5,13},{6,0},{7,15},{8,10},{9,17},{... | collective-permute-start | bytes 2088968 | tf_op jit(solution)/shard_map/ppermute | solution.py:52
  77.0 17.7 %collective-permute-start.7 = (bf16[2,272,640]{2,1,0:T(8,128)(2,1)S(1)}, bf16[2,272,640]{2,1,0:T(8,128)(2,1)S(1)}, u32[]{:S(2)}, u32[]{:S(2)}) collective-permute-start(bf16[2,272,640]{2,1,0:T(8,128)(2,1)S(1)} %shard_map.114), channel_id=1, source_target_pairs={{0,6},{1,25},{2,0},{3,27},{4,2},{5,29},{6,4},{7,31},{8,14},{9,1},{... | collective-permute-start | bytes 2088968 | tf_op jit(solution)/shard_map/ppermute | solution.py:52
  79.3 17.3 %collective-permute-start.9 = (bf16[2,272,640]{2,1,0:T(8,128)(2,1)S(1)}, bf16[2,272,640]{2,1,0:T(8,128)(2,1)S(1)}, u32[]{:S(2)}, u32[]{:S(2)}) collective-permute-start(bf16[2,272,640]{2,1,0:T(8,128)(2,1)S(1)} %shard_map.113), channel_id=1, source_target_pairs={{0,4},{1,17},{2,6},{3,19},{4,0},{5,21},{6,2},{7,23},{8,12},{9,25},... | collective-permute-start | bytes 2088968 | tf_op jit(solution)/shard_map/ppermute | solution.py:52
  98.6 10.2 %collective-permute-start.10 = (bf16[256,640]{1,0:T(8,128)(2,1)S(1)}, bf16[256,640]{1,0:T(8,128)(2,1)S(1)}, u32[]{:S(2)}, u32[]{:S(2)}) collective-permute-start(bf16[256,640]{1,0:T(8,128)(2,1)S(1)} %get-tuple-element.43), channel_id=1, source_target_pairs={{0,1},{1,0},{2,3},{3,2},{4,5},{5,4},{6,7},{7,6},{8,9},{9,8},{10,11... | collective-permute-start | bytes 983048 | tf_op jit(solution)/shard_map/ppermute | solution.py:56

commit v8 on v7

--- a/solution.py
+++ b/solution.py
@@ -115,7 +115,9 @@
 
 def prefix_kernel(place_ref, in_ref, out_ref):
     rows = in_ref.shape[1]
-    row = lax.broadcasted_iota(jnp.int32, (rows, 128), 0) + ((place_ref[0] + pl.program_id(0)) & 1) * rows
+    row = lax.broadcasted_iota(jnp.int32, (rows, 128), 0) + (place_ref[0] & 1) * (FROWS // 2)
+    row = jnp.where(row >= FROWS, row - FROWS, row)
+    row = jnp.where(row >= FROWS, row - FROWS, row)
     high = (row == FEATS) | (row == FEATS + 1)
     low = (row == FEATS + 2) | (row == FEATS + 3)
     total = jnp.zeros((rows, 128), F32)
@@ -230,19 +232,21 @@
         c.start()
     for c in copies:
         c.wait()
-    for r in range(2 * SIDE):
-        wanted[r : r + 1] = ids[r].astype(F32).astype(jnp.int32)[0:1]
+    entry = jnp.concatenate([ids[r].astype(F32)[0:1] for r in range(2 * SIDE)], axis=0).astype(jnp.int32)
+    xo, yo, co = entry >> 4, (entry >> 2) & (SIDE - 1), (entry >> 1) & 1
+    on_x = core == 0
+    line = jnp.where(on_x, yo, xo) == jnp.where(on_x, y, x)
+    away = jnp.where(on_x, xo - x, yo - y) & (SIDE - 1)
+    code = (away * 2 + (co ^ core)) * 2 + (entry & 1)
+    wanted[...] = jnp.where((entry >= 0) & line, code, -1)
     pltpu.async_copy(wanted, found_ref, sems.at[SIDE]).wait()
 
     def search(r, carry):
         count = jnp.int32(0)
         for i in range(LISTED):
             entry = found_ref[r, i]
-            xo, yo, co = entry >> 4, (entry >> 2) & (SIDE - 1), (entry >> 1) & 1
-            mine = (entry >= 0) & jnp.where(core == 0, yo == y, xo == x)
-            away = jnp.where(core == 0, xo - x, yo - y) & (SIDE - 1)
-            found_ref[r, count] = (away * 2 + (co ^ core)) * 2 + (entry & 1)
-            count = count + mine.astype(jnp.int32)
+            found_ref[r, count] = entry
+            count = count + (entry >= 0).astype(jnp.int32)
         count_ref[r] = count
         return carry
 
@@ -253,9 +257,7 @@
     groups = readers // 2
     q_in, kv_in, outs = refs[:groups], refs[groups : groups + SIDE], refs[groups + SIDE : readers + SIDE]
     q_buf, g_buf, s_buf, m_buf, a_buf, q_sems, g_sems = refs[readers + SIDE :]
-    copies = [pltpu.make_async_copy(q_in[i], q_buf.at[pl.ds(2 * i, 2)], q_sems.at[i]) for i in range(groups)]
-    for c in copies:
-        c.start()
+    copies = [pltpu.make_async_copy(q_in[r // 2].at[r % 2], q_buf.at[r], q_sems.at[r]) for r in range(readers)]
     lane = lax.broadcasted_iota(jnp.int32, (TOK, 128), 1)
     heads = [(h, slice(h * 128, (h + 1) * 128)) for h in range(HALF_HEADS)]
 
@@ -267,17 +269,18 @@
 
                 @pl.when((code >> 2) == away)
                 def _():
-                    source = kv_in[away].at[(code >> 1) & 1, :, rows, :]
-                    pltpu.make_async_copy(source, g_buf.at[slot, i], g_sems.at[slot, i]).start()
+                    for kind in range(2):
+                        source = kv_in[away].at[(code >> 1) & 1, kind, rows, :]
+                        pltpu.make_async_copy(source, g_buf.at[slot, i, kind], g_sems.at[slot, i, kind]).start()
 
             return carry
 
         lax.fori_loop(0, counts[base + r], one, 0)
 
-    def arrived(r, slot):
+    def arrived(r, slot, kind):
         def one(i, carry):
-            source = kv_in[0].at[0, :, pl.ds(0, BLK), :]
-            pltpu.make_async_copy(source, g_buf.at[slot, i], g_sems.at[slot, i]).wait()
+            source = kv_in[0].at[0, kind, pl.ds(0, BLK), :]
+            pltpu.make_async_copy(source, g_buf.at[slot, i, kind], g_sems.at[slot, i, kind]).wait()
             return carry
 
         lax.fori_loop(0, counts[base + r], one, 0)
@@ -331,7 +334,9 @@
                 s = jnp.concatenate(parts, axis=0)
                 s_buf[LISTED // 2, h, :, 0:128] = s
                 m_buf[h] = s
+            arrived(r, slot, 0)
         else:
+            arrived(r, slot, 0)
             score(0, True)
         start = 0 if own else 1
 
@@ -354,7 +359,9 @@
                     v = with_ones(own_kv[r, 1, rows, at])
                     parts.append(jnp.dot(p[rows], v, preferred_element_type=F32))
                 a_buf[h] = jnp.concatenate(parts, axis=0)
+            arrived(r, slot, 1)
         else:
+            arrived(r, slot, 1)
             weigh(0, True)
 
         def more_weights(j, carry):
@@ -378,9 +385,10 @@
         out_ref[slot, TOK:QROWS, 0:TOK] = packed.T[0 : QROWS - TOK].astype(BF)
 
     own_kv = kv_in[0]
+    copies[0].start()
     fetch(0, 0)
-    for c in copies:
-        c.wait()
+    for c in copies[1:]:
+        c.start()
     for g, out_ref in enumerate(outs):
 
         def one(i, carry, g=g, out_ref=out_ref):
@@ -390,7 +398,7 @@
             def _():
                 fetch(r + 1, 1 - i)
 
-            arrived(r, i)
+            pltpu.make_async_copy(q_in[0].at[0], q_buf.at[r], q_sems.at[r]).wait()
             reader(r, i, out_ref)
             return carry
 
@@ -476,8 +484,8 @@
             pltpu.VMEM((LISTED // 2 + 1, HALF_HEADS, TOK, 256), F32),
             pltpu.VMEM((HALF_HEADS, TOK, 128), F32),
             pltpu.VMEM((HALF_HEADS, TOK, 256), F32),
-            pltpu.SemaphoreType.DMA((groups,)),
-            pltpu.SemaphoreType.DMA((2, LISTED)),
+            pltpu.SemaphoreType.DMA((readers,)),
+            pltpu.SemaphoreType.DMA((2, LISTED, 2)),
         ],
         compiler_params=room(18),
         cost_estimate=cost(readers * 4e8, 8e6),
@@ -560,14 +568,12 @@
 
     blocks = (kv, kv_right, kv_far, kv_left)
     slices, num, den, phi = lax.optimization_barrier((slices, num, den, phi))
-    part = pl.BlockSpec((shards, FROWS // 2, 128), lambda g: (0, g, 0))
     prefix = pl.pallas_call(
         prefix_kernel,
         name="prefix",
-        grid=(slices.shape[1] // (FROWS // 2),),
         out_shape=hbm_shape(*slices.shape),
-        in_specs=[SMEM, part],
-        out_specs=part,
+        in_specs=[SMEM, VMEM],
+        out_specs=VMEM,
         compiler_params=room(6),
         cost_estimate=cost(0, 2e6),
     )(place, slices)

time: 111 us -> 112 us (level)
  the two profiles are of different devices: /device:TPU:1 before, /device:TPU:153 now
where the time goes in v8:
time: 112 us; the launch traced here: 111 us
  Pallas kernels  49.1 us (44%)
  starting transfers between devices  39.1 us (35%)
  waiting for transfers between devices  20.6 us (18%)
  between operations  1.56 us (1%)
    ppermute x9, waiting for transfers between devices, move(): return lax.ppermute(a, 'files', along(what, step))  20.1 us
    pallas_call x4, Pallas kernels, attend(): pl.pallas_call(functools.partial(attend_kernel, own, base, readers), out_...  19.3 us
    ppermute x9, starting transfers between devices, move(): return lax.ppermute(a, 'files', along(what, step))  14.1 us
    ppermute x2, starting transfers between devices, swap_cores(): lax.ppermute(a, 'files', [(i, i ^ 1) for i in range(SIDE * SIDE * CORES)])  11.6 us
    pallas_call x1, Pallas kernels, layers(): pl.pallas_call(local_kernel, name='local', grid=steps, out_shape=[hbm_sha...  6.81 us
    all_to_all x1, starting transfers between devices, layers(): lax.all_to_all(state.reshape(shards, HEADS * FROWS // shards, 128), 'seq'...  6.65 us
    all_to_all x1, starting transfers between devices, layers(): lax.all_to_all(prefix, 'seq', 0, 0, tiled=True).reshape(HEADS, FROWS, 128)  6.65 us
    pallas_call x1, Pallas kernels, layers(): pl.pallas_call(finish_kernel, name='finish', grid=steps, out_shape=shape(...  5.62 us
  transfers between devices with their start and end apart: 13, of which 6 were waited for; matrix products, arithmetic and copies ran while one was open for 0% of the time, Pallas kernels for 42%

profile of v8, /device:TPU:153, one launch (start us, length us, event | category | flops | bytes accessed | tf_op | source)
XLA Modules:
  0.0 111.0 jit_solution(17909614613538907266)
XLA Ops:
  1.3 0.0 copy-start
  1.3 0.6 copy-done
  1.9 0.0 copy-start.1
  1.9 1.7 %pack.1 = bf16[784,640]{1,0:T(8,128)(2,1)S(1)} custom-call(s32[1]{0:T(128)} %bitcast.10.me_ref, s32[8]{0:T(128)S(1)} %bitcast.20, s32[1]{0:T(128)} %bitcast.18.count_ref, bf16[256,1280]{1,0:T(8,128)(2,1)} %bitcast.22, bf16[256,1280]{1,0:T(8,128)(2,1)} %bitcast.24, bf16[256,1280]{1,0:T(8,128)(2,1)} %bitcast.26), custom_call_target="tpu_custom_call" | custom-call | bytes 2000000 | tf_op jit(solution)/shard_map/pack/pallas_call | solution.py:505
  3.7 0.8 collective-permute-start
  4.4 0.0 copy-done.1
  4.5 1.7 %own.1 = (bf16[2,2,256,640]{3,2,1,0:T(8,128)(2,1)S(1)}, bf16[2,272,640]{2,1,0:T(8,128)(2,1)S(1)}) custom-call(s32[1]{0:T(128)} %bitcast.10.me_ref, s32[8]{0:T(128)S(1)} %bitcast.21, s32[1]{0:T(128)} %bitcast.19.count_ref, bf16[256,1280]{1,0:T(8,128)(2,1)} %bitcast.23, bf16[256,1280]{1,0:T(8,128)(2,1)} %bitcast.25, bf16[256,1280]{1,0:T(8,128)(2,1)} %bitcast.27), custom_call_target="tpu_custom_call" | custom-call | bytes 2000000 | tf_op jit(solution)/shard_map/own/pallas_call | solution.py:517
  6.2 0.5 collective-permute-done.mate_ref
  6.7 0.4 merge.1
  7.0 0.5 collective-permute-start.4
  7.6 5.4 %state.1 = bf16[20,160,128]{2,1,0:T(8,128)(2,1)} custom-call(bf16[320,256]{1,0:T(8,128)(2,1)} %bitcast.34, bf16[256,2560]{1,0:T(8,128)(2,1)} %bitcast.31, bf16[4,320,64]{2,1,0:T(8,128)(2,1)} %constant.13.clone.select_ref, f32[3,160,128]{2,1,0:T(8,128)} %constant.14.clone.vector_ref), custom_call_target="tpu_custom_call" | custom-call | flops 1000000000 | bytes 4000000 | tf_op jit(solution)/shard_map/state/pallas_call | solution.py:546
  13.0 6.6 %all-to-all-start = ((bf16[8,400,128]{2,1,0:T(8,128)(2,1)}), bf16[8,400,128]{2,1,0:T(8,128)(2,1)}, u32[]{:S(2)}, u32[]{:S(2)}) async-start(bf16[8,400,128]{2,1,0:T(8,128)(2,1)} %bitcast.29), calls=%async_computation | async-start | bytes 1638400 | tf_op jit(solution)/shard_map/all_to_all | solution.py:556
  19.7 1.2 %collective-permute-start.1 = (bf16[2,272,640]{2,1,0:T(8,128)(2,1)S(1)}, bf16[2,272,640]{2,1,0:T(8,128)(2,1)}, u32[]{:S(2)}, u32[]{:S(2)}) collective-permute-start(bf16[2,272,640]{2,1,0:T(8,128)(2,1)S(1)} %get-tuple-element.38.refs_3_.refs_0_), channel_id=1, source_target_pairs={{0,2},{1,9},{2,4},{3,11},{4,6},{5,13},{6,0},{7,15},{8,10},{9,17},{... | collective-permute-start | bytes 2088968 | tf_op jit(solution)/shard_map/ppermute | solution.py:52
  20.9 2.2 %collective-permute-start.6 = (bf16[2,2,256,640]{3,2,1,0:T(8,128)(2,1)S(1)}, bf16[2,2,256,640]{3,2,1,0:T(8,128)(2,1)}, u32[]{:S(2)}, u32[]{:S(2)}) collective-permute-start(bf16[2,2,256,640]{3,2,1,0:T(8,128)(2,1)S(1)} %get-tuple-element.35.refs_1_), channel_id=1, source_target_pairs={{0,8},{1,3},{2,10},{3,5},{4,12},{5,7},{6,14},{7,1},{8,16},{9,11},{... | collective-permute-start | bytes 3932168 | tf_op jit(solution)/shard_map/ppermute | solution.py:52
  23.1 2.1 %collective-permute-done.4.refs_2_ = bf16[2,2,256,640]{3,2,1,0:T(8,128)(2,1)S(1)} collective-permute-done((bf16[2,2,256,640]{3,2,1,0:T(8,128)(2,1)S(1)}, bf16[2,2,256,640]{3,2,1,0:T(8,128)(2,1)S(1)}, u32[]{:S(2)}, u32[]{:S(2)}) %collective-permute-start.4) | collective-permute-done | bytes 1310752 | tf_op jit(solution)/shard_map/ppermute | solution.py:52
  25.2 0.0 collective-permute-start.5
  25.2 2.5 %collective-permute-start.3 = (bf16[2,272,640]{2,1,0:T(8,128)(2,1)S(1)}, bf16[2,272,640]{2,1,0:T(8,128)(2,1)}, u32[]{:S(2)}, u32[]{:S(2)}) collective-permute-start(bf16[2,272,640]{2,1,0:T(8,128)(2,1)S(1)} %get-tuple-element.38.refs_3_.refs_0_), channel_id=1, source_target_pairs={{0,6},{1,25},{2,0},{3,27},{4,2},{5,29},{6,4},{7,31},{8,14},{9,1},{... | collective-permute-start | bytes 2088968 | tf_op jit(solution)/shard_map/ppermute | solution.py:52
  27.7 7.0 %collective-permute-done.1.refs_1_.refs_0_ = bf16[2,272,640]{2,1,0:T(8,128)(2,1)} collective-permute-done((bf16[2,272,640]{2,1,0:T(8,128)(2,1)S(1)}, bf16[2,272,640]{2,1,0:T(8,128)(2,1)}, u32[]{:S(2)}, u32[]{:S(2)}) %collective-permute-start.1) | collective-permute-done | bytes 696352 | tf_op jit(solution)/shard_map/ppermute | solution.py:52
  34.7 1.5 %collective-permute-start.2 = (bf16[2,272,640]{2,1,0:T(8,128)(2,1)}, bf16[2,272,640]{2,1,0:T(8,128)(2,1)}, u32[]{:S(2)}, u32[]{:S(2)}) collective-permute-start(bf16[2,272,640]{2,1,0:T(8,128)(2,1)} %collective-permute-done.1.refs_1_.refs_0_), channel_id=1, source_target_pairs={{0,2},{1,9},{2,4},{3,11},{4,6},{5,13},{6,0},{7,15},{8,10},{9,17},{... | collective-permute-start | bytes 2088968 | tf_op jit(solution)/shard_map/ppermute | solution.py:52
  36.2 6.8 %local.1 = (bf16[256,2560]{1,0:T(8,128)(2,1)}, f32[256,128]{1,0:T(8,128)}, bf16[20,160,256]{2,1,0:T(8,128)(2,1)}) custom-call(bf16[320,256]{1,0:T(8,128)(2,1)} %bitcast.33, bf16[320,256]{1,0:T(8,128)(2,1)} %bitcast.35, bf16[256,2560]{1,0:T(8,128)(2,1)} %bitcast.32, bf16[4,320,64]{2,1,0:T(8,128)(2,1)} %constant.13.clone.select_ref, ...), custom_call_target="tpu_custom_call" | custom-call | flops 4000000000 | bytes 8000000 | tf_op jit(solution)/shard_map/local/pallas_call | solution.py:558
  43.0 0.0 all-to-all-done.in_ref
  43.0 2.8 %prefix.1 = bf16[8,400,128]{2,1,0:T(8,128)(2,1)} custom-call(s32[1]{0:T(128)} %bitcast.7.place_ref, bf16[8,400,128]{2,1,0:T(8,128)(2,1)} %all-to-all-done.in_ref), custom_call_target="tpu_custom_call" | custom-call | bytes 2000000 | tf_op jit(solution)/shard_map/prefix/pallas_call | solution.py:571
  45.8 6.6 %all-to-all-start.1 = ((bf16[8,400,128]{2,1,0:T(8,128)(2,1)}), bf16[8,400,128]{2,1,0:T(8,128)(2,1)}, u32[]{:S(2)}, u32[]{:S(2)}) async-start(bf16[8,400,128]{2,1,0:T(8,128)(2,1)} %prefix.1), calls=%async_computation.1 | async-start | bytes 1638400 | tf_op jit(solution)/shard_map/all_to_all | solution.py:580
  52.5 0.0 collective-permute-done.3.refs_2_.refs_0_
  52.5 0.0 collective-permute-done.2.refs_0_
  52.5 2.4 %search.1 = (s32[8,128]{1,0:T(8,128)S(1)}, s32[8]{0:T(128)S(1)}) custom-call(s32[1]{0:T(128)} %bitcast.10.me_ref, bf16[2,272,640]{2,1,0:T(8,128)(2,1)} %collective-permute-done.2.refs_0_, bf16[2,272,640]{2,1,0:T(8,128)(2,1)} %collective-permute-done.1.refs_1_.refs_0_, bf16[2,272,640]{2,1,0:T(8,128)(2,1)} %collective-permute-done.3.refs_2_.refs_0_, ...), custom_call_target="tpu_custom_call" | custom-call | bytes 100000 | tf_op jit(solution)/shard_map/search/pallas_call | solution.py:581
  54.9 0.0 collective-permute-done.6.refs_4_
  54.9 0.0 collective-permute-done.5.refs_3_
  54.9 4.3 %shard_map.113 = bf16[2,272,640]{2,1,0:T(8,128)(2,1)S(1)} custom-call(s32[8,128]{1,0:T(8,128)S(1)} %get-tuple-element.33.found, s32[8]{0:T(128)S(1)} %get-tuple-element.34.counts, bf16[2,272,640]{2,1,0:T(8,128)(2,1)} %collective-permute-done.2.refs_0_, bf16[2,2,256,640]{3,2,1,0:T(8,128)(2,1)S(1)} %get-tuple-element.35.refs_1_, ...), custom_call_target="tpu_custom_call" | custom-call | flops 800000000 | bytes 8000000 | tf_op jit(solution)/shard_map/pallas_call | solution.py:476
  59.3 4.3 %shard_map.114 = bf16[2,272,640]{2,1,0:T(8,128)(2,1)S(1)} custom-call(s32[8,128]{1,0:T(8,128)S(1)} %get-tuple-element.33.found, s32[8]{0:T(128)S(1)} %get-tuple-element.34.counts, bf16[2,272,640]{2,1,0:T(8,128)(2,1)} %collective-permute-done.1.refs_1_.refs_0_, bf16[2,2,256,640]{3,2,1,0:T(8,128)(2,1)S(1)} %get-tuple-element.35.refs_1_, ...), custom_call_target="tpu_custom_call" | custom-call | flops 800000000 | bytes 8000000 | tf_op jit(solution)/shard_map/pallas_call | solution.py:476
  63.6 5.7 %shard_map.115 = bf16[2,272,640]{2,1,0:T(8,128)(2,1)S(1)} custom-call(s32[8,128]{1,0:T(8,128)S(1)} %get-tuple-element.33.found, s32[8]{0:T(128)S(1)} %get-tuple-element.34.counts, bf16[2,272,640]{2,1,0:T(8,128)(2,1)} %collective-permute-done.3.refs_2_.refs_0_, bf16[2,2,256,640]{3,2,1,0:T(8,128)(2,1)S(1)} %get-tuple-element.35.refs_1_, ...), custom_call_target="tpu_custom_call" | custom-call | flops 800000000 | bytes 8000000 | tf_op jit(solution)/shard_map/pallas_call | solution.py:476
  69.4 4.1 %collective-permute-start.8 = (bf16[2,272,640]{2,1,0:T(8,128)(2,1)S(1)}, bf16[2,272,640]{2,1,0:T(8,128)(2,1)S(1)}, u32[]{:S(2)}, u32[]{:S(2)}) collective-permute-start(bf16[2,272,640]{2,1,0:T(8,128)(2,1)S(1)} %shard_map.115), channel_id=1, source_target_pairs={{0,2},{1,9},{2,4},{3,11},{4,6},{5,13},{6,0},{7,15},{8,10},{9,17},{... | collective-permute-start | bytes 2088968 | tf_op jit(solution)/shard_map/ppermute | solution.py:52
  73.4 1.0 collective-permute-start.7
  74.5 1.1 collective-permute-start.9
  75.5 4.9 %shard_map.116.refs_0_ = bf16[2,272,640]{2,1,0:T(8,128)(2,1)S(1)} custom-call(s32[8,128]{1,0:T(8,128)S(1)} %get-tuple-element.33.found, s32[8]{0:T(128)S(1)} %get-tuple-element.34.counts, bf16[2,272,640]{2,1,0:T(8,128)(2,1)S(1)} %get-tuple-element.38.refs_3_.refs_0_, bf16[2,2,256,640]{3,2,1,0:T(8,128)(2,1)S(1)} %get-tuple-element.35.refs_1_, ...), custom_call_target="tpu_custom_call" | custom-call | flops 800000000 | bytes 8000000 | tf_op jit(solution)/shard_map/pallas_call | solution.py:476
  80.4 2.3 %collective-permute-done.8.refs_2_ = bf16[2,272,640]{2,1,0:T(8,128)(2,1)S(1)} collective-permute-done((bf16[2,272,640]{2,1,0:T(8,128)(2,1)S(1)}, bf16[2,272,640]{2,1,0:T(8,128)(2,1)S(1)}, u32[]{:S(2)}, u32[]{:S(2)}) %collective-permute-start.8) | collective-permute-done | bytes 696352 | tf_op jit(solution)/shard_map/ppermute | solution.py:52
  82.8 0.8 collective-permute-done.7.refs_1_
  83.6 7.8 %collective-permute-done.9.refs_3_ = bf16[2,272,640]{2,1,0:T(8,128)(2,1)S(1)} collective-permute-done((bf16[2,272,640]{2,1,0:T(8,128)(2,1)S(1)}, bf16[2,272,640]{2,1,0:T(8,128)(2,1)S(1)}, u32[]{:S(2)}, u32[]{:S(2)}) %collective-permute-start.9) | collective-permute-done | bytes 696352 | tf_op jit(solution)/shard_map/ppermute | solution.py:52
  91.4 2.0 %join.1 = (bf16[256,640]{1,0:T(8,128)(2,1)S(1)}, bf16[256,640]{1,0:T(8,128)(2,1)S(1)}) custom-call(bf16[2,272,640]{2,1,0:T(8,128)(2,1)S(1)} %shard_map.116.refs_0_, bf16[2,272,640]{2,1,0:T(8,128)(2,1)S(1)} %collective-permute-done.7.refs_1_, bf16[2,272,640]{2,1,0:T(8,128)(2,1)S(1)} %collective-permute-done.8.refs_2_, ...), custom_call_target="tpu_custom_call" | custom-call | bytes 4000000 | tf_op jit(solution)/shard_map/join/pallas_call | solution.py:605
  93.4 10.9 %collective-permute-start.10 = (bf16[256,640]{1,0:T(8,128)(2,1)S(1)}, bf16[256,640]{1,0:T(8,128)(2,1)S(1)}, u32[]{:S(2)}, u32[]{:S(2)}) collective-permute-start(bf16[256,640]{1,0:T(8,128)(2,1)S(1)} %get-tuple-element.43), channel_id=1, source_target_pairs={{0,1},{1,0},{2,3},{3,2},{4,5},{5,4},{6,7},{7,6},{8,9},{9,8},{10,11... | collective-permute-start | bytes 983048 | tf_op jit(solution)/shard_map/ppermute | solution.py:56
  104.3 0.0 all-to-all-done.1
  104.3 5.6 %finish.1 = bf16[256,2560]{1,0:T(8,128)(2,1)} custom-call(bf16[256,2560]{1,0:T(8,128)(2,1)} %get-tuple-element.26.num_ref, f32[256,128]{1,0:T(8,128)} %get-tuple-element.27.den_ref, bf16[20,160,256]{2,1,0:T(8,128)(2,1)} %get-tuple-element.28.phi_ref, bf16[20,160,128]{2,1,0:T(8,128)(2,1)} %bitcast.8.state_ref), custom_call_target="tpu_custom_call" | custom-call | flops 400000000 | bytes 8000000 | tf_op jit(solution)/shard_map/finish/pallas_call | solution.py:627
  110.0 0.0 collective-permute-done.10.other_ref
  110.0 0.8 place.1
Async XLA Ops:
  1.3 0.7 copy-start
  1.9 2.5 %copy-start.1 = (s32[1,1,8]{2,1,0:T(1,128)S(1)}, s32[1,1,8]{2,1,0:T(1,128)}, u32[]{:S(2)}) copy-start(s32[1,1,8]{2,1,0:T(1,128)} %param.16) | copy-start | bytes 100
  3.7 3.0 %collective-permute-start = (bf16[784,640]{1,0:T(8,128)(2,1)S(1)}, bf16[784,640]{1,0:T(8,128)(2,1)S(1)}, u32[]{:S(2)}, u32[]{:S(2)}) collective-permute-start(bf16[784,640]{1,0:T(8,128)(2,1)S(1)} %pack.1), channel_id=1, source_target_pairs={{0,1},{1,0},{2,3},{3,2},{4,5},{5,4},{6,7},{7,6},{8,9},{9,8},{10,11... | collective-permute-start | bytes 3010568 | tf_op jit(solution)/shard_map/ppermute | solution.py:56
  7.0 18.1 %collective-permute-start.4 = (bf16[2,2,256,640]{3,2,1,0:T(8,128)(2,1)S(1)}, bf16[2,2,256,640]{3,2,1,0:T(8,128)(2,1)S(1)}, u32[]{:S(2)}, u32[]{:S(2)}) collective-permute-start(bf16[2,2,256,640]{3,2,1,0:T(8,128)(2,1)S(1)} %get-tuple-element.35.refs_1_), channel_id=1, source_target_pairs={{0,24},{1,7},{2,26},{3,1},{4,28},{5,3},{6,30},{7,5},{8,0},{9,15},{... | collective-permute-start | bytes 3932168 | tf_op jit(solution)/shard_map/ppermute | solution.py:52
  13.0 30.0 %all-to-all-start = ((bf16[8,400,128]{2,1,0:T(8,128)(2,1)}), bf16[8,400,128]{2,1,0:T(8,128)(2,1)}, u32[]{:S(2)}, u32[]{:S(2)}) async-start(bf16[8,400,128]{2,1,0:T(8,128)(2,1)} %bitcast.29), calls=%async_computation | async-start | bytes 1638400 | tf_op jit(solution)/shard_map/all_to_all | solution.py:556
  19.7 15.0 %collective-permute-start.1 = (bf16[2,272,640]{2,1,0:T(8,128)(2,1)S(1)}, bf16[2,272,640]{2,1,0:T(8,128)(2,1)}, u32[]{:S(2)}, u32[]{:S(2)}) collective-permute-start(bf16[2,272,640]{2,1,0:T(8,128)(2,1)S(1)} %get-tuple-element.38.refs_3_.refs_0_), channel_id=1, source_target_pairs={{0,2},{1,9},{2,4},{3,11},{4,6},{5,13},{6,0},{7,15},{8,10},{9,17},{... | collective-permute-start | bytes 2088968 | tf_op jit(solution)/shard_map/ppermute | solution.py:52
  20.9 34.0 %collective-permute-start.6 = (bf16[2,2,256,640]{3,2,1,0:T(8,128)(2,1)S(1)}, bf16[2,2,256,640]{3,2,1,0:T(8,128)(2,1)}, u32[]{:S(2)}, u32[]{:S(2)}) collective-permute-start(bf16[2,2,256,640]{3,2,1,0:T(8,128)(2,1)S(1)} %get-tuple-element.35.refs_1_), channel_id=1, source_target_pairs={{0,8},{1,3},{2,10},{3,5},{4,12},{5,7},{6,14},{7,1},{8,16},{9,11},{... | collective-permute-start | bytes 3932168 | tf_op jit(solution)/shard_map/ppermute | solution.py:52
  25.2 29.7 %collective-permute-start.5 = (bf16[2,2,256,640]{3,2,1,0:T(8,128)(2,1)S(1)}, bf16[2,2,256,640]{3,2,1,0:T(8,128)(2,1)}, u32[]{:S(2)}, u32[]{:S(2)}) collective-permute-start(bf16[2,2,256,640]{3,2,1,0:T(8,128)(2,1)S(1)} %collective-permute-done.4.refs_2_), channel_id=1, source_target_pairs={{0,24},{1,7},{2,26},{3,1},{4,28},{5,3},{6,30},{7,5},{8,0},{9,15},{... | collective-permute-start | bytes 3932168 | tf_op jit(solution)/shard_map/ppermute | solution.py:52
  25.2 27.3 %collective-permute-start.3 = (bf16[2,272,640]{2,1,0:T(8,128)(2,1)S(1)}, bf16[2,272,640]{2,1,0:T(8,128)(2,1)}, u32[]{:S(2)}, u32[]{:S(2)}) collective-permute-start(bf16[2,272,640]{2,1,0:T(8,128)(2,1)S(1)} %get-tuple-element.38.refs_3_.refs_0_), channel_id=1, source_target_pairs={{0,6},{1,25},{2,0},{3,27},{4,2},{5,29},{6,4},{7,31},{8,14},{9,1},{... | collective-permute-start | bytes 2088968 | tf_op jit(solution)/shard_map/ppermute | solution.py:52
  34.7 17.8 %collective-permute-start.2 = (bf16[2,272,640]{2,1,0:T(8,128)(2,1)}, bf16[2,272,640]{2,1,0:T(8,128)(2,1)}, u32[]{:S(2)}, u32[]{:S(2)}) collective-permute-start(bf16[2,272,640]{2,1,0:T(8,128)(2,1)} %collective-permute-done.1.refs_1_.refs_0_), channel_id=1, source_target_pairs={{0,2},{1,9},{2,4},{3,11},{4,6},{5,13},{6,0},{7,15},{8,10},{9,17},{... | collective-permute-start | bytes 2088968 | tf_op jit(solution)/shard_map/ppermute | solution.py:52
  45.8 58.5 %all-to-all-start.1 = ((bf16[8,400,128]{2,1,0:T(8,128)(2,1)}), bf16[8,400,128]{2,1,0:T(8,128)(2,1)}, u32[]{:S(2)}, u32[]{:S(2)}) async-start(bf16[8,400,128]{2,1,0:T(8,128)(2,1)} %prefix.1), calls=%async_computation.1 | async-start | bytes 1638400 | tf_op jit(solution)/shard_map/all_to_all | solution.py:580
  69.4 13.4 %collective-permute-start.8 = (bf16[2,272,640]{2,1,0:T(8,128)(2,1)S(1)}, bf16[2,272,640]{2,1,0:T(8,128)(2,1)S(1)}, u32[]{:S(2)}, u32[]{:S(2)}) collective-permute-start(bf16[2,272,640]{2,1,0:T(8,128)(2,1)S(1)} %shard_map.115), channel_id=1, source_target_pairs={{0,2},{1,9},{2,4},{3,11},{4,6},{5,13},{6,0},{7,15},{8,10},{9,17},{... | collective-permute-start | bytes 2088968 | tf_op jit(solution)/shard_map/ppermute | solution.py:52
  73.4 10.2 %collective-permute-start.7 = (bf16[2,272,640]{2,1,0:T(8,128)(2,1)S(1)}, bf16[2,272,640]{2,1,0:T(8,128)(2,1)S(1)}, u32[]{:S(2)}, u32[]{:S(2)}) collective-permute-start(bf16[2,272,640]{2,1,0:T(8,128)(2,1)S(1)} %shard_map.114), channel_id=1, source_target_pairs={{0,6},{1,25},{2,0},{3,27},{4,2},{5,29},{6,4},{7,31},{8,14},{9,1},{... | collective-permute-start | bytes 2088968 | tf_op jit(solution)/shard_map/ppermute | solution.py:52
  74.5 17.0 %collective-permute-start.9 = (bf16[2,272,640]{2,1,0:T(8,128)(2,1)S(1)}, bf16[2,272,640]{2,1,0:T(8,128)(2,1)S(1)}, u32[]{:S(2)}, u32[]{:S(2)}) collective-permute-start(bf16[2,272,640]{2,1,0:T(8,128)(2,1)S(1)} %shard_map.113), channel_id=1, source_target_pairs={{0,4},{1,17},{2,6},{3,19},{4,0},{5,21},{6,2},{7,23},{8,12},{9,25},... | collective-permute-start | bytes 2088968 | tf_op jit(solution)/shard_map/ppermute | solution.py:52
  93.4 16.5 %collective-permute-start.10 = (bf16[256,640]{1,0:T(8,128)(2,1)S(1)}, bf16[256,640]{1,0:T(8,128)(2,1)S(1)}, u32[]{:S(2)}, u32[]{:S(2)}) collective-permute-start(bf16[256,640]{1,0:T(8,128)(2,1)S(1)} %get-tuple-element.43), channel_id=1, source_target_pairs={{0,1},{1,0},{2,3},{3,2},{4,5},{5,4},{6,7},{7,6},{8,9},{9,8},{10,11... | collective-permute-start | bytes 983048 | tf_op jit(solution)/shard_map/ppermute | solution.py:56

commit v9 on v7

--- a/solution.py
+++ b/solution.py
@@ -115,7 +115,9 @@
 
 def prefix_kernel(place_ref, in_ref, out_ref):
     rows = in_ref.shape[1]
-    row = lax.broadcasted_iota(jnp.int32, (rows, 128), 0) + ((place_ref[0] + pl.program_id(0)) & 1) * rows
+    row = lax.broadcasted_iota(jnp.int32, (rows, 128), 0) + (place_ref[0] & 1) * (FROWS // 2)
+    row = jnp.where(row >= FROWS, row - FROWS, row)
+    row = jnp.where(row >= FROWS, row - FROWS, row)
     high = (row == FEATS) | (row == FEATS + 1)
     low = (row == FEATS + 2) | (row == FEATS + 3)
     total = jnp.zeros((rows, 128), F32)
@@ -230,19 +232,21 @@
         c.start()
     for c in copies:
         c.wait()
-    for r in range(2 * SIDE):
-        wanted[r : r + 1] = ids[r].astype(F32).astype(jnp.int32)[0:1]
+    entry = jnp.concatenate([ids[r].astype(F32)[0:1] for r in range(2 * SIDE)], axis=0).astype(jnp.int32)
+    xo, yo, co = entry >> 4, (entry >> 2) & (SIDE - 1), (entry >> 1) & 1
+    on_x = core == 0
+    line = jnp.where(on_x, yo, xo) == jnp.where(on_x, y, x)
+    away = jnp.where(on_x, xo - x, yo - y) & (SIDE - 1)
+    code = (away * 2 + (co ^ core)) * 2 + (entry & 1)
+    wanted[...] = jnp.where((entry >= 0) & line, code, -1)
     pltpu.async_copy(wanted, found_ref, sems.at[SIDE]).wait()
 
     def search(r, carry):
         count = jnp.int32(0)
         for i in range(LISTED):
             entry = found_ref[r, i]
-            xo, yo, co = entry >> 4, (entry >> 2) & (SIDE - 1), (entry >> 1) & 1
-            mine = (entry >= 0) & jnp.where(core == 0, yo == y, xo == x)
-            away = jnp.where(core == 0, xo - x, yo - y) & (SIDE - 1)
-            found_ref[r, count] = (away * 2 + (co ^ core)) * 2 + (entry & 1)
-            count = count + mine.astype(jnp.int32)
+            found_ref[r, count] = entry
+            count = count + (entry >= 0).astype(jnp.int32)
         count_ref[r] = count
         return carry
 
@@ -560,14 +564,12 @@
 
     blocks = (kv, kv_right, kv_far, kv_left)
     slices, num, den, phi = lax.optimization_barrier((slices, num, den, phi))
-    part = pl.BlockSpec((shards, FROWS // 2, 128), lambda g: (0, g, 0))
     prefix = pl.pallas_call(
         prefix_kernel,
         name="prefix",
-        grid=(slices.shape[1] // (FROWS // 2),),
         out_shape=hbm_shape(*slices.shape),
-        in_specs=[SMEM, part],
-        out_specs=part,
+        in_specs=[SMEM, VMEM],
+        out_specs=VMEM,
         compiler_params=room(6),
         cost_estimate=cost(0, 2e6),
     )(place, slices)

time: 111 us -> 109 us (0.982)
  Pallas kernels: 49.1 us -> 47.5 us
    pallas_call x1, Pallas kernels: 4.04 us -> 2.82 us  [layers(): pl.pallas_call(prefix_kernel, name='prefix', out_shape=hbm_shape(*slices....]
  transfers between devices with their start and end apart: 13 -> 13, of which waited for: 6 -> 6; matrix products, arithmetic and copies ran while one was open for 0% -> 0% of each run, Pallas kernels for 42% -> 41%
where the time goes in v9:
time: 109 us; the launch traced here: 108 us
  Pallas kernels  47.5 us (44%)
  starting transfers between devices  37 us (34%)
  waiting for transfers between devices  21.5 us (20%)
  between operations  1.57 us (1%)
    ppermute x9, waiting for transfers between devices, move(): return lax.ppermute(a, 'files', along(what, step))  21 us
    pallas_call x4, Pallas kernels, attend(): pl.pallas_call(functools.partial(attend_kernel, own, base, readers), out_...  17.7 us
    ppermute x9, starting transfers between devices, move(): return lax.ppermute(a, 'files', along(what, step))  14.7 us
    all_to_all x1, starting transfers between devices, layers(): lax.all_to_all(state.reshape(shards, HEADS * FROWS // shards, 128), 'seq'...  8.17 us
    ppermute x2, starting transfers between devices, swap_cores(): lax.ppermute(a, 'files', [(i, i ^ 1) for i in range(SIDE * SIDE * CORES)])  7.82 us
    pallas_call x1, Pallas kernels, layers(): pl.pallas_call(local_kernel, name='local', grid=steps, out_shape=[hbm_sha...  6.81 us
    all_to_all x1, starting transfers between devices, layers(): lax.all_to_all(prefix, 'seq', 0, 0, tiled=True).reshape(HEADS, FROWS, 128)  6.32 us
    pallas_call x1, Pallas kernels, layers(): pl.pallas_call(finish_kernel, name='finish', grid=steps, out_shape=shape(...  5.62 us
  transfers between devices with their start and end apart: 13, of which 6 were waited for; matrix products, arithmetic and copies ran while one was open for 0% of the time, Pallas kernels for 41%

profile of v9, /device:TPU:1, one launch (start us, length us, event | category | flops | bytes accessed | tf_op | source)
XLA Modules:
  0.0 108.2 jit_solution(2903169283476608111)
XLA Ops:
  1.3 0.0 copy-start
  1.3 0.6 copy-done
  1.9 0.0 copy-start.1
  1.9 1.7 %pack.1 = bf16[784,640]{1,0:T(8,128)(2,1)S(1)} custom-call(s32[1]{0:T(128)} %bitcast.10.me_ref, s32[8]{0:T(128)S(1)} %bitcast.20, s32[1]{0:T(128)} %bitcast.18.count_ref, bf16[256,1280]{1,0:T(8,128)(2,1)} %bitcast.22, bf16[256,1280]{1,0:T(8,128)(2,1)} %bitcast.24, bf16[256,1280]{1,0:T(8,128)(2,1)} %bitcast.26), custom_call_target="tpu_custom_call" | custom-call | bytes 2000000 | tf_op jit(solution)/shard_map/pack/pallas_call | solution.py:501
  3.7 3.3 %collective-permute-start = (bf16[784,640]{1,0:T(8,128)(2,1)S(1)}, bf16[784,640]{1,0:T(8,128)(2,1)S(1)}, u32[]{:S(2)}, u32[]{:S(2)}) collective-permute-start(bf16[784,640]{1,0:T(8,128)(2,1)S(1)} %pack.1), channel_id=1, source_target_pairs={{0,1},{1,0},{2,3},{3,2},{4,5},{5,4},{6,7},{7,6},{8,9},{9,8},{10,11... | collective-permute-start | bytes 3010568 | tf_op jit(solution)/shard_map/ppermute | solution.py:56
  7.0 0.0 copy-done.1
  7.0 1.7 %own.1 = (bf16[2,2,256,640]{3,2,1,0:T(8,128)(2,1)S(1)}, bf16[2,272,640]{2,1,0:T(8,128)(2,1)S(1)}) custom-call(s32[1]{0:T(128)} %bitcast.10.me_ref, s32[8]{0:T(128)S(1)} %bitcast.21, s32[1]{0:T(128)} %bitcast.19.count_ref, bf16[256,1280]{1,0:T(8,128)(2,1)} %bitcast.23, bf16[256,1280]{1,0:T(8,128)(2,1)} %bitcast.25, bf16[256,1280]{1,0:T(8,128)(2,1)} %bitcast.27), custom_call_target="tpu_custom_call" | custom-call | bytes 2000000 | tf_op jit(solution)/shard_map/own/pallas_call | solution.py:513
  8.7 0.5 collective-permute-done.mate_ref
  9.2 0.4 merge.1
  9.6 1.1 %collective-permute-start.4 = (bf16[2,2,256,640]{3,2,1,0:T(8,128)(2,1)S(1)}, bf16[2,2,256,640]{3,2,1,0:T(8,128)(2,1)S(1)}, u32[]{:S(2)}, u32[]{:S(2)}) collective-permute-start(bf16[2,2,256,640]{3,2,1,0:T(8,128)(2,1)S(1)} %get-tuple-element.35.refs_1_), channel_id=1, source_target_pairs={{0,24},{1,7},{2,26},{3,1},{4,28},{5,3},{6,30},{7,5},{8,0},{9,15},{... | collective-permute-start | bytes 3932168 | tf_op jit(solution)/shard_map/ppermute | solution.py:52
  10.7 5.5 %state.1 = bf16[20,160,128]{2,1,0:T(8,128)(2,1)} custom-call(bf16[320,256]{1,0:T(8,128)(2,1)} %bitcast.34, bf16[256,2560]{1,0:T(8,128)(2,1)} %bitcast.31, bf16[4,320,64]{2,1,0:T(8,128)(2,1)} %constant.13.clone.select_ref, f32[3,160,128]{2,1,0:T(8,128)} %constant.14.clone.vector_ref), custom_call_target="tpu_custom_call" | custom-call | flops 1000000000 | bytes 4000000 | tf_op jit(solution)/shard_map/state/pallas_call | solution.py:542
  16.1 8.2 %all-to-all-start = ((bf16[8,400,128]{2,1,0:T(8,128)(2,1)}), bf16[8,400,128]{2,1,0:T(8,128)(2,1)}, u32[]{:S(2)}, u32[]{:S(2)}) async-start(bf16[8,400,128]{2,1,0:T(8,128)(2,1)} %bitcast.29), calls=%async_computation | async-start | bytes 1638400 | tf_op jit(solution)/shard_map/all_to_all | solution.py:552
  24.3 1.2 %collective-permute-start.1 = (bf16[2,272,640]{2,1,0:T(8,128)(2,1)S(1)}, bf16[2,272,640]{2,1,0:T(8,128)(2,1)}, u32[]{:S(2)}, u32[]{:S(2)}) collective-permute-start(bf16[2,272,640]{2,1,0:T(8,128)(2,1)S(1)} %get-tuple-element.38.refs_3_.refs_0_), channel_id=1, source_target_pairs={{0,2},{1,9},{2,4},{3,11},{4,6},{5,13},{6,0},{7,15},{8,10},{9,17},{... | collective-permute-start | bytes 2088968 | tf_op jit(solution)/shard_map/ppermute | solution.py:52
  25.5 0.0 collective-permute-start.6
  25.5 0.9 collective-permute-done.4.refs_2_
  26.4 1.9 %collective-permute-start.5 = (bf16[2,2,256,640]{3,2,1,0:T(8,128)(2,1)S(1)}, bf16[2,2,256,640]{3,2,1,0:T(8,128)(2,1)}, u32[]{:S(2)}, u32[]{:S(2)}) collective-permute-start(bf16[2,2,256,640]{3,2,1,0:T(8,128)(2,1)S(1)} %collective-permute-done.4.refs_2_), channel_id=1, source_target_pairs={{0,24},{1,7},{2,26},{3,1},{4,28},{5,3},{6,30},{7,5},{8,0},{9,15},{... | collective-permute-start | bytes 3932168 | tf_op jit(solution)/shard_map/ppermute | solution.py:52
  28.3 2.8 %collective-permute-start.3 = (bf16[2,272,640]{2,1,0:T(8,128)(2,1)S(1)}, bf16[2,272,640]{2,1,0:T(8,128)(2,1)}, u32[]{:S(2)}, u32[]{:S(2)}) collective-permute-start(bf16[2,272,640]{2,1,0:T(8,128)(2,1)S(1)} %get-tuple-element.38.refs_3_.refs_0_), channel_id=1, source_target_pairs={{0,6},{1,25},{2,0},{3,27},{4,2},{5,29},{6,4},{7,31},{8,14},{9,1},{... | collective-permute-start | bytes 2088968 | tf_op jit(solution)/shard_map/ppermute | solution.py:52
  31.1 9.4 %collective-permute-done.1.refs_1_.refs_0_ = bf16[2,272,640]{2,1,0:T(8,128)(2,1)} collective-permute-done((bf16[2,272,640]{2,1,0:T(8,128)(2,1)S(1)}, bf16[2,272,640]{2,1,0:T(8,128)(2,1)}, u32[]{:S(2)}, u32[]{:S(2)}) %collective-permute-start.1) | collective-permute-done | bytes 696352 | tf_op jit(solution)/shard_map/ppermute | solution.py:52
  40.5 1.5 %collective-permute-start.2 = (bf16[2,272,640]{2,1,0:T(8,128)(2,1)}, bf16[2,272,640]{2,1,0:T(8,128)(2,1)}, u32[]{:S(2)}, u32[]{:S(2)}) collective-permute-start(bf16[2,272,640]{2,1,0:T(8,128)(2,1)} %collective-permute-done.1.refs_1_.refs_0_), channel_id=1, source_target_pairs={{0,2},{1,9},{2,4},{3,11},{4,6},{5,13},{6,0},{7,15},{8,10},{9,17},{... | collective-permute-start | bytes 2088968 | tf_op jit(solution)/shard_map/ppermute | solution.py:52
  42.0 6.8 %local.1 = (bf16[256,2560]{1,0:T(8,128)(2,1)}, f32[256,128]{1,0:T(8,128)}, bf16[20,160,256]{2,1,0:T(8,128)(2,1)}) custom-call(bf16[320,256]{1,0:T(8,128)(2,1)} %bitcast.33, bf16[320,256]{1,0:T(8,128)(2,1)} %bitcast.35, bf16[256,2560]{1,0:T(8,128)(2,1)} %bitcast.32, bf16[4,320,64]{2,1,0:T(8,128)(2,1)} %constant.13.clone.select_ref, ...), custom_call_target="tpu_custom_call" | custom-call | flops 4000000000 | bytes 8000000 | tf_op jit(solution)/shard_map/local/pallas_call | solution.py:554
  48.8 0.0 all-to-all-done.in_ref
  48.8 2.8 %prefix.1 = bf16[8,400,128]{2,1,0:T(8,128)(2,1)} custom-call(s32[1]{0:T(128)} %bitcast.7.place_ref, bf16[8,400,128]{2,1,0:T(8,128)(2,1)} %all-to-all-done.in_ref), custom_call_target="tpu_custom_call" | custom-call | bytes 2000000 | tf_op jit(solution)/shard_map/prefix/pallas_call | solution.py:567
  51.7 6.3 %all-to-all-start.1 = ((bf16[8,400,128]{2,1,0:T(8,128)(2,1)}), bf16[8,400,128]{2,1,0:T(8,128)(2,1)}, u32[]{:S(2)}, u32[]{:S(2)}) async-start(bf16[8,400,128]{2,1,0:T(8,128)(2,1)} %prefix.1), calls=%async_computation.1 | async-start | bytes 1638400 | tf_op jit(solution)/shard_map/all_to_all | solution.py:576
  58.0 0.0 collective-permute-done.3.refs_2_.refs_0_
  58.0 0.0 collective-permute-done.2.refs_0_
  58.0 2.4 %search.1 = (s32[8,128]{1,0:T(8,128)S(1)}, s32[8]{0:T(128)S(1)}) custom-call(s32[1]{0:T(128)} %bitcast.10.me_ref, bf16[2,272,640]{2,1,0:T(8,128)(2,1)} %collective-permute-done.2.refs_0_, bf16[2,272,640]{2,1,0:T(8,128)(2,1)} %collective-permute-done.1.refs_1_.refs_0_, bf16[2,272,640]{2,1,0:T(8,128)(2,1)} %collective-permute-done.3.refs_2_.refs_0_, ...), custom_call_target="tpu_custom_call" | custom-call | bytes 100000 | tf_op jit(solution)/shard_map/search/pallas_call | solution.py:577
  60.4 0.0 collective-permute-done.6.refs_4_
  60.4 0.0 collective-permute-done.5.refs_3_
  60.4 4.1 %shard_map.113 = bf16[2,272,640]{2,1,0:T(8,128)(2,1)S(1)} custom-call(s32[8,128]{1,0:T(8,128)S(1)} %get-tuple-element.33.found, s32[8]{0:T(128)S(1)} %get-tuple-element.34.counts, bf16[2,272,640]{2,1,0:T(8,128)(2,1)} %collective-permute-done.2.refs_0_, bf16[2,2,256,640]{3,2,1,0:T(8,128)(2,1)S(1)} %get-tuple-element.35.refs_1_, ...), custom_call_target="tpu_custom_call" | custom-call | flops 800000000 | bytes 8000000 | tf_op jit(solution)/shard_map/pallas_call | solution.py:472
  64.5 4.1 %shard_map.114 = bf16[2,272,640]{2,1,0:T(8,128)(2,1)S(1)} custom-call(s32[8,128]{1,0:T(8,128)S(1)} %get-tuple-element.33.found, s32[8]{0:T(128)S(1)} %get-tuple-element.34.counts, bf16[2,272,640]{2,1,0:T(8,128)(2,1)} %collective-permute-done.1.refs_1_.refs_0_, bf16[2,2,256,640]{3,2,1,0:T(8,128)(2,1)S(1)} %get-tuple-element.35.refs_1_, ...), custom_call_target="tpu_custom_call" | custom-call | flops 800000000 | bytes 8000000 | tf_op jit(solution)/shard_map/pallas_call | solution.py:472
  68.6 4.0 %shard_map.115 = bf16[2,272,640]{2,1,0:T(8,128)(2,1)S(1)} custom-call(s32[8,128]{1,0:T(8,128)S(1)} %get-tuple-element.33.found, s32[8]{0:T(128)S(1)} %get-tuple-element.34.counts, bf16[2,272,640]{2,1,0:T(8,128)(2,1)} %collective-permute-done.3.refs_2_.refs_0_, bf16[2,2,256,640]{3,2,1,0:T(8,128)(2,1)S(1)} %get-tuple-element.35.refs_1_, ...), custom_call_target="tpu_custom_call" | custom-call | flops 800000000 | bytes 8000000 | tf_op jit(solution)/shard_map/pallas_call | solution.py:472
  72.6 2.8 %collective-permute-start.8 = (bf16[2,272,640]{2,1,0:T(8,128)(2,1)S(1)}, bf16[2,272,640]{2,1,0:T(8,128)(2,1)S(1)}, u32[]{:S(2)}, u32[]{:S(2)}) collective-permute-start(bf16[2,272,640]{2,1,0:T(8,128)(2,1)S(1)} %shard_map.115), channel_id=1, source_target_pairs={{0,2},{1,9},{2,4},{3,11},{4,6},{5,13},{6,0},{7,15},{8,10},{9,17},{... | collective-permute-start | bytes 2088968 | tf_op jit(solution)/shard_map/ppermute | solution.py:52
  75.4 2.3 %collective-permute-start.7 = (bf16[2,272,640]{2,1,0:T(8,128)(2,1)S(1)}, bf16[2,272,640]{2,1,0:T(8,128)(2,1)S(1)}, u32[]{:S(2)}, u32[]{:S(2)}) collective-permute-start(bf16[2,272,640]{2,1,0:T(8,128)(2,1)S(1)} %shard_map.114), channel_id=1, source_target_pairs={{0,6},{1,25},{2,0},{3,27},{4,2},{5,29},{6,4},{7,31},{8,14},{9,1},{... | collective-permute-start | bytes 2088968 | tf_op jit(solution)/shard_map/ppermute | solution.py:52
  77.7 1.1 %collective-permute-start.9 = (bf16[2,272,640]{2,1,0:T(8,128)(2,1)S(1)}, bf16[2,272,640]{2,1,0:T(8,128)(2,1)S(1)}, u32[]{:S(2)}, u32[]{:S(2)}) collective-permute-start(bf16[2,272,640]{2,1,0:T(8,128)(2,1)S(1)} %shard_map.113), channel_id=1, source_target_pairs={{0,4},{1,17},{2,6},{3,19},{4,0},{5,21},{6,2},{7,23},{8,12},{9,25},... | collective-permute-start | bytes 2088968 | tf_op jit(solution)/shard_map/ppermute | solution.py:52
  78.8 5.5 %shard_map.116.refs_0_ = bf16[2,272,640]{2,1,0:T(8,128)(2,1)S(1)} custom-call(s32[8,128]{1,0:T(8,128)S(1)} %get-tuple-element.33.found, s32[8]{0:T(128)S(1)} %get-tuple-element.34.counts, bf16[2,272,640]{2,1,0:T(8,128)(2,1)S(1)} %get-tuple-element.38.refs_3_.refs_0_, bf16[2,2,256,640]{3,2,1,0:T(8,128)(2,1)S(1)} %get-tuple-element.35.refs_1_, ...), custom_call_target="tpu_custom_call" | custom-call | flops 800000000 | bytes 8000000 | tf_op jit(solution)/shard_map/pallas_call | solution.py:472
  84.3 2.0 %collective-permute-done.8.refs_2_ = bf16[2,272,640]{2,1,0:T(8,128)(2,1)S(1)} collective-permute-done((bf16[2,272,640]{2,1,0:T(8,128)(2,1)S(1)}, bf16[2,272,640]{2,1,0:T(8,128)(2,1)S(1)}, u32[]{:S(2)}, u32[]{:S(2)}) %collective-permute-start.8) | collective-permute-done | bytes 696352 | tf_op jit(solution)/shard_map/ppermute | solution.py:52
  86.3 6.8 %collective-permute-done.7.refs_1_ = bf16[2,272,640]{2,1,0:T(8,128)(2,1)S(1)} collective-permute-done((bf16[2,272,640]{2,1,0:T(8,128)(2,1)S(1)}, bf16[2,272,640]{2,1,0:T(8,128)(2,1)S(1)}, u32[]{:S(2)}, u32[]{:S(2)}) %collective-permute-start.7) | collective-permute-done | bytes 696352 | tf_op jit(solution)/shard_map/ppermute | solution.py:52
  93.2 1.8 %collective-permute-done.9.refs_3_ = bf16[2,272,640]{2,1,0:T(8,128)(2,1)S(1)} collective-permute-done((bf16[2,272,640]{2,1,0:T(8,128)(2,1)S(1)}, bf16[2,272,640]{2,1,0:T(8,128)(2,1)S(1)}, u32[]{:S(2)}, u32[]{:S(2)}) %collective-permute-start.9) | collective-permute-done | bytes 696352 | tf_op jit(solution)/shard_map/ppermute | solution.py:52
  95.0 2.0 %join.1 = (bf16[256,640]{1,0:T(8,128)(2,1)S(1)}, bf16[256,640]{1,0:T(8,128)(2,1)S(1)}) custom-call(bf16[2,272,640]{2,1,0:T(8,128)(2,1)S(1)} %shard_map.116.refs_0_, bf16[2,272,640]{2,1,0:T(8,128)(2,1)S(1)} %collective-permute-done.7.refs_1_, bf16[2,272,640]{2,1,0:T(8,128)(2,1)S(1)} %collective-permute-done.8.refs_2_, ...), custom_call_target="tpu_custom_call" | custom-call | bytes 4000000 | tf_op jit(solution)/shard_map/join/pallas_call | solution.py:601
  97.0 4.5 %collective-permute-start.10 = (bf16[256,640]{1,0:T(8,128)(2,1)S(1)}, bf16[256,640]{1,0:T(8,128)(2,1)S(1)}, u32[]{:S(2)}, u32[]{:S(2)}) collective-permute-start(bf16[256,640]{1,0:T(8,128)(2,1)S(1)} %get-tuple-element.43), channel_id=1, source_target_pairs={{0,1},{1,0},{2,3},{3,2},{4,5},{5,4},{6,7},{7,6},{8,9},{9,8},{10,11... | collective-permute-start | bytes 983048 | tf_op jit(solution)/shard_map/ppermute | solution.py:56
  101.6 0.0 all-to-all-done.1
  101.6 5.6 %finish.1 = bf16[256,2560]{1,0:T(8,128)(2,1)} custom-call(bf16[256,2560]{1,0:T(8,128)(2,1)} %get-tuple-element.26.num_ref, f32[256,128]{1,0:T(8,128)} %get-tuple-element.27.den_ref, bf16[20,160,256]{2,1,0:T(8,128)(2,1)} %get-tuple-element.28.phi_ref, bf16[20,160,128]{2,1,0:T(8,128)(2,1)} %bitcast.8.state_ref), custom_call_target="tpu_custom_call" | custom-call | flops 400000000 | bytes 8000000 | tf_op jit(solution)/shard_map/finish/pallas_call | solution.py:623
  107.2 0.0 collective-permute-done.10.other_ref
  107.2 0.8 place.1
Async XLA Ops:
  1.3 0.7 copy-start
  1.9 5.0 %copy-start.1 = (s32[1,1,8]{2,1,0:T(1,128)S(1)}, s32[1,1,8]{2,1,0:T(1,128)}, u32[]{:S(2)}) copy-start(s32[1,1,8]{2,1,0:T(1,128)} %param.16) | copy-start | bytes 100
  3.7 5.5 %collective-permute-start = (bf16[784,640]{1,0:T(8,128)(2,1)S(1)}, bf16[784,640]{1,0:T(8,128)(2,1)S(1)}, u32[]{:S(2)}, u32[]{:S(2)}) collective-permute-start(bf16[784,640]{1,0:T(8,128)(2,1)S(1)} %pack.1), channel_id=1, source_target_pairs={{0,1},{1,0},{2,3},{3,2},{4,5},{5,4},{6,7},{7,6},{8,9},{9,8},{10,11... | collective-permute-start | bytes 3010568 | tf_op jit(solution)/shard_map/ppermute | solution.py:56
  9.6 16.8 %collective-permute-start.4 = (bf16[2,2,256,640]{3,2,1,0:T(8,128)(2,1)S(1)}, bf16[2,2,256,640]{3,2,1,0:T(8,128)(2,1)S(1)}, u32[]{:S(2)}, u32[]{:S(2)}) collective-permute-start(bf16[2,2,256,640]{3,2,1,0:T(8,128)(2,1)S(1)} %get-tuple-element.35.refs_1_), channel_id=1, source_target_pairs={{0,24},{1,7},{2,26},{3,1},{4,28},{5,3},{6,30},{7,5},{8,0},{9,15},{... | collective-permute-start | bytes 3932168 | tf_op jit(solution)/shard_map/ppermute | solution.py:52
  16.1 32.7 %all-to-all-start = ((bf16[8,400,128]{2,1,0:T(8,128)(2,1)}), bf16[8,400,128]{2,1,0:T(8,128)(2,1)}, u32[]{:S(2)}, u32[]{:S(2)}) async-start(bf16[8,400,128]{2,1,0:T(8,128)(2,1)} %bitcast.29), calls=%async_computation | async-start | bytes 1638400 | tf_op jit(solution)/shard_map/all_to_all | solution.py:552
  24.3 16.2 %collective-permute-start.1 = (bf16[2,272,640]{2,1,0:T(8,128)(2,1)S(1)}, bf16[2,272,640]{2,1,0:T(8,128)(2,1)}, u32[]{:S(2)}, u32[]{:S(2)}) collective-permute-start(bf16[2,272,640]{2,1,0:T(8,128)(2,1)S(1)} %get-tuple-element.38.refs_3_.refs_0_), channel_id=1, source_target_pairs={{0,2},{1,9},{2,4},{3,11},{4,6},{5,13},{6,0},{7,15},{8,10},{9,17},{... | collective-permute-start | bytes 2088968 | tf_op jit(solution)/shard_map/ppermute | solution.py:52
  25.5 34.9 %collective-permute-start.6 = (bf16[2,2,256,640]{3,2,1,0:T(8,128)(2,1)S(1)}, bf16[2,2,256,640]{3,2,1,0:T(8,128)(2,1)}, u32[]{:S(2)}, u32[]{:S(2)}) collective-permute-start(bf16[2,2,256,640]{3,2,1,0:T(8,128)(2,1)S(1)} %get-tuple-element.35.refs_1_), channel_id=1, source_target_pairs={{0,8},{1,3},{2,10},{3,5},{4,12},{5,7},{6,14},{7,1},{8,16},{9,11},{... | collective-permute-start | bytes 3932168 | tf_op jit(solution)/shard_map/ppermute | solution.py:52
  26.4 34.0 %collective-permute-start.5 = (bf16[2,2,256,640]{3,2,1,0:T(8,128)(2,1)S(1)}, bf16[2,2,256,640]{3,2,1,0:T(8,128)(2,1)}, u32[]{:S(2)}, u32[]{:S(2)}) collective-permute-start(bf16[2,2,256,640]{3,2,1,0:T(8,128)(2,1)S(1)} %collective-permute-done.4.refs_2_), channel_id=1, source_target_pairs={{0,24},{1,7},{2,26},{3,1},{4,28},{5,3},{6,30},{7,5},{8,0},{9,15},{... | collective-permute-start | bytes 3932168 | tf_op jit(solution)/shard_map/ppermute | solution.py:52
  28.3 29.6 %collective-permute-start.3 = (bf16[2,272,640]{2,1,0:T(8,128)(2,1)S(1)}, bf16[2,272,640]{2,1,0:T(8,128)(2,1)}, u32[]{:S(2)}, u32[]{:S(2)}) collective-permute-start(bf16[2,272,640]{2,1,0:T(8,128)(2,1)S(1)} %get-tuple-element.38.refs_3_.refs_0_), channel_id=1, source_target_pairs={{0,6},{1,25},{2,0},{3,27},{4,2},{5,29},{6,4},{7,31},{8,14},{9,1},{... | collective-permute-start | bytes 2088968 | tf_op jit(solution)/shard_map/ppermute | solution.py:52
  40.5 17.5 %collective-permute-start.2 = (bf16[2,272,640]{2,1,0:T(8,128)(2,1)}, bf16[2,272,640]{2,1,0:T(8,128)(2,1)}, u32[]{:S(2)}, u32[]{:S(2)}) collective-permute-start(bf16[2,272,640]{2,1,0:T(8,128)(2,1)} %collective-permute-done.1.refs_1_.refs_0_), channel_id=1, source_target_pairs={{0,2},{1,9},{2,4},{3,11},{4,6},{5,13},{6,0},{7,15},{8,10},{9,17},{... | collective-permute-start | bytes 2088968 | tf_op jit(solution)/shard_map/ppermute | solution.py:52
  51.7 49.9 %all-to-all-start.1 = ((bf16[8,400,128]{2,1,0:T(8,128)(2,1)}), bf16[8,400,128]{2,1,0:T(8,128)(2,1)}, u32[]{:S(2)}, u32[]{:S(2)}) async-start(bf16[8,400,128]{2,1,0:T(8,128)(2,1)} %prefix.1), calls=%async_computation.1 | async-start | bytes 1638400 | tf_op jit(solution)/shard_map/all_to_all | solution.py:576
  72.6 13.7 %collective-permute-start.8 = (bf16[2,272,640]{2,1,0:T(8,128)(2,1)S(1)}, bf16[2,272,640]{2,1,0:T(8,128)(2,1)S(1)}, u32[]{:S(2)}, u32[]{:S(2)}) collective-permute-start(bf16[2,272,640]{2,1,0:T(8,128)(2,1)S(1)} %shard_map.115), channel_id=1, source_target_pairs={{0,2},{1,9},{2,4},{3,11},{4,6},{5,13},{6,0},{7,15},{8,10},{9,17},{... | collective-permute-start | bytes 2088968 | tf_op jit(solution)/shard_map/ppermute | solution.py:52
  75.4 17.7 %collective-permute-start.7 = (bf16[2,272,640]{2,1,0:T(8,128)(2,1)S(1)}, bf16[2,272,640]{2,1,0:T(8,128)(2,1)S(1)}, u32[]{:S(2)}, u32[]{:S(2)}) collective-permute-start(bf16[2,272,640]{2,1,0:T(8,128)(2,1)S(1)} %shard_map.114), channel_id=1, source_target_pairs={{0,6},{1,25},{2,0},{3,27},{4,2},{5,29},{6,4},{7,31},{8,14},{9,1},{... | collective-permute-start | bytes 2088968 | tf_op jit(solution)/shard_map/ppermute | solution.py:52
  77.7 17.3 %collective-permute-start.9 = (bf16[2,272,640]{2,1,0:T(8,128)(2,1)S(1)}, bf16[2,272,640]{2,1,0:T(8,128)(2,1)S(1)}, u32[]{:S(2)}, u32[]{:S(2)}) collective-permute-start(bf16[2,272,640]{2,1,0:T(8,128)(2,1)S(1)} %shard_map.113), channel_id=1, source_target_pairs={{0,4},{1,17},{2,6},{3,19},{4,0},{5,21},{6,2},{7,23},{8,12},{9,25},... | collective-permute-start | bytes 2088968 | tf_op jit(solution)/shard_map/ppermute | solution.py:52
  97.0 10.2 %collective-permute-start.10 = (bf16[256,640]{1,0:T(8,128)(2,1)S(1)}, bf16[256,640]{1,0:T(8,128)(2,1)S(1)}, u32[]{:S(2)}, u32[]{:S(2)}) collective-permute-start(bf16[256,640]{1,0:T(8,128)(2,1)S(1)} %get-tuple-element.43), channel_id=1, source_target_pairs={{0,1},{1,0},{2,3},{3,2},{4,5},{5,4},{6,7},{7,6},{8,9},{9,8},{10,11... | collective-permute-start | bytes 983048 | tf_op jit(solution)/shard_map/ppermute | solution.py:56
